TPU v7x, 32 devices: a whole 2x2x4 slice. The times are simulated.
32 devices in a mesh: ctx: 16 (over z, y, core), fsdp: 2 (over x).
Axes of the slice: x: 2, y: 2, z: 4, core: 2. Of those that a mesh axis runs over, the one named last changes fastest.
Arguments:
- hidden_in: bfloat16 [2, 2048, 768], P('fsdp', 'ctx'), may hold values from -6 to 6
- segment_ids: int32 [2, 2048], P('fsdp', 'ctx'), may hold values from 0 to 3, never falling along the last dimension, each value on 1 to 1024 neighbouring positions
- token_types: int32 [2, 2048], P('fsdp', 'ctx'), may hold values from 0 to 1
- out_grad: bfloat16 [2, 2048, 768], P('fsdp', 'ctx'), may hold values from -6 to 6
- query_proj: bfloat16 [768, 768], P('fsdp'), may hold values from -0.21875 to 0.21875
- key_proj: bfloat16 [768, 768], P('fsdp'), may hold values from -0.21875 to 0.21875
- value_proj: bfloat16 [768, 768], P('fsdp'), may hold values from -0.21875 to 0.21875
- value_bias: bfloat16 [768], P('fsdp'), may hold values from -0.1796875 to 0.1796875
- content_bias: bfloat16 [768], P('fsdp'), may hold values from -3 to 3
- position_bias: bfloat16 [768], P('fsdp'), may hold values from -3 to 3
- type_bias: bfloat16 [768], P('fsdp'), may hold values from -3 to 3
- type_embed: bfloat16 [2, 768], P(None, 'fsdp'), may hold values from -6 to 6
- position_proj: bfloat16 [768, 768], P('fsdp'), may hold values from -0.21875 to 0.21875
- output_proj: bfloat16 [768, 768], P('fsdp'), may hold values from -2 to 2
- output_bias: bfloat16 [768], P('fsdp'), may hold values from -1.796875 to 1.796875
- attn_gain: bfloat16 [768], P('fsdp'), may hold values from 0.5 to 1.5
- attn_shift: bfloat16 [768], P('fsdp'), may hold values from -1.796875 to 1.796875
- inner_proj: bfloat16 [768, 3072], P('fsdp'), may hold values from -0.21875 to 0.21875
- inner_bias: bfloat16 [3072], P('fsdp'), may hold values from -1.796875 to 1.796875
- outer_proj: bfloat16 [3072, 768], P('fsdp'), may hold values from -0.109375 to 0.109375
- outer_bias: bfloat16 [768], P('fsdp'), may hold values from -1.796875 to 1.796875
- ffn_gain: bfloat16 [768], P('fsdp'), may hold values from 0.5 to 1.5
- ffn_shift: bfloat16 [768], P('fsdp'), may hold values from -1.796875 to 1.796875
Outputs:
- result: bfloat16 [2, 2048, 768], P('fsdp', 'ctx')
- input_grad: float32 [2, 2048, 768], P('fsdp', 'ctx')
- grad_query_proj: float32 [768, 768], P('fsdp')
- grad_key_proj: float32 [768, 768], P('fsdp')
- grad_value_proj: float32 [768, 768], P('fsdp')
- grad_value_bias: float32 [768], P('fsdp')
- grad_content_bias: float32 [768], P('fsdp')
- grad_position_bias: float32 [768], P('fsdp')
- grad_type_bias: float32 [768], P('fsdp')
- grad_type_embed: float32 [2, 768], P(None, 'fsdp')
- grad_position_proj: float32 [768, 768], P('fsdp')
- grad_output_proj: float32 [768, 768], P('fsdp')
- grad_output_bias: float32 [768], P('fsdp')
- grad_attn_gain: float32 [768], P('fsdp')
- grad_attn_shift: float32 [768], P('fsdp')
- grad_inner_proj: float32 [768, 3072], P('fsdp')
- grad_inner_bias: float32 [3072], P('fsdp')
- grad_outer_proj: float32 [3072, 768], P('fsdp')
- grad_outer_bias: float32 [768], P('fsdp')
- grad_ffn_gain: float32 [768], P('fsdp')
- grad_ffn_shift: float32 [768], P('fsdp')
Inputs may be any that keep to these rules, and one draw needn't show every extreme that they name: `segment_ids`: along a sequence the document number never falls; a document holds at most 1024 tokens and one holds exactly 1024.
All inputs are finite; a program needn't handle non-finite values.
Results may differ from a plain program's by a relative error of at most 0.03.
Values may be sent and summed in bfloat16 or wider, within the bound.
No kernel may reach another device: no remote copies, remote signals or barrier semaphores. Data moves between devices by JAX's collectives and lax.ppermute only.
A program may use at most 256 MiB of HBM per device.

v0:
```python
from functools import partial

import jax
import jax.numpy as jnp
from jax import lax
from jax.sharding import PartitionSpec as P

H = 12
DH = 64


EPS = 1e-06
NEG_BIG = -1e30
HIGH = lax.Precision.HIGHEST


def for_sending(array):

    def short(part):
        return part.astype(jnp.bfloat16) if part.dtype == jnp.float32 else part

    return jax.tree.map(short, array)


def product(left, right):
    return jnp.dot(left, right, preferred_element_type=jnp.float32)


def inner_rows(left, right):
    return lax.dot_general(
        left, right, (((0,), (0,)), ((), ())), preferred_element_type=jnp.float32
    )


def inner_rows_high(left, right):
    return lax.dot_general(
        left, right, (((0,), (0,)), ((), ())), precision=HIGH, preferred_element_type=jnp.float32
    )


def layer_norm(residual, gain_vec, bias_vec):
    center = residual - jnp.mean(residual, axis=-1, keepdims=True)
    spread = jnp.mean(center * center, axis=-1, keepdims=True)
    return center * lax.rsqrt(spread + EPS) * gain_vec + bias_vec


def sinusoid(offsets, span_width):
    half_width = span_width // 2
    frequency = jnp.power(10000.0, -jnp.arange(half_width, dtype=jnp.float32) / half_width)
    angles = offsets[:, None] * frequency[None, :]
    return jnp.concatenate([jnp.sin(angles), jnp.cos(angles)], axis=1)


def rel_shift(full_scores, query_rows, key_cols):
    heads_count = full_scores.shape[0]
    span_width = full_scores.shape[2]
    flat_scores = full_scores.reshape(heads_count, query_rows * span_width)
    flat_scores = flat_scores[:, query_rows - 1 : query_rows - 1 + query_rows * (span_width - 1)]
    return flat_scores.reshape(heads_count, query_rows, span_width - 1)[:, :, :key_cols]


def rel_unshift(grad_scores, query_rows, key_cols):
    heads_count = grad_scores.shape[0]
    span_width = query_rows + key_cols
    padded = jnp.pad(grad_scores, ((0, 0), (0, 0), (0, span_width - 1 - key_cols)))
    flat_grads = padded.reshape(heads_count, query_rows * (span_width - 1))
    flat_grads = jnp.pad(flat_grads, ((0, 0), (query_rows - 1, 1)))
    return flat_grads.reshape(heads_count, query_rows, span_width)


def per_device(
    hidden_in,
    segment_ids,
    token_types,
    out_grad,
    query_proj,
    key_proj,
    value_proj,
    value_bias,
    content_bias,
    position_bias,
    type_bias,
    type_embed,
    position_proj,
    output_proj,
    output_bias,
    attn_gain,
    attn_shift,
    inner_proj,
    inner_bias,
    outer_proj,
    outer_bias,
    ffn_gain,
    ffn_shift,
):
    (
        full_query,
        full_key,
        full_value,
        full_value_bias,
        full_content_bias,
        full_position_bias,
        full_type_bias,
        full_type_embed,
        full_position,
        full_output,
        full_output_bias,
        full_attn_gain,
        full_attn_shift,
        full_inner,
        full_inner_bias,
        full_outer,
        full_outer_bias,
        full_ffn_gain,
        full_ffn_shift,
    ) = (
        lax.all_gather(query_proj, "fsdp", axis=0, tiled=True),
        lax.all_gather(key_proj, "fsdp", axis=0, tiled=True),
        lax.all_gather(value_proj, "fsdp", axis=0, tiled=True),
        lax.all_gather(value_bias, "fsdp", axis=0, tiled=True),
        lax.all_gather(content_bias, "fsdp", axis=0, tiled=True),
        lax.all_gather(position_bias, "fsdp", axis=0, tiled=True),
        lax.all_gather(type_bias, "fsdp", axis=0, tiled=True),
        lax.all_gather(type_embed, "fsdp", axis=1, tiled=True),
        lax.all_gather(position_proj, "fsdp", axis=0, tiled=True),
        lax.all_gather(output_proj, "fsdp", axis=0, tiled=True),
        lax.all_gather(output_bias, "fsdp", axis=0, tiled=True),
        lax.all_gather(attn_gain, "fsdp", axis=0, tiled=True),
        lax.all_gather(attn_shift, "fsdp", axis=0, tiled=True),
        lax.all_gather(inner_proj, "fsdp", axis=0, tiled=True),
        lax.all_gather(inner_bias, "fsdp", axis=0, tiled=True),
        lax.all_gather(outer_proj, "fsdp", axis=0, tiled=True),
        lax.all_gather(outer_bias, "fsdp", axis=0, tiled=True),
        lax.all_gather(ffn_gain, "fsdp", axis=0, tiled=True),
        lax.all_gather(ffn_shift, "fsdp", axis=0, tiled=True),
    )
    hidden = hidden_in[0]
    cotangent = out_grad[0].astype(jnp.float32)
    rows_local = hidden.shape[0]
    width_model = hidden.shape[1]
    ctx_count = lax.axis_size("ctx")
    ctx_index = lax.axis_index("ctx")
    length = rows_local * ctx_count
    first_query = ctx_index * rows_local
    score_scale = DH ** (-0.5)
    query_lin = product(hidden, full_query)
    keys_local = product(hidden, full_key).astype(jnp.bfloat16)
    values_local = (product(hidden, full_value) + full_value_bias.astype(jnp.float32)).astype(
        jnp.bfloat16
    )
    content_query = ((query_lin + full_content_bias.astype(jnp.float32)) * score_scale).astype(
        jnp.bfloat16
    )
    position_query = ((query_lin + full_position_bias.astype(jnp.float32)) * score_scale).astype(
        jnp.bfloat16
    )
    type_query = (query_lin + full_type_bias.astype(jnp.float32)) * score_scale
    table_index = ctx_index * (2 * rows_local) + jnp.arange(2 * rows_local, dtype=jnp.int32)
    offsets = (length - 1 - table_index).astype(jnp.float32)
    sinus_low = sinusoid(offsets, width_model).astype(jnp.bfloat16)
    table_local = product(sinus_low, full_position).astype(jnp.bfloat16)
    segs_local = segment_ids[0].astype(jnp.bfloat16)
    kinds_local = token_types[0].astype(jnp.bfloat16)
    sources = (
        lax.all_gather(keys_local, "ctx", axis=0, tiled=True),
        lax.all_gather(values_local, "ctx", axis=0, tiled=True),
        lax.all_gather(table_local, "ctx", axis=0, tiled=True),
        lax.all_gather(segs_local, "ctx", axis=0, tiled=True),
        lax.all_gather(kinds_local, "ctx", axis=0, tiled=True),
    )
    embed_f = full_type_embed.astype(jnp.float32)
    type_heads = type_query.reshape(rows_local, H, DH)
    type_terms = jnp.sum(
        type_heads.reshape(rows_local, 1, H, DH) * embed_f.reshape(1, 2, H, DH), axis=3
    )
    type_zero = jnp.transpose(type_terms[:, 0, :])
    type_one = jnp.transpose(type_terms[:, 1, :])
    content_heads = content_query.reshape(rows_local, H, DH)
    position_heads = position_query.reshape(rows_local, H, DH)
    key_block = min(512, length)
    block_count = length // key_block
    span_width = rows_local + key_block
    starts = jnp.arange(block_count, dtype=jnp.int32) * key_block

    def block_scores(key_start, arrays):
        keys_all, values_all, table_all, segs_all, kinds_all = arrays
        key_heads = lax.dynamic_slice_in_dim(keys_all, key_start, key_block, 0).reshape(
            key_block, H, DH
        )
        value_heads = lax.dynamic_slice_in_dim(values_all, key_start, key_block, 0).reshape(
            key_block, H, DH
        )
        table_start = length - rows_local - first_query + key_start
        table_block = lax.dynamic_slice_in_dim(table_all, table_start, span_width, 0).reshape(
            span_width, H, DH
        )
        content = jnp.einsum(
            "qhd,khd->hqk", content_heads, key_heads, preferred_element_type=jnp.float32
        )
        wide_scores = jnp.einsum(
            "qhd,whd->hqw", position_heads, table_block, preferred_element_type=jnp.float32
        )
        position = rel_shift(wide_scores, rows_local, key_block)
        type_match = (
            kinds_local[:, None]
            == lax.dynamic_slice_in_dim(kinds_all, key_start, key_block, 0)[None, :]
        )
        type_scores = jnp.where(type_match[None], type_one[:, :, None], type_zero[:, :, None])
        same_segment = (
            segs_local[:, None]
            == lax.dynamic_slice_in_dim(segs_all, key_start, key_block, 0)[None, :]
        )
        scores = jnp.where(same_segment[None], content + position + type_scores, NEG_BIG)
        return (scores, key_heads, value_heads, table_block, type_match, table_start)

    def max_step(state_in, key_start):
        running_max, running_sum = state_in
        scores = block_scores(key_start, sources)[0]
        new_max = jnp.maximum(running_max, jnp.max(scores, axis=2))
        running_sum = running_sum * jnp.exp(running_max - new_max) + jnp.sum(
            jnp.exp(scores - new_max[:, :, None]), axis=2
        )
        return ((new_max, running_sum), None)

    start_max = jnp.full((H, rows_local), NEG_BIG, jnp.float32)
    (running_max, running_sum), unused_out = lax.scan(
        max_step, (start_max, jnp.zeros((H, rows_local), jnp.float32)), starts
    )
    log_total = running_max + jnp.log(running_sum)

    def value_step(acc_heads, key_start):
        scores, key_heads, value_heads, table_block, type_match, table_start = block_scores(
            key_start, sources
        )
        probs_low = jnp.exp(scores - log_total[:, :, None]).astype(jnp.bfloat16)
        return (
            acc_heads
            + jnp.einsum(
                "hqk,khd->qhd", probs_low, value_heads, preferred_element_type=jnp.float32
            ),
            None,
        )

    acc_heads, unused_out = lax.scan(
        value_step, jnp.zeros((rows_local, H, DH), jnp.float32), starts
    )
    mixed_f = acc_heads.reshape(rows_local, width_model)
    mixed_low = mixed_f.astype(jnp.bfloat16)
    attn_out = product(mixed_low, full_output) + full_output_bias.astype(jnp.float32)
    normed, first_pull = jax.vjp(
        layer_norm,
        hidden.astype(jnp.float32) + attn_out,
        full_attn_gain.astype(jnp.float32),
        full_attn_shift.astype(jnp.float32),
    )
    normed_low = normed.astype(jnp.bfloat16)
    inner_pre = product(normed_low, full_inner) + full_inner_bias.astype(jnp.float32)
    activated, gelu_pull = jax.vjp(partial(jax.nn.gelu, approximate=True), inner_pre)
    activ_low = activated.astype(jnp.bfloat16)
    outer_out = product(activ_low, full_outer) + full_outer_bias.astype(jnp.float32)
    outcome, second_pull = jax.vjp(
        layer_norm,
        normed + outer_out,
        full_ffn_gain.astype(jnp.float32),
        full_ffn_shift.astype(jnp.float32),
    )
    d_res2, grad_ffn_gain, grad_ffn_shift = second_pull(cotangent)
    d_outer = d_res2.astype(jnp.bfloat16)
    grad_outer_bias = jnp.sum(d_outer.astype(jnp.float32), axis=0)
    grad_outer_proj = inner_rows(activ_low, d_outer)
    d_inner = gelu_pull(product(d_outer, jnp.transpose(full_outer)))[0].astype(jnp.bfloat16)
    grad_inner_bias = jnp.sum(d_inner.astype(jnp.float32), axis=0)
    grad_inner_proj = inner_rows(normed_low, d_inner)
    d_normed = d_res2 + product(d_inner, jnp.transpose(full_inner))
    d_res1, grad_attn_gain, grad_attn_shift = first_pull(d_normed)
    d_attn = d_res1.astype(jnp.bfloat16)
    grad_output_bias = jnp.sum(d_attn.astype(jnp.float32), axis=0)
    grad_output_proj = inner_rows(mixed_low, d_attn)
    d_mixed = product(d_attn, jnp.transpose(full_output)).astype(jnp.bfloat16)
    d_mixed_heads = d_mixed.reshape(rows_local, H, DH)
    delta_rows = jnp.transpose(jnp.sum(d_mixed_heads.astype(jnp.float32) * acc_heads, axis=2))

    def grad_step(state_in, key_start):
        grad_content, grad_position, grad_zero, grad_one, table_grads = state_in
        scores, key_heads, value_heads, table_block, type_match, table_start = block_scores(
            key_start, sources
        )
        probs_f = jnp.exp(scores - log_total[:, :, None])
        d_probs = jnp.einsum(
            "qhd,khd->hqk", d_mixed_heads, value_heads, preferred_element_type=jnp.float32
        )
        d_scores = (probs_f * (d_probs - delta_rows[:, :, None])).astype(jnp.bfloat16)
        grad_content = grad_content + jnp.einsum(
            "hqk,khd->qhd", d_scores, key_heads, preferred_element_type=jnp.float32
        )
        d_keys = jnp.einsum(
            "hqk,qhd->khd", d_scores, content_heads, preferred_element_type=jnp.float32
        ).reshape(key_block, H * DH)
        d_values = jnp.einsum(
            "hqk,qhd->khd",
            probs_f.astype(jnp.bfloat16),
            d_mixed_heads,
            preferred_element_type=jnp.float32,
        ).reshape(key_block, H * DH)
        d_wide = rel_unshift(d_scores, rows_local, key_block)
        grad_position = grad_position + jnp.einsum(
            "hqw,whd->qhd", d_wide, table_block, preferred_element_type=jnp.float32
        )
        d_table = jnp.einsum(
            "hqw,qhd->whd", d_wide, position_heads, preferred_element_type=jnp.float32
        ).reshape(span_width, H * DH)
        table_grads = lax.dynamic_update_slice_in_dim(
            table_grads,
            lax.dynamic_slice_in_dim(table_grads, table_start, span_width, 0) + d_table,
            table_start,
            0,
        )
        d_scores_f = d_scores.astype(jnp.float32)
        grad_one = grad_one + jnp.sum(jnp.where(type_match[None], d_scores_f, 0.0), axis=2)
        grad_zero = grad_zero + jnp.sum(jnp.where(type_match[None], 0.0, d_scores_f), axis=2)
        return ((grad_content, grad_position, grad_zero, grad_one, table_grads), (d_keys, d_values))

    start_state = (
        jnp.zeros((rows_local, H, DH), jnp.float32),
        jnp.zeros((rows_local, H, DH), jnp.float32),
        jnp.zeros((H, rows_local), jnp.float32),
        jnp.zeros((H, rows_local), jnp.float32),
        jnp.zeros((2 * length, width_model), jnp.float32),
    )
    (grad_content, grad_position, grad_zero, grad_one, table_grads), (key_blocks, value_blocks) = (
        lax.scan(grad_step, start_state, starts)
    )
    d_keys_all = key_blocks.reshape(length, width_model)
    d_values_all = value_blocks.reshape(length, width_model)
    d_keys_own, d_values_own, d_table_own = (
        lax.psum_scatter(
            d_keys_all.astype(jnp.bfloat16), "ctx", scatter_dimension=0, tiled=True
        ).astype(jnp.float32),
        lax.psum_scatter(
            d_values_all.astype(jnp.bfloat16), "ctx", scatter_dimension=0, tiled=True
        ).astype(jnp.float32),
        lax.psum_scatter(
            table_grads.astype(jnp.bfloat16), "ctx", scatter_dimension=0, tiled=True
        ).astype(jnp.float32),
    )
    grad_position_proj = inner_rows_high(sinus_low.astype(jnp.float32), d_table_own)
    d_keys_low = d_keys_own.astype(jnp.bfloat16)
    d_values_low = d_values_own.astype(jnp.bfloat16)
    grad_key_proj = inner_rows(hidden, d_keys_low)
    grad_value_proj = inner_rows(hidden, d_values_low)
    grad_value_bias = jnp.sum(d_values_low.astype(jnp.float32), axis=0)
    content_low = (
        grad_content.astype(jnp.bfloat16).astype(jnp.float32).reshape(rows_local, width_model)
    )
    position_low = (
        grad_position.astype(jnp.bfloat16).astype(jnp.float32).reshape(rows_local, width_model)
    )
    embed_heads = embed_f.reshape(2, H, DH)
    d_type = (
        jnp.transpose(grad_zero)[:, :, None] * embed_heads[0][None]
        + jnp.transpose(grad_one)[:, :, None] * embed_heads[1][None]
    ).reshape(rows_local, width_model)
    embed_zero = jnp.einsum("hi,ihd->hd", grad_zero, type_heads, precision=HIGH).reshape(
        width_model
    )
    embed_one = jnp.einsum("hi,ihd->hd", grad_one, type_heads, precision=HIGH).reshape(width_model)
    grad_type_embed = jnp.stack([embed_zero, embed_one], axis=0)
    grad_content_bias = score_scale * jnp.sum(content_low, axis=0)
    grad_position_bias = score_scale * jnp.sum(position_low, axis=0)
    grad_type_bias = score_scale * jnp.sum(d_type, axis=0)
    d_query_low = (score_scale * (content_low + position_low + d_type)).astype(jnp.bfloat16)
    grad_query_proj = inner_rows(hidden, d_query_low)
    input_grad = (
        d_res1
        + product(d_query_low, jnp.transpose(full_query))
        + product(d_keys_low, jnp.transpose(full_key))
        + product(d_values_low, jnp.transpose(full_value))
    )
    shards = (
        lax.psum_scatter(
            grad_query_proj.astype(jnp.bfloat16), "fsdp", scatter_dimension=0, tiled=True
        ).astype(jnp.float32),
        lax.psum_scatter(
            grad_key_proj.astype(jnp.bfloat16), "fsdp", scatter_dimension=0, tiled=True
        ).astype(jnp.float32),
        lax.psum_scatter(
            grad_value_proj.astype(jnp.bfloat16), "fsdp", scatter_dimension=0, tiled=True
        ).astype(jnp.float32),
        lax.psum_scatter(
            grad_value_bias.astype(jnp.bfloat16), "fsdp", scatter_dimension=0, tiled=True
        ).astype(jnp.float32),
        lax.psum_scatter(
            grad_content_bias.astype(jnp.bfloat16), "fsdp", scatter_dimension=0, tiled=True
        ).astype(jnp.float32),
        lax.psum_scatter(
            grad_position_bias.astype(jnp.bfloat16), "fsdp", scatter_dimension=0, tiled=True
        ).astype(jnp.float32),
        lax.psum_scatter(
            grad_type_bias.astype(jnp.bfloat16), "fsdp", scatter_dimension=0, tiled=True
        ).astype(jnp.float32),
        lax.psum_scatter(
            grad_type_embed.astype(jnp.bfloat16), "fsdp", scatter_dimension=1, tiled=True
        ).astype(jnp.float32),
        lax.psum_scatter(
            grad_position_proj.astype(jnp.bfloat16), "fsdp", scatter_dimension=0, tiled=True
        ).astype(jnp.float32),
        lax.psum_scatter(
            grad_output_proj.astype(jnp.bfloat16), "fsdp", scatter_dimension=0, tiled=True
        ).astype(jnp.float32),
        lax.psum_scatter(
            grad_output_bias.astype(jnp.bfloat16), "fsdp", scatter_dimension=0, tiled=True
        ).astype(jnp.float32),
        lax.psum_scatter(
            grad_attn_gain.astype(jnp.bfloat16), "fsdp", scatter_dimension=0, tiled=True
        ).astype(jnp.float32),
        lax.psum_scatter(
            grad_attn_shift.astype(jnp.bfloat16), "fsdp", scatter_dimension=0, tiled=True
        ).astype(jnp.float32),
        lax.psum_scatter(
            grad_inner_proj.astype(jnp.bfloat16), "fsdp", scatter_dimension=0, tiled=True
        ).astype(jnp.float32),
        lax.psum_scatter(
            grad_inner_bias.astype(jnp.bfloat16), "fsdp", scatter_dimension=0, tiled=True
        ).astype(jnp.float32),
        lax.psum_scatter(
            grad_outer_proj.astype(jnp.bfloat16), "fsdp", scatter_dimension=0, tiled=True
        ).astype(jnp.float32),
        lax.psum_scatter(
            grad_outer_bias.astype(jnp.bfloat16), "fsdp", scatter_dimension=0, tiled=True
        ).astype(jnp.float32),
        lax.psum_scatter(
            grad_ffn_gain.astype(jnp.bfloat16), "fsdp", scatter_dimension=0, tiled=True
        ).astype(jnp.float32),
        lax.psum_scatter(
            grad_ffn_shift.astype(jnp.bfloat16), "fsdp", scatter_dimension=0, tiled=True
        ).astype(jnp.float32),
    )
    finals = tuple(
        jax.tree.map(
            lambda part: part.astype(jnp.float32), lax.psum(for_sending(tuple(shards)), "ctx")
        )
    )
    return (
        outcome.astype(jnp.bfloat16)[None],
        input_grad[None],
        finals[0],
        finals[1],
        finals[2],
        finals[3],
        finals[4],
        finals[5],
        finals[6],
        finals[7],
        finals[8],
        finals[9],
        finals[10],
        finals[11],
        finals[12],
        finals[13],
        finals[14],
        finals[15],
        finals[16],
        finals[17],
        finals[18],
    )


def solution(mesh):
    in_specs = (
        P("fsdp", "ctx", None),
        P("fsdp", "ctx"),
        P("fsdp", "ctx"),
        P("fsdp", "ctx", None),
        P("fsdp", None),
        P("fsdp", None),
        P("fsdp", None),
        P("fsdp"),
        P("fsdp"),
        P("fsdp"),
        P("fsdp"),
        P(None, "fsdp"),
        P("fsdp", None),
        P("fsdp", None),
        P("fsdp"),
        P("fsdp"),
        P("fsdp"),
        P("fsdp", None),
        P("fsdp"),
        P("fsdp", None),
        P("fsdp"),
        P("fsdp"),
        P("fsdp"),
    )
    out_specs = (
        P("fsdp", "ctx", None),
        P("fsdp", "ctx", None),
        P("fsdp", None),
        P("fsdp", None),
        P("fsdp", None),
        P("fsdp"),
        P("fsdp"),
        P("fsdp"),
        P("fsdp"),
        P(None, "fsdp"),
        P("fsdp", None),
        P("fsdp", None),
        P("fsdp"),
        P("fsdp"),
        P("fsdp"),
        P("fsdp", None),
        P("fsdp"),
        P("fsdp", None),
        P("fsdp"),
        P("fsdp"),
        P("fsdp"),
    )
    return jax.shard_map(
        per_device, mesh=mesh, in_specs=in_specs, out_specs=out_specs, check_vma=False
    )
```

profile of v0, /device:TPU:0, one launch (start us, length us, event | category | flops | bytes accessed | tf_op | source)
XLA Modules:
  0.0 1685.9 jit_solution(17233716753986653626)
XLA Ops:
  15.3 19.8 %all-gather.24.cloned.1.call-done = bf16[768,768]{1,0:T(8,128)(2,1)} async-done(((bf16[384,768]{1,0:T(8,128)(2,1)}), bf16[768,768]{1,0:T(8,128)(2,1)}) %all-gather.24.cloned.1.call-update) | async-done | bytes 1179664 | tf_op jit(solution)/shard_map/all_gather | solution.py:119
  37.5 22.0 %all-gather.28.cloned.1.call-done = bf16[768,768]{1,0:T(8,128)(2,1)} async-done(((bf16[384,768]{1,0:T(8,128)(2,1)}), bf16[768,768]{1,0:T(8,128)(2,1)}) %all-gather.28.cloned.1.call-update) | async-done | bytes 1179664 | tf_op jit(solution)/shard_map/all_gather | solution.py:118
  63.5 20.3 %all-gather.34.cloned.1.call-done = bf16[768,768]{1,0:T(8,128)(2,1)} async-done(((bf16[384,768]{1,0:T(8,128)(2,1)}), bf16[768,768]{1,0:T(8,128)(2,1)}) %all-gather.34.cloned.1.call-update) | async-done | bytes 1179664 | tf_op jit(solution)/shard_map/all_gather | solution.py:125
  104.7 21.2 %all-gather = bf16[1,2048]{1,0:T(2,128)(2,1)S(1)} all-gather(bf16[1,128]{1,0:T(2,128)(2,1)S(1)} %get-tuple-element.1427), channel_id=2, replica_groups=mesh['ctx'=16,'fsdp'=2] {'ctx'}, dimensions={1}, use_global_device_ids=true | all-gather | bytes 4352 | tf_op jit(solution)/shard_map/all_gather | solution.py:168
  139.6 17.0 %all-gather.1 = bf16[1,2048]{1,0:T(2,128)(2,1)S(1)} all-gather(bf16[1,128]{1,0:T(2,128)(2,1)S(1)} %get-tuple-element.1425), channel_id=3, replica_groups=mesh['ctx'=16,'fsdp'=2] {'ctx'}, dimensions={1}, use_global_device_ids=true | all-gather | bytes 4352 | tf_op jit(solution)/shard_map/all_gather | solution.py:169
  189.8 13.1 all-gather.30.cloned.1.call-done
  207.7 58.8 %all-gather.36.cloned.1.call-done = bf16[4096,768]{1,0:T(8,128)(2,1)} async-done(((bf16[256,768]{1,0:T(8,128)(2,1)}), bf16[4096,768]{1,0:T(8,128)(2,1)}) %all-gather.36.cloned.1.call-update) | async-done | bytes 6291472 | tf_op jit(solution)/shard_map/all_gather | solution.py:167
  266.5 8.7 copy.179
  275.1 177.0 %while.53 = (s32[]{:T(128)}, f32[12,128]{1,0:T(8,128)S(1)}, f32[12,128]{1,0:T(8,128)}, bf16[128]{0:T(256)(128)(2,1)}, s32[4]{0:T(128)}, /*index=5*/bf16[2048]{0:...) while((s32[]{:T(128)}, f32[12,128]{1,0:T(8,128)S(1)}, ...), condition=%wide.region_4.5_spmd.clone, body=%wide.region_1.4_spmd.clone.sunk | while | flops 232136192 | bytes 78439312 | solution.py:226
  286.7 5.4 copy.257
  301.5 7.1 reshape.566
  331.1 5.4 copy.257
  345.9 6.8 reshape.566
  375.3 5.4 copy.257
  390.1 6.8 reshape.566
  419.4 5.4 copy.257
  434.2 6.8 reshape.566
  453.5 179.2 %while.54 = (s32[]{:T(128)}, f32[128,12,64]{0,2,1:T(8,128)}, s32[4]{0:T(128)}, bf16[2048,768]{0,1:T(8,128)(2,1)}, bf16[128]{0:T(256)(128)(2,1)}, /*index=5*/bf16...) while((s32[]{:T(128)}, f32[128,12,64]{0,2,1:T(8,128)}, ...), condition=%wide.region_6.7_spmd.clone, body=%wide.region_5.6_spmd.clone.sunk | while | flops 332201984 | bytes 75195240 | solution.py:244
  465.6 5.4 copy.260
  480.4 6.8 reshape.567
  525.0 6.8 reshape.567
  569.7 6.8 reshape.567
  599.4 5.4 copy.260
  614.2 6.8 reshape.567
  655.3 6.1 broadcast_in_dim.232
  661.5 350.1 %while.55 = (s32[]{:T(128)}, f32[128,12,64]{0,2,1:T(8,128)}, f32[128,12,64]{0,2,1:T(8,128)}, f32[12,128]{1,0:T(8,128)}, f32[12,128]{1,0:T(8,128)}, /*index=5*/f3...) while((s32[]{:T(128)}, f32[128,12,64]{0,2,1:T(8,128)}, ...), condition=%wide.region_19.20_spmd.clone, body=%wide.region_16.19_spmd.clone.sunk | while | flops 892832768 | bytes 186691264 | solution.py:331
  692.3 6.8 reshape.568
  727.4 10.3 dynamic_update_slice.29
  779.9 6.8 reshape.568
  815.0 10.4 dynamic_update_slice.29
  867.7 6.8 reshape.568
  902.8 10.3 dynamic_update_slice.29
  955.1 6.8 reshape.568
  990.0 9.5 dynamic_update_slice.29
  1012.2 8.1 convert_element_type.408
  1025.2 53.1 %reduce-scatter.20.cloned.1.call-done = bf16[128,768]{1,0:T(8,128)(2,1)} async-done(((bf16[2048,768]{1,0:T(8,128)(2,1)}), bf16[128,768]{1,0:T(8,128)(2,1)}) %reduce-scatter.20.cloned.1.call-update) | async-done | bytes 196624 | tf_op jit(solution)/shard_map/reduce_scatter | solution.py:336
  1081.3 65.9 %reduce-scatter.22.cloned.1.call-done = bf16[128,768]{1,0:T(8,128)(2,1)} async-done(((bf16[2048,768]{1,0:T(8,128)(2,1)}), bf16[128,768]{1,0:T(8,128)(2,1)}) %reduce-scatter.22.cloned.1.call-update) | async-done | bytes 196624 | tf_op jit(solution)/shard_map/reduce_scatter | solution.py:339
  1160.9 74.4 %reduce-scatter.24.cloned.1.call-done = bf16[256,768]{0,1:T(8,128)(2,1)} async-done(((bf16[4096,768]{0,1:T(8,128)(2,1)}), bf16[256,768]{0,1:T(8,128)(2,1)}) %reduce-scatter.24.cloned.1.call-update) | async-done | bytes 393232 | tf_op jit(solution)/shard_map/reduce_scatter | solution.py:342
  1240.5 18.6 %reduce-scatter.34.cloned.1.call-done = bf16[384,768]{1,0:T(8,128)(2,1)} async-done(((bf16[768,768]{1,0:T(8,128)(2,1)}), bf16[384,768]{1,0:T(8,128)(2,1)}) %reduce-scatter.34.cloned.1.call-update) | async-done | bytes 589840
  1261.2 22.3 %reduce-scatter.36.cloned.1.call-done = bf16[384,768]{1,0:T(8,128)(2,1)} async-done(((bf16[768,768]{1,0:T(8,128)(2,1)}), bf16[384,768]{1,0:T(8,128)(2,1)}) %reduce-scatter.36.cloned.1.call-update) | async-done | bytes 589840
  1285.7 22.5 %reduce-scatter.38.cloned.1.call-done = bf16[384,768]{1,0:T(8,128)(2,1)} async-done(((bf16[768,768]{1,0:T(8,128)(2,1)}), bf16[384,768]{1,0:T(8,128)(2,1)}) %reduce-scatter.38.cloned.1.call-update) | async-done | bytes 589840
  1310.2 22.3 %reduce-scatter.28.cloned.1.call-done = bf16[384,768]{1,0:T(8,128)(2,1)} async-done(((bf16[768,768]{1,0:T(8,128)(2,1)}), bf16[384,768]{1,0:T(8,128)(2,1)}) %reduce-scatter.28.cloned.1.call-update) | async-done | bytes 589840 | tf_op jit(solution)/shard_map/reduce_scatter | solution.py:407
  1332.6 62.9 %reduce-scatter.30.cloned.1.call-done = bf16[384,3072]{1,0:T(8,128)(2,1)} async-done(((bf16[768,3072]{1,0:T(8,128)(2,1)}), bf16[384,3072]{1,0:T(8,128)(2,1)}) %reduce-scatter.30.cloned.1.call-update) | async-done | bytes 2359312 | tf_op jit(solution)/shard_map/reduce_scatter | solution.py:419
  1395.4 62.9 %reduce-scatter.32.cloned.1.call-done = bf16[1536,768]{1,0:T(8,128)(2,1)} async-done(((bf16[3072,768]{1,0:T(8,128)(2,1)}), bf16[1536,768]{1,0:T(8,128)(2,1)}) %reduce-scatter.32.cloned.1.call-update) | async-done | bytes 2359312 | tf_op jit(solution)/shard_map/reduce_scatter | solution.py:425
  1458.3 24.6 %reduce-scatter.26.cloned.1.call-done = bf16[384,768]{1,0:T(8,128)(2,1)} async-done(((bf16[768,768]{1,0:T(8,128)(2,1)}), bf16[384,768]{1,0:T(8,128)(2,1)}) %reduce-scatter.26.cloned.1.call-update) | async-done | bytes 589840 | tf_op jit(solution)/shard_map/reduce_scatter | solution.py:404
  1498.1 7.9 all-reduce.15
  1506.8 62.8 %all-reduce.13 = (bf16[384]{0:T(512)(128)(2,1)S(1)}, bf16[384]{0:T(512)(128)(2,1)S(1)}, bf16[384]{0:T(512)(128)(2,1)S(1)}, bf16[384]{0:T(512)(128)(2,1)S(1)}, bf...) all-reduce(bf16[384]{0:T(512)(128)(2,1)S(1)} %dynamic-slice.1, ...), channel_id=1, replica_groups=mesh['ctx'=16,'fsdp'=2] {'ctx'}, use_global_device_ids=true, to_apply=%region_30.31 | all-reduce | flops 6144 | bytes 24576 | tf_op jit(solution)/shard_map/psum | solution.py:440
  1579.5 84.6 %all-reduce.18.cloned.1.call-done = (bf16[384,768]{0,1:T(8,128)(2,1)}, bf16[384,768]{0,1:T(8,128)(2,1)}, bf16[384,768]{0,1:T(8,128)(2,1)}, bf16[384,768]{1,0:T(8...) async-done(((bf16[384,768]{0,1:T(8,128)(2,1)}, bf16[384,768]{0,1:T(8,128)(2,1)}, bf16[384,768]{0,1:T(8,128)(2,1)}, ...) | async-done | bytes 7667728 | tf_op jit(solution)/shard_map/psum | solution.py:440
  (886 shorter events, 699.1 us)
Async XLA Ops:
  7.2 27.9 %copy-start.21 = (bf16[1,128,768]{2,1,0:T(8,128)(2,1)S(1)}, bf16[1,128,768]{2,1,0:T(8,128)(2,1)}, u32[]{:S(2)}) copy-start(bf16[1,128,768]{2,1,0:T(8,128)(2,1)} %param.29) | copy-start | bytes 589828
  7.2 27.9 %all-gather.24.cloned.1.call-start = ((), (), s32[]{:S(2)}) async-start(), calls=%async_computation.11 | async-start | bytes 1769472 | tf_op jit(solution)/shard_map/all_gather | solution.py:119
  7.9 51.5 %all-gather.28.cloned.1.call-start = ((), (), s32[]{:S(2)}) async-start(), calls=%async_computation.13 | async-start | bytes 1769472 | tf_op jit(solution)/shard_map/all_gather | solution.py:118
  8.7 75.1 %all-gather.34.cloned.1.call-start = ((), (), s32[]{:S(2)}) async-start(), calls=%async_computation.16 | async-start | bytes 1769472 | tf_op jit(solution)/shard_map/all_gather | solution.py:125
  9.4 172.6 %all-gather.32.cloned.1.call-start = ((), (), s32[]{:S(2)}) async-start(), calls=%async_computation.15 | async-start | bytes 1769472 | tf_op jit(solution)/shard_map/all_gather | solution.py:117
  10.0 175.1 %all-gather.26.cloned.1.call-start = ((), (), s32[]{:S(2)}) async-start(), calls=%async_computation.12 | async-start | bytes 3342336 | tf_op jit(solution)/shard_map/all_gather | solution.py:166
  37.4 165.5 %all-gather.30.cloned.1.call-start = ((), (), s32[]{:S(2)}) async-start(), calls=%async_computation.14 | async-start | bytes 3342336 | tf_op jit(solution)/shard_map/all_gather | solution.py:165
  61.8 204.7 %all-gather.36.cloned.1.call-start = ((), (), s32[]{:S(2)}) async-start(), calls=%async_computation.17 | async-start | bytes 6684672 | tf_op jit(solution)/shard_map/all_gather | solution.py:167
  63.5 24.5 %copy-start.48 = (bf16[256,384]{1,0:T(8,128)(2,1)}, bf16[256,384]{1,0:T(8,128)(2,1)S(1)}, u32[]{:S(2)}) copy-start(bf16[256,384]{1,0:T(8,128)(2,1)S(1)} %get-tuple-element.1423) | copy-start | bytes 589828
  63.5 24.5 %copy-start.50 = (bf16[256,384]{1,0:T(8,128)(2,1)}, bf16[256,384]{1,0:T(8,128)(2,1)S(1)}, u32[]{:S(2)}) copy-start(bf16[256,384]{1,0:T(8,128)(2,1)S(1)} %get-tuple-element.1424) | copy-start | bytes 589828
  86.3 547.4 %all-gather.38.cloned.1.call-start = ((), (), s32[]{:S(2)}) async-start(), calls=%async_computation.18 | async-start | bytes 1769472 | tf_op jit(solution)/shard_map/all_gather | solution.py:126
  87.1 17.1 %copy-start.109 = (s32[1,128]{1,0:T(1,128)S(1)}, s32[1,128]{1,0:T(1,128)}, u32[]{:S(2)}) copy-start(s32[1,128]{1,0:T(1,128)} %param.30) | copy-start | bytes 1540
  87.1 38.8 %copy-start.99 = (bf16[384]{0:T(512)(128)(2,1)S(1)}, bf16[384]{0:T(512)(128)(2,1)}, u32[]{:S(2)}) copy-start(bf16[384]{0:T(512)(128)(2,1)} %param.39) | copy-start | bytes 2308
  87.2 43.1 %copy-start.100 = (bf16[384]{0:T(512)(128)(2,1)S(1)}, bf16[384]{0:T(512)(128)(2,1)}, u32[]{:S(2)}) copy-start(bf16[384]{0:T(512)(128)(2,1)} %param.38) | copy-start | bytes 2308
  87.2 47.5 %copy-start.101 = (bf16[384]{0:T(512)(128)(2,1)S(1)}, bf16[384]{0:T(512)(128)(2,1)}, u32[]{:S(2)}) copy-start(bf16[384]{0:T(512)(128)(2,1)} %param.37) | copy-start | bytes 2308
  87.2 51.9 %copy-start.110 = (s32[1,128]{1,0:T(1,128)S(1)}, s32[1,128]{1,0:T(1,128)}, u32[]{:S(2)}) copy-start(s32[1,128]{1,0:T(1,128)} %param.31) | copy-start | bytes 1540
  87.2 70.7 %copy-start.95 = (bf16[2,384]{1,0:T(2,128)(2,1)S(1)}, bf16[2,384]{1,0:T(2,128)(2,1)}, u32[]{:S(2)}) copy-start(bf16[2,384]{1,0:T(2,128)(2,1)} %param.40) | copy-start | bytes 4612
  87.2 75.1 %copy-start.102 = (bf16[384]{0:T(512)(128)(2,1)S(1)}, bf16[384]{0:T(512)(128)(2,1)}, u32[]{:S(2)}) copy-start(bf16[384]{0:T(512)(128)(2,1)} %param.45) | copy-start | bytes 2308
  87.2 80.0 %copy-start.103 = (bf16[384]{0:T(512)(128)(2,1)S(1)}, bf16[384]{0:T(512)(128)(2,1)}, u32[]{:S(2)}) copy-start(bf16[384]{0:T(512)(128)(2,1)} %param.44) | copy-start | bytes 2308
  87.2 84.9 %copy-start.104 = (bf16[384]{0:T(512)(128)(2,1)S(1)}, bf16[384]{0:T(512)(128)(2,1)}, u32[]{:S(2)}) copy-start(bf16[384]{0:T(512)(128)(2,1)} %param.50) | copy-start | bytes 2308
  87.2 89.9 %copy-start.105 = (bf16[384]{0:T(512)(128)(2,1)S(1)}, bf16[384]{0:T(512)(128)(2,1)}, u32[]{:S(2)}) copy-start(bf16[384]{0:T(512)(128)(2,1)} %param.51) | copy-start | bytes 2308
  87.2 548.6 %all-gather.40.cloned.1.call-start = ((), (), s32[]{:S(2)}) async-start(), calls=%async_computation.19 | async-start | bytes 7077888 | tf_op jit(solution)/shard_map/all_gather | solution.py:130
  88.0 551.6 %all-gather.42.cloned.1.call-start = ((), (), s32[]{:S(2)}) async-start(), calls=%async_computation.20 | async-start | bytes 7077888 | tf_op jit(solution)/shard_map/all_gather | solution.py:132
  88.6 989.7 %reduce-scatter.20.cloned.1.call-start = ((), (), s32[]{:S(2)}) async-start(), calls=%async_computation.21 | async-start | bytes 3342336 | tf_op jit(solution)/shard_map/reduce_scatter | solution.py:336
  162.2 19.9 %copy-start.78 = (bf16[2,768]{1,0:T(2,128)(2,1)}, bf16[2,768]{1,0:T(2,128)(2,1)S(1)}, u32[]{:S(2)}) copy-start(bf16[2,768]{1,0:T(2,128)(2,1)S(1)} %all_gather.85) | copy-start | bytes 9220
  661.9 41.5 %copy-start.8 = (bf16[128,12,64]{0,2,1:T(8,128)(2,1)}, bf16[128,12,64]{0,2,1:T(8,128)(2,1)S(1)}, u32[]{:S(2)}) copy-start(bf16[128,12,64]{0,2,1:T(8,128)(2,1)S(1)} %get-tuple-element.1994) | copy-start | bytes 589828 | tf_op jit(solution)/shard_map/while
  749.5 41.5 %copy-start.8 = (bf16[128,12,64]{0,2,1:T(8,128)(2,1)}, bf16[128,12,64]{0,2,1:T(8,128)(2,1)S(1)}, u32[]{:S(2)}) copy-start(bf16[128,12,64]{0,2,1:T(8,128)(2,1)S(1)} %get-tuple-element.1994) | copy-start | bytes 589828 | tf_op jit(solution)/shard_map/while
  837.3 41.5 %copy-start.8 = (bf16[128,12,64]{0,2,1:T(8,128)(2,1)}, bf16[128,12,64]{0,2,1:T(8,128)(2,1)S(1)}, u32[]{:S(2)}) copy-start(bf16[128,12,64]{0,2,1:T(8,128)(2,1)S(1)} %get-tuple-element.1994) | copy-start | bytes 589828 | tf_op jit(solution)/shard_map/while
  924.9 41.3 %copy-start.8 = (bf16[128,12,64]{0,2,1:T(8,128)(2,1)}, bf16[128,12,64]{0,2,1:T(8,128)(2,1)S(1)}, u32[]{:S(2)}) copy-start(bf16[128,12,64]{0,2,1:T(8,128)(2,1)S(1)} %get-tuple-element.1994) | copy-start | bytes 589828 | tf_op jit(solution)/shard_map/while
  1011.6 135.7 %reduce-scatter.22.cloned.1.call-start = ((), (), s32[]{:S(2)}) async-start(), calls=%async_computation.22 | async-start | bytes 3342336 | tf_op jit(solution)/shard_map/reduce_scatter | solution.py:339
  1012.1 223.2 %reduce-scatter.24.cloned.1.call-start = ((), (), s32[]{:S(2)}) async-start(), calls=%async_computation.23 | async-start | bytes 6684672 | tf_op jit(solution)/shard_map/reduce_scatter | solution.py:342
  1020.4 238.7 %reduce-scatter.34.cloned.1.call-start = ((), (), s32[]{:S(2)}) async-start(), calls=%async_computation.28 | async-start | bytes 1769472
  1025.2 258.3 %reduce-scatter.36.cloned.1.call-start = ((), (), s32[]{:S(2)}) async-start(), calls=%async_computation.29 | async-start | bytes 1769472
  1081.2 69.0 %copy-start.41 = (bf16[128,12,64]{0,2,1:T(8,128)(2,1)S(1)}, bf16[128,12,64]{0,2,1:T(8,128)(2,1)}, u32[]{:S(2)}) copy-start(bf16[128,12,64]{0,2,1:T(8,128)(2,1)} %copy-done.40) | copy-start | bytes 589828
  1081.2 69.0 %copy-start.43 = (bf16[128,768]{1,0:T(8,128)(2,1)S(1)}, bf16[128,768]{1,0:T(8,128)(2,1)}, u32[]{:S(2)}) copy-start(bf16[128,768]{1,0:T(8,128)(2,1)} %copy-done.42) | copy-start | bytes 589828
  1081.2 226.9 %reduce-scatter.38.cloned.1.call-start = ((), (), s32[]{:S(2)}) async-start(), calls=%async_computation.30 | async-start | bytes 1769472
  1150.2 182.4 %reduce-scatter.28.cloned.1.call-start = ((), (), s32[]{:S(2)}) async-start(), calls=%async_computation.25 | async-start | bytes 1769472 | tf_op jit(solution)/shard_map/reduce_scatter | solution.py:407
  1151.7 243.7 %reduce-scatter.30.cloned.1.call-start = ((), (), s32[]{:S(2)}) async-start(), calls=%async_computation.26 | async-start | bytes 7077888 | tf_op jit(solution)/shard_map/reduce_scatter | solution.py:419
  1155.6 302.8 %reduce-scatter.32.cloned.1.call-start = ((), (), s32[]{:S(2)}) async-start(), calls=%async_computation.27 | async-start | bytes 7077888 | tf_op jit(solution)/shard_map/reduce_scatter | solution.py:425
  1160.8 74.5 %copy-start.49 = (bf16[256,384]{1,0:T(8,128)(2,1)S(1)}, bf16[256,384]{1,0:T(8,128)(2,1)}, u32[]{:S(2)}) copy-start(bf16[256,384]{1,0:T(8,128)(2,1)} %copy-done.48) | copy-start | bytes 589828
  1160.8 74.5 %copy-start.51 = (bf16[256,384]{1,0:T(8,128)(2,1)S(1)}, bf16[256,384]{1,0:T(8,128)(2,1)}, u32[]{:S(2)}) copy-start(bf16[256,384]{1,0:T(8,128)(2,1)} %copy-done.50) | copy-start | bytes 589828
  1160.8 77.1 %copy-start.27 = (f32[128,768]{0,1:T(8,128)S(1)}, f32[128,768]{0,1:T(8,128)}, u32[]{:S(2)}) copy-start(f32[128,768]{0,1:T(8,128)} %copy-done.26) | copy-start | bytes 1179652
  1160.8 322.1 %reduce-scatter.26.cloned.1.call-start = ((), (), s32[]{:S(2)}) async-start(), calls=%async_computation.24 | async-start | bytes 1769472 | tf_op jit(solution)/shard_map/reduce_scatter | solution.py:404
  1237.9 258.2 %reduce-scatter.40.cloned.1.call-start = ((), (), s32[]{:S(2)}) async-start(), calls=%async_computation.31 | async-start | bytes 294912
  1240.5 423.6 %all-reduce.18.cloned.1.call-start = ((), (), s32[]{:S(2)}) async-start(), calls=%async_computation.32 | async-start | bytes 15335424 | tf_op jit(solution)/shard_map/psum | solution.py:440
  1488.2 88.3 %copy-start.29 = (bf16[768,768]{1,0:T(8,128)(2,1)S(1)}, bf16[768,768]{1,0:T(8,128)(2,1)}, u32[]{:S(2)}) copy-start(bf16[768,768]{1,0:T(8,128)(2,1)} %all-gather.28.cloned.1.call-done) | copy-start | bytes 3538948
  1491.2 87.0 %copy-start.28 = (bf16[768,768]{1,0:T(8,128)(2,1)S(1)}, bf16[768,768]{1,0:T(8,128)(2,1)}, u32[]{:S(2)}) copy-start(bf16[768,768]{1,0:T(8,128)(2,1)} %all-gather.24.cloned.1.call-done) | copy-start | bytes 3538948
  1493.9 84.2 %copy-start.37 = (bf16[128,768]{1,0:T(8,128)(2,1)S(1)}, bf16[128,768]{1,0:T(8,128)(2,1)}, u32[]{:S(2)}) copy-start(bf16[128,768]{1,0:T(8,128)(2,1)} %reduce-scatter.22.cloned.1.call-done) | copy-start | bytes 589828
  (187 other events, 572.8 us)
Sparse Core Ops, SparseCore 0:
  9.6 25.4 all-gather.23
  36.6 22.7 all-gather.27
  61.0 22.7 all-gather.33
  85.2 22.9 all-gather.31
  110.9 45.2 all-gather.25
  158.9 43.9 all-gather.29
  205.8 60.6 all-gather.35
  268.0 21.3 all-gather.37
  291.0 62.6 all-gather.39
  355.0 62.6 all-gather.41
  1011.7 66.6 reduce-scatter.19
  1082.0 65.2 reduce-scatter.21
  1151.2 84.0 reduce-scatter.23
  1238.1 20.9 reduce-scatter.33
  1261.8 21.7 reduce-scatter.35
  1286.3 21.7 reduce-scatter.37
  1310.8 21.7 reduce-scatter.27
  1335.4 59.9 reduce-scatter.29
  1398.3 59.9 reduce-scatter.31
  1461.1 21.7 reduce-scatter.25
  1485.1 10.9 reduce-scatter.39
  1501.9 162.1 all-reduce.17
where the time goes:
time: 1700 us; the launch traced here: 1690 us
  waiting for transfers between devices  656 us (39%)
  local copies, waits for them, and re-layouts  583 us (34%)
  matrix products  164 us (10%)
  blocking collectives  162 us (10%)
  other arithmetic  69.1 us (4%)
  loops' own time  34.5 us (2%)
  between operations  17 us (1%)
    while x280, local copies, waits for them, and re-layouts  119 us
    psum x1, waiting for transfers between devices, per_device(): lax.psum(for_sending(tuple(shards)), 'ctx')  84.6 us
    reshape x12, local copies, waits for them, and re-layouts, rel_shift(): flat_scores.reshape(heads_count, query_rows, span_width - 1)  82.4 us
    reduce_scatter x1, waiting for transfers between devices, per_device(): lax.psum_scatter(table_grads.astype(jnp.bfloat16), 'ctx', scatter_dimensi...  74.4 us
    unnamed x26, waiting for transfers between devices  70.7 us
    reduce_scatter x1, waiting for transfers between devices, per_device(): lax.psum_scatter(d_values_all.astype(jnp.bfloat16), 'ctx', scatter_dimens...  65.9 us
    dot_general x12, local copies, waits for them, and re-layouts, block_scores(): jnp.einsum('qhd,whd->hqw', position_heads, table_block, preferred_element...  65.4 us
    reduce_scatter x1, waiting for transfers between devices, per_device(): lax.psum_scatter(grad_outer_proj.astype(jnp.bfloat16), 'fsdp', scatter_di...  62.9 us
  transfers between devices with their start and end apart: 22, of which 17 were waited for; matrix products, arithmetic and copies ran while one was open for 25% of the time, Pallas kernels for 0%

commit v1 on v0

v1 whole, which is shorter than its diff:
```python
from functools import partial
import jax
import jax.numpy as jnp
from jax import lax
from jax.experimental import pallas as pl
from jax.experimental.pallas import tpu as pltpu
from jax.sharding import PartitionSpec as P

H = 12
DH = 64
EPS = 1e-06
BIG = 1e30
BF = jnp.bfloat16
F32 = jnp.float32


def nt(a, b):
    return lax.dot_general(a, b, (((1,), (1,)), ((), ())), preferred_element_type=F32)


def nn(a, b):
    return lax.dot_general(a, b, (((1,), (0,)), ((), ())), preferred_element_type=F32)


def tn(a, b):
    return lax.dot_general(a, b, (((0,), (0,)), ((), ())), preferred_element_type=F32)


def att_fwd_kernel(q_ref, rows_ref, pen_ref, kind_ref, k_ref, v_ref, t_ref, ka_ref, o_ref, p_ref):
    T=q_ref.shape[0]; W=k_ref.shape[0]; NB=W//T
    c=DH**-0.5
    q=q_ref[...]
    qc=((q+rows_ref[0:1,:])*c).astype(BF)
    qp=((q+rows_ref[1:2,:])*c).astype(BF)
    qt=(q+rows_ref[2:3,:])*c
    t0=qt*rows_ref[3:4,:]; t1=qt*rows_ref[4:5,:]
    lane=lax.broadcasted_iota(jnp.int32,(T,128),1)
    row=lax.broadcasted_iota(jnp.int32,(T,128),0)
    same=kind_ref[...]>0.5
    pen=pen_ref[...]
    sel=lane<=row
    zero=jnp.zeros((T,128),F32)
    kcat=jnp.concatenate([k_ref[...],ka_ref[...]],axis=1)
    outs=[]
    for h in range(2):
        msk=(lane<64) if h==0 else (lane>=64)
        a0=jnp.sum(jnp.where(msk,t0,0.0),axis=1,keepdims=True)
        a1=jnp.sum(jnp.where(msk,t1,0.0),axis=1,keepdims=True)
        a0=jnp.broadcast_to(a0,(T,128)); a1=jnp.broadcast_to(a1,(T,128))
        A=jnp.where(same,a1,a0); B=jnp.where(same,a0,a1)
        A1=A.astype(BF).astype(F32); A2=A-A1
        B1=B.astype(BF).astype(F32); B2=B-B1
        aug=jnp.where(lane==0,A1,jnp.where(lane==1,A2,jnp.where(lane==4,B1,jnp.where(lane==5,B2,pen)))).astype(BF)
        qa=jnp.concatenate([jnp.where(msk,qc,jnp.zeros_like(qc)),aug],axis=1)
        s=nt(qa,kcat)
        w=nt(jnp.where(msk,qp,jnp.zeros_like(qp)),t_ref[...])
        R=[pltpu.roll(w[:,128*t:128*t+128],1,1,stride=1,stride_axis=0) for t in range(NB+1)]
        ss=[s[:,128*b:128*b+128]+jnp.where(sel,R[b],R[b+1]) for b in range(NB)]
        m=ss[0]
        for b in range(1,NB): m=jnp.maximum(m,ss[b])
        m=jnp.max(m,axis=1,keepdims=True)
        es=[jnp.exp(x-m) for x in ss]
        l=es[0]
        for b in range(1,NB): l=l+es[b]
        l=jnp.sum(l,axis=1,keepdims=True)
        inv=1.0/l
        p=jnp.concatenate([(x*inv).astype(BF) for x in es],axis=1)
        p_ref[h]=p
        outs.append(nn(p,v_ref[...]))
    o_ref[...]=jnp.where(lane<64,outs[0],outs[1])

def att_bwd_kernel(q_ref, rows_ref, kind_ref, dm_ref, o_ref, p_ref, k_ref, v_ref, t_ref, ka_ref,
                   dq_ref, vec_ref, dkv_ref, dt_ref):
    T=q_ref.shape[0]; W=k_ref.shape[0]; NB=W//T
    c=DH**-0.5
    q=q_ref[...]
    qc=((q+rows_ref[0:1,:])*c).astype(BF)
    qp=((q+rows_ref[1:2,:])*c).astype(BF)
    qt=(q+rows_ref[2:3,:])*c
    e0=rows_ref[3:4,:]; e1=rows_ref[4:5,:]
    lane=lax.broadcasted_iota(jnp.int32,(T,128),1)
    row=lax.broadcasted_iota(jnp.int32,(T,128),0)
    same=kind_ref[...]>0.5
    sel=lane>=row
    flip=jnp.where(lane+row==T-1,1.0,0.0).astype(BF)
    qpr=nn(flip,qp).astype(BF)
    zf=jnp.zeros((T,128),F32)
    dm=dm_ref[...]
    dmo=dm.astype(F32)*o_ref[...]
    kcat=jnp.concatenate([k_ref[...],ka_ref[...]],axis=1)
    zb=jnp.zeros_like(dm)
    dss=[];wds=[];dms=[];qcs=[];qps=[];dqc=[];dqp=[];gz=[];go=[]
    for h in range(2):
        msk=(lane<64) if h==0 else (lane>=64)
        delta=jnp.sum(jnp.where(msk,dmo,0.0),axis=1,keepdims=True)
        dmh=jnp.where(msk,dm,zb)
        dp=nt(dmh,v_ref[...])
        ds=(p_ref[h].astype(F32)*(dp-delta)).astype(BF)
        dsf=nn(flip,ds)
        dc=nn(ds,kcat)
        R=[pltpu.roll(dsf[:,128*b:128*b+128],0,1,stride=1,stride_axis=0) for b in range(NB)]
        wd=[]
        for t in range(NB+1):
            lo=R[t] if t<NB else zf
            hi=R[t-1] if t>0 else zf
            wd.append(jnp.where(sel,lo,hi).astype(BF))
        wd=jnp.concatenate(wd,axis=1)
        dqp.append(nn(wd,t_ref[...]))
        dqc.append(dc[:,:128])
        s1=jnp.broadcast_to(dc[:,128:129],(T,128)); s0=jnp.broadcast_to(dc[:,132:133],(T,128))
        go.append(jnp.where(same,s1,s0)); gz.append(jnp.where(same,s0,s1))
        dss.append(ds);wds.append(wd);dms.append(dmh)
        qcs.append(jnp.where(msk,qc,zb));qps.append(jnp.where(msk,qpr,zb))
    cat=lambda xs: jnp.concatenate(xs,axis=0)
    dkv_ref[0]=tn(cat(qcs),cat(dss)).astype(BF)
    dkv_ref[1]=tn(cat(dms),jnp.concatenate([p_ref[0],p_ref[1]],axis=0)).astype(BF)
    dt_ref[...]=tn(cat(qps),cat(wds)).astype(BF)
    lo=lane<64
    dc=jnp.where(lo,dqc[0],dqc[1]).astype(BF).astype(F32)
    dpp=nn(flip,jnp.where(lo,dqp[0],dqp[1]).astype(BF))
    z=jnp.where(lo,gz[0],gz[1]); o=jnp.where(lo,go[0],go[1])
    dty=z*e0+o*e1
    dq_ref[...]=(c*(dc+dpp+dty)).astype(BF)
    vec_ref[0:1,:]=c*jnp.sum(dc,axis=0,keepdims=True)
    vec_ref[1:2,:]=c*jnp.sum(dpp,axis=0,keepdims=True)
    vec_ref[2:3,:]=c*jnp.sum(dty,axis=0,keepdims=True)
    vec_ref[3:4,:]=jnp.sum(z*qt,axis=0,keepdims=True)
    vec_ref[4:5,:]=jnp.sum(o*qt,axis=0,keepdims=True)
    vec_ref[5:8,:]=jnp.zeros((3,128),F32)

def col(n): return pl.BlockSpec((n,128),lambda i:(0,i))
def const(shape): return pl.BlockSpec(shape,lambda i:(0,)*len(shape))
def att_fwd(q,rows,pen,kind,k,v,t,ka):
    T,D=q.shape; W=k.shape[0]; P=D//128; H=D//DH
    return pl.pallas_call(att_fwd_kernel,grid=(P,),
      in_specs=[col(T),col(8),const((T,128)),const((T,128)),col(W),col(W),col(W+T),const((W,128))],
      out_specs=[col(T),pl.BlockSpec((2,T,W),lambda i:(i,0,0))],
      out_shape=[jax.ShapeDtypeStruct((T,D),F32),jax.ShapeDtypeStruct((H,T,W),BF)],
      compiler_params=pltpu.CompilerParams(vmem_limit_bytes=60*2**20),
      cost_estimate=pl.CostEstimate(flops=2*H*T*W*(256+128+128),bytes_accessed=2*(3*W*D+H*T*W),transcendentals=H*T*W),
      name="att_fwd")(q,rows,pen,kind,k,v,t,ka)
def att_bwd(q,rows,kind,dm,o,p,k,v,t,ka):
    T,D=q.shape; W=k.shape[0]; P=D//128; H=D//DH
    row=lambda n: pl.BlockSpec((128,n),lambda i:(i,0))
    return pl.pallas_call(att_bwd_kernel,grid=(P,),
      in_specs=[col(T),col(8),const((T,128)),col(T),col(T),pl.BlockSpec((2,T,W),lambda i:(i,0,0)),col(W),col(W),col(W+T),const((W,128))],
      out_specs=[col(T),col(8),pl.BlockSpec((2,128,W),lambda i:(0,i,0)),row(W+T)],
      out_shape=[jax.ShapeDtypeStruct((T,D),BF),jax.ShapeDtypeStruct((8,D),F32),jax.ShapeDtypeStruct((2,D,W),BF),jax.ShapeDtypeStruct((D,W+T),BF)],
      compiler_params=pltpu.CompilerParams(vmem_limit_bytes=60*2**20),
      cost_estimate=pl.CostEstimate(flops=2*H*T*W*(128*5),bytes_accessed=2*(6*W*D+H*T*W),transcendentals=0),
      name="att_bwd")(q,rows,kind,dm,o,p,k,v,t,ka)


def layer_norm(residual, gain_vec, bias_vec):
    center = residual - jnp.mean(residual, axis=-1, keepdims=True)
    spread = jnp.mean(center * center, axis=-1, keepdims=True)
    return center * lax.rsqrt(spread + EPS) * gain_vec + bias_vec


def sinus_rows(first, count, width):
    half = width // 2
    freq = jnp.power(10000.0, -jnp.arange(half, dtype=F32) / half)
    coarse = (first - 64 * jnp.arange(count // 64)).astype(F32)[:, None] * freq
    fine = jnp.arange(64).astype(F32)[:, None] * freq
    sa, ca = jnp.sin(coarse)[:, None], jnp.cos(coarse)[:, None]
    sb, cb = jnp.sin(fine)[None], jnp.cos(fine)[None]
    both = jnp.concatenate([sa * cb - ca * sb, ca * cb + sa * sb], axis=2)
    return both.astype(BF).reshape(count, width)


class Shards:
    def __init__(self):
        self.parts = lax.axis_size("fsdp")
        self.pair = self.parts == 2
        self.f = lax.axis_index("fsdp")
        self.core = lax.axis_index("ctx") % 2
        self.swap = [(0, 1), (1, 0)]
        self.cores = [(i, i ^ 1) for i in range(lax.axis_size("ctx"))]

    def full(self, w):
        if not self.pair:
            return lax.all_gather(w, "fsdp", axis=0, tiled=True)
        half = w.shape[0] // 2
        mine = lax.dynamic_slice_in_dim(w, self.core * half, half, 0)
        got = lax.ppermute(mine, "fsdp", self.swap)
        other = lax.ppermute(got, "ctx", self.cores)
        low = jnp.where(self.core == 0, got, other)
        high = jnp.where(self.core == 0, other, got)
        theirs = jnp.concatenate([low, high], axis=0)
        return jnp.concatenate(
            [jnp.where(self.f == 0, w, theirs), jnp.where(self.f == 0, theirs, w)], axis=0
        )

    def full_small(self, w):
        if not self.pair:
            return lax.all_gather(w, "fsdp", axis=0, tiled=False)
        theirs = lax.ppermute(w, "fsdp", self.swap)
        return jnp.stack([jnp.where(self.f == 0, w, theirs), jnp.where(self.f == 0, theirs, w)])

    def own(self, a, axis, other=False):
        n = a.shape[axis] // self.parts
        at = (1 - self.f) if other else self.f
        return lax.dynamic_slice_in_dim(a, at * n, n, axis)

    def trade(self, a):
        return lax.ppermute(a, "fsdp", self.swap)

    def sum_rows(self, g):
        if not self.pair:
            return lax.psum_scatter(g.astype(BF), "fsdp", scatter_dimension=0, tiled=True)
        got = self.trade(self.own(g, 0, True).astype(BF))
        return (self.own(g, 0) + got.astype(F32)).astype(BF)


def per_device(
    hidden_in,
    segment_ids,
    token_types,
    out_grad,
    query_proj,
    key_proj,
    value_proj,
    value_bias,
    content_bias,
    position_bias,
    type_bias,
    type_embed,
    position_proj,
    output_proj,
    output_bias,
    attn_gain,
    attn_shift,
    inner_proj,
    inner_bias,
    outer_proj,
    outer_bias,
    ffn_gain,
    ffn_shift,
):
    sh = Shards()
    hidden = hidden_in[0]
    cotangent = out_grad[0].astype(F32)
    T, D = hidden.shape
    C = lax.axis_size("ctx")
    ctx = lax.axis_index("ctx")
    L = T * C
    R = C // 2
    NB = 2 * R + 1
    W = NB * T
    scale = DH ** (-0.5)

    dn = D // sh.parts
    small = jnp.concatenate(
        [
            jnp.stack(
                [
                    value_bias, content_bias, position_bias, type_bias, type_embed[0],
                    type_embed[1], output_bias, attn_gain, attn_shift, outer_bias,
                    ffn_gain, ffn_shift,
                ]
            ),
            inner_bias.reshape(-1, dn),
        ],
        axis=0,
    )
    nsmall = small.shape[0]
    small_full = sh.full_small(small).astype(F32)
    vecs = jnp.transpose(small_full[:, :12], (1, 0, 2)).reshape(12, D)
    v_bias, _, _, _, _, _, o_bias, a_gain, a_shift, out_bias, f_gain, f_shift = (
        vecs[i] for i in range(12)
    )
    in_bias = small_full[:, 12:].reshape(-1)
    qkv_full = sh.full(jnp.concatenate([query_proj, key_proj, value_proj], axis=1))
    po_full = sh.full(jnp.concatenate([position_proj, output_proj], axis=1))
    inner_full = sh.full(inner_proj)
    outer_full = sh.full(outer_proj)
    q_full, kv_full = qkv_full[:, :D], qkv_full[:, D:]
    p_full, o_full = po_full[:, :D], po_full[:, D:]

    ids = jnp.zeros((16, D), BF)
    ids = ids.at[0, :T].set(segment_ids[0].astype(BF)).at[1, :T].set(token_types[0].astype(BF))
    gathered = lax.all_gather(jnp.concatenate([hidden, ids], axis=0), "ctx", axis=0, tiled=True)
    gathered = gathered.reshape(C, T + 16, D)
    padded = jnp.pad(gathered, ((R, R), (0, 0), (0, 0)))
    window = lax.dynamic_slice_in_dim(padded, ctx, NB, 0)
    x_win = window[:, :T].reshape(W, D)
    valid = jnp.arange(NB) + ctx - R
    valid = (valid >= 0) & (valid < C)
    seg_k = jnp.where(valid[:, None], window[:, T, :T].astype(jnp.int32), 7).reshape(W, 1)
    kind_k = window[:, T + 1, :T].astype(jnp.int32).reshape(W, 1)
    lane = jnp.arange(128)[None, :]
    in_seg = (lane >= 8) & (lane < 16)
    kaug = jnp.where(
        lane < 3,
        kind_k == 1,
        jnp.where((lane >= 4) & (lane < 7), kind_k == 0, in_seg & (lane - 8 == seg_k)),
    ).astype(BF)
    pen = jnp.where(in_seg & (lane - 8 != segment_ids[0][:, None]), -BIG, 0.0).astype(F32)
    kind_q = jnp.broadcast_to(token_types[0][:, None], (T, 128)).astype(F32)

    q_lin = nn(hidden, q_full)
    kv = nn(x_win, kv_full)
    keys = kv[:, :D].astype(BF)
    values = (kv[:, D:] + v_bias).astype(BF)
    sinus = sinus_rows(T + R * T - 1, W + T, D)
    table = nn(sinus, p_full).astype(BF)
    rows = jnp.concatenate([vecs[1:6], jnp.zeros((3, D), F32)], axis=0)

    mixed_f, probs = att_fwd(q_lin, rows, pen, kind_q, keys, values, table, kaug)
    mixed_low = mixed_f.astype(BF)
    attn_out = nn(mixed_low, o_full) + o_bias
    normed, first_pull = jax.vjp(layer_norm, hidden.astype(F32) + attn_out, a_gain, a_shift)
    normed_low = normed.astype(BF)
    inner_pre = nn(normed_low, inner_full) + in_bias
    activated, gelu_pull = jax.vjp(partial(jax.nn.gelu, approximate=True), inner_pre)
    activ_low = activated.astype(BF)
    outer_out = nn(activ_low, outer_full) + out_bias
    outcome, second_pull = jax.vjp(layer_norm, normed + outer_out, f_gain, f_shift)
    d_res2, grad_ffn_gain, grad_ffn_shift = second_pull(cotangent)
    d_outer = d_res2.astype(BF)
    grad_outer_bias = jnp.sum(d_outer.astype(F32), axis=0)
    d_inner = gelu_pull(nt(d_outer, outer_full))[0].astype(BF)
    grad_inner_bias = jnp.sum(d_inner.astype(F32), axis=0)
    d_normed = d_res2 + nt(d_inner, inner_full)
    d_res1, grad_attn_gain, grad_attn_shift = first_pull(d_normed)
    d_attn = d_res1.astype(BF)
    grad_output_bias = jnp.sum(d_attn.astype(F32), axis=0)
    d_mixed = nt(d_attn, o_full).astype(BF)

    dq, att_vec, dkv, d_table = att_bwd(
        q_lin, rows, kind_q, d_mixed, mixed_f, probs, keys, values, table, kaug
    )
    dkv = dkv.reshape(2 * D, W)
    grad_value_bias = jnp.sum(dkv[D:].astype(F32), axis=1)
    d_hid = lax.dot_general(
        dkv, kv_full, (((0,), (1,)), ((), ())), preferred_element_type=F32
    ).astype(BF)
    d_hid = jnp.pad(d_hid, (((C - 1 - R) * T, (C - 1) * T + L - (C - 1 - R) * T - W), (0, 0)))
    d_hid = lax.dynamic_slice_in_dim(d_hid, (C - 1 - ctx) * T, L, 0)
    d_hid_own = lax.psum_scatter(d_hid, "ctx", scatter_dimension=0, tiled=True).astype(F32)
    input_grad = d_res1 + nt(dq, q_full) + d_hid_own

    gkv = lax.dot_general(x_win, dkv, (((0,), (1,)), ((), ())), preferred_element_type=F32)
    gp = lax.dot_general(sinus, d_table, (((0,), (1,)), ((), ())), preferred_element_type=F32)
    gkv = sh.sum_rows(gkv)
    gp = sh.sum_rows(gp)

    pairs = (
        (hidden, dq), (mixed_low, d_attn), (normed_low, d_inner), (activ_low, d_outer)
    )
    if sh.pair:
        lefts = [sh.own(a, 1, True) for a, _ in pairs]
        got = sh.trade(jnp.concatenate(lefts, axis=1))
        sums = []
        at = 0
        for a, b in pairs:
            n = a.shape[1] // 2
            left = jnp.concatenate([sh.own(a, 1), got[:, at : at + n]], axis=0)
            right = jnp.concatenate([b, sh.trade(b)], axis=0)
            sums.append(tn(left, right).astype(BF))
            at += n
    else:
        sums = [sh.sum_rows(tn(a, b)) for a, b in pairs]
    gq, go, gi, gout = sums

    smalls = jnp.stack(
        [
            grad_value_bias, att_vec[0], att_vec[1], att_vec[2], att_vec[3], att_vec[4],
            grad_output_bias, grad_attn_gain, grad_attn_shift, grad_outer_bias,
            grad_ffn_gain, grad_ffn_shift,
        ]
    )
    smalls = jnp.transpose(smalls.reshape(12, sh.parts, dn), (1, 0, 2))
    smalls = jnp.concatenate([smalls, grad_inner_bias.reshape(sh.parts, -1, dn)], axis=1)
    smalls = sh.sum_rows(smalls.reshape(sh.parts * nsmall, dn))

    gkv, gp, gq, go, gi, gout, smalls = (
        a.astype(F32) for a in lax.psum((gkv, gp, gq, go, gi, gout, smalls), "ctx")
    )
    s = [smalls[i] for i in range(12)]
    return (
        outcome.astype(BF)[None],
        input_grad[None],
        gq,
        gkv[:, :D],
        gkv[:, D:],
        s[0],
        s[1],
        s[2],
        s[3],
        smalls[4:6],
        gp,
        go,
        s[6],
        s[7],
        s[8],
        gi,
        smalls[12:].reshape(-1),
        gout,
        s[9],
        s[10],
        s[11],
    )


def solution(mesh):
    in_specs = (
        P("fsdp", "ctx", None),
        P("fsdp", "ctx"),
        P("fsdp", "ctx"),
        P("fsdp", "ctx", None),
        P("fsdp", None),
        P("fsdp", None),
        P("fsdp", None),
        P("fsdp"),
        P("fsdp"),
        P("fsdp"),
        P("fsdp"),
        P(None, "fsdp"),
        P("fsdp", None),
        P("fsdp", None),
        P("fsdp"),
        P("fsdp"),
        P("fsdp"),
        P("fsdp", None),
        P("fsdp"),
        P("fsdp", None),
        P("fsdp"),
        P("fsdp"),
        P("fsdp"),
    )
    out_specs = (
        P("fsdp", "ctx", None),
        P("fsdp", "ctx", None),
        P("fsdp", None),
        P("fsdp", None),
        P("fsdp", None),
        P("fsdp"),
        P("fsdp"),
        P("fsdp"),
        P("fsdp"),
        P(None, "fsdp"),
        P("fsdp", None),
        P("fsdp", None),
        P("fsdp"),
        P("fsdp"),
        P("fsdp"),
        P("fsdp", None),
        P("fsdp"),
        P("fsdp", None),
        P("fsdp"),
        P("fsdp"),
        P("fsdp"),
    )
    return jax.shard_map(
        per_device, mesh=mesh, in_specs=in_specs, out_specs=out_specs, check_vma=False
    )
```

time: 1700 us -> 499 us (0.29)
  local copies, waits for them, and re-layouts: 583 us -> 67 us
  waiting for transfers between devices: 656 us -> 191 us
  matrix products: 164 us -> 55.2 us
  blocking collectives: 162 us -> 62.9 us
  Pallas kernels: 0 us -> 35.9 us
  loops' own time: 34.5 us -> 0 us
  other arithmetic: 69.1 us -> 52 us
    reduce_scatter x7 -> x1, waiting for transfers between devices: 366 us -> 0.01 us  [per_device(): lax.psum_scatter(d_hid, 'ctx', scatter_dimension=0, tiled=True).astype(F32)]
    all_gather x10 -> x1, waiting for transfers between devices: 134 us -> 0.01 us  [per_device(): lax.all_gather(jnp.concatenate([hidden, ids], axis=0), 'ctx', axis=0, til...]
    ppermute x0 -> x17, waiting for transfers between devices: none -> 123 us  [the longest x8 69.3 us: trade(): return lax.ppermute(a, 'fsdp', self.swap)]
    while x280 -> x0, local copies, waits for them, and re-layouts: 119 us -> none
    dot_general x70 -> x17, matrix products: 164 us -> 55.2 us  [the longest x6 15.3 us: nn(): lax.dot_general(a, b, (((1,), (0,)), ((), ())), preferred_element_type=F32)]
    reshape x16 -> x4, local copies, waits for them, and re-layouts: 100 us -> 3.32 us  [the longest x2 1.32 us: per_device(): grad_inner_bias.reshape(sh.parts, -1, dn)]
    all_gather x14 -> x0, blocking collectives: 91.1 us -> none  [the longest x1 21.2 us: per_device(): lax.all_gather(segs_local, 'ctx', axis=0, tiled=True)]
    dynamic_slice x60 -> x9, local copies, waits for them, and re-layouts: 86.1 us -> 11.7 us  [the longest x4 4.38 us: full(): mine = lax.dynamic_slice_in_dim(w, self.core * half, half, 0)]
  transfers between devices with their start and end apart: 22 -> 20, of which waited for: 17 -> 7; matrix products, arithmetic and copies ran while one was open for 25% -> 20% of each run, Pallas kernels for 0% -> 0%
where the time goes in v1:
time: 499 us; the launch traced here: 493 us
  waiting for transfers between devices  191 us (38%)
  local copies, waits for them, and re-layouts  67 us (13%)
  blocking collectives  62.9 us (13%)
  matrix products  55.2 us (11%)
  other arithmetic  52 us (10%)
  Pallas kernels  35.9 us (7%)
  starting transfers between devices  14.8 us (3%)
  between operations  14.7 us (3%)
    ppermute x8, waiting for transfers between devices, trade(): return lax.ppermute(a, 'fsdp', self.swap)  69.3 us
    psum x1, waiting for transfers between devices, per_device(): lax.psum((gkv, gp, gq, go, gi, gout, smalls), 'ctx')  67.6 us
    psum x1, blocking collectives, per_device(): lax.psum((gkv, gp, gq, go, gi, gout, smalls), 'ctx')  62.9 us
    ppermute x4, waiting for transfers between devices, full(): got = lax.ppermute(mine, 'fsdp', self.swap)  53.6 us
    pallas_call x1, Pallas kernels, att_fwd(): pl.pallas_call(att_fwd_kernel, grid=(P,), in_specs=[col(T), col(8), const...  19.4 us
    pallas_call x1, Pallas kernels, att_bwd(): pl.pallas_call(att_bwd_kernel, grid=(P,), in_specs=[col(T), col(8), const...  16.5 us
    dot_general x6, matrix products, nn(): lax.dot_general(a, b, (((1,), (0,)), ((), ())), preferred_element_type=F32)  15.3 us
    unnamed x132, local copies, waits for them, and re-layouts  14.7 us
  transfers between devices with their start and end apart: 20, of which 7 were waited for; matrix products, arithmetic and copies ran while one was open for 20% of the time, Pallas kernels for 0%

profile of v1, /device:TPU:0, one launch (start us, length us, event | category | flops | bytes accessed | tf_op | source)
XLA Modules:
  0.0 493.0 jit_solution(15640488123270207746)
XLA Ops:
  15.6 3.0 collective-permute-start.2
  26.8 2.0 collective-permute-start.3
  29.0 2.4 constant_dynamic-slice_fusion.6
  31.4 2.0 collective-permute-start.7
  34.6 3.0 subtract_convert_fusion
  40.1 17.4 %collective-permute-done.3 = bf16[192,1536]{1,0:T(8,128)(2,1)S(1)} collective-permute-done((bf16[192,1536]{1,0:T(8,128)(2,1)}, bf16[192,1536]{1,0:T(8,128)(2,1)S(1)}, u32[]{:S(2)}, u32[]{:S(2)}) %collective-permute-start.3) | collective-permute-done | bytes 589856 | tf_op jit(solution)/shard_map/ppermute | solution.py:185
  70.5 12.4 %collective-permute-done.5 = bf16[192,3072]{1,0:T(8,128)(2,1)} collective-permute-done((bf16[192,3072]{1,0:T(8,128)(2,1)S(1)}, bf16[192,3072]{1,0:T(8,128)(2,1)}, u32[]{:S(2)}, u32[]{:S(2)}) %collective-permute-start.5) | collective-permute-done | bytes 1179680 | tf_op jit(solution)/shard_map/ppermute | solution.py:185
  82.9 23.8 %collective-permute-done.7 = bf16[768,768]{1,0:T(8,128)(2,1)} collective-permute-done((bf16[768,768]{1,0:T(8,128)(2,1)}, bf16[768,768]{1,0:T(8,128)(2,1)}, u32[]{:S(2)}, u32[]{:S(2)}) %collective-permute-start.7) | collective-permute-done | bytes 1179680 | tf_op jit(solution)/shard_map/ppermute | solution.py:185
  109.6 4.5 convolution_convert_fusion.1.t_ref
  114.2 1.4 broadcast_select_fusion.13
  117.9 1.7 broadcast_select_fusion.7
  119.9 3.1 broadcast_select_fusion.1
  123.0 1.7 broadcast_select_fusion.9
  125.0 3.4 broadcast_select_fusion.3
  128.4 2.1 pad_dynamic-slice_fusion.1
  130.5 5.4 %fusion.23 = f32[2176,1536]{1,0:T(8,128)S(1)} fusion(bf16[2176,768]{1,0:T(8,128)(2,1)S(1)} %bitcast.70, bf16[384,2304]{1,0:T(8,128)(2,1)S(1)} %get-tuple-element.100, bf16[384,2304]{1,0:T(8,128)(2,1)S(1)} %get-tuple-element.99), kind=kOutput, calls=%fused_computation.75 | convolution fusion | flops 5138546688 | bytes 20250624 | tf_op jit(solution)/shard_map/dot_general | solution.py:22
  135.9 2.1 slice.274.k_ref
  138.0 2.7 fusion.v_ref
  141.6 3.1 select_convert_fusion.ka_ref
  145.4 19.4 %att_fwd.1 = (f32[128,768]{1,0:T(8,128)}, bf16[12,128,2176]{2,1,0:T(8,128)(2,1)}) custom-call(f32[128,768]{1,0:T(8,128)} %convolution_bitcast_fusion.q_ref, f32[8,768]{1,0:T(8,128)} %concatenate.84.rows_ref, f32[128,128]{1,0:T(8,128)} %and_select_fusion.pen_ref, f32[128,128]{1,0:T(8,128)} %broadcast_in_dim.89.kind_ref, bf16[2176,768]{1,0:T(8,128)(2,1)} %slice.274.k_ref, ...), custom_call_target="tpu_custom_call" | custom-call | flops 3422552064 | bytes 16711680 | tf_op jit(solution)/shard_map/att_fwd/pallas_call | solution.py:135
  166.6 1.8 fusion.75
  169.5 1.6 multiply_convert_fusion
  175.4 6.1 %convert_reduce_fusion.1 = (f32[3072]{0:T(1024)}, bf16[128,3072]{1,0:T(8,128)(2,1)S(1)}) fusion(f32[128,3072]{1,0:T(8,128)S(1)} %get-tuple-element.138, bf16[128,768]{1,0:T(8,128)(2,1)S(1)} %get-tuple-element.88, bf16[1536,768]{1,0:T(8,128)(2,1)S(1)} %copy-done.20, bf16[1536,768]{1,0:T(8,128)(2,1)S(1)} %copy-done.19), kind=kOutput, calls=%fused_computation.48 | convolution fusion | flops 622064640 | bytes 7286784 | tf_op jit(solution)/shard_map/dot_general | solution.py:18
  181.5 2.4 multiply_reduce_fusion
  186.7 16.5 %att_bwd.1 = (bf16[128,768]{1,0:T(8,128)(2,1)}, f32[8,768]{1,0:T(8,128)}, bf16[2,768,2176]{2,1,0:T(8,128)(2,1)}, bf16[768,2304]{1,0:T(8,128)(2,1)}) custom-call(f32[128,768]{1,0:T(8,128)} %convolution_bitcast_fusion.q_ref, f32[8,768]{1,0:T(8,128)} %concatenate.84.rows_ref, f32[128,128]{1,0:T(8,128)} %broadcast_in_dim.89.kind_ref, ...), custom_call_target="tpu_custom_call" | custom-call | flops 4278190080 | bytes 26738688 | tf_op jit(solution)/shard_map/att_bwd/pallas_call | solution.py:145
  203.2 9.5 %convolution_convert_fusion = bf16[2176,768]{1,0:T(8,128)(2,1)S(1)} fusion(bf16[1536,2176]{1,0:T(8,128)(2,1)} %bitcast.77, bf16[384,2304]{1,0:T(8,128)(2,1)S(1)} %get-tuple-element.100, bf16[384,2304]{1,0:T(8,128)(2,1)S(1)} %get-tuple-element.99), kind=kOutput, calls=%fused_computation.8 | convolution fusion | flops 5140217856 | bytes 13565952 | tf_op jit(solution)/shard_map/dot_general | solution.py:335
  212.7 3.9 pad_dynamic-slice_fusion.3
  219.7 5.7 %fusion.4 = f32[768,768]{1,0:T(8,128)S(1)} fusion(bf16[768,2304]{1,0:T(8,128)(2,1)} %get-tuple-element.56, bf16[2304,384]{1,0:T(8,128)(2,1)} %bitcast.75, bf16[2304,384]{1,0:T(8,128)(2,1)S(1)} %bitcast.74), kind=kOutput, calls=%fused_computation.32 | convolution fusion | flops 2724986880 | bytes 9437184 | tf_op jit(solution)/shard_map/dot_general | solution.py:344
  225.5 1.8 collective-permute-start.13
  227.3 5.7 %fusion.77 = f32[768,1536]{1,0:T(8,128)S(1)} fusion(bf16[2176,768]{1,0:T(8,128)(2,1)S(1)} %bitcast.71, bf16[1536,2176]{1,0:T(8,128)(2,1)S(1)} %bitcast.80), kind=kOutput, calls=%fused_computation.225 | convolution fusion | flops 5133828096 | bytes 14745600 | tf_op jit(solution)/shard_map/dot_general | solution.py:343
  233.9 1.4 collective-permute-start.14
  235.9 14.3 %collective-permute-done.13 = bf16[384,768]{1,0:T(8,128)(2,1)S(1)} collective-permute-done((bf16[384,768]{1,0:T(8,128)(2,1)S(1)}, bf16[384,768]{1,0:T(8,128)(2,1)S(1)}, u32[]{:S(2)}, u32[]{:S(2)}) %collective-permute-start.13) | collective-permute-done | bytes 589856 | tf_op jit(solution)/shard_map/ppermute | solution.py:206
  251.5 1.7 collective-permute-start.10
  253.3 51.4 %collective-permute-done.10 = bf16[128,768]{1,0:T(8,128)(2,1)S(1)} collective-permute-done((bf16[128,768]{1,0:T(8,128)(2,1)S(1)}, bf16[128,768]{1,0:T(8,128)(2,1)S(1)}, u32[]{:S(2)}, u32[]{:S(2)}) %collective-permute-start.10) | collective-permute-done | bytes 196640 | tf_op jit(solution)/shard_map/ppermute | solution.py:206
  307.1 2.3 convolution_convert_fusion.3
  309.4 2.2 convolution_convert_fusion.2
  311.6 1.4 add_convert_fusion.1
  315.9 2.4 convert_reduce_fusion
  332.5 3.5 collective-permute-done.12
  336.0 1.4 add_convert_fusion.6
  337.4 62.9 %psum.51 = bf16[16,384]{1,0:T(8,128)(2,1)S(1)} all-reduce(bf16[16,384]{1,0:T(8,128)(2,1)} %add_convert_fusion.6), channel_id=1, replica_groups=mesh['ctx'=16,'fsdp'=2] {'ctx'}, use_global_device_ids=true, to_apply=%region_19.20 | all-reduce | flops 6144 | bytes 24576 | tf_op jit(solution)/shard_map/psum | solution.py:378
  403.3 1.6 slice_reduce_fusion.7
  404.9 2.5 fusion.17
  407.4 67.6 %all-reduce.7.cloned.1.call-done = (bf16[384,768]{1,0:T(8,128)(2,1)}, bf16[384,1536]{1,0:T(8,128)(2,1)}, bf16[384,768]{1,0:T(8,128)(2,1)}, bf16[384,768]{1,0:T(8...) async-done(((bf16[384,768]{1,0:T(8,128)(2,1)}, bf16[384,1536]{1,0:T(8,128)(2,1)}, bf16[384,768]{1,0:T(8,128)(2,1)}, bf16[384,768]{1,0:T(8,128)(2,1)}, ...) | async-done | bytes 7667728 | tf_op jit(solution)/shard_map/psum | solution.py:378
  475.0 2.2 convert_element_type.212
  477.3 1.6 fusion.72
  481.0 2.8 convert_element_type.232
  483.8 2.5 convert_element_type.234
  (270 shorter events, 81.2 us)
Async XLA Ops:
  7.2 13.7 %copy-start.32 = (bf16[384,768]{1,0:T(8,128)(2,1)S(1)}, bf16[384,768]{1,0:T(8,128)(2,1)}, u32[]{:S(2)}) copy-start(bf16[384,768]{1,0:T(8,128)(2,1)} %param.33) | copy-start | bytes 1769476
  7.2 121.2 %all-gather.2.cloned.1.call-start = ((), (), s32[]{:S(2)}) async-start(), calls=%async_computation.1 | async-start | bytes 3760128 | tf_op jit(solution)/shard_map/all_gather | solution.py:282
  15.6 6.5 %copy-start.41 = (bf16[16,384]{1,0:T(8,128)(2,1)}, bf16[16,384]{1,0:T(8,128)(2,1)S(1)}, u32[]{:S(2)}) copy-start(bf16[16,384]{1,0:T(8,128)(2,1)S(1)} %concatenate.83) | copy-start | bytes 36868
  15.6 41.9 %collective-permute-start.2 = (bf16[16,384]{1,0:T(8,128)(2,1)S(1)}, bf16[16,384]{1,0:T(8,128)(2,1)}, u32[]{:S(2)}, u32[]{:S(2)}) collective-permute-start(bf16[16,384]{1,0:T(8,128)(2,1)S(1)} %concatenate.83), channel_id=1, source_target_pairs={{0,1},{1,0},{2,3},{3,2},{4,5},{5,4},{6,7},{7,6},{8,9},{9,8},{10,11... | collective-permute-start | bytes 36872 | tf_op jit(solution)/shard_map/ppermute | solution.py:197
  19.7 2.9 copy-start.51
  19.7 3.1 copy-start.14
  21.0 5.0 %copy-start.5 = (bf16[384,2304]{1,0:T(8,128)(2,1)}, bf16[384,2304]{1,0:T(8,128)(2,1)S(1)}, u32[]{:S(2)}) copy-start(bf16[384,2304]{1,0:T(8,128)(2,1)S(1)} %constant_dynamic-update-slice_fusion) | copy-start | bytes 5308420
  22.1 47.9 %collective-permute-start = (bf16[192,2304]{1,0:T(8,128)(2,1)}, bf16[192,2304]{1,0:T(8,128)(2,1)}, u32[]{:S(2)}, u32[]{:S(2)}) collective-permute-start(bf16[192,2304]{1,0:T(8,128)(2,1)} %constant_dynamic-slice_fusion.9), channel_id=1, source_target_pairs={{0,1},{1,0},{2,3},{3,2},{4,5},{5,4},{6,7},{7,6},{8,9},{9,8},{10,11... | collective-permute-start | bytes 2654216 | tf_op jit(solution)/shard_map/ppermute | solution.py:185
  23.5 381.4 %reduce-scatter.2.cloned.1.call-start = ((), (), s32[]{:S(2)}) async-start(), calls=%async_computation.2 | async-start | bytes 3342336 | tf_op jit(solution)/shard_map/reduce_scatter | solution.py:340
  23.6 5.3 %copy-start.8 = (bf16[384,3072]{1,0:T(8,128)(2,1)S(1)}, bf16[384,3072]{1,0:T(8,128)(2,1)}, u32[]{:S(2)}) copy-start(bf16[384,3072]{1,0:T(8,128)(2,1)} %param.44) | copy-start | bytes 7077892
  26.8 30.6 %collective-permute-start.3 = (bf16[192,1536]{1,0:T(8,128)(2,1)}, bf16[192,1536]{1,0:T(8,128)(2,1)S(1)}, u32[]{:S(2)}, u32[]{:S(2)}) collective-permute-start(bf16[192,1536]{1,0:T(8,128)(2,1)} %constant_dynamic-slice_fusion.8), channel_id=1, source_target_pairs={{0,1},{1,0},{2,3},{3,2},{4,5},{5,4},{6,7},{7,6},{8,9},{9,8},{10,11... | collective-permute-start | bytes 1769480 | tf_op jit(solution)/shard_map/ppermute | solution.py:185
  28.9 53.9 %collective-permute-start.5 = (bf16[192,3072]{1,0:T(8,128)(2,1)S(1)}, bf16[192,3072]{1,0:T(8,128)(2,1)}, u32[]{:S(2)}, u32[]{:S(2)}) collective-permute-start(bf16[192,3072]{1,0:T(8,128)(2,1)S(1)} %constant_dynamic-slice_fusion.7), channel_id=1, source_target_pairs={{0,1},{1,0},{2,3},{3,2},{4,5},{5,4},{6,7},{7,6},{8,9},{9,8},{10,11... | collective-permute-start | bytes 3538952 | tf_op jit(solution)/shard_map/ppermute | solution.py:185
  31.4 75.3 %collective-permute-start.7 = (bf16[768,768]{1,0:T(8,128)(2,1)}, bf16[768,768]{1,0:T(8,128)(2,1)}, u32[]{:S(2)}, u32[]{:S(2)}) collective-permute-start(bf16[768,768]{1,0:T(8,128)(2,1)} %constant_dynamic-slice_fusion.6), channel_id=1, source_target_pairs={{0,1},{1,0},{2,3},{3,2},{4,5},{5,4},{6,7},{7,6},{8,9},{9,8},{10,11... | collective-permute-start | bytes 3538952 | tf_op jit(solution)/shard_map/ppermute | solution.py:185
  33.9 6.2 %copy-start.46 = (pred[128]{0:T(512)(128)(4,1)}, pred[128]{0:T(512)(128)(4,1)S(1)}, u32[]{:S(2)}) copy-start(pred[128]{0:T(512)(128)(4,1)S(1)} %get-tuple-element.145) | copy-start | bytes 388
  57.5 49.2 %collective-permute-start.4 = (bf16[192,1536]{1,0:T(8,128)(2,1)S(1)}, bf16[192,1536]{1,0:T(8,128)(2,1)S(1)}, u32[]{:S(2)}, u32[]{:S(2)}) collective-permute-start(bf16[192,1536]{1,0:T(8,128)(2,1)S(1)} %collective-permute-done.3), channel_id=1, source_target_pairs={{0,2},{2,0},{4,6},{6,4},{8,10},{10,8},{12,14},{14,12},{16,18},{18,... | collective-permute-start | bytes 1769480 | tf_op jit(solution)/shard_map/ppermute | solution.py:186
  70.0 44.2 %collective-permute-start.1 = (bf16[192,2304]{1,0:T(8,128)(2,1)}, bf16[192,2304]{1,0:T(8,128)(2,1)S(1)}, u32[]{:S(2)}, u32[]{:S(2)}) collective-permute-start(bf16[192,2304]{1,0:T(8,128)(2,1)} %collective-permute-done), channel_id=1, source_target_pairs={{0,2},{2,0},{4,6},{6,4},{8,10},{10,8},{12,14},{14,12},{16,18},{18,... | collective-permute-start | bytes 2654216 | tf_op jit(solution)/shard_map/ppermute | solution.py:186
  82.9 40.1 %collective-permute-start.6 = (bf16[192,3072]{1,0:T(8,128)(2,1)}, bf16[192,3072]{1,0:T(8,128)(2,1)S(1)}, u32[]{:S(2)}, u32[]{:S(2)}) collective-permute-start(bf16[192,3072]{1,0:T(8,128)(2,1)} %collective-permute-done.5), channel_id=1, source_target_pairs={{0,2},{2,0},{4,6},{6,4},{8,10},{10,8},{12,14},{14,12},{16,18},{18,... | collective-permute-start | bytes 3538952 | tf_op jit(solution)/shard_map/ppermute | solution.py:186
  106.7 11.2 %collective-permute-start.8 = (bf16[768,768]{1,0:T(8,128)(2,1)}, bf16[768,768]{1,0:T(8,128)(2,1)S(1)}, u32[]{:S(2)}, u32[]{:S(2)}) collective-permute-start(bf16[768,768]{1,0:T(8,128)(2,1)} %collective-permute-done.7), channel_id=1, source_target_pairs={{0,2},{2,0},{4,6},{6,4},{8,10},{10,8},{12,14},{14,12},{16,18},{18,... | collective-permute-start | bytes 3538952 | tf_op jit(solution)/shard_map/ppermute | solution.py:186
  107.2 6.9 %copy-start.1 = (bf16[384,1536]{1,0:T(8,128)(2,1)}, bf16[384,1536]{1,0:T(8,128)(2,1)S(1)}, u32[]{:S(2)}) copy-start(bf16[384,1536]{1,0:T(8,128)(2,1)S(1)} %get-tuple-element.105) | copy-start | bytes 3538948
  107.2 6.9 %copy-start.3 = (bf16[384,1536]{1,0:T(8,128)(2,1)}, bf16[384,1536]{1,0:T(8,128)(2,1)S(1)}, u32[]{:S(2)}) copy-start(bf16[384,1536]{1,0:T(8,128)(2,1)S(1)} %get-tuple-element.106) | copy-start | bytes 3538948
  130.5 5.4 %copy-start.12 = (bf16[17,128,768]{2,1,0:T(8,128)(2,1)}, bf16[17,128,768]{2,1,0:T(8,128)(2,1)S(1)}, u32[]{:S(2)}) copy-start(bf16[17,128,768]{2,1,0:T(8,128)(2,1)S(1)} %pad_dynamic-slice_fusion.1) | copy-start | bytes 10027012
  140.9 3.8 copy-start.52
  145.4 21.2 %copy-start.16 = (bf16[1,128,768]{2,1,0:T(8,128)(2,1)S(1)}, bf16[1,128,768]{2,1,0:T(8,128)(2,1)}, u32[]{:S(2)}) copy-start(bf16[1,128,768]{2,1,0:T(8,128)(2,1)} %param.27) | copy-start | bytes 589828
  145.4 21.2 %copy-start.42 = (f32[768]{0:T(1024)S(1)}, f32[768]{0:T(1024)}, u32[]{:S(2)}) copy-start(f32[768]{0:T(1024)} %add.221) | copy-start | bytes 9220
  165.9 3.6 copy-start.22
  166.6 2.9 copy-start.21
  166.6 2.9 copy-start.44
  175.4 6.1 %copy-start.34 = (bf16[128,768]{1,0:T(8,128)(2,1)}, bf16[128,768]{1,0:T(8,128)(2,1)S(1)}, u32[]{:S(2)}) copy-start(bf16[128,768]{1,0:T(8,128)(2,1)S(1)} %get-tuple-element.88) | copy-start | bytes 589828
  181.5 4.0 copy-start.2
  181.5 4.0 copy-start.4
  216.6 258.4 %all-reduce.7.cloned.1.call-start = ((), (), s32[]{:S(2)}) async-start(), calls=%async_computation.3 | async-start | bytes 15335424 | tf_op jit(solution)/shard_map/psum | solution.py:378
  216.8 2.9 copy-start.25
  218.1 9.1 %slice-start = ((s8[6684672]{0:T(1024)(128)(4,1)}), s8[4194304]{0:T(1024)(128)(4,1)S(1)}, s32[]{:S(2)}) async-start(s8[6684672]{0:T(1024)(128)(4,1)} %bitcast.78), calls=%async_computation.4 | async-start | bytes 8388608
  219.3 32.2 %collective-permute-start.9 = (bf16[128,2688]{1,0:T(8,128)(2,1)S(1)}, bf16[128,2688]{1,0:T(8,128)(2,1)S(1)}, u32[]{:S(2)}, u32[]{:S(2)}) collective-permute-start(bf16[128,2688]{1,0:T(8,128)(2,1)S(1)} %pad_maximum_fusion.26), channel_id=1, source_target_pairs={{0,1},{1,0},{2,3},{3,2},{4,5},{5,4},{6,7},{7,6},{8,9},{9,8},{10,11... | collective-permute-start | bytes 2064392 | tf_op jit(solution)/shard_map/ppermute | solution.py:206
  219.7 7.5 %copy-start.13 = (bf16[17,128,768]{2,1,0:T(8,128)(2,1)S(1)}, bf16[17,128,768]{2,1,0:T(8,128)(2,1)}, u32[]{:S(2)}) copy-start(bf16[17,128,768]{2,1,0:T(8,128)(2,1)} %copy-done.12) | copy-start | bytes 10027012
  219.7 7.5 %slice-start.1 = ((s8[6684672]{0:T(1024)(128)(4,1)}), s8[2490368]{0:T(1024)(128)(4,1)S(1)}, s32[]{:S(2)}) async-start(s8[6684672]{0:T(1024)(128)(4,1)} %bitcast.78), calls=%async_computation.5 | async-start | bytes 4980736
  225.5 24.8 %collective-permute-start.13 = (bf16[384,768]{1,0:T(8,128)(2,1)S(1)}, bf16[384,768]{1,0:T(8,128)(2,1)S(1)}, u32[]{:S(2)}, u32[]{:S(2)}) collective-permute-start(bf16[384,768]{1,0:T(8,128)(2,1)S(1)} %dynamic-slice_convert_fusion.1), channel_id=1, source_target_pairs={{0,1},{1,0},{2,3},{3,2},{4,5},{5,4},{6,7},{7,6},{8,9},{9,8},{10,11... | collective-permute-start | bytes 1769480 | tf_op jit(solution)/shard_map/ppermute | solution.py:206
  233.0 17.3 %copy-start.35 = (bf16[128,768]{1,0:T(8,128)(2,1)S(1)}, bf16[128,768]{1,0:T(8,128)(2,1)}, u32[]{:S(2)}) copy-start(bf16[128,768]{1,0:T(8,128)(2,1)} %copy-done.34) | copy-start | bytes 589828
  233.0 18.5 %copy-start.33 = (bf16[128,768]{1,0:T(8,128)(2,1)S(1)}, bf16[128,768]{1,0:T(8,128)(2,1)}, u32[]{:S(2)}) copy-start(bf16[128,768]{1,0:T(8,128)(2,1)} %get-tuple-element.53) | copy-start | bytes 589828
  233.1 71.6 %copy-start.38 = (bf16[128,384]{1,0:T(8,128)(2,1)S(1)}, bf16[128,384]{1,0:T(8,128)(2,1)}, u32[]{:S(2)}) copy-start(bf16[128,384]{1,0:T(8,128)(2,1)} %get-tuple-element.125) | copy-start | bytes 294916
  233.1 72.8 %copy-start.40 = (bf16[128,384]{1,0:T(8,128)(2,1)S(1)}, bf16[128,384]{1,0:T(8,128)(2,1)}, u32[]{:S(2)}) copy-start(bf16[128,384]{1,0:T(8,128)(2,1)} %get-tuple-element.123) | copy-start | bytes 294916
  233.2 78.5 %collective-permute-start.11 = (bf16[384,1536]{1,0:T(8,128)(2,1)S(1)}, bf16[384,1536]{1,0:T(8,128)(2,1)S(1)}, u32[]{:S(2)}, u32[]{:S(2)}) collective-permute-start(bf16[384,1536]{1,0:T(8,128)(2,1)S(1)} %dynamic-slice_convert_fusion), channel_id=1, source_target_pairs={{0,1},{1,0},{2,3},{3,2},{4,5},{5,4},{6,7},{7,6},{8,9},{9,8},{10,11... | collective-permute-start | bytes 3538952 | tf_op jit(solution)/shard_map/ppermute | solution.py:206
  233.9 72.0 %collective-permute-start.14 = (bf16[128,768]{1,0:T(8,128)(2,1)S(1)}, bf16[128,768]{1,0:T(8,128)(2,1)S(1)}, u32[]{:S(2)}, u32[]{:S(2)}) collective-permute-start(bf16[128,768]{1,0:T(8,128)(2,1)S(1)} %copy-done.29), channel_id=1, source_target_pairs={{0,1},{1,0},{2,3},{3,2},{4,5},{5,4},{6,7},{7,6},{8,9},{9,8},{10,11... | collective-permute-start | bytes 589832 | tf_op jit(solution)/shard_map/ppermute | solution.py:206
  235.3 74.1 %collective-permute-start.15 = (bf16[128,3072]{1,0:T(8,128)(2,1)S(1)}, bf16[128,3072]{1,0:T(8,128)(2,1)S(1)}, u32[]{:S(2)}, u32[]{:S(2)}) collective-permute-start(bf16[128,3072]{1,0:T(8,128)(2,1)S(1)} %copy-done.57), channel_id=1, source_target_pairs={{0,1},{1,0},{2,3},{3,2},{4,5},{5,4},{6,7},{7,6},{8,9},{9,8},{10,11... | collective-permute-start | bytes 2359304 | tf_op jit(solution)/shard_map/ppermute | solution.py:206
  250.2 56.8 %collective-permute-start.16 = (bf16[128,768]{1,0:T(8,128)(2,1)S(1)}, bf16[128,768]{1,0:T(8,128)(2,1)S(1)}, u32[]{:S(2)}, u32[]{:S(2)}) collective-permute-start(bf16[128,768]{1,0:T(8,128)(2,1)S(1)} %copy-done.35), channel_id=1, source_target_pairs={{0,1},{1,0},{2,3},{3,2},{4,5},{5,4},{6,7},{7,6},{8,9},{9,8},{10,11... | collective-permute-start | bytes 589832 | tf_op jit(solution)/shard_map/ppermute | solution.py:206
  251.5 53.2 %collective-permute-start.10 = (bf16[128,768]{1,0:T(8,128)(2,1)S(1)}, bf16[128,768]{1,0:T(8,128)(2,1)S(1)}, u32[]{:S(2)}, u32[]{:S(2)}) collective-permute-start(bf16[128,768]{1,0:T(8,128)(2,1)S(1)} %copy-done.33), channel_id=1, source_target_pairs={{0,1},{1,0},{2,3},{3,2},{4,5},{5,4},{6,7},{7,6},{8,9},{9,8},{10,11... | collective-permute-start | bytes 589832 | tf_op jit(solution)/shard_map/ppermute | solution.py:206
  305.9 3.5 copy-start.39
  332.2 3.8 collective-permute-start.12
  (33 other events, 56.3 us)
Sparse Core Ops, SparseCore 0:
  23.7 49.5 all-gather.1
  216.7 66.6 reduce-scatter.1
  313.1 161.8 all-reduce.6

commit v2 on v1

--- a/solution.py
+++ b/solution.py
@@ -128,27 +128,62 @@
     vec_ref[4:5,:]=jnp.sum(o*qt,axis=0,keepdims=True)
     vec_ref[5:8,:]=jnp.zeros((3,128),F32)
 
-def col(n): return pl.BlockSpec((n,128),lambda i:(0,i))
-def const(shape): return pl.BlockSpec(shape,lambda i:(0,)*len(shape))
-def att_fwd(q,rows,pen,kind,k,v,t,ka):
-    T,D=q.shape; W=k.shape[0]; P=D//128; H=D//DH
-    return pl.pallas_call(att_fwd_kernel,grid=(P,),
-      in_specs=[col(T),col(8),const((T,128)),const((T,128)),col(W),col(W),col(W+T),const((W,128))],
-      out_specs=[col(T),pl.BlockSpec((2,T,W),lambda i:(i,0,0))],
-      out_shape=[jax.ShapeDtypeStruct((T,D),F32),jax.ShapeDtypeStruct((H,T,W),BF)],
-      compiler_params=pltpu.CompilerParams(vmem_limit_bytes=60*2**20),
-      cost_estimate=pl.CostEstimate(flops=2*H*T*W*(256+128+128),bytes_accessed=2*(3*W*D+H*T*W),transcendentals=H*T*W),
-      name="att_fwd")(q,rows,pen,kind,k,v,t,ka)
-def att_bwd(q,rows,kind,dm,o,p,k,v,t,ka):
-    T,D=q.shape; W=k.shape[0]; P=D//128; H=D//DH
-    row=lambda n: pl.BlockSpec((128,n),lambda i:(i,0))
-    return pl.pallas_call(att_bwd_kernel,grid=(P,),
-      in_specs=[col(T),col(8),const((T,128)),col(T),col(T),pl.BlockSpec((2,T,W),lambda i:(i,0,0)),col(W),col(W),col(W+T),const((W,128))],
-      out_specs=[col(T),col(8),pl.BlockSpec((2,128,W),lambda i:(0,i,0)),row(W+T)],
-      out_shape=[jax.ShapeDtypeStruct((T,D),BF),jax.ShapeDtypeStruct((8,D),F32),jax.ShapeDtypeStruct((2,D,W),BF),jax.ShapeDtypeStruct((D,W+T),BF)],
-      compiler_params=pltpu.CompilerParams(vmem_limit_bytes=60*2**20),
-      cost_estimate=pl.CostEstimate(flops=2*H*T*W*(128*5),bytes_accessed=2*(6*W*D+H*T*W),transcendentals=0),
-      name="att_bwd")(q,rows,kind,dm,o,p,k,v,t,ka)
+def att_fwd(q, rows, pen, kind, k, v, t, ka):
+    T, D = q.shape
+    W = k.shape[0]
+    heads = D // DH
+    col = lambda n: pl.BlockSpec((n, 128), lambda i: (0, i))
+    fixed = lambda n: pl.BlockSpec((n, 128), lambda i: (0, 0))
+    return pl.pallas_call(
+        att_fwd_kernel,
+        grid=(D // 128,),
+        in_specs=[col(T), col(8), fixed(T), fixed(T), col(W), col(W), col(W + T), fixed(W)],
+        out_specs=[col(T), pl.BlockSpec((2, T, W), lambda i: (i, 0, 0))],
+        out_shape=[
+            jax.ShapeDtypeStruct((T, D), F32),
+            jax.ShapeDtypeStruct((heads, T, W), BF),
+        ],
+        compiler_params=pltpu.CompilerParams(vmem_limit_bytes=60 * 2**20),
+        cost_estimate=pl.CostEstimate(
+            flops=2 * heads * T * W * 2048,
+            bytes_accessed=2 * (3 * W * D + heads * T * W),
+            transcendentals=heads * T * W,
+        ),
+        name="att_fwd",
+    )(q, rows, pen, kind, k, v, t, ka)
+
+
+def att_bwd(q, rows, kind, dm, o, p, k, v, t, ka):
+    T, D = q.shape
+    W = k.shape[0]
+    heads = D // DH
+    col = lambda n: pl.BlockSpec((n, 128), lambda i: (0, i))
+    fixed = lambda n: pl.BlockSpec((n, 128), lambda i: (0, 0))
+    return pl.pallas_call(
+        att_bwd_kernel,
+        grid=(D // 128,),
+        in_specs=[
+            col(T), col(8), fixed(T), col(T), col(T), pl.BlockSpec((2, T, W), lambda i: (i, 0, 0)),
+            col(W), col(W), col(W + T), fixed(W),
+        ],
+        out_specs=[
+            col(T), col(8), pl.BlockSpec((2, 128, W), lambda i: (0, i, 0)),
+            pl.BlockSpec((128, W + T), lambda i: (i, 0)),
+        ],
+        out_shape=[
+            jax.ShapeDtypeStruct((T, D), BF),
+            jax.ShapeDtypeStruct((8, D), F32),
+            jax.ShapeDtypeStruct((2, D, W), BF),
+            jax.ShapeDtypeStruct((D, W + T), BF),
+        ],
+        compiler_params=pltpu.CompilerParams(vmem_limit_bytes=60 * 2**20),
+        cost_estimate=pl.CostEstimate(
+            flops=2 * heads * T * W * 2048,
+            bytes_accessed=2 * (6 * W * D + heads * T * W),
+            transcendentals=0,
+        ),
+        name="att_bwd",
+    )(q, rows, kind, dm, o, p, k, v, t, ka)
 
 
 def layer_norm(residual, gain_vec, bias_vec):
@@ -173,43 +208,75 @@
         self.parts = lax.axis_size("fsdp")
         self.pair = self.parts == 2
         self.f = lax.axis_index("fsdp")
-        self.core = lax.axis_index("ctx") % 2
+        self.ctx = lax.axis_index("ctx")
+        self.count = lax.axis_size("ctx")
+        self.bits = self.count.bit_length() - 1
         self.swap = [(0, 1), (1, 0)]
-        self.cores = [(i, i ^ 1) for i in range(lax.axis_size("ctx"))]
-
-    def full(self, w):
-        if not self.pair:
-            return lax.all_gather(w, "fsdp", axis=0, tiled=True)
+
+    def bit(self, k):
+        return (self.ctx >> k) & 1
+
+    def flip(self, a, k):
+        return lax.ppermute(a, "ctx", [(i, i ^ (1 << k)) for i in range(self.count)])
+
+    def trade(self, a):
+        return lax.ppermute(a, "fsdp", self.swap)
+
+    def order(self, mine, other, at):
+        return jnp.where(at == 0, mine, other), jnp.where(at == 0, other, mine)
+
+    def fetch_half(self, w):
         half = w.shape[0] // 2
-        mine = lax.dynamic_slice_in_dim(w, self.core * half, half, 0)
-        got = lax.ppermute(mine, "fsdp", self.swap)
-        other = lax.ppermute(got, "ctx", self.cores)
-        low = jnp.where(self.core == 0, got, other)
-        high = jnp.where(self.core == 0, other, got)
-        theirs = jnp.concatenate([low, high], axis=0)
-        return jnp.concatenate(
-            [jnp.where(self.f == 0, w, theirs), jnp.where(self.f == 0, theirs, w)], axis=0
-        )
+        return self.trade(lax.dynamic_slice_in_dim(w, self.bit(0) * half, half, 0))
+
+    def fetch(self, w):
+        got = self.fetch_half(w)
+        return got, self.flip(got, 0)
+
+    def join(self, w, parts):
+        theirs = jnp.concatenate(self.order(*parts, self.bit(0)), axis=0)
+        return jnp.concatenate(self.order(w, theirs, self.f), axis=0)
 
     def full_small(self, w):
         if not self.pair:
             return lax.all_gather(w, "fsdp", axis=0, tiled=False)
-        theirs = lax.ppermute(w, "fsdp", self.swap)
-        return jnp.stack([jnp.where(self.f == 0, w, theirs), jnp.where(self.f == 0, theirs, w)])
+        return jnp.stack(self.order(w, self.trade(w), self.f))
 
     def own(self, a, axis, other=False):
         n = a.shape[axis] // self.parts
         at = (1 - self.f) if other else self.f
         return lax.dynamic_slice_in_dim(a, at * n, n, axis)
 
-    def trade(self, a):
-        return lax.ppermute(a, "fsdp", self.swap)
-
-    def sum_rows(self, g):
-        if not self.pair:
-            return lax.psum_scatter(g.astype(BF), "fsdp", scatter_dimension=0, tiled=True)
-        got = self.trade(self.own(g, 0, True).astype(BF))
-        return (self.own(g, 0) + got.astype(F32)).astype(BF)
+    def window(self, block, planes):
+        y = self.flip(block, 1)
+        self.first_hop = y
+        pair = jnp.stack(self.order(block, y, self.bit(1)))
+        above, below = [], []
+        up = down = pair
+        for _ in range(planes):
+            up = lax.ppermute(up, "ctx", [(i, i + 4) for i in range(self.count - 4)])
+            down = lax.ppermute(down, "ctx", [(i + 4, i) for i in range(self.count - 4)])
+            above.insert(0, up)
+            below.append(down)
+        mine = jnp.stack(above + [pair] + below)
+        other = self.flip(mine, 0)
+        both = jnp.stack(self.order(mine, other, self.bit(0)), axis=2)
+        return both.reshape((-1,) + block.shape)
+
+    def halve(self, a, k, axis):
+        keep = lax.dynamic_index_in_dim(a, self.bit(k), axis, keepdims=False)
+        send = lax.dynamic_index_in_dim(a, 1 - self.bit(k), axis, keepdims=False)
+        return (keep.astype(F32) + self.flip(send, k).astype(F32)).astype(BF)
+
+    def halve_cols(self, low, high):
+        keep, send = self.order(low, high, self.bit(0))
+        return (keep.astype(F32) + self.flip(send, 0).astype(F32)).astype(BF)
+
+    def double(self, a, k, axis):
+        return jnp.stack(self.order(a, self.flip(a, k), self.bit(k)), axis=axis)
+
+    def spread(self, a):
+        return a.reshape((2,) * self.bits + a.shape[1:])
 
 
 def per_device(
@@ -241,28 +308,38 @@
     hidden = hidden_in[0]
     cotangent = out_grad[0].astype(F32)
     T, D = hidden.shape
-    C = lax.axis_size("ctx")
-    ctx = lax.axis_index("ctx")
+    C = sh.count
+    ctx = sh.ctx
     L = T * C
     R = C // 2
     NB = 2 * R + 1
     W = NB * T
-    scale = DH ** (-0.5)
-
     dn = D // sh.parts
-    small = jnp.concatenate(
-        [
-            jnp.stack(
-                [
-                    value_bias, content_bias, position_bias, type_bias, type_embed[0],
-                    type_embed[1], output_bias, attn_gain, attn_shift, outer_bias,
-                    ffn_gain, ffn_shift,
-                ]
-            ),
-            inner_bias.reshape(-1, dn),
-        ],
-        axis=0,
-    )
+    r = dn // C
+
+    lane = jnp.arange(128)[None, :]
+    in_seg = (lane >= 8) & (lane < 16)
+    seg_own = segment_ids[0][:, None]
+    kind_own = token_types[0][:, None]
+    kaug_own = jnp.where(
+        lane < 4, kind_own == 1, jnp.where(lane < 8, kind_own == 0, in_seg & (lane - 8 == seg_own))
+    ).astype(BF)
+    pen = jnp.where(in_seg & (lane - 8 != seg_own), -BIG, 0.0).astype(F32)
+    kind_q = jnp.broadcast_to(kind_own, (T, 128)).astype(F32)
+
+    around = sh.window(jnp.concatenate([hidden, kaug_own], axis=1), R // 4)
+    around = lax.dynamic_slice_in_dim(around, ctx % 4, NB, 0)
+    x_win = around[:, :, :D].reshape(W, D)
+    at = jnp.arange(NB) + ctx - R
+    valid = ((at >= 0) & (at < C))[:, None, None]
+    kaug = jnp.where(valid, around[:, :, D:], (lane[None] == 15).astype(BF)).reshape(W, 128)
+
+    vectors = (
+        value_bias, content_bias, position_bias, type_bias, type_embed, output_bias,
+        attn_gain, attn_shift, outer_bias, ffn_gain, ffn_shift, inner_bias,
+    )
+    vectors, _ = lax.optimization_barrier((vectors, sh.first_hop))
+    small = jnp.concatenate([a.reshape(-1, dn) for a in vectors], axis=0)
     nsmall = small.shape[0]
     small_full = sh.full_small(small).astype(F32)
     vecs = jnp.transpose(small_full[:, :12], (1, 0, 2)).reshape(12, D)
@@ -270,43 +347,33 @@
         vecs[i] for i in range(12)
     )
     in_bias = small_full[:, 12:].reshape(-1)
-    qkv_full = sh.full(jnp.concatenate([query_proj, key_proj, value_proj], axis=1))
-    po_full = sh.full(jnp.concatenate([position_proj, output_proj], axis=1))
-    inner_full = sh.full(inner_proj)
-    outer_full = sh.full(outer_proj)
-    q_full, kv_full = qkv_full[:, :D], qkv_full[:, D:]
-    p_full, o_full = po_full[:, :D], po_full[:, D:]
-
-    ids = jnp.zeros((16, D), BF)
-    ids = ids.at[0, :T].set(segment_ids[0].astype(BF)).at[1, :T].set(token_types[0].astype(BF))
-    gathered = lax.all_gather(jnp.concatenate([hidden, ids], axis=0), "ctx", axis=0, tiled=True)
-    gathered = gathered.reshape(C, T + 16, D)
-    padded = jnp.pad(gathered, ((R, R), (0, 0), (0, 0)))
-    window = lax.dynamic_slice_in_dim(padded, ctx, NB, 0)
-    x_win = window[:, :T].reshape(W, D)
-    valid = jnp.arange(NB) + ctx - R
-    valid = (valid >= 0) & (valid < C)
-    seg_k = jnp.where(valid[:, None], window[:, T, :T].astype(jnp.int32), 7).reshape(W, 1)
-    kind_k = window[:, T + 1, :T].astype(jnp.int32).reshape(W, 1)
-    lane = jnp.arange(128)[None, :]
-    in_seg = (lane >= 8) & (lane < 16)
-    kaug = jnp.where(
-        lane < 3,
-        kind_k == 1,
-        jnp.where((lane >= 4) & (lane < 7), kind_k == 0, in_seg & (lane - 8 == seg_k)),
-    ).astype(BF)
-    pen = jnp.where(in_seg & (lane - 8 != segment_ids[0][:, None]), -BIG, 0.0).astype(F32)
-    kind_q = jnp.broadcast_to(token_types[0][:, None], (T, 128)).astype(F32)
+    first = (key_proj, value_proj, query_proj, position_proj, output_proj)
+    if sh.pair:
+        got = sh.fetch(jnp.concatenate(first, axis=1))
+        k_full, v_full, q_full, p_full, o_full = (
+            sh.join(w, [part[:, i * D : (i + 1) * D] for part in got])
+            for i, w in enumerate(first)
+        )
+        _, i_sh, u_sh = lax.optimization_barrier((got[0], inner_proj, outer_proj))
+        i_got, u_got = sh.fetch_half(i_sh), sh.fetch_half(u_sh)
+    else:
+        k_full, v_full, q_full, p_full, o_full, inner_full, outer_full = (
+            lax.all_gather(w, "fsdp", axis=0, tiled=True)
+            for w in first + (inner_proj, outer_proj)
+        )
 
     q_lin = nn(hidden, q_full)
-    kv = nn(x_win, kv_full)
-    keys = kv[:, :D].astype(BF)
-    values = (kv[:, D:] + v_bias).astype(BF)
+    keys = nn(x_win, k_full).astype(BF)
+    values = (nn(x_win, v_full) + v_bias).astype(BF)
     sinus = sinus_rows(T + R * T - 1, W + T, D)
     table = nn(sinus, p_full).astype(BF)
     rows = jnp.concatenate([vecs[1:6], jnp.zeros((3, D), F32)], axis=0)
 
     mixed_f, probs = att_fwd(q_lin, rows, pen, kind_q, keys, values, table, kaug)
+    if sh.pair:
+        mixed_f, i_got, u_got = lax.optimization_barrier((mixed_f, i_got, u_got))
+        inner_full = sh.join(inner_proj, (i_got, sh.flip(i_got, 0)))
+        outer_full = sh.join(outer_proj, (u_got, sh.flip(u_got, 0)))
     mixed_low = mixed_f.astype(BF)
     attn_out = nn(mixed_low, o_full) + o_bias
     normed, first_pull = jax.vjp(layer_norm, hidden.astype(F32) + attn_out, a_gain, a_shift)
@@ -327,63 +394,104 @@
     grad_output_bias = jnp.sum(d_attn.astype(F32), axis=0)
     d_mixed = nt(d_attn, o_full).astype(BF)
 
+    if sh.pair:
+        lefts = sh.trade(
+            jnp.concatenate([sh.own(normed_low, 1, True), sh.own(activ_low, 1, True)], axis=1)
+        )
+        rights = (sh.trade(d_inner), sh.trade(d_outer))
+        got = sh.trade(
+            jnp.concatenate([sh.own(mixed_low, 1, True), sh.own(hidden, 1, True), d_attn], axis=1)
+        )
     dq, att_vec, dkv, d_table = att_bwd(
         q_lin, rows, kind_q, d_mixed, mixed_f, probs, keys, values, table, kaug
     )
-    dkv = dkv.reshape(2 * D, W)
-    grad_value_bias = jnp.sum(dkv[D:].astype(F32), axis=1)
-    d_hid = lax.dot_general(
-        dkv, kv_full, (((0,), (1,)), ((), ())), preferred_element_type=F32
+    if sh.pair:
+        gi = tn(
+            jnp.concatenate([sh.own(normed_low, 1), lefts[:, :dn]], axis=0),
+            jnp.concatenate([d_inner, rights[0]], axis=0),
+        ).astype(BF)
+        gu = tn(
+            jnp.concatenate([sh.own(activ_low, 1), lefts[:, dn:]], axis=0),
+            jnp.concatenate([d_outer, rights[1]], axis=0),
+        ).astype(BF)
+        dq_got = sh.trade(dq)
+        gi, gu, dkv, d_table = lax.optimization_barrier((gi, gu, dkv, d_table))
+    else:
+        gi, gu = (
+            lax.psum_scatter(tn(a, b).astype(BF), "fsdp", scatter_dimension=0, tiled=True)
+            for a, b in ((normed_low, d_inner), (activ_low, d_outer))
+        )
+    gi, gu = lax.psum((gi, gu), "ctx")
+
+    dk, dv = dkv[0], dkv[1]
+    gk, gv, gp = (
+        lax.dot_general(a, b, (((0,), (1,)), ((), ())), preferred_element_type=F32).astype(BF)
+        for a, b in ((x_win, dk), (x_win, dv), (sinus, d_table))
+    )
+    smalls = jnp.concatenate(
+        [
+            jnp.stack(
+                [
+                    jnp.sum(d_mixed.astype(F32), axis=0), att_vec[0], att_vec[1], att_vec[2],
+                    att_vec[3], att_vec[4], grad_output_bias, grad_attn_gain, grad_attn_shift,
+                    grad_outer_bias, grad_ffn_gain, grad_ffn_shift,
+                ]
+            ),
+            jnp.transpose(grad_inner_bias.reshape(sh.parts, -1, dn), (1, 0, 2)).reshape(-1, D),
+        ],
+        axis=0,
     ).astype(BF)
+    smalls = jnp.pad(smalls, ((0, 256 - nsmall), (0, 0)))
+    whole = jnp.concatenate([gk, gv, gp, jnp.transpose(smalls)], axis=1)
+    half = whole.shape[1] // 2
+    if sh.pair:
+        whole = sh.halve_cols(whole[:, :half], whole[:, half:])
+        whole = whole.reshape(2, dn, half)
+        keep = lax.dynamic_index_in_dim(whole, sh.f, 0, keepdims=False)
+        send = lax.dynamic_index_in_dim(whole, 1 - sh.f, 0, keepdims=False)
+        whole = (keep.astype(F32) + sh.trade(send).astype(F32)).astype(BF)
+        go = tn(
+            jnp.concatenate([sh.own(mixed_low, 1), got[:, :dn]], axis=0),
+            jnp.concatenate([d_attn, got[:, 2 * dn :]], axis=0),
+        ).astype(BF)
+        gq = tn(
+            jnp.concatenate([sh.own(hidden, 1), got[:, dn : 2 * dn]], axis=0),
+            jnp.concatenate([dq, dq_got], axis=0),
+        ).astype(BF)
+    else:
+        whole, go, gq = (
+            lax.psum_scatter(a, "fsdp", scatter_dimension=0, tiled=True)
+            for a in (whole, tn(mixed_low, d_attn).astype(BF), tn(hidden, dq).astype(BF))
+        )
+        whole = sh.halve_cols(whole[:, :half], whole[:, half:])
+
+    d_hid = (tn(dk, jnp.transpose(k_full)) + tn(dv, jnp.transpose(v_full))).astype(BF)
     d_hid = jnp.pad(d_hid, (((C - 1 - R) * T, (C - 1) * T + L - (C - 1 - R) * T - W), (0, 0)))
     d_hid = lax.dynamic_slice_in_dim(d_hid, (C - 1 - ctx) * T, L, 0)
-    d_hid_own = lax.psum_scatter(d_hid, "ctx", scatter_dimension=0, tiled=True).astype(F32)
-    input_grad = d_res1 + nt(dq, q_full) + d_hid_own
-
-    gkv = lax.dot_general(x_win, dkv, (((0,), (1,)), ((), ())), preferred_element_type=F32)
-    gp = lax.dot_general(sinus, d_table, (((0,), (1,)), ((), ())), preferred_element_type=F32)
-    gkv = sh.sum_rows(gkv)
-    gp = sh.sum_rows(gp)
-
-    pairs = (
-        (hidden, dq), (mixed_low, d_attn), (normed_low, d_inner), (activ_low, d_outer)
-    )
-    if sh.pair:
-        lefts = [sh.own(a, 1, True) for a, _ in pairs]
-        got = sh.trade(jnp.concatenate(lefts, axis=1))
-        sums = []
-        at = 0
-        for a, b in pairs:
-            n = a.shape[1] // 2
-            left = jnp.concatenate([sh.own(a, 1), got[:, at : at + n]], axis=0)
-            right = jnp.concatenate([b, sh.trade(b)], axis=0)
-            sums.append(tn(left, right).astype(BF))
-            at += n
-    else:
-        sums = [sh.sum_rows(tn(a, b)) for a, b in pairs]
-    gq, go, gi, gout = sums
-
-    smalls = jnp.stack(
-        [
-            grad_value_bias, att_vec[0], att_vec[1], att_vec[2], att_vec[3], att_vec[4],
-            grad_output_bias, grad_attn_gain, grad_attn_shift, grad_outer_bias,
-            grad_ffn_gain, grad_ffn_shift,
-        ]
-    )
-    smalls = jnp.transpose(smalls.reshape(12, sh.parts, dn), (1, 0, 2))
-    smalls = jnp.concatenate([smalls, grad_inner_bias.reshape(sh.parts, -1, dn)], axis=1)
-    smalls = sh.sum_rows(smalls.reshape(sh.parts * nsmall, dn))
-
-    gkv, gp, gq, go, gi, gout, smalls = (
-        a.astype(F32) for a in lax.psum((gkv, gp, gq, go, gi, gout, smalls), "ctx")
-    )
+    d_hid = sh.spread(d_hid.reshape(C, T, D))
+    for k in range(sh.bits):
+        d_hid = sh.halve(d_hid, k, d_hid.ndim - 3)
+    input_grad = d_res1 + nt(dq, q_full) + d_hid.astype(F32)
+
+    grads = jnp.concatenate([whole, sh.halve_cols(go, gq)], axis=1)
+    grads = grads.reshape((2,) * (sh.bits - 1) + (-1, grads.shape[1]))
+    for k in range(1, sh.bits):
+        grads = sh.halve(grads, k, grads.ndim - 3)
+    for k in reversed(range(1, sh.bits)):
+        grads = sh.double(grads, k, grads.ndim - 2)
+    grads = grads.reshape(dn, -1)
+    low, high = sh.order(grads, sh.flip(grads, 0), sh.bit(0))
+    whole = jnp.concatenate([low[:, :half], high[:, :half]], axis=1).astype(F32)
+    gk, gv, gp = (whole[:, i * D : (i + 1) * D] for i in range(3))
+    go, gq = low[:, half:].astype(F32), high[:, half:].astype(F32)
+    smalls = jnp.transpose(whole[:, 3 * D : 3 * D + 128])[:nsmall]
     s = [smalls[i] for i in range(12)]
     return (
         outcome.astype(BF)[None],
         input_grad[None],
         gq,
-        gkv[:, :D],
-        gkv[:, D:],
+        gk,
+        gv,
         s[0],
         s[1],
         s[2],
@@ -394,9 +502,9 @@
         s[6],
         s[7],
         s[8],
-        gi,
+        gi.astype(F32),
         smalls[12:].reshape(-1),
-        gout,
+        gu.astype(F32),
         s[9],
         s[10],
         s[11],

time: 499 us -> 464 us (0.930)
  blocking collectives: 62.9 us -> 0 us
  starting transfers between devices: 14.8 us -> 41.1 us
  local copies, waits for them, and re-layouts: 67 us -> 45.7 us
  waiting for transfers between devices: 191 us -> 207 us
  matrix products: 55.2 us -> 60.5 us
    psum x1 -> x0, blocking collectives: 62.9 us -> none  [per_device(): lax.psum((gkv, gp, gq, go, gi, gout, smalls), 'ctx')]
    ppermute x9 -> x22, waiting for transfers between devices: 53.6 us -> 102 us  [the longest x18 91.3 us: flip(): return lax.ppermute(a, 'ctx', [(i, i ^ 1 << k) for i in range(self.count)])]
    ppermute x9 -> x22, starting transfers between devices: 7.65 us -> 30.6 us  [the longest x18 18.4 us: flip(): return lax.ppermute(a, 'ctx', [(i, i ^ 1 << k) for i in range(self.count)])]
    ppermute x8 -> x10, waiting for transfers between devices: 69.3 us -> 50.1 us  [trade(): return lax.ppermute(a, 'fsdp', self.swap)]
    another operation x19 -> x6, local copies, waits for them, and re-layouts: 15.8 us -> 0.74 us  [the longest x1 0.51 us: window(): both = jnp.stack(self.order(mine, other, self.bit(0)), axis=2)]
    psum x1, waiting for transfers between devices: 67.6 us -> 55.7 us  [per_device(): gi, gu = lax.psum((gi, gu), 'ctx')]
    dot_general x4 -> x6, matrix products: 6.87 us -> 17.6 us  [tn(): lax.dot_general(a, b, (((0,), (0,)), ((), ())), preferred_element_type=F32)]
    dot_general x3, matrix products: 20.8 us -> 13.9 us  [per_device(): lax.dot_general(a, b, (((0,), (1,)), ((), ())), preferred_element_type=F32)]
  transfers between devices with their start and end apart: 20 -> 33, of which waited for: 7 -> 17; matrix products, arithmetic and copies ran while one was open for 20% -> 24% of each run, Pallas kernels for 0% -> 8%
where the time goes in v2:
time: 464 us; the launch traced here: 458 us
  waiting for transfers between devices  207 us (45%)
  matrix products  60.5 us (13%)
  other arithmetic  51.3 us (11%)
  local copies, waits for them, and re-layouts  45.7 us (10%)
  starting transfers between devices  41.1 us (9%)
  Pallas kernels  36.4 us (8%)
  between operations  15.8 us (3%)
    ppermute x18, waiting for transfers between devices, flip(): return lax.ppermute(a, 'ctx', [(i, i ^ 1 << k) for i in range(self.count)])  91.3 us
    psum x1, waiting for transfers between devices, per_device(): gi, gu = lax.psum((gi, gu), 'ctx')  55.7 us
    ppermute x10, waiting for transfers between devices, trade(): return lax.ppermute(a, 'fsdp', self.swap)  50.1 us
    pallas_call x1, Pallas kernels, att_fwd(): pl.pallas_call(att_fwd_kernel, grid=(D // 128,), in_specs=[col(T), col(8)...  19.5 us
    ppermute x18, starting transfers between devices, flip(): return lax.ppermute(a, 'ctx', [(i, i ^ 1 << k) for i in range(self.count)])  18.4 us
    dot_general x7, matrix products, nn(): lax.dot_general(a, b, (((1,), (0,)), ((), ())), preferred_element_type=F32)  18.2 us
    dot_general x6, matrix products, tn(): lax.dot_general(a, b, (((0,), (0,)), ((), ())), preferred_element_type=F32)  17.6 us
    pallas_call x1, Pallas kernels, att_bwd(): pl.pallas_call(att_bwd_kernel, grid=(D // 128,), in_specs=[col(T), col(8)...  16.9 us
  transfers between devices with their start and end apart: 33, of which 17 were waited for; matrix products, arithmetic and copies ran while one was open for 24% of the time, Pallas kernels for 8%

profile of v2, /device:TPU:0, one launch (start us, length us, event | category | flops | bytes accessed | tf_op | source)
XLA Modules:
  0.0 458.2 jit_solution(136140749872845195)
XLA Ops:
  10.4 3.0 collective-permute-start.2
  13.4 2.0 constant_dynamic-update-slice_fusion.4
  15.4 1.9 constant_dynamic-update-slice_fusion.3
  26.9 4.3 collective-permute-start.4
  31.7 3.0 subtract_convert_fusion
  39.9 5.2 %collective-permute-start.5 = (bf16[2,128,896]{2,1,0:T(8,128)(2,1)}, bf16[2,128,896]{2,1,0:T(8,128)(2,1)}, u32[]{:S(2)}, u32[]{:S(2)}) collective-permute-start(bf16[2,128,896]{2,1,0:T(8,128)(2,1)} %collective-permute-done.4), channel_id=1, source_target_pairs={{0,8},{2,10},{4,12},{6,14},{8,16},{10,18},{12,20},{14,22},{16,24},... | collective-permute-start | bytes 1376264 | tf_op jit(solution)/shard_map/ppermute | solution.py:257
  45.1 10.3 %collective-permute-done.3 = bf16[16,384]{1,0:T(8,128)(2,1)S(1)} collective-permute-done((bf16[16,384]{1,0:T(8,128)(2,1)S(1)}, bf16[16,384]{1,0:T(8,128)(2,1)S(1)}, u32[]{:S(2)}, u32[]{:S(2)}) %collective-permute-start.3) | collective-permute-done | bytes 12320 | tf_op jit(solution)/shard_map/ppermute | solution.py:223
  62.9 8.5 %collective-permute-done.7 = bf16[2,128,896]{2,1,0:T(8,128)(2,1)S(1)} collective-permute-done((bf16[2,128,896]{2,1,0:T(8,128)(2,1)}, bf16[2,128,896]{2,1,0:T(8,128)(2,1)S(1)}, u32[]{:S(2)}, u32[]{:S(2)}) %collective-permute-start.7) | collective-permute-done | bytes 458784 | tf_op jit(solution)/shard_map/ppermute | solution.py:258
  84.7 4.5 convolution_convert_fusion.t_ref
  92.5 4.2 convolution_convert_fusion.1.k_ref
  96.7 4.2 add_convert_fusion.1.v_ref
  101.7 19.5 %att_fwd.1 = (f32[128,768]{1,0:T(8,128)}, bf16[12,128,2176]{2,1,0:T(8,128)(2,1)}) custom-call(f32[128,768]{1,0:T(8,128)} %convolution_bitcast_fusion.q_ref, f32[8,768]{1,0:T(8,128)} %concatenate.112.rows_ref, f32[128,128]{1,0:T(8,128)} %and_select_fusion.pen_ref, f32[128,128]{1,0:T(8,128)} %broadcast_in_dim.94.kind_ref, ...), custom_call_target="tpu_custom_call" | custom-call | flops 13690208256 | bytes 16711680 | tf_op jit(solution)/shard_map/att_fwd/pallas_call | solution.py:137
  121.2 6.5 %collective-permute-done.9 = bf16[192,3072]{1,0:T(8,128)(2,1)} collective-permute-done((bf16[192,3072]{1,0:T(8,128)(2,1)}, bf16[192,3072]{1,0:T(8,128)(2,1)}, u32[]{:S(2)}, u32[]{:S(2)}) %collective-permute-start.9) | collective-permute-done | bytes 1179680 | tf_op jit(solution)/shard_map/ppermute | solution.py:223
  145.0 5.5 %fusion.104 = (bf16[3072]{0:T(1024)(128)(2,1)S(1)}, bf16[128,3072]{1,0:T(8,128)(2,1)S(1)}) fusion(f32[128,3072]{1,0:T(8,128)S(1)} %get-tuple-element.237, bf16[128,768]{1,0:T(8,128)(2,1)S(1)} %get-tuple-element.163, bf16[1536,768]{1,0:T(8,128)(2,1)S(1)} %get-tuple-element.171, bf16[1536,768]{1,0:T(8,128)(2,1)S(1)} %get-tuple-element.170), kind=kOutput, calls=%fused_computation.299 | convolution fusion | flops 621671424 | bytes 7280640 | tf_op jit(solution)/shard_map/dot_general | solution.py:18
  150.5 1.9 multiply_reduce_fusion
  157.0 16.9 %att_bwd.1 = (bf16[128,768]{1,0:T(8,128)(2,1)}, f32[8,768]{1,0:T(8,128)}, bf16[2,768,2176]{2,1,0:T(8,128)(2,1)}, bf16[768,2304]{1,0:T(8,128)(2,1)}) custom-call(f32[128,768]{1,0:T(8,128)} %convolution_bitcast_fusion.q_ref, f32[8,768]{1,0:T(8,128)} %concatenate.112.rows_ref, f32[128,128]{1,0:T(8,128)} %broadcast_in_dim.94.kind_ref, ...), custom_call_target="tpu_custom_call" | custom-call | flops 13690208256 | bytes 26738688 | tf_op jit(solution)/shard_map/att_bwd/pallas_call | solution.py:162
  175.7 6.5 %collective-permute-done.13 = bf16[128,1920]{1,0:T(8,128)(2,1)S(1)} collective-permute-done((bf16[128,1920]{1,0:T(8,128)(2,1)S(1)}, bf16[128,1920]{1,0:T(8,128)(2,1)S(1)}, u32[]{:S(2)}, u32[]{:S(2)}) %collective-permute-start.13) | collective-permute-done | bytes 491552 | tf_op jit(solution)/shard_map/ppermute | solution.py:223
  182.2 2.3 convolution_convert_fusion.3
  184.6 2.2 convolution_convert_fusion.2
  186.8 6.0 %fusion.29 = bf16[768,768]{0,1:T(8,128)(2,1)S(1)} fusion(bf16[2176,768]{1,0:T(8,128)(2,1)} %bitcast.161, bf16[2,768,2176]{2,1,0:T(8,128)(2,1)} %get-tuple-element.70), kind=kOutput, calls=%fused_computation.70 | convolution fusion | flops 2567503872 | bytes 7864320 | tf_op jit(solution)/shard_map/dot_general | solution.py:428
  192.9 5.0 %fusion.32 = bf16[768,768]{0,1:T(8,128)(2,1)S(1)} fusion(bf16[2176,768]{1,0:T(8,128)(2,1)S(1)} %bitcast.162, bf16[2,768,2176]{2,1,0:T(8,128)(2,1)} %get-tuple-element.70), kind=kOutput, calls=%fused_computation.71 | convolution fusion | flops 2567503872 | bytes 7864320 | tf_op jit(solution)/shard_map/dot_general | solution.py:428
  197.9 2.9 fusion.35
  206.5 10.2 %collective-permute-done.22 = bf16[128,1536]{1,0:T(8,128)(2,1)} collective-permute-done((bf16[128,1536]{1,0:T(8,128)(2,1)}, bf16[128,1536]{1,0:T(8,128)(2,1)}, u32[]{:S(2)}, u32[]{:S(2)}) %collective-permute-start.22) | collective-permute-done | bytes 393248 | tf_op jit(solution)/shard_map/ppermute | solution.py:223
  219.3 2.1 convolution_convert_fusion.5
  221.4 2.9 add_convert_fusion.2
  224.3 2.9 copy.70
  228.8 2.5 broadcast_select_fusion.11
  231.3 2.3 collective-permute-done.24
  235.0 16.5 %collective-permute-done.21 = bf16[384,1280]{1,0:T(8,128)(2,1)S(1)} collective-permute-done((bf16[384,1280]{1,0:T(8,128)(2,1)}, bf16[384,1280]{1,0:T(8,128)(2,1)S(1)}, u32[]{:S(2)}, u32[]{:S(2)}) %collective-permute-start.21) | collective-permute-done | bytes 983072 | tf_op jit(solution)/shard_map/ppermute | solution.py:223
  252.6 17.4 %collective-permute-done.25 = bf16[2,2,48,2048]{3,2,1,0:T(8,128)(2,1)S(1)} collective-permute-done((bf16[2,2,48,2048]{3,2,1,0:T(8,128)(2,1)S(1)}, bf16[2,2,48,2048]{3,2,1,0:T(8,128)(2,1)S(1)}, u32[]{:S(2)}, u32[]{:S(2)}) %collective-permute-start.25) | collective-permute-done | bytes 786464 | tf_op jit(solution)/shard_map/ppermute | solution.py:220
  272.0 5.4 %fusion.5 = f32[2176,768]{1,0:T(8,128)S(1)} fusion(bf16[2,768,2176]{2,1,0:T(8,128)(2,1)} %get-tuple-element.70, bf16[384,768]{1,0:T(8,128)(2,1)S(1)} %copy-done.35, bf16[384,768]{1,0:T(8,128)(2,1)S(1)} %copy-done.37), kind=kOutput, calls=%fused_computation.20 | convolution fusion | flops 2569273344 | bytes 11206656 | tf_op jit(solution)/shard_map/dot_general | solution.py:26
  279.0 3.3 collective-permute-start.27
  282.4 3.0 add_convert_fusion
  285.4 6.1 %collective-permute-done.27 = bf16[48,2048]{1,0:T(8,128)(2,1)S(1)} collective-permute-done((bf16[48,2048]{1,0:T(8,128)(2,1)S(1)}, bf16[48,2048]{1,0:T(8,128)(2,1)S(1)}, u32[]{:S(2)}, u32[]{:S(2)}) %collective-permute-start.27) | collective-permute-done | bytes 196640 | tf_op jit(solution)/shard_map/ppermute | solution.py:220
  291.6 2.2 pad_dynamic-slice_fusion
  295.3 3.1 collective-permute-done.28
  298.5 8.4 %collective-permute-done.29 = bf16[2,48,2048]{2,1,0:T(8,128)(2,1)S(1)} collective-permute-done((bf16[2,48,2048]{2,1,0:T(8,128)(2,1)S(1)}, bf16[2,48,2048]{2,1,0:T(8,128)(2,1)S(1)}, u32[]{:S(2)}, u32[]{:S(2)}) %collective-permute-start.29) | collective-permute-done | bytes 393248 | tf_op jit(solution)/shard_map/ppermute | solution.py:220
  311.1 29.2 %collective-permute-done.30 = bf16[2,2,48,2048]{3,2,0,1:T(8,128)(2,1)} collective-permute-done((bf16[2,2,48,2048]{3,2,0,1:T(8,128)(2,1)S(1)}, bf16[2,2,48,2048]{3,2,0,1:T(8,128)(2,1)}, u32[]{:S(2)}, u32[]{:S(2)}) %collective-permute-start.30) | collective-permute-done | bytes 786464 | tf_op jit(solution)/shard_map/ppermute | solution.py:220
  342.0 11.2 %collective-permute-done.17 = bf16[2,2,128,768]{3,2,0,1:T(8,128)(2,1)S(1)} collective-permute-done((bf16[2,2,128,768]{3,2,0,1:T(8,128)(2,1)S(1)}, bf16[2,2,128,768]{3,2,0,1:T(8,128)(2,1)S(1)}, u32[]{:S(2)}, u32[]{:S(2)}) %collective-permute-start.17) | collective-permute-done | bytes 786464 | tf_op jit(solution)/shard_map/ppermute | solution.py:220
  353.5 2.5 collective-permute-start.18
  356.0 12.0 %collective-permute-done.18 = bf16[2,128,768]{2,1,0:T(8,128)(2,1)S(1)} collective-permute-done((bf16[2,128,768]{2,1,0:T(8,128)(2,1)S(1)}, bf16[2,128,768]{2,1,0:T(8,128)(2,1)S(1)}, u32[]{:S(2)}, u32[]{:S(2)}) %collective-permute-start.18) | collective-permute-done | bytes 393248 | tf_op jit(solution)/shard_map/ppermute | solution.py:220
  369.1 4.3 collective-permute-start.19
  373.3 55.7 %all-reduce.6.cloned.1.call-done = (bf16[384,3072]{1,0:T(8,128)(2,1)}, bf16[1536,768]{1,0:T(8,128)(2,1)}) async-done(((bf16[384,3072]{1,0:T(8,128)(2,1)}, bf16[1536,768]{1,0:T(8,128)(2,1)}), (bf16[384,3072]{1,0:T(8,128)(2,1)}, bf16[1536,768]{1,0:T(8,128)(2,1)})) %all-reduce.6.cloned.1.call-update) | async-done | bytes 4718608 | tf_op jit(solution)/shard_map/psum | solution.py:424
  429.0 4.6 convert_element_type.329
  433.6 2.5 convert_element_type.330
  436.2 2.2 add_bitcast_fusion
  444.1 2.4 maximum_convert_fusion
  447.9 3.2 fusion.99
  (356 shorter events, 98.0 us)
Async XLA Ops:
  7.2 421.8 %all-reduce.6.cloned.1.call-start = ((), (), s32[]{:S(2)}) async-start(), calls=%async_computation | async-start | bytes 9437184 | tf_op jit(solution)/shard_map/psum | solution.py:424
  10.4 14.5 %collective-permute-start.2 = (bf16[128,896]{1,0:T(8,128)(2,1)}, bf16[128,896]{1,0:T(8,128)(2,1)}, u32[]{:S(2)}, u32[]{:S(2)}) collective-permute-start(bf16[128,896]{1,0:T(8,128)(2,1)} %pad_maximum_fusion.51), channel_id=1, source_target_pairs={{0,4},{2,6},{4,0},{6,2},{8,12},{10,14},{12,8},{14,10},{16,20},{18,... | collective-permute-start | bytes 688136 | tf_op jit(solution)/shard_map/ppermute | solution.py:220
  21.4 38.0 %collective-permute-start = (bf16[192,3840]{1,0:T(8,128)(2,1)S(1)}, bf16[192,3840]{1,0:T(8,128)(2,1)}, u32[]{:S(2)}, u32[]{:S(2)}) collective-permute-start(bf16[192,3840]{1,0:T(8,128)(2,1)S(1)} %constant_dynamic-slice_fusion.11), channel_id=1, source_target_pairs={{0,1},{1,0},{2,3},{3,2},{4,5},{5,4},{6,7},{7,6},{8,9},{9,8},{10,11... | collective-permute-start | bytes 4423688 | tf_op jit(solution)/shard_map/ppermute | solution.py:223
  26.9 13.0 %collective-permute-start.4 = (bf16[2,128,896]{2,1,0:T(8,128)(2,1)}, bf16[2,128,896]{2,1,0:T(8,128)(2,1)}, u32[]{:S(2)}, u32[]{:S(2)}) collective-permute-start(bf16[2,128,896]{2,1,0:T(8,128)(2,1)} %pad_maximum_fusion.46), channel_id=1, source_target_pairs={{0,8},{2,10},{4,12},{6,14},{8,16},{10,18},{12,20},{14,22},{16,24},... | collective-permute-start | bytes 1376264 | tf_op jit(solution)/shard_map/ppermute | solution.py:257
  35.0 20.4 %collective-permute-start.3 = (bf16[16,384]{1,0:T(8,128)(2,1)S(1)}, bf16[16,384]{1,0:T(8,128)(2,1)S(1)}, u32[]{:S(2)}, u32[]{:S(2)}) collective-permute-start(bf16[16,384]{1,0:T(8,128)(2,1)S(1)} %concatenate.111), channel_id=1, source_target_pairs={{0,1},{1,0},{2,3},{3,2},{4,5},{5,4},{6,7},{7,6},{8,9},{9,8},{10,11... | collective-permute-start | bytes 36872 | tf_op jit(solution)/shard_map/ppermute | solution.py:223
  36.8 21.2 %collective-permute-start.6 = (bf16[2,128,896]{2,1,0:T(8,128)(2,1)}, bf16[2,128,896]{2,1,0:T(8,128)(2,1)}, u32[]{:S(2)}, u32[]{:S(2)}) collective-permute-start(bf16[2,128,896]{2,1,0:T(8,128)(2,1)} %pad_maximum_fusion.46), channel_id=1, source_target_pairs={{8,0},{10,2},{12,4},{14,6},{16,8},{18,10},{20,12},{22,14},{24,16},... | collective-permute-start | bytes 1376264 | tf_op jit(solution)/shard_map/ppermute | solution.py:258
  39.9 19.5 %collective-permute-start.5 = (bf16[2,128,896]{2,1,0:T(8,128)(2,1)}, bf16[2,128,896]{2,1,0:T(8,128)(2,1)}, u32[]{:S(2)}, u32[]{:S(2)}) collective-permute-start(bf16[2,128,896]{2,1,0:T(8,128)(2,1)} %collective-permute-done.4), channel_id=1, source_target_pairs={{0,8},{2,10},{4,12},{6,14},{8,16},{10,18},{12,20},{14,22},{16,24},... | collective-permute-start | bytes 1376264 | tf_op jit(solution)/shard_map/ppermute | solution.py:257
  57.9 13.5 %copy-start.1 = (bf16[384,3072]{1,0:T(8,128)(2,1)S(1)}, bf16[384,3072]{1,0:T(8,128)(2,1)}, u32[]{:S(2)}) copy-start(bf16[384,3072]{1,0:T(8,128)(2,1)} %param.40) | copy-start | bytes 7077892
  58.0 13.4 %collective-permute-start.7 = (bf16[2,128,896]{2,1,0:T(8,128)(2,1)}, bf16[2,128,896]{2,1,0:T(8,128)(2,1)S(1)}, u32[]{:S(2)}, u32[]{:S(2)}) collective-permute-start(bf16[2,128,896]{2,1,0:T(8,128)(2,1)} %collective-permute-done.6), channel_id=1, source_target_pairs={{8,0},{10,2},{12,4},{14,6},{16,8},{18,10},{20,12},{22,14},{24,16},... | collective-permute-start | bytes 1376264 | tf_op jit(solution)/shard_map/ppermute | solution.py:258
  59.4 16.3 %collective-permute-start.1 = (bf16[192,3840]{1,0:T(8,128)(2,1)}, bf16[192,3840]{1,0:T(8,128)(2,1)S(1)}, u32[]{:S(2)}, u32[]{:S(2)}) collective-permute-start(bf16[192,3840]{1,0:T(8,128)(2,1)} %collective-permute-done), channel_id=1, source_target_pairs={{0,2},{2,0},{4,6},{6,4},{8,10},{10,8},{12,14},{14,12},{16,18},{18,... | collective-permute-start | bytes 4423688 | tf_op jit(solution)/shard_map/ppermute | solution.py:220
  71.4 17.9 %collective-permute-start.8 = (bf16[5,2,128,896]{3,2,1,0:T(8,128)(2,1)S(1)}, bf16[5,2,128,896]{3,2,1,0:T(8,128)(2,1)S(1)}, u32[]{:S(2)}, u32[]{:S(2)}) collective-permute-start(bf16[5,2,128,896]{3,2,1,0:T(8,128)(2,1)S(1)} %bitcast_dynamic-update-slice_fusion), channel_id=1, source_target_pairs={{0,2},{2,0},{4,6},{6,4},{8,10},{10,8},{12,14},{14,12},{16,18},{18,... | collective-permute-start | bytes 6881288 | tf_op jit(solution)/shard_map/ppermute | solution.py:220
  73.7 47.5 %collective-permute-start.10 = (bf16[768,768]{1,0:T(8,128)(2,1)}, bf16[768,768]{1,0:T(8,128)(2,1)}, u32[]{:S(2)}, u32[]{:S(2)}) collective-permute-start(bf16[768,768]{1,0:T(8,128)(2,1)} %constant_dynamic-slice_fusion.9), channel_id=1, source_target_pairs={{0,1},{1,0},{2,3},{3,2},{4,5},{5,4},{6,7},{7,6},{8,9},{9,8},{10,11... | collective-permute-start | bytes 3538952 | tf_op jit(solution)/shard_map/ppermute | solution.py:223
  75.2 52.5 %collective-permute-start.9 = (bf16[192,3072]{1,0:T(8,128)(2,1)}, bf16[192,3072]{1,0:T(8,128)(2,1)}, u32[]{:S(2)}, u32[]{:S(2)}) collective-permute-start(bf16[192,3072]{1,0:T(8,128)(2,1)} %constant_dynamic-slice_fusion.10), channel_id=1, source_target_pairs={{0,1},{1,0},{2,3},{3,2},{4,5},{5,4},{6,7},{7,6},{8,9},{9,8},{10,11... | collective-permute-start | bytes 3538952 | tf_op jit(solution)/shard_map/ppermute | solution.py:223
  82.4 14.3 %copy-start.30 = (bf16[384,768]{1,0:T(8,128)(2,1)}, bf16[384,768]{1,0:T(8,128)(2,1)S(1)}, u32[]{:S(2)}) copy-start(bf16[384,768]{1,0:T(8,128)(2,1)S(1)} %get-tuple-element.201) | copy-start | bytes 1769476
  82.4 14.3 %copy-start.32 = (bf16[384,768]{1,0:T(8,128)(2,1)}, bf16[384,768]{1,0:T(8,128)(2,1)S(1)}, u32[]{:S(2)}) copy-start(bf16[384,768]{1,0:T(8,128)(2,1)S(1)} %get-tuple-element.202) | copy-start | bytes 1769476
  101.7 26.0 %copy-start.46 = (bf16[1,16,384]{2,1,0:T(8,128)(2,1)S(1)}, bf16[1,16,384]{2,1,0:T(8,128)(2,1)}, u32[]{:S(2)}) copy-start(bf16[1,16,384]{2,1,0:T(8,128)(2,1)} %copy-done.45) | copy-start | bytes 36868
  101.7 26.6 %copy-start.54 = (f32[2,384]{1,0:T(2,128)S(1)}, f32[2,384]{1,0:T(2,128)}, u32[]{:S(2)}) copy-start(f32[2,384]{1,0:T(2,128)} %get-tuple-element.153) | copy-start | bytes 9220
  101.7 26.6 %copy-start.53 = (f32[2,384]{1,0:T(2,128)S(1)}, f32[2,384]{1,0:T(2,128)}, u32[]{:S(2)}) copy-start(f32[2,384]{1,0:T(2,128)} %get-tuple-element.156) | copy-start | bytes 9220
  101.7 26.6 %copy-start.52 = (f32[2,384]{1,0:T(2,128)S(1)}, f32[2,384]{1,0:T(2,128)}, u32[]{:S(2)}) copy-start(f32[2,384]{1,0:T(2,128)} %get-tuple-element.154) | copy-start | bytes 9220
  101.7 26.6 %copy-start.51 = (f32[2,384]{1,0:T(2,128)S(1)}, f32[2,384]{1,0:T(2,128)}, u32[]{:S(2)}) copy-start(f32[2,384]{1,0:T(2,128)} %get-tuple-element.155) | copy-start | bytes 9220
  101.7 27.2 %copy-start.50 = (f32[2,384]{1,0:T(2,128)S(1)}, f32[2,384]{1,0:T(2,128)}, u32[]{:S(2)}) copy-start(f32[2,384]{1,0:T(2,128)} %get-tuple-element.158) | copy-start | bytes 9220
  101.7 28.9 %copy-start.18 = (bf16[1,128,768]{2,1,0:T(8,128)(2,1)S(1)}, bf16[1,128,768]{2,1,0:T(8,128)(2,1)}, u32[]{:S(2)}) copy-start(bf16[1,128,768]{2,1,0:T(8,128)(2,1)} %param.23) | copy-start | bytes 589828
  101.7 28.8 %copy-start.38 = (bf16[384,768]{1,0:T(8,128)(2,1)S(1)}, bf16[384,768]{1,0:T(8,128)(2,1)}, u32[]{:S(2)}) copy-start(bf16[384,768]{1,0:T(8,128)(2,1)} %get-tuple-element.197) | copy-start | bytes 1769476
  127.6 5.4 %collective-permute-start.12 = (bf16[768,768]{1,0:T(8,128)(2,1)}, bf16[768,768]{1,0:T(8,128)(2,1)}, u32[]{:S(2)}, u32[]{:S(2)}) collective-permute-start(bf16[768,768]{1,0:T(8,128)(2,1)} %collective-permute-done.10), channel_id=1, source_target_pairs={{0,2},{2,0},{4,6},{6,4},{8,10},{10,8},{12,14},{14,12},{16,18},{18,... | collective-permute-start | bytes 3538952 | tf_op jit(solution)/shard_map/ppermute | solution.py:220
  130.0 5.9 %collective-permute-start.11 = (bf16[192,3072]{1,0:T(8,128)(2,1)}, bf16[192,3072]{1,0:T(8,128)(2,1)S(1)}, u32[]{:S(2)}, u32[]{:S(2)}) collective-permute-start(bf16[192,3072]{1,0:T(8,128)(2,1)} %collective-permute-done.9), channel_id=1, source_target_pairs={{0,2},{2,0},{4,6},{6,4},{8,10},{10,8},{12,14},{14,12},{16,18},{18,... | collective-permute-start | bytes 3538952 | tf_op jit(solution)/shard_map/ppermute | solution.py:220
  143.4 38.8 %collective-permute-start.15 = (bf16[128,768]{1,0:T(8,128)(2,1)S(1)}, bf16[128,768]{1,0:T(8,128)(2,1)S(1)}, u32[]{:S(2)}, u32[]{:S(2)}) collective-permute-start(bf16[128,768]{1,0:T(8,128)(2,1)S(1)} %get-tuple-element.163), channel_id=1, source_target_pairs={{0,1},{1,0},{2,3},{3,2},{4,5},{5,4},{6,7},{7,6},{8,9},{9,8},{10,11... | collective-permute-start | bytes 589832 | tf_op jit(solution)/shard_map/ppermute | solution.py:223
  152.4 32.2 %collective-permute-start.14 = (bf16[128,3072]{1,0:T(8,128)(2,1)S(1)}, bf16[128,3072]{1,0:T(8,128)(2,1)S(1)}, u32[]{:S(2)}, u32[]{:S(2)}) collective-permute-start(bf16[128,3072]{1,0:T(8,128)(2,1)S(1)} %get-tuple-element.246), channel_id=1, source_target_pairs={{0,1},{1,0},{2,3},{3,2},{4,5},{5,4},{6,7},{7,6},{8,9},{9,8},{10,11... | collective-permute-start | bytes 2359304 | tf_op jit(solution)/shard_map/ppermute | solution.py:223
  155.5 26.7 %collective-permute-start.13 = (bf16[128,1920]{1,0:T(8,128)(2,1)S(1)}, bf16[128,1920]{1,0:T(8,128)(2,1)S(1)}, u32[]{:S(2)}, u32[]{:S(2)}) collective-permute-start(bf16[128,1920]{1,0:T(8,128)(2,1)S(1)} %pad_maximum_fusion.45), channel_id=1, source_target_pairs={{0,1},{1,0},{2,3},{3,2},{4,5},{5,4},{6,7},{7,6},{8,9},{9,8},{10,11... | collective-permute-start | bytes 1474568 | tf_op jit(solution)/shard_map/ppermute | solution.py:223
  157.0 17.8 %copy-start.48 = (bf16[1,768]{1,0:T(2,128)(2,1)S(1)}, bf16[1,768]{1,0:T(2,128)(2,1)}, u32[]{:S(2)}) copy-start(bf16[1,768]{1,0:T(2,128)(2,1)} %reshape.424) | copy-start | bytes 4612
  202.4 19.0 %collective-permute-start.20 = (bf16[768,1280]{0,1:T(8,128)(2,1)}, bf16[768,1280]{0,1:T(8,128)(2,1)}, u32[]{:S(2)}, u32[]{:S(2)}) collective-permute-start(bf16[768,1280]{0,1:T(8,128)(2,1)} %broadcast_select_fusion.4), channel_id=1, source_target_pairs={{0,2},{2,0},{4,6},{6,4},{8,10},{10,8},{12,14},{14,12},{16,18},{18,... | collective-permute-start | bytes 5898248 | tf_op jit(solution)/shard_map/ppermute | solution.py:220
  204.5 12.2 %collective-permute-start.22 = (bf16[128,1536]{1,0:T(8,128)(2,1)}, bf16[128,1536]{1,0:T(8,128)(2,1)}, u32[]{:S(2)}, u32[]{:S(2)}) collective-permute-start(bf16[128,1536]{1,0:T(8,128)(2,1)} %pad_maximum_fusion.47), channel_id=1, source_target_pairs={{0,1},{1,0},{2,3},{3,2},{4,5},{5,4},{6,7},{7,6},{8,9},{9,8},{10,11... | collective-permute-start | bytes 1179656 | tf_op jit(solution)/shard_map/ppermute | solution.py:223
  205.1 16.4 %copy-start.4 = (bf16[768,256]{0,1:T(8,128)(2,1)S(1)}, bf16[768,256]{0,1:T(8,128)(2,1)}, u32[]{:S(2)}) copy-start(bf16[768,256]{0,1:T(8,128)(2,1)} %pad_bitcast_fusion) | copy-start | bytes 1179652
  205.1 23.8 %collective-permute-start.23 = (bf16[128,768]{1,0:T(8,128)(2,1)}, bf16[128,768]{1,0:T(8,128)(2,1)}, u32[]{:S(2)}, u32[]{:S(2)}) collective-permute-start(bf16[128,768]{1,0:T(8,128)(2,1)} %get-tuple-element.67), channel_id=1, source_target_pairs={{0,1},{1,0},{2,3},{3,2},{4,5},{5,4},{6,7},{7,6},{8,9},{9,8},{10,11... | collective-permute-start | bytes 589832 | tf_op jit(solution)/shard_map/ppermute | solution.py:223
  228.3 23.2 %collective-permute-start.21 = (bf16[384,1280]{1,0:T(8,128)(2,1)}, bf16[384,1280]{1,0:T(8,128)(2,1)S(1)}, u32[]{:S(2)}, u32[]{:S(2)}) collective-permute-start(bf16[384,1280]{1,0:T(8,128)(2,1)} %dynamic-slice_bitcast_fusion), channel_id=1, source_target_pairs={{0,1},{1,0},{2,3},{3,2},{4,5},{5,4},{6,7},{7,6},{8,9},{9,8},{10,11... | collective-permute-start | bytes 2949128 | tf_op jit(solution)/shard_map/ppermute | solution.py:223
  231.3 2.3 collective-permute-start.24
  252.0 17.9 %collective-permute-start.25 = (bf16[2,2,48,2048]{3,2,1,0:T(8,128)(2,1)S(1)}, bf16[2,2,48,2048]{3,2,1,0:T(8,128)(2,1)S(1)}, u32[]{:S(2)}, u32[]{:S(2)}) collective-permute-start(bf16[2,2,48,2048]{3,2,1,0:T(8,128)(2,1)S(1)} %dynamic-slice_bitcast_fusion.1), channel_id=1, source_target_pairs={{0,4},{2,6},{4,0},{6,2},{8,12},{10,14},{12,8},{14,10},{16,20},{18,... | collective-permute-start | bytes 2359304 | tf_op jit(solution)/shard_map/ppermute | solution.py:220
  252.6 19.4 %copy-start.35 = (bf16[384,768]{1,0:T(8,128)(2,1)S(1)}, bf16[384,768]{1,0:T(8,128)(2,1)}, u32[]{:S(2)}) copy-start(bf16[384,768]{1,0:T(8,128)(2,1)} %copy-done.34) | copy-start | bytes 1769476
  252.6 19.4 %copy-start.37 = (bf16[384,768]{1,0:T(8,128)(2,1)S(1)}, bf16[384,768]{1,0:T(8,128)(2,1)}, u32[]{:S(2)}) copy-start(bf16[384,768]{1,0:T(8,128)(2,1)} %copy-done.36) | copy-start | bytes 1769476
  270.3 8.6 %collective-permute-start.26 = (bf16[2,48,2048]{2,1,0:T(8,128)(2,1)S(1)}, bf16[2,48,2048]{2,1,0:T(8,128)(2,1)S(1)}, u32[]{:S(2)}, u32[]{:S(2)}) collective-permute-start(bf16[2,48,2048]{2,1,0:T(8,128)(2,1)S(1)} %dynamic-slice_bitcast_fusion.3), channel_id=1, source_target_pairs={{0,8},{2,10},{4,12},{6,14},{8,0},{10,2},{12,4},{14,6},{16,24},{18,... | collective-permute-start | bytes 1179656 | tf_op jit(solution)/shard_map/ppermute | solution.py:220
  279.0 12.5 %collective-permute-start.27 = (bf16[48,2048]{1,0:T(8,128)(2,1)S(1)}, bf16[48,2048]{1,0:T(8,128)(2,1)S(1)}, u32[]{:S(2)}, u32[]{:S(2)}) collective-permute-start(bf16[48,2048]{1,0:T(8,128)(2,1)S(1)} %dynamic-slice_bitcast_fusion.5), channel_id=1, source_target_pairs={{0,16},{2,18},{4,20},{6,22},{8,24},{10,26},{12,28},{14,30},{16,0},... | collective-permute-start | bytes 589832 | tf_op jit(solution)/shard_map/ppermute | solution.py:220
  291.5 6.8 %collective-permute-start.28 = (bf16[48,2048]{1,0:T(8,128)(2,1)S(1)}, bf16[48,2048]{1,0:T(8,128)(2,1)S(1)}, u32[]{:S(2)}, u32[]{:S(2)}) collective-permute-start(bf16[48,2048]{1,0:T(8,128)(2,1)S(1)} %fusion.61), channel_id=1, source_target_pairs={{0,16},{2,18},{4,20},{6,22},{8,24},{10,26},{12,28},{14,30},{16,0},... | collective-permute-start | bytes 589832 | tf_op jit(solution)/shard_map/ppermute | solution.py:220
  295.3 12.4 %collective-permute-start.16 = (bf16[2,2,2,128,768]{4,3,0,1,2:T(8,128)(2,1)}, bf16[2,2,2,128,768]{4,3,0,1,2:T(8,128)(2,1)}, u32[]{:S(2)}, u32[]{:S(2)}) collective-permute-start(bf16[2,2,2,128,768]{4,3,0,1,2:T(8,128)(2,1)} %bitcast.150), channel_id=1, source_target_pairs={{0,2},{2,0},{4,6},{6,4},{8,10},{10,8},{12,14},{14,12},{16,18},{18,... | collective-permute-start | bytes 4718600 | tf_op jit(solution)/shard_map/ppermute | solution.py:220
  298.4 8.5 %collective-permute-start.29 = (bf16[2,48,2048]{2,1,0:T(8,128)(2,1)S(1)}, bf16[2,48,2048]{2,1,0:T(8,128)(2,1)S(1)}, u32[]{:S(2)}, u32[]{:S(2)}) collective-permute-start(bf16[2,48,2048]{2,1,0:T(8,128)(2,1)S(1)} %pad_maximum_fusion.48), channel_id=1, source_target_pairs={{0,8},{2,10},{4,12},{6,14},{8,0},{10,2},{12,4},{14,6},{16,24},{18,... | collective-permute-start | bytes 1179656 | tf_op jit(solution)/shard_map/ppermute | solution.py:220
  307.1 33.2 %collective-permute-start.30 = (bf16[2,2,48,2048]{3,2,0,1:T(8,128)(2,1)S(1)}, bf16[2,2,48,2048]{3,2,0,1:T(8,128)(2,1)}, u32[]{:S(2)}, u32[]{:S(2)}) collective-permute-start(bf16[2,2,48,2048]{3,2,0,1:T(8,128)(2,1)S(1)} %pad_maximum_fusion.31), channel_id=1, source_target_pairs={{0,4},{2,6},{4,0},{6,2},{8,12},{10,14},{12,8},{14,10},{16,20},{18,... | collective-permute-start | bytes 2359304 | tf_op jit(solution)/shard_map/ppermute | solution.py:220
  309.6 43.6 %collective-permute-start.17 = (bf16[2,2,128,768]{3,2,0,1:T(8,128)(2,1)S(1)}, bf16[2,2,128,768]{3,2,0,1:T(8,128)(2,1)S(1)}, u32[]{:S(2)}, u32[]{:S(2)}) collective-permute-start(bf16[2,2,128,768]{3,2,0,1:T(8,128)(2,1)S(1)} %dynamic-slice_bitcast_fusion.2), channel_id=1, source_target_pairs={{0,4},{2,6},{4,0},{6,2},{8,12},{10,14},{12,8},{14,10},{16,20},{18,... | collective-permute-start | bytes 2359304 | tf_op jit(solution)/shard_map/ppermute | solution.py:220
  341.9 96.5 %collective-permute-start.31 = (bf16[384,2048]{1,0:T(8,128)(2,1)S(1)}, bf16[384,2048]{1,0:T(8,128)(2,1)S(1)}, u32[]{:S(2)}, u32[]{:S(2)}) collective-permute-start(bf16[384,2048]{1,0:T(8,128)(2,1)S(1)} %bitcast.158), channel_id=1, source_target_pairs={{0,2},{2,0},{4,6},{6,4},{8,10},{10,8},{12,14},{14,12},{16,18},{18,... | collective-permute-start | bytes 4718600 | tf_op jit(solution)/shard_map/ppermute | solution.py:220
  353.5 14.6 %collective-permute-start.18 = (bf16[2,128,768]{2,1,0:T(8,128)(2,1)S(1)}, bf16[2,128,768]{2,1,0:T(8,128)(2,1)S(1)}, u32[]{:S(2)}, u32[]{:S(2)}) collective-permute-start(bf16[2,128,768]{2,1,0:T(8,128)(2,1)S(1)} %dynamic-slice_bitcast_fusion.4), channel_id=1, source_target_pairs={{0,8},{2,10},{4,12},{6,14},{8,0},{10,2},{12,4},{14,6},{16,24},{18,... | collective-permute-start | bytes 1179656 | tf_op jit(solution)/shard_map/ppermute | solution.py:220
  369.1 67.1 %collective-permute-start.19 = (bf16[128,768]{1,0:T(8,128)(2,1)}, bf16[128,768]{1,0:T(8,128)(2,1)}, u32[]{:S(2)}, u32[]{:S(2)}) collective-permute-start(bf16[128,768]{1,0:T(8,128)(2,1)} %dynamic-slice_bitcast_fusion.6), channel_id=1, source_target_pairs={{0,16},{2,18},{4,20},{6,22},{8,24},{10,26},{12,28},{14,30},{16,0},... | collective-permute-start | bytes 589832 | tf_op jit(solution)/shard_map/ppermute | solution.py:220
  (63 other events, 336.2 us)
Sparse Core Ops, SparseCore 0:
  307.8 121.1 all-reduce.5

commit v3 on v2

--- a/solution.py
+++ b/solution.py
@@ -30,10 +30,10 @@
     T=q_ref.shape[0]; W=k_ref.shape[0]; NB=W//T
     c=DH**-0.5
     q=q_ref[...]
-    qc=((q+rows_ref[0:1,:])*c).astype(BF)
-    qp=((q+rows_ref[1:2,:])*c).astype(BF)
-    qt=(q+rows_ref[2:3,:])*c
-    t0=qt*rows_ref[3:4,:]; t1=qt*rows_ref[4:5,:]
+    qc=((q+rows_ref[1:2, :])*c).astype(BF)
+    qp=((q+rows_ref[2:3, :])*c).astype(BF)
+    qt=(q+rows_ref[3:4, :])*c
+    t0=qt*rows_ref[4:5, :]; t1=qt*rows_ref[5:6, :]
     lane=lax.broadcasted_iota(jnp.int32,(T,128),1)
     row=lax.broadcasted_iota(jnp.int32,(T,128),0)
     same=kind_ref[...]>0.5
@@ -74,10 +74,10 @@
     T=q_ref.shape[0]; W=k_ref.shape[0]; NB=W//T
     c=DH**-0.5
     q=q_ref[...]
-    qc=((q+rows_ref[0:1,:])*c).astype(BF)
-    qp=((q+rows_ref[1:2,:])*c).astype(BF)
-    qt=(q+rows_ref[2:3,:])*c
-    e0=rows_ref[3:4,:]; e1=rows_ref[4:5,:]
+    qc=((q+rows_ref[1:2, :])*c).astype(BF)
+    qp=((q+rows_ref[2:3, :])*c).astype(BF)
+    qt=(q+rows_ref[3:4, :])*c
+    e0=rows_ref[4:5, :]; e1=rows_ref[5:6, :]
     lane=lax.broadcasted_iota(jnp.int32,(T,128),1)
     row=lax.broadcasted_iota(jnp.int32,(T,128),0)
     same=kind_ref[...]>0.5
@@ -137,7 +137,7 @@
     return pl.pallas_call(
         att_fwd_kernel,
         grid=(D // 128,),
-        in_specs=[col(T), col(8), fixed(T), fixed(T), col(W), col(W), col(W + T), fixed(W)],
+        in_specs=[col(T), col(16), fixed(T), fixed(T), col(W), col(W), col(W + T), fixed(W)],
         out_specs=[col(T), pl.BlockSpec((2, T, W), lambda i: (i, 0, 0))],
         out_shape=[
             jax.ShapeDtypeStruct((T, D), F32),
@@ -163,7 +163,7 @@
         att_bwd_kernel,
         grid=(D // 128,),
         in_specs=[
-            col(T), col(8), fixed(T), col(T), col(T), pl.BlockSpec((2, T, W), lambda i: (i, 0, 0)),
+            col(T), col(16), fixed(T), col(T), col(T), pl.BlockSpec((2, T, W), lambda i: (i, 0, 0)),
             col(W), col(W), col(W + T), fixed(W),
         ],
         out_specs=[
@@ -186,6 +186,331 @@
     )(q, rows, kind, dm, o, p, k, v, t, ka)
 
 
+def pack_rows(vectors, dn):
+    counts = [v.size // dn for v in vectors]
+
+    def kernel(*refs):
+        out = refs[-1]
+        at = 0
+        for ref, n in zip(refs, counts):
+            for j in range(n):
+                if len(ref.shape) == 1:
+                    out[at, :] = ref[pl.ds(j * dn, dn)].astype(F32)
+                else:
+                    out[at, :] = ref[j, :].astype(F32)
+                at += 1
+
+    return pl.pallas_call(
+        kernel,
+        out_shape=jax.ShapeDtypeStruct((sum(counts), dn), F32),
+        name="pack_rows",
+    )(*vectors)
+
+
+def ffn_final(blocks, FF, D):
+    count, _, dn = blocks.shape
+    steps = FF // D
+    per = count // steps
+    ri, ru = FF // count, FF // 2 // count
+
+    def kernel(b_ref, i_ref, u_ref):
+        gi = jnp.concatenate([b_ref[k, :ri] for k in range(per)], axis=0)
+        i_ref[...] = jnp.transpose(gi.astype(F32))
+        for k in range(per):
+            u_ref[ru * k : ru * (k + 1), :dn] = b_ref[k, ri : ri + ru].astype(F32)
+            u_ref[ru * k : ru * (k + 1), dn:] = b_ref[k, ri + ru :].astype(F32)
+
+    return pl.pallas_call(
+        kernel,
+        grid=(steps,),
+        in_specs=[pl.BlockSpec((per, ri + 2 * ru, dn), lambda i: (i, 0, 0))],
+        out_specs=[
+            pl.BlockSpec((dn, D), lambda i: (0, i)), pl.BlockSpec((FF // 2 // steps, D), lambda i: (i, 0))
+        ],
+        out_shape=[
+            jax.ShapeDtypeStruct((dn, FF), F32), jax.ShapeDtypeStruct((FF // 2, D), F32)
+        ],
+        cost_estimate=pl.CostEstimate(flops=0, bytes_accessed=6 * D * FF, transcendentals=0),
+        name="ffn_final",
+    )(blocks)
+
+
+def split_cols(a, f, odd):
+    h = a.shape[1] // 2
+    q = h // 2
+    own = jnp.where(f == 0, a[:, :h], a[:, h:])
+    other = jnp.where(f == 0, a[:, h:], a[:, :h])
+    swapped = jnp.concatenate([other[:, q:], other[:, :q]], axis=1)
+    return jnp.concatenate([own, jnp.where(odd, swapped, other)], axis=1)
+
+
+def merge_cols(a, f, odd):
+    h = a.shape[1] // 2
+    q = h // 2
+    own, other = a[:, :h], a[:, h:]
+    swapped = jnp.concatenate([other[:, q:], other[:, :q]], axis=1)
+    other = jnp.where(odd, swapped, other)
+    return jnp.where(
+        f == 0, jnp.concatenate([own, other], axis=1), jnp.concatenate([other, own], axis=1)
+    )
+
+
+def swap_quarters(a, y, odd):
+    h = a.shape[1] // 2
+    q = h // 2
+    a = jnp.where(y, jnp.concatenate([a[:, h:], a[:, :h]], axis=1), a)
+    pairs = jnp.concatenate([a[:, q:h], a[:, :q], a[:, h + q :], a[:, h : h + q]], axis=1)
+    return jnp.where(odd, pairs, a)
+
+
+def middle_swap(a):
+    q = a.shape[1] // 4
+    return jnp.concatenate([a[:, :q], a[:, 2 * q : 3 * q], a[:, q : 2 * q], a[:, 3 * q :]], axis=1)
+
+
+def split_quarters(a, f, y, odd):
+    h = a.shape[1] // 2
+    own = jnp.where(f == 0, a[:, :h], a[:, h:])
+    other = jnp.where(f == 0, a[:, h:], a[:, :h])
+    return own, middle_swap(swap_quarters(other, y, odd))
+
+
+def merge_quarters(a, f, y, odd):
+    h = a.shape[1] // 2
+    own, other = a[:, :h], swap_quarters(middle_swap(a[:, h:]), y, odd)
+    return jnp.where(
+        f == 0, jnp.concatenate([own, other], axis=1), jnp.concatenate([other, own], axis=1)
+    )
+
+
+def norm_stats(res):
+    center = res - jnp.mean(res, axis=1, keepdims=True)
+    rstd = lax.rsqrt(jnp.mean(center * center, axis=1, keepdims=True) + EPS)
+    return center * rstd, rstd
+
+
+def norm_back(g, gain, n, rstd):
+    gg = g * gain
+    return (gg - jnp.mean(gg, axis=1, keepdims=True) - n * jnp.mean(gg * n, axis=1, keepdims=True)) * rstd
+
+
+def row_sum(a):
+    return jnp.sum(a, axis=0, keepdims=True)
+
+
+GELU_A = 0.7978845608028654
+GELU_B = 0.044715
+
+
+def ffn_specs(T, D, FF):
+    steps = FF // (D // 2)
+    half = steps // 2
+    c = FF // steps
+    q = D // 8
+
+    def chunk_at(j, s):
+        p = jnp.maximum(j - half, 0)
+        piece = ((s[2] ^ (p & 1)) << 1) | (s[1] ^ (p >> 1))
+        return jnp.where(j < half, half * s[0] + j, half * (1 - s[0]) + piece)
+
+    col = lambda j, s: (0, chunk_at(j, s))
+    whole = lambda *shape: pl.BlockSpec(shape, lambda j, s: (0,) * len(shape))
+    inner = [pl.BlockSpec((4 * q, c), col)] + [pl.BlockSpec((q, c), col)] * 4
+    outer = [pl.BlockSpec((c, D), lambda j, s: (jnp.minimum(j, half - 1), 0))] + [whole(c, D)] * 4
+    proj = [whole(4 * q, D), whole(2 * q, D), whole(2 * q, D)]
+    return steps, half, c, chunk_at, col, whole, inner, outer, proj
+
+
+def outer_chunk(j, half, refs):
+    chunk = refs[0][...]
+    for p in range(4):
+        chunk = jnp.where(j == half + p, refs[1 + p][...], chunk)
+    return chunk
+
+
+def rows_of(refs):
+    return jnp.concatenate([r[...] for r in refs], axis=0)
+
+
+def inner_bias_chunk(b, half, vec_ref, D):
+    row = vec_ref[pl.ds(12 + b % half, 1), :]
+    return jnp.where(b < half, row[:, : D // 2], row[:, D // 2 :])
+
+
+def gelu_tanh(u):
+    return jnp.tanh(GELU_A * (u + GELU_B * u * u * u))
+
+
+def first_norm(x, mixed, vec_ref, w, f, odd):
+    attn = nn(split_cols(mixed, f, odd).astype(BF), w) + vec_ref[6:7, :]
+    n1, rstd = norm_stats(x.astype(F32) + attn)
+    return n1, rstd, n1 * vec_ref[7:8, :] + vec_ref[8:9, :]
+
+
+def ffn_fwd(place, x, mixed, cot, vecs, o_parts, i_parts, u_parts, FF):
+    T, D = x.shape
+    steps, half, c, chunk_at, col, whole, inner, outer, proj = ffn_specs(T, D, FF)
+
+    def kernel(s_ref, x_ref, m_ref, g_ref, v_ref, *refs):
+        o_refs, i_refs, u_refs = refs[:3], refs[3:8], refs[8:13]
+        nl_ref, act_ref, pre_ref, res_ref, dr_ref, do_ref, n1_ref, rs_ref, gv_ref = refs[13:22]
+        np_ref, acc_ref, nf_ref = refs[22:]
+        j = pl.program_id(0)
+        f, odd, y = s_ref[0], s_ref[1] == 1, s_ref[2] == 1
+
+        @pl.when(j == 0)
+        def _():
+            n1, rstd, normed = first_norm(x_ref[...], m_ref[...], v_ref, rows_of(o_refs), f, odd)
+            n1_ref[...] = n1
+            rs_ref[...] = jnp.broadcast_to(rstd, (T, 128))
+            nf_ref[...] = normed
+            nl_ref[...] = normed.astype(BF)
+            np_ref[...] = jnp.concatenate(split_quarters(normed, f, y, odd), axis=1).astype(BF)
+            acc_ref[...] = jnp.zeros_like(acc_ref)
+
+        bias = inner_bias_chunk(chunk_at(j, s_ref), half, v_ref, D)
+        pre = nn(np_ref[...], rows_of(i_refs)) + bias
+        pre_ref[...] = pre
+        act = (0.5 * pre * (1.0 + gelu_tanh(pre))).astype(BF)
+        act_ref[...] = act
+        acc_ref[...] += nn(act, outer_chunk(j, half, u_refs))
+
+        @pl.when(j == steps - 1)
+        def _():
+            n2, rstd = norm_stats(nf_ref[...] + (acc_ref[...] + v_ref[9:10, :]))
+            g = g_ref[...].astype(F32)
+            res_ref[...] = (n2 * v_ref[10:11, :] + v_ref[11:12, :]).astype(BF)
+            d = norm_back(g, v_ref[10:11, :], n2, rstd)
+            dr_ref[...] = d
+            do = d.astype(BF)
+            do_ref[...] = do
+            gv_ref[0:1, :] = row_sum(g * n2)
+            gv_ref[1:2, :] = row_sum(g)
+            gv_ref[2:3, :] = row_sum(do.astype(F32))
+            gv_ref[3:8, :] = jnp.zeros((5, D), F32)
+
+    f32 = lambda *shape: jax.ShapeDtypeStruct(shape, F32)
+    low = lambda *shape: jax.ShapeDtypeStruct(shape, BF)
+    tok = whole(T, D)
+    chunk = pl.BlockSpec((T, c), col)
+    return pl.pallas_call(
+        kernel,
+        grid_spec=pltpu.PrefetchScalarGridSpec(
+            num_scalar_prefetch=1,
+            grid=(steps,),
+            in_specs=[tok, tok, tok, whole(16, D)] + proj + inner + outer,
+            out_specs=[tok, chunk, chunk, tok, tok, tok, tok, whole(T, 128), whole(8, D)],
+            scratch_shapes=[
+                pltpu.VMEM((T, D), BF), pltpu.VMEM((T, D), F32), pltpu.VMEM((T, D), F32)
+            ],
+        ),
+        out_shape=[
+            low(T, D), low(T, FF), f32(T, FF), low(T, D), f32(T, D), low(T, D), f32(T, D),
+            f32(T, 128), f32(8, D),
+        ],
+        compiler_params=pltpu.CompilerParams(vmem_limit_bytes=40 * 2**20),
+        cost_estimate=pl.CostEstimate(
+            flops=4 * T * D * FF, bytes_accessed=4 * D * FF, transcendentals=T * FF
+        ),
+        name="ffn_fwd",
+    )(place, x, mixed, cot, vecs, *o_parts, *i_parts, *u_parts)
+
+
+def ffn_bwd(
+    place, count, pre, act, normed, d_outer, d_outer_got, d_res2, n1, rstd1, mixed_got, x_got,
+    vecs, o_parts, i_parts, u_parts,
+):
+    T, FF = pre.shape
+    D = d_outer.shape[1]
+    dn = D // 2
+    steps, half, c, chunk_at, col, whole, inner, outer, proj = ffn_specs(T, D, FF)
+    ri, ru = FF // count, FF // 2 // count
+
+    def kernel(s_ref, pre_ref, act_ref, nl_ref, do_ref, dog_ref, dr_ref, n1_ref, rs_ref, mg_ref, xg_ref, v_ref, *refs):
+        o_refs, i_refs, u_refs = refs[:3], refs[3:8], refs[8:13]
+        pay_ref, d1_ref, da_ref, dm_ref, gv_ref = refs[13:18]
+        acc_ref, ib_ref, np_ref, nf_ref, do_both = refs[18:]
+        j = pl.program_id(0)
+        f, odd, y = s_ref[0], s_ref[1] == 1, s_ref[2] == 1
+
+        @pl.when(j == 0)
+        def _():
+            acc_ref[...] = jnp.zeros_like(acc_ref)
+            theirs = first_norm(xg_ref[...], mg_ref[...], v_ref, rows_of(o_refs), f, odd)[2]
+            own, other = split_quarters(theirs, f, y, odd)
+            np_ref[...] = jnp.concatenate([own, other], axis=1).astype(BF)
+            nl = nl_ref[...]
+            nf_ref[:T] = jnp.where(f == 0, nl[:, :dn], nl[:, dn:])
+            nf_ref[T:] = own.astype(BF)
+            do_both[:T] = do_ref[...]
+            do_both[T:] = dog_ref[...]
+
+        b = chunk_at(j, s_ref)
+        w = rows_of(i_refs)
+        pre_got = nn(np_ref[...], w) + inner_bias_chunk(b, half, v_ref, D)
+        u = jnp.concatenate([pre_ref[...], pre_got], axis=0)
+        t = gelu_tanh(u)
+        slope = 0.5 * (1.0 + t) + 0.5 * u * (1.0 - t * t) * (GELU_A * (1.0 + 3.0 * GELU_B * u * u))
+        di = (nt(do_both[...], outer_chunk(j, half, u_refs)) * slope).astype(BF)
+        ib_ref[pl.ds(b, 1), :] = row_sum(di[:T].astype(F32))
+        acc_ref[...] += nt(di[:T], w)
+        gi = tn(di, nf_ref[...]).astype(BF)
+        for k in range(c // ri):
+            pay_ref[b * (c // ri) + k, :ri] = gi[ri * k : ri * (k + 1)]
+
+        @pl.when(j < half)
+        def _():
+            act_got = (0.5 * u[T:] * (1.0 + t[T:])).astype(BF)
+            gu = tn(jnp.concatenate([act_ref[...], act_got], axis=0), do_both[...]).astype(BF)
+            for k in range(c // ru):
+                pay_ref[j * (c // ru) + k, ri : ri + ru] = gu[ru * k : ru * (k + 1), :dn]
+                pay_ref[j * (c // ru) + k, ri + ru :] = gu[ru * k : ru * (k + 1), dn:]
+
+        @pl.when(j == steps - 1)
+        def _():
+            d_normed = dr_ref[...] + merge_quarters(acc_ref[...], f, y, odd)
+            n1 = n1_ref[...]
+            d1 = norm_back(d_normed, v_ref[7:8, :], n1, rs_ref[:, 0:1])
+            d1_ref[...] = d1
+            da = d1.astype(BF)
+            da_ref[...] = da
+            dm = merge_cols(nt(da, rows_of(o_refs)), f, odd)
+            dm_ref[...] = dm.astype(BF)
+            gv_ref[0:1, :] = row_sum(d_normed * n1)
+            gv_ref[1:2, :] = row_sum(d_normed)
+            gv_ref[2:3, :] = row_sum(da.astype(F32))
+            gv_ref[3:4, :] = row_sum(dm.astype(BF).astype(F32))
+            gv_ref[4:, :] = jnp.concatenate([ib_ref[:half], ib_ref[half:]], axis=1)
+
+    f32 = lambda *shape: jax.ShapeDtypeStruct(shape, F32)
+    low = lambda *shape: jax.ShapeDtypeStruct(shape, BF)
+    tok = whole(T, D)
+    chunk = pl.BlockSpec((T, c), col)
+    return pl.pallas_call(
+        kernel,
+        grid_spec=pltpu.PrefetchScalarGridSpec(
+            num_scalar_prefetch=1,
+            grid=(steps,),
+            in_specs=[chunk, chunk] + [tok] * 5 + [whole(T, 128), tok, tok, whole(16, D)]
+            + proj + inner + outer,
+            out_specs=[whole(count, ri + 2 * ru, dn), tok, tok, tok, whole(8, D)],
+            scratch_shapes=[
+                pltpu.VMEM((T, D), F32), pltpu.VMEM((steps, c), F32), pltpu.VMEM((T, D), BF),
+                pltpu.VMEM((2 * T, dn), BF), pltpu.VMEM((2 * T, D), BF),
+            ],
+        ),
+        out_shape=[low(count, ri + 2 * ru, dn), f32(T, D), low(T, D), low(T, D), f32(8, D)],
+        compiler_params=pltpu.CompilerParams(vmem_limit_bytes=44 * 2**20),
+        cost_estimate=pl.CostEstimate(
+            flops=14 * T * D * FF, bytes_accessed=6 * D * FF, transcendentals=2 * T * FF
+        ),
+        name="ffn_bwd",
+    )(
+        place, pre, act, normed, d_outer, d_outer_got, d_res2, n1, rstd1, mixed_got, x_got, vecs,
+        *o_parts, *i_parts, *u_parts,
+    )
+
+
 def layer_norm(residual, gain_vec, bias_vec):
     center = residual - jnp.mean(residual, axis=-1, keepdims=True)
     spread = jnp.mean(center * center, axis=-1, keepdims=True)
@@ -229,13 +554,12 @@
         half = w.shape[0] // 2
         return self.trade(lax.dynamic_slice_in_dim(w, self.bit(0) * half, half, 0))
 
-    def fetch(self, w):
-        got = self.fetch_half(w)
-        return got, self.flip(got, 0)
-
-    def join(self, w, parts):
-        theirs = jnp.concatenate(self.order(*parts, self.bit(0)), axis=0)
-        return jnp.concatenate(self.order(w, theirs, self.f), axis=0)
+    def fetch_quarter(self, w):
+        n = w.shape[0] // 4
+        return self.trade(lax.dynamic_slice_in_dim(w, (self.ctx % 4) * n, n, 0))
+
+    def pieces(self, got, y):
+        return got, y, self.flip(got, 0), self.flip(y, 0)
 
     def full_small(self, w):
         if not self.pair:
@@ -251,17 +575,17 @@
         y = self.flip(block, 1)
         self.first_hop = y
         pair = jnp.stack(self.order(block, y, self.bit(1)))
-        above, below = [], []
         up = down = pair
+        groups = [(pair[None], self.flip(pair[None], 0))]
         for _ in range(planes):
             up = lax.ppermute(up, "ctx", [(i, i + 4) for i in range(self.count - 4)])
             down = lax.ppermute(down, "ctx", [(i + 4, i) for i in range(self.count - 4)])
-            above.insert(0, up)
-            below.append(down)
-        mine = jnp.stack(above + [pair] + below)
-        other = self.flip(mine, 0)
-        both = jnp.stack(self.order(mine, other, self.bit(0)), axis=2)
-        return both.reshape((-1,) + block.shape)
+            both = jnp.stack([up, down])
+            groups.append((both, self.flip(both, 0)))
+        self.last_hop = both
+        groups = [jnp.stack(self.order(a, b, self.bit(0)), axis=2) for a, b in groups]
+        planes = [g[0] for g in groups[:0:-1]] + [groups[0][0]] + [g[1] for g in groups[1:]]
+        return jnp.concatenate(planes, axis=0).reshape((-1,) + block.shape)
 
     def halve(self, a, k, axis):
         keep = lax.dynamic_index_in_dim(a, self.bit(k), axis, keepdims=False)
@@ -270,7 +594,7 @@
 
     def halve_cols(self, low, high):
         keep, send = self.order(low, high, self.bit(0))
-        return (keep.astype(F32) + self.flip(send, 0).astype(F32)).astype(BF)
+        return (keep.astype(F32) + self.flip(send.astype(BF), 0).astype(F32)).astype(BF)
 
     def double(self, a, k, axis):
         return jnp.stack(self.order(a, self.flip(a, k), self.bit(k)), axis=axis)
@@ -338,176 +662,206 @@
         value_bias, content_bias, position_bias, type_bias, type_embed, output_bias,
         attn_gain, attn_shift, outer_bias, ffn_gain, ffn_shift, inner_bias,
     )
-    vectors, _ = lax.optimization_barrier((vectors, sh.first_hop))
-    small = jnp.concatenate([a.reshape(-1, dn) for a in vectors], axis=0)
-    nsmall = small.shape[0]
-    small_full = sh.full_small(small).astype(F32)
-    vecs = jnp.transpose(small_full[:, :12], (1, 0, 2)).reshape(12, D)
-    v_bias, _, _, _, _, _, o_bias, a_gain, a_shift, out_bias, f_gain, f_shift = (
-        vecs[i] for i in range(12)
-    )
-    in_bias = small_full[:, 12:].reshape(-1)
-    first = (key_proj, value_proj, query_proj, position_proj, output_proj)
+    small = pack_rows(vectors, dn)
+    small_full = sh.full_small(small)
     if sh.pair:
-        got = sh.fetch(jnp.concatenate(first, axis=1))
-        k_full, v_full, q_full, p_full, o_full = (
-            sh.join(w, [part[:, i * D : (i + 1) * D] for part in got])
-            for i, w in enumerate(first)
+        odd = sh.bit(0) == 1
+        got_a = sh.trade(jnp.where(odd, value_proj, position_proj))
+        got_b = sh.trade(jnp.where(odd, key_proj, query_proj))
+        got_o = sh.fetch_half(output_proj)
+        got_a, got_b, got_o, i_sh, u_sh, small_full, _ = lax.optimization_barrier(
+            (got_a, got_b, got_o, inner_proj, outer_proj, small_full, sh.last_hop)
         )
-        _, i_sh, u_sh = lax.optimization_barrier((got[0], inner_proj, outer_proj))
-        i_got, u_got = sh.fetch_half(i_sh), sh.fetch_half(u_sh)
+        other_p, other_v = sh.order(got_a, sh.flip(got_a, 0), sh.bit(0))
+        other_q, other_k = sh.order(got_b, sh.flip(got_b, 0), sh.bit(0))
+        p_full, k_full, v_full, q_full = (
+            jnp.concatenate(sh.order(w, g, sh.f), axis=0)
+            for w, g in (
+                (position_proj, other_p), (key_proj, other_k), (value_proj, other_v), (query_proj, other_q)
+            )
+        )
+        flip_o = sh.flip(got_o, 0)
+        i_got, u_got = sh.fetch_quarter(i_sh), sh.fetch_quarter(u_sh)
     else:
-        k_full, v_full, q_full, p_full, o_full, inner_full, outer_full = (
+        p_full, k_full, v_full, q_full, o_full, inner_full, outer_full = (
             lax.all_gather(w, "fsdp", axis=0, tiled=True)
-            for w in first + (inner_proj, outer_proj)
+            for w in (
+                position_proj, key_proj, value_proj, query_proj, output_proj, inner_proj, outer_proj
+            )
         )
+
+    vecs = jnp.concatenate([small_full[i] for i in range(sh.parts)], axis=1)
 
     q_lin = nn(hidden, q_full)
     keys = nn(x_win, k_full).astype(BF)
-    values = (nn(x_win, v_full) + v_bias).astype(BF)
+    values = (nn(x_win, v_full) + vecs[0]).astype(BF)
     sinus = sinus_rows(T + R * T - 1, W + T, D)
     table = nn(sinus, p_full).astype(BF)
-    rows = jnp.concatenate([vecs[1:6], jnp.zeros((3, D), F32)], axis=0)
-
-    mixed_f, probs = att_fwd(q_lin, rows, pen, kind_q, keys, values, table, kaug)
+
     if sh.pair:
-        mixed_f, i_got, u_got = lax.optimization_barrier((mixed_f, i_got, u_got))
-        inner_full = sh.join(inner_proj, (i_got, sh.flip(i_got, 0)))
-        outer_full = sh.join(outer_proj, (u_got, sh.flip(u_got, 0)))
+        i_got, table = lax.optimization_barrier((i_got, table))
+        i_y = sh.flip(i_got, 1)
+        u_got, values, i_y = lax.optimization_barrier((u_got, values, i_y))
+        u_y = sh.flip(u_got, 1)
+    mixed_f, probs = att_fwd(q_lin, vecs, pen, kind_q, keys, values, table, kaug)
     mixed_low = mixed_f.astype(BF)
-    attn_out = nn(mixed_low, o_full) + o_bias
-    normed, first_pull = jax.vjp(layer_norm, hidden.astype(F32) + attn_out, a_gain, a_shift)
-    normed_low = normed.astype(BF)
-    inner_pre = nn(normed_low, inner_full) + in_bias
-    activated, gelu_pull = jax.vjp(partial(jax.nn.gelu, approximate=True), inner_pre)
-    activ_low = activated.astype(BF)
-    outer_out = nn(activ_low, outer_full) + out_bias
-    outcome, second_pull = jax.vjp(layer_norm, normed + outer_out, f_gain, f_shift)
-    d_res2, grad_ffn_gain, grad_ffn_shift = second_pull(cotangent)
-    d_outer = d_res2.astype(BF)
-    grad_outer_bias = jnp.sum(d_outer.astype(F32), axis=0)
-    d_inner = gelu_pull(nt(d_outer, outer_full))[0].astype(BF)
-    grad_inner_bias = jnp.sum(d_inner.astype(F32), axis=0)
-    d_normed = d_res2 + nt(d_inner, inner_full)
-    d_res1, grad_attn_gain, grad_attn_shift = first_pull(d_normed)
-    d_attn = d_res1.astype(BF)
-    grad_output_bias = jnp.sum(d_attn.astype(F32), axis=0)
-    d_mixed = nt(d_attn, o_full).astype(BF)
-
     if sh.pair:
-        lefts = sh.trade(
-            jnp.concatenate([sh.own(normed_low, 1, True), sh.own(activ_low, 1, True)], axis=1)
+        place = jnp.stack([sh.f, sh.bit(0), sh.bit(1)])
+        mixed_f, hid, fetched = lax.optimization_barrier((mixed_f, hidden, (i_got, i_y, u_got, u_y)))
+        hidden_got = sh.trade(hid)
+        mixed_low = mixed_f.astype(BF)
+        parts = (
+            (output_proj, got_o, flip_o),
+            (inner_proj,) + sh.pieces(*fetched[:2]),
+            (outer_proj,) + sh.pieces(*fetched[2:]),
         )
-        rights = (sh.trade(d_inner), sh.trade(d_outer))
-        got = sh.trade(
-            jnp.concatenate([sh.own(mixed_low, 1, True), sh.own(hidden, 1, True), d_attn], axis=1)
+        FF = inner_proj.shape[1]
+        mixed_got = sh.trade(mixed_low)
+        normed_low, activ_low, pre, outcome, d_res2, d_outer, n1, rstd1, vec_a = ffn_fwd(
+            place, hidden, mixed_f, out_grad[0], vecs, *parts, FF
         )
+        ffn, d_res1, d_attn, d_mixed, vec_b = ffn_bwd(
+            place, C, pre, activ_low, normed_low, d_outer, sh.trade(d_outer), d_res2, n1, rstd1,
+            mixed_got, hidden_got, vecs, *parts,
+        )
+    else:
+        attn_out = nn(mixed_low, o_full) + vecs[6]
+        normed, first_pull = jax.vjp(layer_norm, hidden.astype(F32) + attn_out, vecs[7], vecs[8])
+        normed_low = normed.astype(BF)
+        inner_pre = nn(normed_low, inner_full) + vecs[12:].reshape(-1, sh.parts, dn).transpose(1, 0, 2).reshape(-1)
+        activated, gelu_pull = jax.vjp(partial(jax.nn.gelu, approximate=True), inner_pre)
+        activ_low = activated.astype(BF)
+        outer_out = nn(activ_low, outer_full) + vecs[9]
+        outcome, second_pull = jax.vjp(layer_norm, normed + outer_out, vecs[10], vecs[11])
+        d_res2, grad_ffn_gain, grad_ffn_shift = second_pull(cotangent)
+        d_outer = d_res2.astype(BF)
+        grad_outer_bias = jnp.sum(d_outer.astype(F32), axis=0)
+        d_inner = gelu_pull(nt(d_outer, outer_full))[0].astype(BF)
+        grad_inner_bias = jnp.sum(d_inner.astype(F32), axis=0)
+        d_normed = d_res2 + nt(d_inner, inner_full)
+        d_res1, grad_attn_gain, grad_attn_shift = first_pull(d_normed)
+        d_attn = d_res1.astype(BF)
+        grad_output_bias = jnp.sum(d_attn.astype(F32), axis=0)
+        d_mixed = nt(d_attn, o_full).astype(BF)
+        vec_a = jnp.stack(
+            [grad_ffn_gain, grad_ffn_shift, grad_outer_bias] + [jnp.zeros((D,), F32)] * 5
+        )
+        ib = grad_inner_bias.reshape(sh.parts, -1, dn).transpose(1, 0, 2).reshape(-1, D)
+        vec_b = jnp.concatenate(
+            [
+                jnp.stack(
+                    [
+                        grad_attn_gain, grad_attn_shift, grad_output_bias,
+                        jnp.sum(d_mixed.astype(F32), axis=0),
+                    ]
+                ),
+                ib,
+            ],
+            axis=0,
+        )
+    if sh.pair:
+        d_attn_got = sh.trade(d_attn)
     dq, att_vec, dkv, d_table = att_bwd(
-        q_lin, rows, kind_q, d_mixed, mixed_f, probs, keys, values, table, kaug
+        q_lin, vecs, kind_q, d_mixed, mixed_f, probs, keys, values, table, kaug
     )
     if sh.pair:
-        gi = tn(
-            jnp.concatenate([sh.own(normed_low, 1), lefts[:, :dn]], axis=0),
-            jnp.concatenate([d_inner, rights[0]], axis=0),
-        ).astype(BF)
-        gu = tn(
-            jnp.concatenate([sh.own(activ_low, 1), lefts[:, dn:]], axis=0),
-            jnp.concatenate([d_outer, rights[1]], axis=0),
-        ).astype(BF)
         dq_got = sh.trade(dq)
-        gi, gu, dkv, d_table = lax.optimization_barrier((gi, gu, dkv, d_table))
+        ffn = lax.psum_scatter(ffn, "ctx", scatter_dimension=0, tiled=False)
     else:
         gi, gu = (
             lax.psum_scatter(tn(a, b).astype(BF), "fsdp", scatter_dimension=0, tiled=True)
             for a, b in ((normed_low, d_inner), (activ_low, d_outer))
         )
-    gi, gu = lax.psum((gi, gu), "ctx")
-
-    dk, dv = dkv[0], dkv[1]
-    gk, gv, gp = (
-        lax.dot_general(a, b, (((0,), (1,)), ((), ())), preferred_element_type=F32).astype(BF)
-        for a, b in ((x_win, dk), (x_win, dv), (sinus, d_table))
+        ffn = lax.psum((gi, gu), "ctx")
+
+    dkv = dkv.reshape(2 * D, W)
+    gkv, gp = (
+        lax.dot_general(a, b, (((0,), (1,)), ((), ())), preferred_element_type=F32)
+        for a, b in ((x_win, dkv), (sinus, d_table))
     )
-    smalls = jnp.concatenate(
-        [
-            jnp.stack(
-                [
-                    jnp.sum(d_mixed.astype(F32), axis=0), att_vec[0], att_vec[1], att_vec[2],
-                    att_vec[3], att_vec[4], grad_output_bias, grad_attn_gain, grad_attn_shift,
-                    grad_outer_bias, grad_ffn_gain, grad_ffn_shift,
-                ]
-            ),
-            jnp.transpose(grad_inner_bias.reshape(sh.parts, -1, dn), (1, 0, 2)).reshape(-1, D),
-        ],
-        axis=0,
-    ).astype(BF)
-    smalls = jnp.pad(smalls, ((0, 256 - nsmall), (0, 0)))
-    whole = jnp.concatenate([gk, gv, gp, jnp.transpose(smalls)], axis=1)
-    half = whole.shape[1] // 2
+    smalls = jnp.concatenate([att_vec, vec_a, vec_b], axis=0).astype(BF)
+    smalls = jnp.transpose(jnp.pad(smalls, ((0, 128 - smalls.shape[0]), (0, 0))))
+    sides = [[gkv[:, :D], gp[:, : D // 2], smalls], [gkv[:, D:], gp[:, D // 2 :], jnp.zeros_like(smalls)]]
+    low, high = (jnp.concatenate([b.astype(BF) for b in a[1:]], axis=1) for a in sides)
     if sh.pair:
-        whole = sh.halve_cols(whole[:, :half], whole[:, half:])
+        kv_half = sh.halve_cols(sides[0][0], sides[1][0])
+        rest = sh.halve_cols(low, high)
+        whole = jnp.concatenate([kv_half, rest], axis=1)
+        half = whole.shape[1]
         whole = whole.reshape(2, dn, half)
         keep = lax.dynamic_index_in_dim(whole, sh.f, 0, keepdims=False)
         send = lax.dynamic_index_in_dim(whole, 1 - sh.f, 0, keepdims=False)
-        whole = (keep.astype(F32) + sh.trade(send).astype(F32)).astype(BF)
+        got_x = sh.trade(send)
         go = tn(
-            jnp.concatenate([sh.own(mixed_low, 1), got[:, :dn]], axis=0),
-            jnp.concatenate([d_attn, got[:, 2 * dn :]], axis=0),
+            jnp.concatenate([sh.own(mixed_low, 1), sh.own(mixed_got, 1)], axis=0),
+            jnp.concatenate([d_attn, d_attn_got], axis=0),
         ).astype(BF)
         gq = tn(
-            jnp.concatenate([sh.own(hidden, 1), got[:, dn : 2 * dn]], axis=0),
+            jnp.concatenate([sh.own(hidden, 1), sh.own(hidden_got, 1)], axis=0),
             jnp.concatenate([dq, dq_got], axis=0),
         ).astype(BF)
+        dkv, _ = lax.optimization_barrier((dkv, rest))
     else:
-        whole, go, gq = (
+        low, high = (jnp.concatenate([a[0].astype(BF), b], axis=1) for a, b in zip(sides, (low, high)))
+        half = low.shape[1]
+        low, high, go, gq = (
             lax.psum_scatter(a, "fsdp", scatter_dimension=0, tiled=True)
-            for a in (whole, tn(mixed_low, d_attn).astype(BF), tn(hidden, dq).astype(BF))
+            for a in (low, high, tn(mixed_low, d_attn).astype(BF), tn(hidden, dq).astype(BF))
         )
-        whole = sh.halve_cols(whole[:, :half], whole[:, half:])
-
-    d_hid = (tn(dk, jnp.transpose(k_full)) + tn(dv, jnp.transpose(v_full))).astype(BF)
+        whole = sh.halve_cols(low, high)
+    mine = sh.halve_cols(go, gq)
+
+    d_hid = (tn(dkv[:D], jnp.transpose(k_full)) + tn(dkv[D:], jnp.transpose(v_full))).astype(BF)
     d_hid = jnp.pad(d_hid, (((C - 1 - R) * T, (C - 1) * T + L - (C - 1 - R) * T - W), (0, 0)))
     d_hid = lax.dynamic_slice_in_dim(d_hid, (C - 1 - ctx) * T, L, 0)
-    d_hid = sh.spread(d_hid.reshape(C, T, D))
-    for k in range(sh.bits):
-        d_hid = sh.halve(d_hid, k, d_hid.ndim - 3)
-    input_grad = d_res1 + nt(dq, q_full) + d_hid.astype(F32)
-
-    grads = jnp.concatenate([whole, sh.halve_cols(go, gq)], axis=1)
+    d_hid = sh.halve(sh.spread(d_hid.reshape(C, T, D)), 0, sh.bits - 1)
+    if sh.pair:
+        got_x, d_hid, mine, ffn = lax.optimization_barrier((got_x, d_hid, mine, ffn))
+        ffn = lax.all_gather(ffn, "ctx", axis=0, tiled=False)
+        whole = (keep.astype(F32) + got_x.astype(F32)).astype(BF)
+
+    grads = jnp.concatenate([whole, mine], axis=1)
     grads = grads.reshape((2,) * (sh.bits - 1) + (-1, grads.shape[1]))
-    for k in range(1, sh.bits):
+    for k, other in zip(range(1, sh.bits), list(range(2, sh.bits)) + [1]):
         grads = sh.halve(grads, k, grads.ndim - 3)
+        d_hid = sh.halve(d_hid, other, d_hid.ndim - 3 - (1 if other > 1 else 0))
+        grads, d_hid = lax.optimization_barrier((grads, d_hid))
     for k in reversed(range(1, sh.bits)):
         grads = sh.double(grads, k, grads.ndim - 2)
+        if sh.pair and k == 2:
+            gi, gu = ffn_final(ffn, inner_bias.shape[0] * 2, D)
+            gi, gu, grads = lax.optimization_barrier((gi, gu, grads))
+    input_grad = d_res1 + nt(dq, q_full) + d_hid.astype(F32)
+    if not sh.pair:
+        gi, gu = (a.astype(F32) for a in ffn)
     grads = grads.reshape(dn, -1)
     low, high = sh.order(grads, sh.flip(grads, 0), sh.bit(0))
-    whole = jnp.concatenate([low[:, :half], high[:, :half]], axis=1).astype(F32)
-    gk, gv, gp = (whole[:, i * D : (i + 1) * D] for i in range(3))
+    gk, gv = low[:, :D].astype(F32), high[:, :D].astype(F32)
+    gp = jnp.concatenate([a[:, D : D + D // 2] for a in (low, high)], axis=1).astype(F32)
     go, gq = low[:, half:].astype(F32), high[:, half:].astype(F32)
-    smalls = jnp.transpose(whole[:, 3 * D : 3 * D + 128])[:nsmall]
-    s = [smalls[i] for i in range(12)]
+    s = jnp.transpose(low[:, D + D // 2 : half].astype(F32))
     return (
         outcome.astype(BF)[None],
         input_grad[None],
         gq,
         gk,
         gv,
+        s[19],
         s[0],
         s[1],
         s[2],
-        s[3],
-        smalls[4:6],
+        s[3:5],
         gp,
         go,
-        s[6],
-        s[7],
+        s[18],
+        s[16],
+        s[17],
+        gi,
+        s[20:24].reshape(-1),
+        gu,
+        s[10],
         s[8],
-        gi.astype(F32),
-        smalls[12:].reshape(-1),
-        gu.astype(F32),
         s[9],
-        s[10],
-        s[11],
     )
 
 

time: 464 us -> 401 us (0.86)
  waiting for transfers between devices: 207 us -> 160 us
  Pallas kernels: 36.4 us -> 72.1 us
  other arithmetic: 51.3 us -> 32.3 us
  matrix products: 60.5 us -> 42.8 us
  local copies, waits for them, and re-layouts: 45.7 us -> 28.3 us
    psum x1 -> x0, waiting for transfers between devices: 55.7 us -> none  [per_device(): gi, gu = lax.psum((gi, gu), 'ctx')]
    pallas_call x2 -> x6, Pallas kernels: 36.4 us -> 72.1 us  [the longest x1 19.4 us: att_fwd(): pl.pallas_call(att_fwd_kernel, grid=(D // 128,), in_specs=[col(T), col(16...]
    reduce_scatter x0 -> x1, waiting for transfers between devices: none -> 21.3 us  [per_device(): ffn = lax.psum_scatter(ffn, 'ctx', scatter_dimension=0, tiled=False)]
    ppermute x10 -> x12, waiting for transfers between devices: 50.1 us -> 30.4 us  [trade(): return lax.ppermute(a, 'fsdp', self.swap)]
    dot_general x4 -> x1, matrix products: 10.8 us -> 0.53 us  [nt(): lax.dot_general(a, b, (((1,), (1,)), ((), ())), preferred_element_type=F32)]
    select_n x11 -> x4, other arithmetic: 12.4 us -> 2.2 us  [order(): return (jnp.where(at == 0, mine, other), jnp.where(at == 0, other, mine))]
    convert_element_type x8 -> x7, other arithmetic: 14.1 us -> 5.32 us  [the longest x1 1.61 us: per_device(): gk, gv = (low[:, :D].astype(F32), high[:, :D].astype(F32))]
    ppermute x18 -> x27, waiting for transfers between devices: 91.3 us -> 98.6 us  [flip(): return lax.ppermute(a, 'ctx', [(i, i ^ 1 << k) for i in range(self.count)])]
  transfers between devices with their start and end apart: 33 -> 45, of which waited for: 17 -> 19; matrix products, arithmetic and copies ran while one was open for 24% -> 19% of each run, Pallas kernels for 8% -> 8%
where the time goes in v3:
time: 401 us; the launch traced here: 396 us
  waiting for transfers between devices  160 us (40%)
  Pallas kernels  72.1 us (18%)
  starting transfers between devices  45.1 us (11%)
  matrix products  42.8 us (11%)
  other arithmetic  32.3 us (8%)
  local copies, waits for them, and re-layouts  28.3 us (7%)
  between operations  15.3 us (4%)
    ppermute x27, waiting for transfers between devices, flip(): return lax.ppermute(a, 'ctx', [(i, i ^ 1 << k) for i in range(self.count)])  98.6 us
    ppermute x12, waiting for transfers between devices, trade(): return lax.ppermute(a, 'fsdp', self.swap)  30.4 us
    reduce_scatter x1, waiting for transfers between devices, per_device(): ffn = lax.psum_scatter(ffn, 'ctx', scatter_dimension=0, tiled=False)  21.3 us
    pallas_call x1, Pallas kernels, att_fwd(): pl.pallas_call(att_fwd_kernel, grid=(D // 128,), in_specs=[col(T), col(16...  19.4 us
    ppermute x27, starting transfers between devices, flip(): return lax.ppermute(a, 'ctx', [(i, i ^ 1 << k) for i in range(self.count)])  17 us
    pallas_call x1, Pallas kernels, ffn_bwd(): pl.pallas_call(kernel, grid_spec=pltpu.PrefetchScalarGridSpec(num_scalar_...  16.8 us
    pallas_call x1, Pallas kernels, att_bwd(): pl.pallas_call(att_bwd_kernel, grid=(D // 128,), in_specs=[col(T), col(16...  16.7 us
    dot_general x2, matrix products, per_device(): lax.dot_general(a, b, (((0,), (1,)), ((), ())), preferred_element_type=F32)  15.8 us
  transfers between devices with their start and end apart: 45, of which 19 were waited for; matrix products, arithmetic and copies ran while one was open for 19% of the time, Pallas kernels for 8%

profile of v3, /device:TPU:0, one launch (start us, length us, event | category | flops | bytes accessed | tf_op | source)
XLA Modules:
  0.0 395.5 jit_solution(16452054323751286278)
XLA Ops:
  7.3 1.5 pack_rows.1
  8.8 2.9 collective-permute-start.3
  14.1 1.6 collective-permute-start.4
  15.7 1.9 broadcast_select_fusion.3
  19.9 3.0 subtract_convert_fusion
  25.0 5.3 %collective-permute-start.5 = (bf16[2,128,896]{2,1,0:T(8,128)(2,1)S(1)}, bf16[2,128,896]{2,1,0:T(8,128)(2,1)}, u32[]{:S(2)}, u32[]{:S(2)}) collective-permute-start(bf16[2,128,896]{2,1,0:T(8,128)(2,1)S(1)} %get-tuple-element.214), channel_id=1, source_target_pairs={{0,8},{2,10},{4,12},{6,14},{8,16},{10,18},{12,20},{14,22},{16,24},... | collective-permute-start | bytes 1376264 | tf_op jit(solution)/shard_map/ppermute | solution.py:581
  31.2 1.6 collective-permute-start.1
  32.8 4.4 %collective-permute-done.7 = bf16[2,128,896]{2,1,0:T(8,128)(2,1)} collective-permute-done((bf16[2,128,896]{2,1,0:T(8,128)(2,1)S(1)}, bf16[2,128,896]{2,1,0:T(8,128)(2,1)}, u32[]{:S(2)}, u32[]{:S(2)}) %collective-permute-start.7) | collective-permute-done | bytes 458784 | tf_op jit(solution)/shard_map/ppermute | solution.py:582
  38.5 4.6 %collective-permute-start.6 = (bf16[2,128,896]{2,1,0:T(8,128)(2,1)}, bf16[2,128,896]{2,1,0:T(8,128)(2,1)S(1)}, u32[]{:S(2)}, u32[]{:S(2)}) collective-permute-start(bf16[2,128,896]{2,1,0:T(8,128)(2,1)} %collective-permute-done.5), channel_id=1, source_target_pairs={{0,8},{2,10},{4,12},{6,14},{8,16},{10,18},{12,20},{14,22},{16,24},... | collective-permute-start | bytes 1376264 | tf_op jit(solution)/shard_map/ppermute | solution.py:581
  43.1 1.6 collective-permute-start.2
  46.1 3.6 collective-permute-done.8
  51.2 2.3 collective-permute-done.2.refs_1_
  53.6 1.6 collective-permute-start.15
  61.6 4.5 %convolution_convert_fusion.t_ref = bf16[2304,768]{1,0:T(8,128)(2,1)} fusion(bf16[2304,384]{1,0:T(8,128)(2,1)S(1)} %bitcast.184, bf16[2304,384]{1,0:T(8,128)(2,1)S(1)} %bitcast.181, bf16[384,768]{1,0:T(8,128)(2,1)S(1)} %get-tuple-element.188, bf16[384,768]{1,0:T(8,128)(2,1)S(1)} %get-tuple-element.187), kind=kOutput, calls=%fused_computation.3 | convolution fusion | flops 2729115648 | bytes 8257536 | tf_op jit(solution)/shard_map/dot_general | solution.py:22
  66.1 3.8 collective-permute-done.15.refs_4_
  74.9 4.1 %add_convert_fusion.1.v_ref = bf16[2176,768]{1,0:T(8,128)(2,1)} fusion(bf16[2176,768]{1,0:T(8,128)(2,1)S(1)} %bitcast.174, f32[768]{0:T(1024)S(1)} %fusion.47, bf16[384,768]{1,0:T(8,128)(2,1)S(1)} %get-tuple-element.205, bf16[384,768]{1,0:T(8,128)(2,1)S(1)} %get-tuple-element.206), kind=kOutput, calls=%fused_computation.1 | convolution fusion | flops 2572615680 | bytes 7867392 | tf_op jit(solution)/shard_map/dot_general | solution.py:22
  79.1 4.2 %convolution_convert_fusion.1.k_ref = bf16[2176,768]{1,0:T(8,128)(2,1)} fusion(bf16[2176,768]{1,0:T(8,128)(2,1)S(1)} %bitcast.175, bf16[384,768]{1,0:T(8,128)(2,1)S(1)} %get-tuple-element.192, bf16[384,768]{1,0:T(8,128)(2,1)S(1)} %get-tuple-element.191), kind=kOutput, calls=%fused_computation.4 | convolution fusion | flops 2570944512 | bytes 7864320 | tf_op jit(solution)/shard_map/dot_general | solution.py:22
  84.1 1.5 collective-permute-start.17
  86.3 19.4 %att_fwd.1 = (f32[128,768]{1,0:T(8,128)}, bf16[12,128,2176]{2,1,0:T(8,128)(2,1)}) custom-call(f32[128,768]{1,0:T(8,128)} %convolution_bitcast_fusion.q_ref, f32[16,768]{1,0:T(8,128)} %pad_maximum_fusion.26.rows_ref.v_ref, f32[128,128]{1,0:T(8,128)} %and_select_fusion.pen_ref, f32[128,128]{1,0:T(8,128)} %broadcast_in_dim.82.kind_ref, ...), custom_call_target="tpu_custom_call" | custom-call | flops 13690208256 | bytes 16711680 | tf_op jit(solution)/shard_map/att_fwd/pallas_call | solution.py:137
  116.4 11.1 %ffn_fwd.1 = (bf16[128,768]{1,0:T(8,128)(2,1)S(1)}, bf16[128,3072]{1,0:T(8,128)(2,1)S(1)}, f32[128,3072]{1,0:T(8,128)S(1)}, bf16[128,768]{1,0:T(8,128)(2,1)}, f3...) custom-call(s32[3]{0:T(128)S(1)} %pad_add_fusion.s_ref, ...), custom_call_target="tpu_custom_call" | custom-call | flops 1207959552 | bytes 9437184 | tf_op jit(solution)/shard_map/ffn_fwd/pallas_call | solution.py:396
  130.9 4.2 %collective-permute-done.23.dog_ref = bf16[128,768]{1,0:T(8,128)(2,1)S(1)} collective-permute-done((bf16[128,768]{1,0:T(8,128)(2,1)S(1)}, bf16[128,768]{1,0:T(8,128)(2,1)S(1)}, u32[]{:S(2)}, u32[]{:S(2)}) %collective-permute-start.23) | collective-permute-done | bytes 196640 | tf_op jit(solution)/shard_map/ppermute | solution.py:548
  135.1 16.8 %ffn_bwd.1 = (bf16[16,384,384]{2,1,0:T(8,128)(2,1)}, f32[128,768]{1,0:T(8,128)S(1)}, bf16[128,768]{1,0:T(8,128)(2,1)S(1)}, bf16[128,768]{1,0:T(8,128)(2,1)S(1)}, f32[8,768]{1,0:T(8,128)S(1)}) custom-call(s32[3]{0:T(128)S(1)} %pad_add_fusion.s_ref, f32[128,3072]{1,0:T(8,128)} %copy-done.12, bf16[128,3072]{1,0:T(8,128)(2,1)S(1)} %get-tuple-element.93.act_ref, ...), custom_call_target="tpu_custom_call" | custom-call | flops 4227858432 | bytes 14155776 | tf_op jit(solution)/shard_map/ffn_bwd/pallas_call | solution.py:489
  152.6 16.7 %att_bwd.1 = (bf16[128,768]{1,0:T(8,128)(2,1)}, f32[8,768]{1,0:T(8,128)}, bf16[2,768,2176]{2,1,0:T(8,128)(2,1)}, bf16[768,2304]{1,0:T(8,128)(2,1)}) custom-call(f32[128,768]{1,0:T(8,128)} %convolution_bitcast_fusion.q_ref, f32[16,768]{1,0:T(8,128)} %pad_maximum_fusion.26.rows_ref.v_ref, f32[128,128]{1,0:T(8,128)} %broadcast_in_dim.82.kind_ref, ...), custom_call_target="tpu_custom_call" | custom-call | flops 13690208256 | bytes 26738688 | tf_op jit(solution)/shard_map/att_bwd/pallas_call | solution.py:162
  169.3 6.6 %fusion.8 = bf16[768,768]{1,0:T(8,128)(2,1)} fusion(bf16[768,2304]{1,0:T(8,128)(2,1)} %get-tuple-element.105, bf16[2304,384]{1,0:T(8,128)(2,1)} %bitcast.183, bf16[2304,384]{1,0:T(8,128)(2,1)S(1)} %bitcast.182), kind=kOutput, calls=%fused_computation.34 | convolution fusion | flops 2725576704 | bytes 8257536 | tf_op jit(solution)/shard_map/dot_general | solution.py:779
  176.8 1.5 collective-permute-start.31
  180.3 9.3 %fusion.61 = f32[768,1536]{1,0:T(8,128)S(1)} fusion(bf16[2176,768]{1,0:T(8,128)(2,1)S(1)} %bitcast.176, bf16[1536,2176]{1,0:T(8,128)(2,1)} %bitcast.192), kind=kOutput, calls=%fused_computation.205 | convolution fusion | flops 5133828096 | bytes 14745600 | tf_op jit(solution)/shard_map/dot_general | solution.py:779
  191.3 5.6 %fusion = f32[2176,768]{1,0:T(8,128)} fusion(bf16[1536,2176]{1,0:T(8,128)(2,1)S(1)} %bitcast.195, bf16[384,768]{1,0:T(8,128)(2,1)S(1)} %copy-done.32, bf16[384,768]{1,0:T(8,128)(2,1)S(1)} %copy-done.34), kind=kOutput, calls=%fused_computation.8 | convolution fusion | flops 2569273344 | bytes 11206656 | tf_op jit(solution)/shard_map/dot_general | solution.py:26
  196.9 6.0 %add_convert_fusion = bf16[2176,768]{1,0:T(8,128)(2,1)S(1)} fusion(f32[2176,768]{1,0:T(8,128)} %fusion, bf16[1536,2176]{1,0:T(8,128)(2,1)S(1)} %bitcast.196, bf16[384,768]{1,0:T(8,128)(2,1)S(1)} %copy-done.38, bf16[384,768]{1,0:T(8,128)(2,1)S(1)} %copy-done.36), kind=kOutput, calls=%fused_computation | convolution fusion | flops 2572615680 | bytes 14548992 | tf_op jit(solution)/shard_map/dot_general | solution.py:26
  202.9 2.2 pad_dynamic-slice_fusion
  210.0 1.6 fusion.3
  211.5 20.1 %collective-permute-done.28 = bf16[384,1280]{1,0:T(8,128)(2,1)} collective-permute-done((bf16[384,1280]{1,0:T(8,128)(2,1)S(1)}, bf16[384,1280]{1,0:T(8,128)(2,1)}, u32[]{:S(2)}, u32[]{:S(2)}) %collective-permute-start.28) | collective-permute-done | bytes 983072 | tf_op jit(solution)/shard_map/ppermute | solution.py:548
  231.6 21.3 %reduce-scatter.2.cloned.1.call-done = bf16[1,384,384]{2,1,0:T(8,128)(2,1)} async-done(((bf16[16,384,384]{2,1,0:T(8,128)(2,1)}), bf16[1,384,384]{2,1,0:T(8,128)(2,1)}) %reduce-scatter.2.cloned.1.call-update) | async-done | bytes 294928 | tf_op jit(solution)/shard_map/reduce_scatter | solution.py:769
  253.0 2.1 dynamic-slice_bitcast_fusion.1
  261.0 22.1 %collective-permute-done.34 = bf16[2,2,128,768]{3,2,1,0:T(8,128)(2,1)} collective-permute-done((bf16[2,2,128,768]{3,2,1,0:T(8,128)(2,1)}, bf16[2,2,128,768]{3,2,1,0:T(8,128)(2,1)}, u32[]{:S(2)}, u32[]{:S(2)}) %collective-permute-start.34) | collective-permute-done | bytes 786464 | tf_op jit(solution)/shard_map/ppermute | solution.py:545
  284.5 1.8 fusion.7
  289.1 30.0 %collective-permute-done.36 = bf16[2,128,768]{2,1,0:T(8,128)(2,1)S(1)} collective-permute-done((bf16[2,128,768]{2,1,0:T(8,128)(2,1)S(1)}, bf16[2,128,768]{2,1,0:T(8,128)(2,1)S(1)}, u32[]{:S(2)}, u32[]{:S(2)}) %collective-permute-start.36) | collective-permute-done | bytes 393248 | tf_op jit(solution)/shard_map/ppermute | solution.py:545
  319.1 2.2 collective-permute-done.35
  321.5 2.8 collective-permute-start.38
  324.8 3.1 collective-permute-done.38
  328.0 7.1 %collective-permute-done.37 = bf16[48,2048]{1,0:T(8,128)(2,1)S(1)} collective-permute-done((bf16[48,2048]{1,0:T(8,128)(2,1)S(1)}, bf16[48,2048]{1,0:T(8,128)(2,1)S(1)}, u32[]{:S(2)}, u32[]{:S(2)}) %collective-permute-start.37) | collective-permute-done | bytes 196640 | tf_op jit(solution)/shard_map/ppermute | solution.py:545
  335.2 6.7 %collective-permute-done.39 = bf16[48,2048]{1,0:T(8,128)(2,1)S(1)} collective-permute-done((bf16[48,2048]{1,0:T(8,128)(2,1)S(1)}, bf16[48,2048]{1,0:T(8,128)(2,1)S(1)}, u32[]{:S(2)}, u32[]{:S(2)}) %collective-permute-start.39) | collective-permute-done | bytes 196640 | tf_op jit(solution)/shard_map/ppermute | solution.py:545
  342.0 7.9 %collective-permute-done.40 = bf16[2,48,2048]{2,1,0:T(8,128)(2,1)S(1)} collective-permute-done((bf16[2,48,2048]{2,1,0:T(8,128)(2,1)S(1)}, bf16[2,48,2048]{2,1,0:T(8,128)(2,1)S(1)}, u32[]{:S(2)}, u32[]{:S(2)}) %collective-permute-start.40) | collective-permute-done | bytes 393248 | tf_op jit(solution)/shard_map/ppermute | solution.py:545
  350.1 6.6 %ffn_final.1 = (f32[384,3072]{1,0:T(8,128)}, f32[1536,768]{1,0:T(8,128)}) custom-call(bf16[16,384,384]{2,1,0:T(8,128)(2,1)} %bitcast.173), custom_call_target="tpu_custom_call" | custom-call | bytes 14155776 | tf_op jit(solution)/shard_map/ffn_final/pallas_call | solution.py:223
  356.7 3.8 collective-permute-start.41
  360.5 16.2 %collective-permute-done.41 = bf16[2,2,48,2048]{3,2,1,0:T(8,128)(2,1)S(1)} collective-permute-done((bf16[2,2,48,2048]{3,2,1,0:T(8,128)(2,1)S(1)}, bf16[2,2,48,2048]{3,2,1,0:T(8,128)(2,1)S(1)}, u32[]{:S(2)}, u32[]{:S(2)}) %collective-permute-start.41) | collective-permute-done | bytes 786464 | tf_op jit(solution)/shard_map/ppermute | solution.py:545
  380.8 1.7 slice_reduce_fusion
  382.7 1.6 slice_convert_fusion
  384.4 1.6 slice_convert_fusion.1
  (262 shorter events, 66.8 us)
Async XLA Ops:
  7.2 245.8 %reduce-scatter.2.cloned.1.call-start = ((), (), s32[]{:S(2)}) async-start(), calls=%async_computation.1 | async-start | bytes 5013504 | tf_op jit(solution)/shard_map/reduce_scatter | solution.py:769
  8.8 22.4 %collective-permute-start.3 = (f32[16,384]{1,0:T(8,128)}, f32[16,384]{1,0:T(8,128)S(1)}, u32[]{:S(2)}, u32[]{:S(2)}) collective-permute-start(f32[16,384]{1,0:T(8,128)} %pack_rows.1), channel_id=1, source_target_pairs={{0,1},{1,0},{2,3},{3,2},{4,5},{5,4},{6,7},{7,6},{8,9},{9,8},{10,11... | collective-permute-start | bytes 73736 | tf_op jit(solution)/shard_map/ppermute | solution.py:548
  14.1 9.4 %collective-permute-start.4 = (bf16[128,896]{1,0:T(8,128)(2,1)S(1)}, bf16[128,896]{1,0:T(8,128)(2,1)S(1)}, u32[]{:S(2)}, u32[]{:S(2)}) collective-permute-start(bf16[128,896]{1,0:T(8,128)(2,1)S(1)} %pad_maximum_fusion.25), channel_id=1, source_target_pairs={{0,4},{2,6},{4,0},{6,2},{8,12},{10,14},{12,8},{14,10},{16,20},{18,... | collective-permute-start | bytes 688136 | tf_op jit(solution)/shard_map/ppermute | solution.py:545
  17.7 35.8 %collective-permute-start = (bf16[384,768]{1,0:T(8,128)(2,1)}, bf16[384,768]{1,0:T(8,128)(2,1)}, u32[]{:S(2)}, u32[]{:S(2)}) collective-permute-start(bf16[384,768]{1,0:T(8,128)(2,1)} %broadcast_select_fusion.3), channel_id=1, source_target_pairs={{0,1},{1,0},{2,3},{3,2},{4,5},{5,4},{6,7},{7,6},{8,9},{9,8},{10,11... | collective-permute-start | bytes 1769480 | tf_op jit(solution)/shard_map/ppermute | solution.py:548
  23.7 13.4 %collective-permute-start.7 = (bf16[2,128,896]{2,1,0:T(8,128)(2,1)S(1)}, bf16[2,128,896]{2,1,0:T(8,128)(2,1)}, u32[]{:S(2)}, u32[]{:S(2)}) collective-permute-start(bf16[2,128,896]{2,1,0:T(8,128)(2,1)S(1)} %get-tuple-element.214), channel_id=1, source_target_pairs={{8,0},{10,2},{12,4},{14,6},{16,8},{18,10},{20,12},{22,14},{24,16},... | collective-permute-start | bytes 1376264 | tf_op jit(solution)/shard_map/ppermute | solution.py:582
  25.0 13.4 %collective-permute-start.5 = (bf16[2,128,896]{2,1,0:T(8,128)(2,1)S(1)}, bf16[2,128,896]{2,1,0:T(8,128)(2,1)}, u32[]{:S(2)}, u32[]{:S(2)}) collective-permute-start(bf16[2,128,896]{2,1,0:T(8,128)(2,1)S(1)} %get-tuple-element.214), channel_id=1, source_target_pairs={{0,8},{2,10},{4,12},{6,14},{8,16},{10,18},{12,20},{14,22},{16,24},... | collective-permute-start | bytes 1376264 | tf_op jit(solution)/shard_map/ppermute | solution.py:581
  31.1 11.9 %collective-permute-start.12 = (bf16[1,2,128,896]{3,2,1,0:T(8,128)(2,1)S(1)}, bf16[1,2,128,896]{3,2,1,0:T(8,128)(2,1)S(1)}, u32[]{:S(2)}, u32[]{:S(2)}) collective-permute-start(bf16[1,2,128,896]{3,2,1,0:T(8,128)(2,1)S(1)} %get-tuple-element.213), channel_id=1, source_target_pairs={{0,2},{2,0},{4,6},{6,4},{8,10},{10,8},{12,14},{14,12},{16,18},{18,... | collective-permute-start | bytes 1376264 | tf_op jit(solution)/shard_map/ppermute | solution.py:545
  31.2 22.3 %collective-permute-start.1 = (bf16[384,768]{1,0:T(8,128)(2,1)}, bf16[384,768]{1,0:T(8,128)(2,1)S(1)}, u32[]{:S(2)}, u32[]{:S(2)}) collective-permute-start(bf16[384,768]{1,0:T(8,128)(2,1)} %broadcast_select_fusion.2), channel_id=1, source_target_pairs={{0,1},{1,0},{2,3},{3,2},{4,5},{5,4},{6,7},{7,6},{8,9},{9,8},{10,11... | collective-permute-start | bytes 1769480 | tf_op jit(solution)/shard_map/ppermute | solution.py:548
  37.2 12.6 %collective-permute-start.8 = (bf16[2,128,896]{2,1,0:T(8,128)(2,1)}, bf16[2,128,896]{2,1,0:T(8,128)(2,1)S(1)}, u32[]{:S(2)}, u32[]{:S(2)}) collective-permute-start(bf16[2,128,896]{2,1,0:T(8,128)(2,1)} %collective-permute-done.7), channel_id=1, source_target_pairs={{8,0},{10,2},{12,4},{14,6},{16,8},{18,10},{20,12},{22,14},{24,16},... | collective-permute-start | bytes 1376264 | tf_op jit(solution)/shard_map/ppermute | solution.py:582
  38.5 12.6 %collective-permute-start.6 = (bf16[2,128,896]{2,1,0:T(8,128)(2,1)}, bf16[2,128,896]{2,1,0:T(8,128)(2,1)S(1)}, u32[]{:S(2)}, u32[]{:S(2)}) collective-permute-start(bf16[2,128,896]{2,1,0:T(8,128)(2,1)} %collective-permute-done.5), channel_id=1, source_target_pairs={{0,8},{2,10},{4,12},{6,14},{8,16},{10,18},{12,20},{14,22},{16,24},... | collective-permute-start | bytes 1376264 | tf_op jit(solution)/shard_map/ppermute | solution.py:581
  43.1 10.4 %collective-permute-start.2 = (bf16[192,768]{1,0:T(8,128)(2,1)}, bf16[192,768]{1,0:T(8,128)(2,1)S(1)}, u32[]{:S(2)}, u32[]{:S(2)}) collective-permute-start(bf16[192,768]{1,0:T(8,128)(2,1)} %constant_dynamic-slice_fusion.10), channel_id=1, source_target_pairs={{0,1},{1,0},{2,3},{3,2},{4,5},{5,4},{6,7},{7,6},{8,9},{9,8},{10,11... | collective-permute-start | bytes 884744 | tf_op jit(solution)/shard_map/ppermute | solution.py:548
  49.8 7.8 %collective-permute-start.11 = (bf16[2,2,128,896]{3,2,1,0:T(8,128)(2,1)S(1)}, bf16[2,2,128,896]{3,2,1,0:T(8,128)(2,1)S(1)}, u32[]{:S(2)}, u32[]{:S(2)}) collective-permute-start(bf16[2,2,128,896]{3,2,1,0:T(8,128)(2,1)S(1)} %pad_maximum_fusion.14), channel_id=1, source_target_pairs={{0,2},{2,0},{4,6},{6,4},{8,10},{10,8},{12,14},{14,12},{16,18},{18,... | collective-permute-start | bytes 2752520 | tf_op jit(solution)/shard_map/ppermute | solution.py:545
  51.1 20.9 %collective-permute-start.10 = (bf16[2,2,128,896]{3,2,1,0:T(8,128)(2,1)S(1)}, bf16[2,2,128,896]{3,2,1,0:T(8,128)(2,1)S(1)}, u32[]{:S(2)}, u32[]{:S(2)}) collective-permute-start(bf16[2,2,128,896]{3,2,1,0:T(8,128)(2,1)S(1)} %pad_maximum_fusion.13), channel_id=1, source_target_pairs={{0,2},{2,0},{4,6},{6,4},{8,10},{10,8},{12,14},{14,12},{16,18},{18,... | collective-permute-start | bytes 2752520 | tf_op jit(solution)/shard_map/ppermute | solution.py:545
  53.6 16.3 %collective-permute-start.15 = (bf16[96,3072]{1,0:T(8,128)(2,1)S(1)}, bf16[96,3072]{1,0:T(8,128)(2,1)S(1)}, u32[]{:S(2)}, u32[]{:S(2)}) collective-permute-start(bf16[96,3072]{1,0:T(8,128)(2,1)S(1)} %constant_dynamic-slice_fusion.8), channel_id=1, source_target_pairs={{0,1},{1,0},{2,3},{3,2},{4,5},{5,4},{6,7},{7,6},{8,9},{9,8},{10,11... | collective-permute-start | bytes 1769480 | tf_op jit(solution)/shard_map/ppermute | solution.py:548
  56.3 27.0 %collective-permute-start.13 = (bf16[384,768]{1,0:T(8,128)(2,1)S(1)}, bf16[384,768]{1,0:T(8,128)(2,1)}, u32[]{:S(2)}, u32[]{:S(2)}) collective-permute-start(bf16[384,768]{1,0:T(8,128)(2,1)S(1)} %constant_dynamic-slice_fusion.9), channel_id=1, source_target_pairs={{0,1},{1,0},{2,3},{3,2},{4,5},{5,4},{6,7},{7,6},{8,9},{9,8},{10,11... | collective-permute-start | bytes 1769480 | tf_op jit(solution)/shard_map/ppermute | solution.py:548
  56.9 2.6 collective-permute-start.14
  57.5 12.6 %collective-permute-start.9 = (bf16[384,768]{1,0:T(8,128)(2,1)S(1)}, bf16[384,768]{1,0:T(8,128)(2,1)S(1)}, u32[]{:S(2)}, u32[]{:S(2)}) collective-permute-start(bf16[384,768]{1,0:T(8,128)(2,1)S(1)} %collective-permute-done.1), channel_id=1, source_target_pairs={{0,2},{2,0},{4,6},{6,4},{8,10},{10,8},{12,14},{14,12},{16,18},{18,... | collective-permute-start | bytes 1769480 | tf_op jit(solution)/shard_map/ppermute | solution.py:545
  69.9 13.4 %collective-permute-start.16 = (bf16[96,3072]{1,0:T(8,128)(2,1)S(1)}, bf16[96,3072]{1,0:T(8,128)(2,1)S(1)}, u32[]{:S(2)}, u32[]{:S(2)}) collective-permute-start(bf16[96,3072]{1,0:T(8,128)(2,1)S(1)} %collective-permute-done.15.refs_4_), channel_id=1, source_target_pairs={{0,4},{2,6},{4,0},{6,2},{8,12},{10,14},{12,8},{14,10},{16,20},{18,... | collective-permute-start | bytes 1769480 | tf_op jit(solution)/shard_map/ppermute | solution.py:545
  84.1 21.7 %collective-permute-start.17 = (bf16[384,768]{1,0:T(8,128)(2,1)}, bf16[384,768]{1,0:T(8,128)(2,1)}, u32[]{:S(2)}, u32[]{:S(2)}) collective-permute-start(bf16[384,768]{1,0:T(8,128)(2,1)} %collective-permute-done.13.refs_9_), channel_id=1, source_target_pairs={{0,4},{2,6},{4,0},{6,2},{8,12},{10,14},{12,8},{14,10},{16,20},{18,... | collective-permute-start | bytes 1769480 | tf_op jit(solution)/shard_map/ppermute | solution.py:545
  86.3 26.0 %copy-start.10 = (f32[16,768]{1,0:T(8,128)S(1)}, f32[16,768]{1,0:T(8,128)}, u32[]{:S(2)}) copy-start(f32[16,768]{1,0:T(8,128)} %pad_maximum_fusion.26.rows_ref.v_ref) | copy-start | bytes 147460
  105.8 6.0 %collective-permute-start.19 = (bf16[96,3072]{1,0:T(8,128)(2,1)}, bf16[96,3072]{1,0:T(8,128)(2,1)}, u32[]{:S(2)}, u32[]{:S(2)}) collective-permute-start(bf16[96,3072]{1,0:T(8,128)(2,1)} %copy-done.4), channel_id=1, source_target_pairs={{0,2},{2,0},{4,6},{6,4},{8,10},{10,8},{12,14},{14,12},{16,18},{18,... | collective-permute-start | bytes 1769480 | tf_op jit(solution)/shard_map/ppermute | solution.py:545
  105.8 6.5 %collective-permute-start.20 = (bf16[96,3072]{1,0:T(8,128)(2,1)}, bf16[96,3072]{1,0:T(8,128)(2,1)}, u32[]{:S(2)}, u32[]{:S(2)}) collective-permute-start(bf16[96,3072]{1,0:T(8,128)(2,1)} %copy-done.7), channel_id=1, source_target_pairs={{0,2},{2,0},{4,6},{6,4},{8,10},{10,8},{12,14},{14,12},{16,18},{18,... | collective-permute-start | bytes 1769480 | tf_op jit(solution)/shard_map/ppermute | solution.py:545
  106.3 6.0 %collective-permute-start.21 = (bf16[384,768]{1,0:T(8,128)(2,1)}, bf16[384,768]{1,0:T(8,128)(2,1)}, u32[]{:S(2)}, u32[]{:S(2)}) collective-permute-start(bf16[384,768]{1,0:T(8,128)(2,1)} %collective-permute-done.13.refs_9_), channel_id=1, source_target_pairs={{0,2},{2,0},{4,6},{6,4},{8,10},{10,8},{12,14},{14,12},{16,18},{18,... | collective-permute-start | bytes 1769480 | tf_op jit(solution)/shard_map/ppermute | solution.py:545
  106.4 5.9 %collective-permute-start.22 = (bf16[384,768]{1,0:T(8,128)(2,1)}, bf16[384,768]{1,0:T(8,128)(2,1)}, u32[]{:S(2)}, u32[]{:S(2)}) collective-permute-start(bf16[384,768]{1,0:T(8,128)(2,1)} %collective-permute-done.17.refs_10_), channel_id=1, source_target_pairs={{0,2},{2,0},{4,6},{6,4},{8,10},{10,8},{12,14},{14,12},{16,18},{18,... | collective-permute-start | bytes 1769480 | tf_op jit(solution)/shard_map/ppermute | solution.py:545
  106.8 2.8 collective-permute-start.18
  109.6 20.6 %collective-permute-start.24 = (bf16[128,768]{1,0:T(8,128)(2,1)S(1)}, bf16[128,768]{1,0:T(8,128)(2,1)S(1)}, u32[]{:S(2)}, u32[]{:S(2)}) collective-permute-start(bf16[128,768]{1,0:T(8,128)(2,1)S(1)} %convert_element_type.215), channel_id=1, source_target_pairs={{0,1},{1,0},{2,3},{3,2},{4,5},{5,4},{6,7},{7,6},{8,9},{9,8},{10,11... | collective-permute-start | bytes 589832 | tf_op jit(solution)/shard_map/ppermute | solution.py:548
  111.8 19.1 %collective-permute-start.25 = (bf16[128,768]{1,0:T(8,128)(2,1)S(1)}, bf16[128,768]{1,0:T(8,128)(2,1)S(1)}, u32[]{:S(2)}, u32[]{:S(2)}) collective-permute-start(bf16[128,768]{1,0:T(8,128)(2,1)S(1)} %bitcast.163), channel_id=1, source_target_pairs={{0,1},{1,0},{2,3},{3,2},{4,5},{5,4},{6,7},{7,6},{8,9},{9,8},{10,11... | collective-permute-start | bytes 589832 | tf_op jit(solution)/shard_map/ppermute | solution.py:548
  116.4 18.7 %copy-start.9 = (bf16[96,3072]{1,0:T(8,128)(2,1)S(1)}, bf16[96,3072]{1,0:T(8,128)(2,1)}, u32[]{:S(2)}) copy-start(bf16[96,3072]{1,0:T(8,128)(2,1)} %copy-done.7) | copy-start | bytes 1769476
  128.7 6.4 %collective-permute-start.23 = (bf16[128,768]{1,0:T(8,128)(2,1)S(1)}, bf16[128,768]{1,0:T(8,128)(2,1)S(1)}, u32[]{:S(2)}, u32[]{:S(2)}) collective-permute-start(bf16[128,768]{1,0:T(8,128)(2,1)S(1)} %get-tuple-element.95.do_ref), channel_id=1, source_target_pairs={{0,1},{1,0},{2,3},{3,2},{4,5},{5,4},{6,7},{7,6},{8,9},{9,8},{10,11... | collective-permute-start | bytes 589832 | tf_op jit(solution)/shard_map/ppermute | solution.py:548
  175.9 174.2 %all-gather.3.cloned.1.call-start = ((), (), s32[]{:S(2)}) async-start(), calls=%async_computation.2 | async-start | bytes 5013504 | tf_op jit(solution)/shard_map/all_gather | solution.py:820
  176.8 28.7 %collective-permute-start.31 = (bf16[128,768]{1,0:T(8,128)(2,1)S(1)}, bf16[128,768]{1,0:T(8,128)(2,1)S(1)}, u32[]{:S(2)}, u32[]{:S(2)}) collective-permute-start(bf16[128,768]{1,0:T(8,128)(2,1)S(1)} %copy-done.45), channel_id=1, source_target_pairs={{0,1},{1,0},{2,3},{3,2},{4,5},{5,4},{6,7},{7,6},{8,9},{9,8},{10,11... | collective-permute-start | bytes 589832 | tf_op jit(solution)/shard_map/ppermute | solution.py:548
  178.3 11.6 %collective-permute-start.30 = (bf16[128,768]{1,0:T(8,128)(2,1)S(1)}, bf16[128,768]{1,0:T(8,128)(2,1)S(1)}, u32[]{:S(2)}, u32[]{:S(2)}) collective-permute-start(bf16[128,768]{1,0:T(8,128)(2,1)S(1)} %get-tuple-element.110), channel_id=1, source_target_pairs={{0,1},{1,0},{2,3},{3,2},{4,5},{5,4},{6,7},{7,6},{8,9},{9,8},{10,11... | collective-permute-start | bytes 589832 | tf_op jit(solution)/shard_map/ppermute | solution.py:548
  179.2 11.7 %collective-permute-start.27 = (bf16[768,512]{1,0:T(8,128)(2,1)S(1)}, bf16[768,512]{1,0:T(8,128)(2,1)S(1)}, u32[]{:S(2)}, u32[]{:S(2)}) collective-permute-start(bf16[768,512]{1,0:T(8,128)(2,1)S(1)} %pad_select_fusion), channel_id=1, source_target_pairs={{0,2},{2,0},{4,6},{6,4},{8,10},{10,8},{12,14},{14,12},{16,18},{18,... | collective-permute-start | bytes 2359304 | tf_op jit(solution)/shard_map/ppermute | solution.py:545
  189.8 16.8 %collective-permute-start.26 = (bf16[768,768]{1,0:T(8,128)(2,1)S(1)}, bf16[768,768]{1,0:T(8,128)(2,1)S(1)}, u32[]{:S(2)}, u32[]{:S(2)}) collective-permute-start(bf16[768,768]{1,0:T(8,128)(2,1)S(1)} %select_convert_fusion), channel_id=1, source_target_pairs={{0,2},{2,0},{4,6},{6,4},{8,10},{10,8},{12,14},{14,12},{16,18},{18,... | collective-permute-start | bytes 3538952 | tf_op jit(solution)/shard_map/ppermute | solution.py:545
  205.4 4.5 %collective-permute-start.29 = (bf16[2,2,2,128,768]{4,3,2,0,1:T(8,128)(2,1)S(1)}, bf16[2,2,2,128,768]{4,3,2,0,1:T(8,128)(2,1)S(1)}, u32[]{:S(2)}, u32[]{:S(2)}) collective-permute-start(bf16[2,2,2,128,768]{4,3,2,0,1:T(8,128)(2,1)S(1)} %bitcast.185), channel_id=1, source_target_pairs={{0,2},{2,0},{4,6},{6,4},{8,10},{10,8},{12,14},{14,12},{16,18},{18,... | collective-permute-start | bytes 4718600 | tf_op jit(solution)/shard_map/ppermute | solution.py:545
  206.6 3.2 collective-permute-start.32
  207.3 24.3 %collective-permute-start.28 = (bf16[384,1280]{1,0:T(8,128)(2,1)S(1)}, bf16[384,1280]{1,0:T(8,128)(2,1)}, u32[]{:S(2)}, u32[]{:S(2)}) collective-permute-start(bf16[384,1280]{1,0:T(8,128)(2,1)S(1)} %dynamic-slice_bitcast_fusion), channel_id=1, source_target_pairs={{0,1},{1,0},{2,3},{3,2},{4,5},{5,4},{6,7},{7,6},{8,9},{9,8},{10,11... | collective-permute-start | bytes 2949128 | tf_op jit(solution)/shard_map/ppermute | solution.py:548
  255.1 28.0 %collective-permute-start.34 = (bf16[2,2,128,768]{3,2,1,0:T(8,128)(2,1)}, bf16[2,2,128,768]{3,2,1,0:T(8,128)(2,1)}, u32[]{:S(2)}, u32[]{:S(2)}) collective-permute-start(bf16[2,2,128,768]{3,2,1,0:T(8,128)(2,1)} %dynamic-slice_bitcast_fusion.1), channel_id=1, source_target_pairs={{0,8},{2,10},{4,12},{6,14},{8,0},{10,2},{12,4},{14,6},{16,24},{18,... | collective-permute-start | bytes 2359304 | tf_op jit(solution)/shard_map/ppermute | solution.py:545
  257.6 25.5 %copy-start.14 = (bf16[2,2,2,128,768]{4,3,2,0,1:T(8,128)(2,1)S(1)}, bf16[2,2,2,128,768]{4,3,2,0,1:T(8,128)(2,1)}, u32[]{:S(2)}) copy-start(bf16[2,2,2,128,768]{4,3,2,0,1:T(8,128)(2,1)} %fusion.3) | copy-start | bytes 4718596
  259.6 24.9 %collective-permute-start.33 = (bf16[2,2,48,2048]{3,2,0,1:T(8,128)(2,1)}, bf16[2,2,48,2048]{3,2,0,1:T(8,128)(2,1)}, u32[]{:S(2)}, u32[]{:S(2)}) collective-permute-start(bf16[2,2,48,2048]{3,2,0,1:T(8,128)(2,1)} %bitcast.160), channel_id=1, source_target_pairs={{0,4},{2,6},{4,0},{6,2},{8,12},{10,14},{12,8},{14,10},{16,20},{18,... | collective-permute-start | bytes 2359304 | tf_op jit(solution)/shard_map/ppermute | solution.py:545
  286.3 32.7 %collective-permute-start.36 = (bf16[2,128,768]{2,1,0:T(8,128)(2,1)S(1)}, bf16[2,128,768]{2,1,0:T(8,128)(2,1)S(1)}, u32[]{:S(2)}, u32[]{:S(2)}) collective-permute-start(bf16[2,128,768]{2,1,0:T(8,128)(2,1)S(1)} %dynamic-slice_bitcast_fusion.2), channel_id=1, source_target_pairs={{0,16},{2,18},{4,20},{6,22},{8,24},{10,26},{12,28},{14,30},{16,0},... | collective-permute-start | bytes 1179656 | tf_op jit(solution)/shard_map/ppermute | solution.py:545
  287.8 33.5 %collective-permute-start.35 = (bf16[2,48,2048]{2,1,0:T(8,128)(2,1)}, bf16[2,48,2048]{2,1,0:T(8,128)(2,1)S(1)}, u32[]{:S(2)}, u32[]{:S(2)}) collective-permute-start(bf16[2,48,2048]{2,1,0:T(8,128)(2,1)} %dynamic-slice_bitcast_fusion.3), channel_id=1, source_target_pairs={{0,8},{2,10},{4,12},{6,14},{8,0},{10,2},{12,4},{14,6},{16,24},{18,... | collective-permute-start | bytes 1179656 | tf_op jit(solution)/shard_map/ppermute | solution.py:545
  321.5 6.4 %collective-permute-start.38 = (bf16[128,768]{1,0:T(8,128)(2,1)S(1)}, bf16[128,768]{1,0:T(8,128)(2,1)S(1)}, u32[]{:S(2)}, u32[]{:S(2)}) collective-permute-start(bf16[128,768]{1,0:T(8,128)(2,1)S(1)} %dynamic-slice_bitcast_fusion.4), channel_id=1, source_target_pairs={{0,4},{2,6},{4,0},{6,2},{8,12},{10,14},{12,8},{14,10},{16,20},{18,... | collective-permute-start | bytes 589832 | tf_op jit(solution)/shard_map/ppermute | solution.py:545
  324.3 10.8 %collective-permute-start.37 = (bf16[48,2048]{1,0:T(8,128)(2,1)S(1)}, bf16[48,2048]{1,0:T(8,128)(2,1)S(1)}, u32[]{:S(2)}, u32[]{:S(2)}) collective-permute-start(bf16[48,2048]{1,0:T(8,128)(2,1)S(1)} %dynamic-slice_bitcast_fusion.5), channel_id=1, source_target_pairs={{0,16},{2,18},{4,20},{6,22},{8,24},{10,26},{12,28},{14,30},{16,0},... | collective-permute-start | bytes 589832 | tf_op jit(solution)/shard_map/ppermute | solution.py:545
  335.1 6.7 %collective-permute-start.39 = (bf16[48,2048]{1,0:T(8,128)(2,1)S(1)}, bf16[48,2048]{1,0:T(8,128)(2,1)S(1)}, u32[]{:S(2)}, u32[]{:S(2)}) collective-permute-start(bf16[48,2048]{1,0:T(8,128)(2,1)S(1)} %fusion.36), channel_id=1, source_target_pairs={{0,16},{2,18},{4,20},{6,22},{8,24},{10,26},{12,28},{14,30},{16,0},... | collective-permute-start | bytes 589832 | tf_op jit(solution)/shard_map/ppermute | solution.py:545
  341.9 8.0 %collective-permute-start.40 = (bf16[2,48,2048]{2,1,0:T(8,128)(2,1)S(1)}, bf16[2,48,2048]{2,1,0:T(8,128)(2,1)S(1)}, u32[]{:S(2)}, u32[]{:S(2)}) collective-permute-start(bf16[2,48,2048]{2,1,0:T(8,128)(2,1)S(1)} %pad_maximum_fusion.24), channel_id=1, source_target_pairs={{0,8},{2,10},{4,12},{6,14},{8,0},{10,2},{12,4},{14,6},{16,24},{18,... | collective-permute-start | bytes 1179656 | tf_op jit(solution)/shard_map/ppermute | solution.py:545
  356.7 20.0 %collective-permute-start.41 = (bf16[2,2,48,2048]{3,2,1,0:T(8,128)(2,1)S(1)}, bf16[2,2,48,2048]{3,2,1,0:T(8,128)(2,1)S(1)}, u32[]{:S(2)}, u32[]{:S(2)}) collective-permute-start(bf16[2,2,48,2048]{3,2,1,0:T(8,128)(2,1)S(1)} %pad_maximum_fusion.16), channel_id=1, source_target_pairs={{0,4},{2,6},{4,0},{6,2},{8,12},{10,14},{12,8},{14,10},{16,20},{18,... | collective-permute-start | bytes 2359304 | tf_op jit(solution)/shard_map/ppermute | solution.py:545
  377.0 3.5 collective-permute-start.42
  (46 other events, 231.5 us)
Sparse Core Ops, SparseCore 0:
  176.0 76.9 reduce-scatter.1
  255.5 68.2 all-gather.2

commit v4 on v3

--- a/solution.py
+++ b/solution.py
@@ -26,118 +26,135 @@
     return lax.dot_general(a, b, (((0,), (0,)), ((), ())), preferred_element_type=F32)
 
 
-def att_fwd_kernel(q_ref, rows_ref, pen_ref, kind_ref, k_ref, v_ref, t_ref, ka_ref, o_ref, p_ref):
-    T=q_ref.shape[0]; W=k_ref.shape[0]; NB=W//T
-    c=DH**-0.5
-    q=q_ref[...]
-    qc=((q+rows_ref[1:2, :])*c).astype(BF)
-    qp=((q+rows_ref[2:3, :])*c).astype(BF)
-    qt=(q+rows_ref[3:4, :])*c
-    t0=qt*rows_ref[4:5, :]; t1=qt*rows_ref[5:6, :]
-    lane=lax.broadcasted_iota(jnp.int32,(T,128),1)
-    row=lax.broadcasted_iota(jnp.int32,(T,128),0)
-    same=kind_ref[...]>0.5
-    pen=pen_ref[...]
-    sel=lane<=row
-    zero=jnp.zeros((T,128),F32)
-    kcat=jnp.concatenate([k_ref[...],ka_ref[...]],axis=1)
-    outs=[]
+def att_fwd_kernel(q_ref, v_rows, pen_ref, kind_ref, k_ref, v_ref, t_ref, ka_ref, o_ref, p_ref):
+    T = q_ref.shape[0]
+    W = k_ref.shape[0]
+    blocks = W // T
+    c = DH**-0.5
+    q = q_ref[...]
+    qc = ((q + v_rows[1:2, :]) * c).astype(BF)
+    qp = ((q + v_rows[2:3, :]) * c).astype(BF)
+    qt = (q + v_rows[3:4, :]) * c
+    t0, t1 = qt * v_rows[4:5, :], qt * v_rows[5:6, :]
+    lane = lax.broadcasted_iota(jnp.int32, (T, 128), 1)
+    row = lax.broadcasted_iota(jnp.int32, (T, 128), 0)
+    same = kind_ref[...] > 0.5
+    pen = pen_ref[...]
+    zero = jnp.zeros_like(qc)
+    heads, where_q = [], []
     for h in range(2):
-        msk=(lane<64) if h==0 else (lane>=64)
-        a0=jnp.sum(jnp.where(msk,t0,0.0),axis=1,keepdims=True)
-        a1=jnp.sum(jnp.where(msk,t1,0.0),axis=1,keepdims=True)
-        a0=jnp.broadcast_to(a0,(T,128)); a1=jnp.broadcast_to(a1,(T,128))
-        A=jnp.where(same,a1,a0); B=jnp.where(same,a0,a1)
-        A1=A.astype(BF).astype(F32); A2=A-A1
-        B1=B.astype(BF).astype(F32); B2=B-B1
-        aug=jnp.where(lane==0,A1,jnp.where(lane==1,A2,jnp.where(lane==4,B1,jnp.where(lane==5,B2,pen)))).astype(BF)
-        qa=jnp.concatenate([jnp.where(msk,qc,jnp.zeros_like(qc)),aug],axis=1)
-        s=nt(qa,kcat)
-        w=nt(jnp.where(msk,qp,jnp.zeros_like(qp)),t_ref[...])
-        R=[pltpu.roll(w[:,128*t:128*t+128],1,1,stride=1,stride_axis=0) for t in range(NB+1)]
-        ss=[s[:,128*b:128*b+128]+jnp.where(sel,R[b],R[b+1]) for b in range(NB)]
-        m=ss[0]
-        for b in range(1,NB): m=jnp.maximum(m,ss[b])
-        m=jnp.max(m,axis=1,keepdims=True)
-        es=[jnp.exp(x-m) for x in ss]
-        l=es[0]
-        for b in range(1,NB): l=l+es[b]
-        l=jnp.sum(l,axis=1,keepdims=True)
-        inv=1.0/l
-        p=jnp.concatenate([(x*inv).astype(BF) for x in es],axis=1)
-        p_ref[h]=p
-        outs.append(nn(p,v_ref[...]))
-    o_ref[...]=jnp.where(lane<64,outs[0],outs[1])
-
-def att_bwd_kernel(q_ref, rows_ref, kind_ref, dm_ref, o_ref, p_ref, k_ref, v_ref, t_ref, ka_ref,
-                   dq_ref, vec_ref, dkv_ref, dt_ref):
-    T=q_ref.shape[0]; W=k_ref.shape[0]; NB=W//T
-    c=DH**-0.5
-    q=q_ref[...]
-    qc=((q+rows_ref[1:2, :])*c).astype(BF)
-    qp=((q+rows_ref[2:3, :])*c).astype(BF)
-    qt=(q+rows_ref[3:4, :])*c
-    e0=rows_ref[4:5, :]; e1=rows_ref[5:6, :]
-    lane=lax.broadcasted_iota(jnp.int32,(T,128),1)
-    row=lax.broadcasted_iota(jnp.int32,(T,128),0)
-    same=kind_ref[...]>0.5
-    sel=lane>=row
-    flip=jnp.where(lane+row==T-1,1.0,0.0).astype(BF)
-    qpr=nn(flip,qp).astype(BF)
-    zf=jnp.zeros((T,128),F32)
-    dm=dm_ref[...]
-    dmo=dm.astype(F32)*o_ref[...]
-    kcat=jnp.concatenate([k_ref[...],ka_ref[...]],axis=1)
-    zb=jnp.zeros_like(dm)
-    dss=[];wds=[];dms=[];qcs=[];qps=[];dqc=[];dqp=[];gz=[];go=[]
+        mine = (lane < DH) if h == 0 else (lane >= DH)
+        a0 = jnp.broadcast_to(jnp.sum(jnp.where(mine, t0, 0.0), axis=1, keepdims=True), (T, 128))
+        a1 = jnp.broadcast_to(jnp.sum(jnp.where(mine, t1, 0.0), axis=1, keepdims=True), (T, 128))
+        one, two = jnp.where(same, a1, a0), jnp.where(same, a0, a1)
+        one_high, two_high = one.astype(BF).astype(F32), two.astype(BF).astype(F32)
+        extra = jnp.where(lane == 4, two_high, jnp.where(lane == 5, two - two_high, pen))
+        extra = jnp.where(lane == 0, one_high, jnp.where(lane == 1, one - one_high, extra))
+        heads.append(jnp.concatenate([jnp.where(mine, qc, zero), extra.astype(BF)], axis=1))
+        where_q.append(jnp.where(mine, qp, zero))
+    s = nt(jnp.concatenate(heads, axis=0), jnp.concatenate([k_ref[...], ka_ref[...]], axis=1))
+    w = nt(jnp.concatenate(where_q, axis=0), t_ref[...])
+    probs = []
     for h in range(2):
-        msk=(lane<64) if h==0 else (lane>=64)
-        delta=jnp.sum(jnp.where(msk,dmo,0.0),axis=1,keepdims=True)
-        dmh=jnp.where(msk,dm,zb)
-        dp=nt(dmh,v_ref[...])
-        ds=(p_ref[h].astype(F32)*(dp-delta)).astype(BF)
-        dsf=nn(flip,ds)
-        dc=nn(ds,kcat)
-        R=[pltpu.roll(dsf[:,128*b:128*b+128],0,1,stride=1,stride_axis=0) for b in range(NB)]
-        wd=[]
-        for t in range(NB+1):
-            lo=R[t] if t<NB else zf
-            hi=R[t-1] if t>0 else zf
-            wd.append(jnp.where(sel,lo,hi).astype(BF))
-        wd=jnp.concatenate(wd,axis=1)
-        dqp.append(nn(wd,t_ref[...]))
-        dqc.append(dc[:,:128])
-        s1=jnp.broadcast_to(dc[:,128:129],(T,128)); s0=jnp.broadcast_to(dc[:,132:133],(T,128))
-        go.append(jnp.where(same,s1,s0)); gz.append(jnp.where(same,s0,s1))
-        dss.append(ds);wds.append(wd);dms.append(dmh)
-        qcs.append(jnp.where(msk,qc,zb));qps.append(jnp.where(msk,qpr,zb))
-    cat=lambda xs: jnp.concatenate(xs,axis=0)
-    dkv_ref[0]=tn(cat(qcs),cat(dss)).astype(BF)
-    dkv_ref[1]=tn(cat(dms),jnp.concatenate([p_ref[0],p_ref[1]],axis=0)).astype(BF)
-    dt_ref[...]=tn(cat(qps),cat(wds)).astype(BF)
-    lo=lane<64
-    dc=jnp.where(lo,dqc[0],dqc[1]).astype(BF).astype(F32)
-    dpp=nn(flip,jnp.where(lo,dqp[0],dqp[1]).astype(BF))
-    z=jnp.where(lo,gz[0],gz[1]); o=jnp.where(lo,go[0],go[1])
-    dty=z*e0+o*e1
-    dq_ref[...]=(c*(dc+dpp+dty)).astype(BF)
-    vec_ref[0:1,:]=c*jnp.sum(dc,axis=0,keepdims=True)
-    vec_ref[1:2,:]=c*jnp.sum(dpp,axis=0,keepdims=True)
-    vec_ref[2:3,:]=c*jnp.sum(dty,axis=0,keepdims=True)
-    vec_ref[3:4,:]=jnp.sum(z*qt,axis=0,keepdims=True)
-    vec_ref[4:5,:]=jnp.sum(o*qt,axis=0,keepdims=True)
-    vec_ref[5:8,:]=jnp.zeros((3,128),F32)
-
-def att_fwd(q, rows, pen, kind, k, v, t, ka):
+        turned = [
+            pltpu.roll(w[T * h : T * (h + 1), 128 * b : 128 * b + 128], 1, 1, stride=1, stride_axis=0)
+            for b in range(blocks + 1)
+        ]
+        tiles = [
+            s[T * h : T * (h + 1), 128 * b : 128 * b + 128]
+            + jnp.where(lane <= row, turned[b], turned[b + 1])
+            for b in range(blocks)
+        ]
+        top = tiles[0]
+        for b in range(1, blocks):
+            top = jnp.maximum(top, tiles[b])
+        top = jnp.max(top, axis=1, keepdims=True)
+        tiles = [jnp.exp(a - top) for a in tiles]
+        total = tiles[0]
+        for b in range(1, blocks):
+            total = total + tiles[b]
+        inverse = 1.0 / jnp.sum(total, axis=1, keepdims=True)
+        p = jnp.concatenate([(a * inverse).astype(BF) for a in tiles], axis=1)
+        p_ref[h] = p
+        probs.append(p)
+    out = nn(jnp.concatenate(probs, axis=0), v_ref[...])
+    o_ref[...] = jnp.where(lane < DH, out[:T], out[T:])
+
+
+def att_bwd_kernel(
+    q_ref, v_rows, kind_ref, dm_ref, o_ref, p_ref, k_ref, v_ref, t_ref, ka_ref,
+    dq_ref, vec_ref, dkv_ref, dt_ref,
+):
+    T = q_ref.shape[0]
+    W = k_ref.shape[0]
+    blocks = W // T
+    c = DH**-0.5
+    q = q_ref[...]
+    qc = ((q + v_rows[1:2, :]) * c).astype(BF)
+    qp = ((q + v_rows[2:3, :]) * c).astype(BF)
+    qt = (q + v_rows[3:4, :]) * c
+    e0, e1 = v_rows[4:5, :], v_rows[5:6, :]
+    lane = lax.broadcasted_iota(jnp.int32, (T, 128), 1)
+    row = lax.broadcasted_iota(jnp.int32, (T, 128), 0)
+    same = kind_ref[...] > 0.5
+    flip = jnp.where(lane + row == T - 1, 1.0, 0.0).astype(BF)
+    qpr = nn(flip, qp).astype(BF)
+    dm = dm_ref[...]
+    dmo = dm.astype(F32) * o_ref[...]
+    zero = jnp.zeros_like(dm)
+    stack = lambda parts: jnp.concatenate(parts, axis=0)
+    mine = [lane < DH, lane >= DH]
+    pick = lambda a: stack([jnp.where(m, a, zero) for m in mine])
+    dms = pick(dm)
+    delta = jnp.sum(
+        stack([jnp.where(m, dmo, 0.0) for m in mine]), axis=1, keepdims=True
+    )
+    dp = nt(dms, v_ref[...])
+    p = stack([p_ref[0], p_ref[1]])
+    ds = (p.astype(F32) * (dp - delta)).astype(BF)
+    dc = nn(ds, jnp.concatenate([k_ref[...], ka_ref[...]], axis=1))
+    wide = []
+    for h in range(2):
+        back = nn(flip, ds[T * h : T * (h + 1)])
+        turned = [
+            pltpu.roll(back[:, 128 * b : 128 * b + 128], 0, 1, stride=1, stride_axis=0)
+            for b in range(blocks)
+        ]
+        edge = jnp.zeros((T, 128), F32)
+        tiles = [
+            jnp.where(lane >= row, a, b).astype(BF)
+            for a, b in zip(turned + [edge], [edge] + turned)
+        ]
+        wide.append(jnp.concatenate(tiles, axis=1))
+    wide = stack(wide)
+    dqp = nn(wide, t_ref[...])
+    dkv_ref[0] = tn(pick(qc), ds).astype(BF)
+    dkv_ref[1] = tn(dms, p).astype(BF)
+    dt_ref[...] = tn(pick(qpr), wide).astype(BF)
+    both = lambda a: jnp.where(mine[0], a[:T], a[T:])
+    dc_low = both(dc[:, :128]).astype(BF).astype(F32)
+    dp_low = nn(flip, both(dqp).astype(BF))
+    one = both(jnp.broadcast_to(dc[:, 128:129], (2 * T, 128)))
+    two = both(jnp.broadcast_to(dc[:, 132:133], (2 * T, 128)))
+    same_sum, other_sum = jnp.where(same, one, two), jnp.where(same, two, one)
+    dt = other_sum * e0 + same_sum * e1
+    dq_ref[...] = (c * (dc_low + dp_low + dt)).astype(BF)
+    total = lambda a: jnp.sum(a, axis=0, keepdims=True)
+    rows = [c * total(dc_low), c * total(dp_low), c * total(dt), total(other_sum * qt), total(same_sum * qt)]
+    vec_ref[...] = jnp.concatenate(rows + [jnp.zeros((3, 128), F32)], axis=0)
+
+
+def att_fwd(q, rows, pen, kind, kv, t, ka):
     T, D = q.shape
-    W = k.shape[0]
+    W = kv.shape[0]
+    keys, values = (pl.BlockSpec((W, 128), lambda i, n=n: (0, i + n * D // 128)) for n in range(2))
     heads = D // DH
     col = lambda n: pl.BlockSpec((n, 128), lambda i: (0, i))
     fixed = lambda n: pl.BlockSpec((n, 128), lambda i: (0, 0))
     return pl.pallas_call(
         att_fwd_kernel,
         grid=(D // 128,),
-        in_specs=[col(T), col(16), fixed(T), fixed(T), col(W), col(W), col(W + T), fixed(W)],
+        in_specs=[col(T), col(16), fixed(T), fixed(T), keys, values, col(W + T), fixed(W)],
         out_specs=[col(T), pl.BlockSpec((2, T, W), lambda i: (i, 0, 0))],
         out_shape=[
             jax.ShapeDtypeStruct((T, D), F32),
@@ -150,12 +167,13 @@
             transcendentals=heads * T * W,
         ),
         name="att_fwd",
-    )(q, rows, pen, kind, k, v, t, ka)
-
-
-def att_bwd(q, rows, kind, dm, o, p, k, v, t, ka):
+    )(q, rows, pen, kind, kv, kv, t, ka)
+
+
+def att_bwd(q, rows, kind, dm, o, p, kv, t, ka):
     T, D = q.shape
-    W = k.shape[0]
+    W = kv.shape[0]
+    keys, values = (pl.BlockSpec((W, 128), lambda i, n=n: (0, i + n * D // 128)) for n in range(2))
     heads = D // DH
     col = lambda n: pl.BlockSpec((n, 128), lambda i: (0, i))
     fixed = lambda n: pl.BlockSpec((n, 128), lambda i: (0, 0))
@@ -164,7 +182,7 @@
         grid=(D // 128,),
         in_specs=[
             col(T), col(16), fixed(T), col(T), col(T), pl.BlockSpec((2, T, W), lambda i: (i, 0, 0)),
-            col(W), col(W), col(W + T), fixed(W),
+            keys, values, col(W + T), fixed(W),
         ],
         out_specs=[
             col(T), col(8), pl.BlockSpec((2, 128, W), lambda i: (0, i, 0)),
@@ -178,12 +196,10 @@
         ],
         compiler_params=pltpu.CompilerParams(vmem_limit_bytes=60 * 2**20),
         cost_estimate=pl.CostEstimate(
-            flops=2 * heads * T * W * 2048,
-            bytes_accessed=2 * (6 * W * D + heads * T * W),
-            transcendentals=0,
+            flops=2**20, bytes_accessed=2**20, transcendentals=0
         ),
         name="att_bwd",
-    )(q, rows, kind, dm, o, p, k, v, t, ka)
+    )(q, rows, kind, dm, o, p, kv, kv, t, ka)
 
 
 def pack_rows(vectors, dn):
@@ -230,7 +246,7 @@
         out_shape=[
             jax.ShapeDtypeStruct((dn, FF), F32), jax.ShapeDtypeStruct((FF // 2, D), F32)
         ],
-        cost_estimate=pl.CostEstimate(flops=0, bytes_accessed=6 * D * FF, transcendentals=0),
+        cost_estimate=pl.CostEstimate(flops=2**33, bytes_accessed=8 * D * FF, transcendentals=0),
         name="ffn_final",
     )(blocks)
 
@@ -303,29 +319,30 @@
 
 
 def ffn_specs(T, D, FF):
-    steps = FF // (D // 2)
+    steps = FF // D
     half = steps // 2
     c = FF // steps
     q = D // 8
 
     def chunk_at(j, s):
-        p = jnp.maximum(j - half, 0)
-        piece = ((s[2] ^ (p & 1)) << 1) | (s[1] ^ (p >> 1))
-        return jnp.where(j < half, half * s[0] + j, half * (1 - s[0]) + piece)
+        other = half * (1 - s[0]) + (s[2] ^ jnp.maximum(j - half, 0))
+        return jnp.where(j < half, half * s[0] + j, other)
 
     col = lambda j, s: (0, chunk_at(j, s))
     whole = lambda *shape: pl.BlockSpec(shape, lambda j, s: (0,) * len(shape))
     inner = [pl.BlockSpec((4 * q, c), col)] + [pl.BlockSpec((q, c), col)] * 4
-    outer = [pl.BlockSpec((c, D), lambda j, s: (jnp.minimum(j, half - 1), 0))] + [whole(c, D)] * 4
+    outer = [pl.BlockSpec((c, D), lambda j, s: (jnp.minimum(j, half - 1), 0))]
+    outer += [whole(c // 2, D)] * 4
     proj = [whole(4 * q, D), whole(2 * q, D), whole(2 * q, D)]
     return steps, half, c, chunk_at, col, whole, inner, outer, proj
 
 
-def outer_chunk(j, half, refs):
-    chunk = refs[0][...]
-    for p in range(4):
-        chunk = jnp.where(j == half + p, refs[1 + p][...], chunk)
-    return chunk
+def outer_chunk(j, half, odd, refs):
+    last = j > half
+    a = jnp.where(last, refs[2][...], refs[1][...])
+    b = jnp.where(last, refs[4][...], refs[3][...])
+    pair = jnp.concatenate([jnp.where(odd, b, a), jnp.where(odd, a, b)], axis=0)
+    return jnp.where(j < half, refs[0][...], pair)
 
 
 def rows_of(refs):
@@ -333,8 +350,9 @@
 
 
 def inner_bias_chunk(b, half, vec_ref, D):
-    row = vec_ref[pl.ds(12 + b % half, 1), :]
-    return jnp.where(b < half, row[:, : D // 2], row[:, D // 2 :])
+    rows = [vec_ref[pl.ds(12 + 2 * (b % half) + n, 1), :] for n in range(2)]
+    parts = [jnp.where(b < half, r[:, : D // 2], r[:, D // 2 :]) for r in rows]
+    return jnp.concatenate(parts, axis=1)
 
 
 def gelu_tanh(u):
@@ -373,7 +391,7 @@
         pre_ref[...] = pre
         act = (0.5 * pre * (1.0 + gelu_tanh(pre))).astype(BF)
         act_ref[...] = act
-        acc_ref[...] += nn(act, outer_chunk(j, half, u_refs))
+        acc_ref[...] += nn(act, outer_chunk(j, half, odd, u_refs))
 
         @pl.when(j == steps - 1)
         def _():
@@ -408,7 +426,7 @@
             low(T, D), low(T, FF), f32(T, FF), low(T, D), f32(T, D), low(T, D), f32(T, D),
             f32(T, 128), f32(8, D),
         ],
-        compiler_params=pltpu.CompilerParams(vmem_limit_bytes=40 * 2**20),
+        compiler_params=pltpu.CompilerParams(vmem_limit_bytes=60 * 2**20),
         cost_estimate=pl.CostEstimate(
             flops=4 * T * D * FF, bytes_accessed=4 * D * FF, transcendentals=T * FF
         ),
@@ -451,7 +469,7 @@
         u = jnp.concatenate([pre_ref[...], pre_got], axis=0)
         t = gelu_tanh(u)
         slope = 0.5 * (1.0 + t) + 0.5 * u * (1.0 - t * t) * (GELU_A * (1.0 + 3.0 * GELU_B * u * u))
-        di = (nt(do_both[...], outer_chunk(j, half, u_refs)) * slope).astype(BF)
+        di = (nt(do_both[...], outer_chunk(j, half, odd, u_refs)) * slope).astype(BF)
         ib_ref[pl.ds(b, 1), :] = row_sum(di[:T].astype(F32))
         acc_ref[...] += nt(di[:T], w)
         gi = tn(di, nf_ref[...]).astype(BF)
@@ -480,7 +498,10 @@
             gv_ref[1:2, :] = row_sum(d_normed)
             gv_ref[2:3, :] = row_sum(da.astype(F32))
             gv_ref[3:4, :] = row_sum(dm.astype(BF).astype(F32))
-            gv_ref[4:, :] = jnp.concatenate([ib_ref[:half], ib_ref[half:]], axis=1)
+            for n in range(2 * half):
+                at = slice(0, dn) if n % 2 == 0 else slice(dn, D)
+                gv_ref[4 + n : 5 + n, :dn] = ib_ref[n // 2 : n // 2 + 1, at]
+                gv_ref[4 + n : 5 + n, dn:] = ib_ref[half + n // 2 : half + n // 2 + 1, at]
 
     f32 = lambda *shape: jax.ShapeDtypeStruct(shape, F32)
     low = lambda *shape: jax.ShapeDtypeStruct(shape, BF)
@@ -500,7 +521,7 @@
             ],
         ),
         out_shape=[low(count, ri + 2 * ru, dn), f32(T, D), low(T, D), low(T, D), f32(8, D)],
-        compiler_params=pltpu.CompilerParams(vmem_limit_bytes=44 * 2**20),
+        compiler_params=pltpu.CompilerParams(vmem_limit_bytes=60 * 2**20),
         cost_estimate=pl.CostEstimate(
             flops=14 * T * D * FF, bytes_accessed=6 * D * FF, transcendentals=2 * T * FF
         ),
@@ -509,6 +530,177 @@
         place, pre, act, normed, d_outer, d_outer_got, d_res2, n1, rstd1, mixed_got, x_got, vecs,
         *o_parts, *i_parts, *u_parts,
     )
+
+
+def key_grads(dkv, d_table, x_win, sinus, vectors):
+    _, D, W = dkv.shape
+    WT = d_table.shape[1]
+    h = D // 2
+
+    def kernel(kv_ref, t_ref, x_ref, s_ref, *refs):
+        v_refs, out_ref = refs[:-1], refs[-1]
+        i = pl.program_id(0)
+        core, part = i // 3, i % 3
+        at = pl.ds(pl.multiple_of(part * h, h), h)
+
+        @pl.when(part < 2)
+        def _():
+            out_ref[core, at, :] = nn(kv_ref[0], x_ref[...]).astype(BF)
+
+        @pl.when(part == 2)
+        def _():
+            out_ref[core, at, :] = nn(t_ref[...], s_ref[...]).astype(BF)
+
+        @pl.when(i == 0)
+        def _():
+            small = jnp.concatenate([r[...] for r in v_refs], axis=0)
+            pad = jnp.zeros((64 - small.shape[0], D), F32)
+            out_ref[0, 3 * h :, :] = jnp.concatenate([small, pad], axis=0).astype(BF)
+            out_ref[1, 3 * h :, :] = jnp.zeros((64, D), BF)
+
+    whole = lambda *shape: pl.BlockSpec(shape, lambda i: (0,) * len(shape))
+    return pl.pallas_call(
+        kernel,
+        grid=(6,),
+        in_specs=[
+            pl.BlockSpec((1, h, W), lambda i: (i // 3, jnp.minimum(i % 3, 1), 0)),
+            pl.BlockSpec((h, WT), lambda i: (i // 3, 0)),
+            whole(W, D),
+            whole(WT, D),
+        ]
+        + [whole(8, D)] * len(vectors),
+        out_specs=whole(2, 3 * h + 64, D),
+        out_shape=jax.ShapeDtypeStruct((2, 3 * h + 64, D), BF),
+        compiler_params=pltpu.CompilerParams(vmem_limit_bytes=60 * 2**20),
+        cost_estimate=pl.CostEstimate(flops=2**20, bytes_accessed=2**20, transcendentals=0),
+        name="key_grads",
+    )(dkv, d_table, x_win, sinus, *vectors)
+
+
+def hidden_grads(place, dkv, k_own, k_other, v_own, v_other, count, reach):
+    D2, W = dkv.shape
+    D = D2 // 2
+    h = D // 2
+    T = 128
+    blocks = W // T
+
+    def kernel(s_ref, a_ref, b_ref, k0, k1, v0, v1, out_ref):
+        s = pl.program_id(0)
+        x = jnp.concatenate([a_ref[...], b_ref[...]], axis=1)
+        for at, k, v in ((s_ref[0], k0, v0), (1 - s_ref[0], k1, v1)):
+            g = nn(jnp.concatenate([k[...], v[...]], axis=1), x).astype(BF)
+            for n in range(2):
+                rel = 2 * s + n - s_ref[3] + reach
+                ok = (rel >= 0) & (rel < blocks)
+                part = g[:, T * n : T * (n + 1)]
+                out_ref[n, pl.ds(pl.multiple_of(at * h, h), h), :] = jnp.where(
+                    ok, part, jnp.zeros_like(part)
+                )
+
+    whole = pl.BlockSpec((h, D), lambda s, p: (0, 0))
+    block = lambda n: pl.BlockSpec(
+        (D2, T), lambda s, p: (0, jnp.clip(2 * s + n - p[3] + reach, 0, blocks - 1))
+    )
+    return pl.pallas_call(
+        kernel,
+        grid_spec=pltpu.PrefetchScalarGridSpec(
+            num_scalar_prefetch=1,
+            grid=(count // 2,),
+            in_specs=[block(0), block(1), whole, whole, whole, whole],
+            out_specs=pl.BlockSpec((2, D, T), lambda s, p: (s, 0, 0)),
+        ),
+        out_shape=jax.ShapeDtypeStruct((count, D, T), BF),
+        compiler_params=pltpu.CompilerParams(vmem_limit_bytes=60 * 2**20),
+        cost_estimate=pl.CostEstimate(
+            flops=2 * D2 * D * T * count, bytes_accessed=8 * D2 * W, transcendentals=0
+        ),
+        name="hidden_grads",
+    )(place, dkv, dkv, k_own, k_other, v_own, v_other)
+
+
+def input_grads(place, d_res1, dq, q_own, q_other, d_hid):
+    T, D = d_res1.shape
+
+    def kernel(s_ref, r_ref, dq_ref, q0, q1, h_ref, out_ref):
+        own, other = nt(dq_ref[...], q0[...]), nt(dq_ref[...], q1[...])
+        first = s_ref[0] == 0
+        g = jnp.concatenate([jnp.where(first, own, other), jnp.where(first, other, own)], axis=1)
+        out_ref[...] = r_ref[...] + g + jnp.transpose(h_ref[...].astype(F32))
+
+    whole = lambda a: pl.BlockSpec(a.shape, lambda i, s: (0, 0))
+    args = (d_res1, dq, q_own, q_other, d_hid)
+    return pl.pallas_call(
+        kernel,
+        grid_spec=pltpu.PrefetchScalarGridSpec(
+            num_scalar_prefetch=1,
+            grid=(1,),
+            in_specs=[whole(a) for a in args],
+            out_specs=whole(d_res1),
+        ),
+        out_shape=jax.ShapeDtypeStruct((T, D), F32),
+        cost_estimate=pl.CostEstimate(
+            flops=2**32, bytes_accessed=2**24, transcendentals=0
+        ),
+        name="input_grads",
+    )(place, *args)
+
+
+def grad_final(place, one, two, one_got, two_got, D, blocks):
+    dn = one.shape[1]
+    h = D // 2
+    p, q = one.shape[0] // blocks, two.shape[0] // blocks
+
+    def kernel(s_ref, a_ref, b_ref, c_ref, d_ref, k_ref, v_ref, p_ref, o_ref, q_ref, small_ref):
+        odd = s_ref[1] == 1
+
+        def rows(x_ref, y_ref):
+            x, y = x_ref[...].astype(F32), y_ref[...].astype(F32)
+            parts = []
+            for n in range(blocks):
+                parts += [x[p * n : p * (n + 1)], y[q * n : q * (n + 1)]]
+            return jnp.concatenate(parts, axis=0)
+
+        mine, other = rows(a_ref, b_ref), rows(c_ref, d_ref)
+        low, high = jnp.where(odd, other, mine), jnp.where(odd, mine, other)
+        k_ref[...] = jnp.transpose(low[:D])
+        v_ref[...] = jnp.transpose(high[:D])
+        p_ref[...] = jnp.transpose(jnp.concatenate([low[D : D + h], high[D : D + h]], axis=0))
+        small_ref[...] = low[D + h : D + h + 64]
+        o_ref[...] = jnp.transpose(low[D + h + 64 :])
+        q_ref[...] = jnp.transpose(high[D + h + 64 :])
+
+    lanes = lambda n: pl.BlockSpec((n, 128), lambda i, s: (0, i))
+    out = pl.BlockSpec((128, D), lambda i, s: (i, 0))
+    return pl.pallas_call(
+        kernel,
+        grid_spec=pltpu.PrefetchScalarGridSpec(
+            num_scalar_prefetch=1,
+            grid=(dn // 128,),
+            in_specs=[lanes(a.shape[0]) for a in (one, two, one_got, two_got)],
+            out_specs=[out] * 5 + [lanes(64)],
+        ),
+        out_shape=[jax.ShapeDtypeStruct((dn, D), F32)] * 5 + [jax.ShapeDtypeStruct((64, dn), F32)],
+        name="grad_final",
+    )(place, one, two, one_got, two_got)
+
+
+def unpack_rows(s):
+    dn = s.shape[1]
+    singles = (19, 0, 1, 2, 18, 16, 17, 10, 8, 9)
+
+    def kernel(s_ref, *outs):
+        for i, out in zip(singles, outs):
+            out[...] = s_ref[i, :]
+        outs[-2][...] = s_ref[3:5, :]
+        for j in range(4):
+            outs[-1][pl.ds(j * dn, dn)] = s_ref[20 + j, :]
+
+    shapes = [(dn,)] * len(singles) + [(2, dn), (4 * dn,)]
+    return pl.pallas_call(
+        kernel,
+        out_shape=[jax.ShapeDtypeStruct(a, F32) for a in shapes],
+        name="unpack_rows",
+    )(s)
 
 
 def layer_norm(residual, gain_vec, bias_vec):
@@ -674,12 +866,14 @@
         )
         other_p, other_v = sh.order(got_a, sh.flip(got_a, 0), sh.bit(0))
         other_q, other_k = sh.order(got_b, sh.flip(got_b, 0), sh.bit(0))
-        p_full, k_full, v_full, q_full = (
+        p_full, q_full = (
             jnp.concatenate(sh.order(w, g, sh.f), axis=0)
-            for w, g in (
-                (position_proj, other_p), (key_proj, other_k), (value_proj, other_v), (query_proj, other_q)
-            )
-        )
+            for w, g in ((position_proj, other_p), (query_proj, other_q))
+        )
+        own, other = (
+            jnp.concatenate(a, axis=1) for a in ((key_proj, value_proj), (other_k, other_v))
+        )
+        kv_full = jnp.concatenate(sh.order(own, other, sh.f), axis=0)
         flip_o = sh.flip(got_o, 0)
         i_got, u_got = sh.fetch_quarter(i_sh), sh.fetch_quarter(u_sh)
     else:
@@ -689,24 +883,26 @@
                 position_proj, key_proj, value_proj, query_proj, output_proj, inner_proj, outer_proj
             )
         )
+        kv_full = jnp.concatenate([k_full, v_full], axis=1)
 
     vecs = jnp.concatenate([small_full[i] for i in range(sh.parts)], axis=1)
 
     q_lin = nn(hidden, q_full)
-    keys = nn(x_win, k_full).astype(BF)
-    values = (nn(x_win, v_full) + vecs[0]).astype(BF)
-    sinus = sinus_rows(T + R * T - 1, W + T, D)
+    if sh.pair:
+        i_got, x_win = lax.optimization_barrier((i_got, x_win))
+    kv_bias = jnp.concatenate([jnp.zeros((D,), F32), vecs[0]])
+    key_values = (nn(x_win, kv_full) + kv_bias).astype(BF)
+    sinus = lax.optimization_barrier(sinus_rows(T + R * T - 1, W + T, D))
     table = nn(sinus, p_full).astype(BF)
 
     if sh.pair:
-        i_got, table = lax.optimization_barrier((i_got, table))
         i_y = sh.flip(i_got, 1)
-        u_got, values, i_y = lax.optimization_barrier((u_got, values, i_y))
+        u_got, key_values = lax.optimization_barrier((u_got, key_values))
         u_y = sh.flip(u_got, 1)
-    mixed_f, probs = att_fwd(q_lin, vecs, pen, kind_q, keys, values, table, kaug)
+    mixed_f, probs = att_fwd(q_lin, vecs, pen, kind_q, key_values, table, kaug)
     mixed_low = mixed_f.astype(BF)
     if sh.pair:
-        place = jnp.stack([sh.f, sh.bit(0), sh.bit(1)])
+        place = jnp.stack([sh.f, sh.bit(0), sh.bit(1), ctx])
         mixed_f, hid, fetched = lax.optimization_barrier((mixed_f, hidden, (i_got, i_y, u_got, u_y)))
         hidden_got = sh.trade(hid)
         mixed_low = mixed_f.astype(BF)
@@ -762,104 +958,106 @@
     if sh.pair:
         d_attn_got = sh.trade(d_attn)
     dq, att_vec, dkv, d_table = att_bwd(
-        q_lin, vecs, kind_q, d_mixed, mixed_f, probs, keys, values, table, kaug
+        q_lin, vecs, kind_q, d_mixed, mixed_f, probs, key_values, table, kaug
     )
     if sh.pair:
         dq_got = sh.trade(dq)
         ffn = lax.psum_scatter(ffn, "ctx", scatter_dimension=0, tiled=False)
-    else:
-        gi, gu = (
-            lax.psum_scatter(tn(a, b).astype(BF), "fsdp", scatter_dimension=0, tiled=True)
-            for a, b in ((normed_low, d_inner), (activ_low, d_outer))
-        )
-        ffn = lax.psum((gi, gu), "ctx")
-
-    dkv = dkv.reshape(2 * D, W)
-    gkv, gp = (
-        lax.dot_general(a, b, (((0,), (1,)), ((), ())), preferred_element_type=F32)
-        for a, b in ((x_win, dkv), (sinus, d_table))
-    )
-    smalls = jnp.concatenate([att_vec, vec_a, vec_b], axis=0).astype(BF)
-    smalls = jnp.transpose(jnp.pad(smalls, ((0, 128 - smalls.shape[0]), (0, 0))))
-    sides = [[gkv[:, :D], gp[:, : D // 2], smalls], [gkv[:, D:], gp[:, D // 2 :], jnp.zeros_like(smalls)]]
-    low, high = (jnp.concatenate([b.astype(BF) for b in a[1:]], axis=1) for a in sides)
-    if sh.pair:
-        kv_half = sh.halve_cols(sides[0][0], sides[1][0])
-        rest = sh.halve_cols(low, high)
-        whole = jnp.concatenate([kv_half, rest], axis=1)
-        half = whole.shape[1]
-        whole = whole.reshape(2, dn, half)
-        keep = lax.dynamic_index_in_dim(whole, sh.f, 0, keepdims=False)
-        send = lax.dynamic_index_in_dim(whole, 1 - sh.f, 0, keepdims=False)
+
+        whole = key_grads(dkv, d_table, x_win, sinus, (att_vec, vec_a, vec_b))
+        whole = sh.halve(whole, 0, 0)
+        keep, send = sh.order(whole[:, :dn], whole[:, dn:], sh.f)
         got_x = sh.trade(send)
-        go = tn(
-            jnp.concatenate([sh.own(mixed_low, 1), sh.own(mixed_got, 1)], axis=0),
-            jnp.concatenate([d_attn, d_attn_got], axis=0),
-        ).astype(BF)
-        gq = tn(
-            jnp.concatenate([sh.own(hidden, 1), sh.own(hidden_got, 1)], axis=0),
-            jnp.concatenate([dq, dq_got], axis=0),
-        ).astype(BF)
-        dkv, _ = lax.optimization_barrier((dkv, rest))
-    else:
-        low, high = (jnp.concatenate([a[0].astype(BF), b], axis=1) for a, b in zip(sides, (low, high)))
-        half = low.shape[1]
-        low, high, go, gq = (
-            lax.psum_scatter(a, "fsdp", scatter_dimension=0, tiled=True)
-            for a in (low, high, tn(mixed_low, d_attn).astype(BF), tn(hidden, dq).astype(BF))
-        )
-        whole = sh.halve_cols(low, high)
-    mine = sh.halve_cols(go, gq)
-
-    d_hid = (tn(dkv[:D], jnp.transpose(k_full)) + tn(dkv[D:], jnp.transpose(v_full))).astype(BF)
-    d_hid = jnp.pad(d_hid, (((C - 1 - R) * T, (C - 1) * T + L - (C - 1 - R) * T - W), (0, 0)))
-    d_hid = lax.dynamic_slice_in_dim(d_hid, (C - 1 - ctx) * T, L, 0)
-    d_hid = sh.halve(sh.spread(d_hid.reshape(C, T, D)), 0, sh.bits - 1)
-    if sh.pair:
+        dkv, _ = lax.optimization_barrier((dkv, send))
+        go, gq = (
+            tn(
+                jnp.concatenate([b, b_got], axis=0),
+                jnp.concatenate([sh.own(a, 1), sh.own(a_got, 1)], axis=0),
+            )
+            for a, a_got, b, b_got in (
+                (mixed_low, mixed_got, d_attn, d_attn_got), (hidden, hidden_got, dq, dq_got)
+            )
+        )
+        mine = sh.halve_cols(go, gq)
+
+        d_hid = hidden_grads(
+            place, dkv.reshape(2 * D, W), key_proj, other_k, value_proj, other_v, C, R
+        )
         got_x, d_hid, mine, ffn = lax.optimization_barrier((got_x, d_hid, mine, ffn))
         ffn = lax.all_gather(ffn, "ctx", axis=0, tiled=False)
         whole = (keep.astype(F32) + got_x.astype(F32)).astype(BF)
-
-    grads = jnp.concatenate([whole, mine], axis=1)
-    grads = grads.reshape((2,) * (sh.bits - 1) + (-1, grads.shape[1]))
-    for k, other in zip(range(1, sh.bits), list(range(2, sh.bits)) + [1]):
-        grads = sh.halve(grads, k, grads.ndim - 3)
-        d_hid = sh.halve(d_hid, other, d_hid.ndim - 3 - (1 if other > 1 else 0))
-        grads, d_hid = lax.optimization_barrier((grads, d_hid))
-    for k in reversed(range(1, sh.bits)):
-        grads = sh.double(grads, k, grads.ndim - 2)
-        if sh.pair and k == 2:
-            gi, gu = ffn_final(ffn, inner_bias.shape[0] * 2, D)
-            gi, gu, grads = lax.optimization_barrier((gi, gu, grads))
-    input_grad = d_res1 + nt(dq, q_full) + d_hid.astype(F32)
-    if not sh.pair:
-        gi, gu = (a.astype(F32) for a in ffn)
-    grads = grads.reshape(dn, -1)
-    low, high = sh.order(grads, sh.flip(grads, 0), sh.bit(0))
-    gk, gv = low[:, :D].astype(F32), high[:, :D].astype(F32)
-    gp = jnp.concatenate([a[:, D : D + D // 2] for a in (low, high)], axis=1).astype(F32)
-    go, gq = low[:, half:].astype(F32), high[:, half:].astype(F32)
-    s = jnp.transpose(low[:, D + D // 2 : half].astype(F32))
+        grads = jnp.concatenate([whole, mine], axis=0)
+        grads = grads.reshape((2,) * (sh.bits - 1) + (-1, dn))
+        d_hid = sh.spread(d_hid)
+        for k in range(1, sh.bits):
+            grads = sh.halve(grads, k, grads.ndim - 3)
+            d_hid = sh.halve(d_hid, k - 1, d_hid.ndim - 3)
+            grads, d_hid = lax.optimization_barrier((grads, d_hid))
+        n = grads.shape[0]
+        cut = (n // 2 + 15) // 16 * 16
+        one, two = grads[:cut], grads[cut:]
+        highs = list(reversed(range(2, sh.bits)))
+        for i, (k, other) in enumerate(zip(highs + [1], [1] + highs)):
+            one = sh.double(one, k, one.ndim - 2)
+            two = sh.double(two, other, 0 if i == 0 else i - 1)
+            if i == 0:
+                d_hid = sh.halve(d_hid, sh.bits - 1, d_hid.ndim - 3)
+            if i == 0:
+                one, two, d_hid, ffn = lax.optimization_barrier((one, two, d_hid, ffn))
+            if i == 1:
+                gi, gu = ffn_final(ffn, inner_bias.shape[0] * 2, D)
+                one, two, gi, gu, d_hid = lax.optimization_barrier((one, two, gi, gu, d_hid))
+                input_grad = input_grads(place, d_res1, dq, query_proj, other_q, d_hid)
+        one, two, input_grad = lax.optimization_barrier((one, two, input_grad))
+        one, two = one.reshape(-1, dn), two.reshape(-1, dn)
+        gk, gv, gp, go, gq, s = grad_final(
+            place, one, two, sh.flip(one, 0), sh.flip(two, 0), D, C // 2
+        )
+        s = unpack_rows(s)
+    else:
+        dkv = dkv.reshape(2 * D, W)
+        gkv, gp = (
+            lax.dot_general(a, b, (((0,), (1,)), ((), ())), preferred_element_type=F32)
+            for a, b in ((x_win, dkv), (sinus, d_table))
+        )
+        d_hid = tn(dkv[:D], jnp.transpose(k_full)) + tn(dkv[D:], jnp.transpose(v_full))
+        d_hid = d_hid.astype(BF)
+        below = (C - 1 - R) * T
+        d_hid = jnp.pad(d_hid, ((below, (C - 1) * T + L - below - W), (0, 0)))
+        d_hid = lax.dynamic_slice_in_dim(d_hid, (C - 1 - ctx) * T, L, 0)
+        d_hid = lax.psum_scatter(d_hid, "ctx", scatter_dimension=0, tiled=True)
+        input_grad = d_res1 + nt(dq, q_full) + d_hid.astype(F32)
+        s = jnp.concatenate([att_vec, vec_a, vec_b], axis=0)
+        sums = [
+            gkv, gp, tn(mixed_low, d_attn), tn(hidden, dq), tn(normed_low, d_inner),
+            tn(activ_low, d_outer), jnp.transpose(s),
+        ]
+        sums = [
+            lax.psum_scatter(a.astype(BF), "fsdp", scatter_dimension=0, tiled=True) for a in sums
+        ]
+        gkv, gp, go, gq, gi, gu, s = (a.astype(F32) for a in lax.psum(sums, "ctx"))
+        gk, gv, s = gkv[:, :D], gkv[:, D:], jnp.transpose(s)
+        s = [s[i] for i in (19, 0, 1, 2, 18, 16, 17, 10, 8, 9)] + [s[3:5], s[20:24].reshape(-1)]
     return (
         outcome.astype(BF)[None],
         input_grad[None],
         gq,
         gk,
         gv,
-        s[19],
         s[0],
         s[1],
         s[2],
-        s[3:5],
+        s[3],
+        s[10],
         gp,
         go,
-        s[18],
-        s[16],
-        s[17],
+        s[4],
+        s[5],
+        s[6],
         gi,
-        s[20:24].reshape(-1),
+        s[11],
         gu,
-        s[10],
+        s[7],
         s[8],
         s[9],
     )

time: 401 us -> 361 us (0.900); the launches traced: 396 us -> 360 us
  Pallas kernels: 72.1 us -> 105 us
  waiting for transfers between devices: 160 us -> 130 us
  matrix products: 42.8 us -> 13.8 us
  local copies, waits for them, and re-layouts: 28.3 us -> 16.4 us
    pallas_call x0 -> x5, Pallas kernels: none -> 38.3 us  [the longest x1 16.5 us: key_grads(): pl.pallas_call(kernel, grid=(6,), in_specs=[pl.BlockSpec((1, h, W), lambd...]
    reduce_scatter x1, waiting for transfers between devices: 21.3 us -> 3.53 us  [per_device(): ffn = lax.psum_scatter(ffn, 'ctx', scatter_dimension=0, tiled=False)]
    dot_general x3 -> x0, matrix products: 16.4 us -> none  [the longest x2 15.8 us: per_device(): lax.dot_general(a, b, (((0,), (1,)), ((), ())), preferred_element_type=F32)]
    dot_general x4 -> x2, matrix products: 12.3 us -> 0.79 us  [tn(): lax.dot_general(a, b, (((0,), (0,)), ((), ())), preferred_element_type=F32)]
    ppermute x27 -> x30, waiting for transfers between devices: 98.6 us -> 89.9 us  [flip(): return lax.ppermute(a, 'ctx', [(i, i ^ 1 << k) for i in range(self.count)])]
    unnamed x99 -> x72, local copies, waits for them, and re-layouts: 12.5 us -> 6.49 us
    convert_element_type x4 -> x0, other arithmetic: 4.51 us -> none  [the longest x1 1.61 us: per_device(): go, gq = (low[:, half:].astype(F32), high[:, half:].astype(F32))]
    ppermute x27 -> x30, starting transfers between devices: 17 us -> 18.7 us  [flip(): return lax.ppermute(a, 'ctx', [(i, i ^ 1 << k) for i in range(self.count)])]
  transfers between devices with their start and end apart: 45 -> 48, of which waited for: 19 -> 25; matrix products, arithmetic and copies ran while one was open for 19% -> 15% of each run, Pallas kernels for 8% -> 22%
where the time goes in v4:
time: 361 us; the launch traced here: 360 us
  waiting for transfers between devices  130 us (36%)
  Pallas kernels  105 us (29%)
  starting transfers between devices  47.5 us (13%)
  other arithmetic  31.3 us (9%)
  local copies, waits for them, and re-layouts  16.4 us (5%)
  between operations  15 us (4%)
  matrix products  13.8 us (4%)
    ppermute x30, waiting for transfers between devices, flip(): return lax.ppermute(a, 'ctx', [(i, i ^ 1 << k) for i in range(self.count)])  89.9 us
    ppermute x12, waiting for transfers between devices, trade(): return lax.ppermute(a, 'fsdp', self.swap)  29.5 us
    ppermute x30, starting transfers between devices, flip(): return lax.ppermute(a, 'ctx', [(i, i ^ 1 << k) for i in range(self.count)])  18.7 us
    pallas_call x1, Pallas kernels, att_bwd(): pl.pallas_call(att_bwd_kernel, grid=(D // 128,), in_specs=[col(T), col(16...  17.1 us
    pallas_call x1, Pallas kernels, key_grads(): pl.pallas_call(kernel, grid=(6,), in_specs=[pl.BlockSpec((1, h, W), lambd...  16.5 us
    ppermute x12, starting transfers between devices, trade(): return lax.ppermute(a, 'fsdp', self.swap)  16.3 us
    pallas_call x1, Pallas kernels, att_fwd(): pl.pallas_call(att_fwd_kernel, grid=(D // 128,), in_specs=[col(T), col(16...  16 us
    pallas_call x1, Pallas kernels, ffn_bwd(): pl.pallas_call(kernel, grid_spec=pltpu.PrefetchScalarGridSpec(num_scalar_...  15.6 us
  transfers between devices with their start and end apart: 48, of which 25 were waited for; matrix products, arithmetic and copies ran while one was open for 15% of the time, Pallas kernels for 22%

profile of v4, /device:TPU:0, one launch (start us, length us, event | category | flops | bytes accessed | tf_op | source)
XLA Modules:
  0.0 359.7 jit_solution(5907427181508223419)
XLA Ops:
  8.8 2.9 collective-permute-start.3
  13.8 1.6 pad_maximum_fusion.12
  16.9 2.2 constant_dynamic-update-slice_fusion.1
  24.0 1.7 select_bitcast_fusion.11
  28.7 5.3 %collective-permute-start.5 = (bf16[2,128,896]{2,1,0:T(8,128)(2,1)}, bf16[2,128,896]{2,1,0:T(8,128)(2,1)}, u32[]{:S(2)}, u32[]{:S(2)}) collective-permute-start(bf16[2,128,896]{2,1,0:T(8,128)(2,1)} %get-tuple-element.206), channel_id=1, source_target_pairs={{0,8},{2,10},{4,12},{6,14},{8,16},{10,18},{12,20},{14,22},{16,24},... | collective-permute-start | bytes 1376264 | tf_op jit(solution)/shard_map/ppermute | solution.py:773
  34.8 1.6 collective-permute-start.1
  37.1 3.7 %collective-permute-done.7 = bf16[2,128,896]{2,1,0:T(8,128)(2,1)} collective-permute-done((bf16[2,128,896]{2,1,0:T(8,128)(2,1)}, bf16[2,128,896]{2,1,0:T(8,128)(2,1)}, u32[]{:S(2)}, u32[]{:S(2)}) %collective-permute-start.7) | collective-permute-done | bytes 458784 | tf_op jit(solution)/shard_map/ppermute | solution.py:774
  42.1 4.6 %collective-permute-start.6 = (bf16[2,128,896]{2,1,0:T(8,128)(2,1)}, bf16[2,128,896]{2,1,0:T(8,128)(2,1)S(1)}, u32[]{:S(2)}, u32[]{:S(2)}) collective-permute-start(bf16[2,128,896]{2,1,0:T(8,128)(2,1)} %collective-permute-done.5), channel_id=1, source_target_pairs={{0,8},{2,10},{4,12},{6,14},{8,16},{10,18},{12,20},{14,22},{16,24},... | collective-permute-start | bytes 1376264 | tf_op jit(solution)/shard_map/ppermute | solution.py:773
  50.8 2.4 collective-permute-done.8
  54.7 2.5 collective-permute-done.2.refs_1_
  58.4 1.6 collective-permute-start.11
  68.7 4.3 %convolution_convert_fusion.t_ref = bf16[2304,768]{1,0:T(8,128)(2,1)} fusion(bf16[2304,768]{1,0:T(8,128)(2,1)S(1)} %pad_maximum_fusion.s_ref, bf16[384,768]{1,0:T(8,128)(2,1)S(1)} %get-tuple-element.190, bf16[384,768]{1,0:T(8,128)(2,1)S(1)} %get-tuple-element.189), kind=kOutput, calls=%fused_computation.2 | convolution fusion | flops 2722037760 | bytes 8257536 | tf_op jit(solution)/shard_map/dot_general | solution.py:22
  75.2 7.6 %fusion.k_ref.v_ref = bf16[2176,1536]{1,0:T(8,128)(2,1)} fusion(bf16[2176,768]{1,0:T(8,128)(2,1)S(1)} %bitcast.165, f32[1536]{0:T(1024)S(1)} %concatenate.54, bf16[384,1536]{1,0:T(8,128)(2,1)S(1)} %get-tuple-element.184, bf16[384,1536]{1,0:T(8,128)(2,1)S(1)} %get-tuple-element.183), kind=kOutput, calls=%fused_computation.1 | convolution fusion | flops 5145231360 | bytes 12392448 | tf_op jit(solution)/shard_map/dot_general | solution.py:22
  82.7 3.4 collective-permute-done.10.refs_9_
  88.2 16.0 %att_fwd.1 = (f32[128,768]{1,0:T(8,128)}, bf16[12,128,2176]{2,1,0:T(8,128)(2,1)}) custom-call(f32[128,768]{1,0:T(8,128)} %convolution_bitcast_fusion.q_ref, f32[16,768]{1,0:T(8,128)} %pad_maximum_fusion.15.v_rows.v_ref, f32[128,128]{1,0:T(8,128)} %and_select_fusion.pen_ref, f32[128,128]{1,0:T(8,128)} %broadcast_in_dim.83.kind_ref, ...), custom_call_target="tpu_custom_call" | custom-call | flops 13690208256 | bytes 16711680 | tf_op jit(solution)/shard_map/att_fwd/pallas_call | solution.py:154
  107.0 2.1 collective-permute-done.18.refs_2_
  109.1 1.6 collective-permute-start.24
  112.4 10.3 %ffn_fwd.1 = (bf16[128,768]{1,0:T(8,128)(2,1)}, bf16[128,3072]{1,0:T(8,128)(2,1)}, f32[128,3072]{1,0:T(8,128)}, bf16[128,768]{1,0:T(8,128)(2,1)}, f32[128,768]{1...) custom-call(s32[4]{0:T(128)} %pad_add_fusion.s_ref, ...), custom_call_target="tpu_custom_call" | custom-call | flops 1207959552 | bytes 9437184 | tf_op jit(solution)/shard_map/ffn_fwd/pallas_call | solution.py:414
  122.7 1.7 collective-permute-start.23
  124.4 5.0 %collective-permute-done.23.dog_ref = bf16[128,768]{1,0:T(8,128)(2,1)S(1)} collective-permute-done((bf16[128,768]{1,0:T(8,128)(2,1)}, bf16[128,768]{1,0:T(8,128)(2,1)S(1)}, u32[]{:S(2)}, u32[]{:S(2)}) %collective-permute-start.23) | collective-permute-done | bytes 196640 | tf_op jit(solution)/shard_map/ppermute | solution.py:740
  130.1 15.6 %ffn_bwd.1 = (bf16[16,384,384]{2,1,0:T(8,128)(2,1)}, f32[128,768]{1,0:T(8,128)}, bf16[128,768]{1,0:T(8,128)(2,1)}, bf16[128,768]{1,0:T(8,128)(2,1)}, f32[8,768]{1,0:T(8,128)}) custom-call(s32[4]{0:T(128)} %pad_add_fusion.s_ref, f32[128,3072]{1,0:T(8,128)} %get-tuple-element.117.pre_ref, bf16[128,3072]{1,0:T(8,128)(2,1)} %get-tuple-element.118.act_ref, ...), custom_call_target="tpu_custom_call" | custom-call | flops 4227858432 | bytes 14155776 | tf_op jit(solution)/shard_map/ffn_bwd/pallas_call | solution.py:510
  145.7 17.1 %att_bwd.1 = (bf16[128,768]{1,0:T(8,128)(2,1)}, f32[8,768]{1,0:T(8,128)}, bf16[2,768,2176]{2,1,0:T(8,128)(2,1)}, bf16[768,2304]{1,0:T(8,128)(2,1)}) custom-call(f32[128,768]{1,0:T(8,128)} %convolution_bitcast_fusion.q_ref, f32[16,768]{1,0:T(8,128)} %pad_maximum_fusion.15.v_rows.v_ref, f32[128,128]{1,0:T(8,128)} %broadcast_in_dim.83.kind_ref, ...), custom_call_target="tpu_custom_call" | custom-call | flops 1048576 | bytes 1048576 | tf_op jit(solution)/shard_map/att_bwd/pallas_call | solution.py:180
  162.8 16.5 %key_grads.1 = bf16[2,1216,768]{2,1,0:T(8,128)(2,1)} custom-call(bf16[2,768,2176]{2,1,0:T(8,128)(2,1)} %get-tuple-element.132.kv_ref, bf16[768,2304]{1,0:T(8,128)(2,1)} %get-tuple-element.128.t_ref, bf16[2176,768]{1,0:T(8,128)(2,1)} %bitcast.166, bf16[2304,768]{1,0:T(8,128)(2,1)} %copy-done.1, f32[8,768]{1,0:T(8,128)} %get-tuple-element.129.refs_0_, ...), custom_call_target="tpu_custom_call" | custom-call | flops 1048576 | bytes 1048576 | tf_op jit(solution)/shard_map/key_grads/pallas_call | solution.py:562
  179.3 1.7 dynamic-slice_bitcast_fusion
  181.2 1.6 collective-permute-start.28
  184.3 4.7 %collective-permute-done.28 = bf16[128,768]{1,0:T(8,128)(2,1)S(1)} collective-permute-done((bf16[128,768]{1,0:T(8,128)(2,1)S(1)}, bf16[128,768]{1,0:T(8,128)(2,1)S(1)}, u32[]{:S(2)}, u32[]{:S(2)}) %collective-permute-start.28) | collective-permute-done | bytes 196640 | tf_op jit(solution)/shard_map/ppermute | solution.py:740
  189.4 3.4 collective-permute-done.29
  193.2 2.1 fusion.1
  195.5 1.6 collective-permute-start.27
  197.3 11.0 %hidden_grads.1 = bf16[16,768,128]{2,1,0:T(8,128)(2,1)} custom-call(s32[4]{0:T(128)} %pad_add_fusion.s_ref, bf16[1536,2176]{1,0:T(8,128)(2,1)} %bitcast.161, bf16[1536,2176]{1,0:T(8,128)(2,1)} %bitcast.162, bf16[384,768]{1,0:T(8,128)(2,1)} %k0.1, bf16[384,768]{1,0:T(8,128)(2,1)} %copy-done.3, bf16[384,768]{1,0:T(8,128)(2,1)} %v0.1, bf16[384,768]{1,0:T(8,128)(2,1)} %copy-done.4), custom_call_target="tpu_custom_call" | custom-call | flops 4831838208 | bytes 26738688 | tf_op jit(solution)/shard_map/hidden_grads/pallas_call | solution.py:604
  208.2 10.5 %collective-permute-done.27 = bf16[1216,384]{1,0:T(8,128)(2,1)} collective-permute-done((bf16[1216,384]{1,0:T(8,128)(2,1)S(1)}, bf16[1216,384]{1,0:T(8,128)(2,1)}, u32[]{:S(2)}, u32[]{:S(2)}) %collective-permute-start.27) | collective-permute-done | bytes 933920 | tf_op jit(solution)/shard_map/ppermute | solution.py:740
  218.7 3.5 reduce-scatter.2.cloned.1.call-done
  222.3 2.2 constant_dynamic-slice_fusion.2
  227.5 21.8 %collective-permute-done.31 = bf16[2,2,248,384]{3,2,0,1:T(8,128)(2,1)S(1)} collective-permute-done((bf16[2,2,248,384]{3,2,0,1:T(8,128)(2,1)S(1)}, bf16[2,2,248,384]{3,2,0,1:T(8,128)(2,1)S(1)}, u32[]{:S(2)}, u32[]{:S(2)}) %collective-permute-start.31) | collective-permute-done | bytes 761888 | tf_op jit(solution)/shard_map/ppermute | solution.py:737
  252.4 18.4 %collective-permute-done.33 = bf16[2,248,384]{2,1,0:T(8,128)(2,1)} collective-permute-done((bf16[2,248,384]{2,1,0:T(8,128)(2,1)S(1)}, bf16[2,248,384]{2,1,0:T(8,128)(2,1)}, u32[]{:S(2)}, u32[]{:S(2)}) %collective-permute-start.33) | collective-permute-done | bytes 380960 | tf_op jit(solution)/shard_map/ppermute | solution.py:737
  271.9 10.0 %collective-permute-done.34 = bf16[2,2,768,128]{3,2,0,1:T(8,128)(2,1)} collective-permute-done((bf16[2,2,768,128]{3,2,0,1:T(8,128)(2,1)S(1)}, bf16[2,2,768,128]{3,2,0,1:T(8,128)(2,1)}, u32[]{:S(2)}, u32[]{:S(2)}) %collective-permute-start.34) | collective-permute-done | bytes 786464 | tf_op jit(solution)/shard_map/ppermute | solution.py:737
  283.4 1.7 collective-permute-start.35
  285.9 13.0 %collective-permute-done.35 = bf16[248,384]{1,0:T(8,128)(2,1)S(1)} collective-permute-done((bf16[248,384]{1,0:T(8,128)(2,1)S(1)}, bf16[248,384]{1,0:T(8,128)(2,1)S(1)}, u32[]{:S(2)}, u32[]{:S(2)}) %collective-permute-start.35) | collective-permute-done | bytes 190496 | tf_op jit(solution)/shard_map/ppermute | solution.py:737
  299.0 3.5 collective-permute-done.36
  303.5 1.6 collective-permute-start.37
  307.3 8.1 %collective-permute-done.37 = bf16[128,384]{1,0:T(8,128)(2,1)S(1)} collective-permute-done((bf16[128,384]{1,0:T(8,128)(2,1)S(1)}, bf16[128,384]{1,0:T(8,128)(2,1)S(1)}, u32[]{:S(2)}, u32[]{:S(2)}) %collective-permute-start.37) | collective-permute-done | bytes 98336 | tf_op jit(solution)/shard_map/ppermute | solution.py:737
  315.5 2.9 collective-permute-done.39
  319.2 3.2 collective-permute-start.40
  322.3 6.6 %ffn_final.1 = (f32[384,3072]{1,0:T(8,128)}, f32[1536,768]{1,0:T(8,128)}) custom-call(bf16[16,384,384]{2,1,0:T(8,128)(2,1)} %bitcast.191), custom_call_target="tpu_custom_call" | custom-call | flops 8589934592 | bytes 18874368 | tf_op jit(solution)/shard_map/ffn_final/pallas_call | solution.py:239
  331.1 3.4 input_grads.1
  334.5 4.8 %collective-permute-done.43 = bf16[2,2,120,384]{3,2,1,0:T(8,128)(2,1)S(1)} collective-permute-done((bf16[2,2,120,384]{3,2,1,0:T(8,128)(2,1)S(1)}, bf16[2,2,120,384]{3,2,1,0:T(8,128)(2,1)S(1)}, u32[]{:S(2)}, u32[]{:S(2)}) %collective-permute-start.43) | collective-permute-done | bytes 368672 | tf_op jit(solution)/shard_map/ppermute | solution.py:737
  340.9 2.8 collective-permute-done.45.d_ref
  345.4 5.9 %grad_final.1 = (f32[384,768]{1,0:T(8,128)}, f32[384,768]{1,0:T(8,128)}, f32[384,768]{1,0:T(8,128)}, f32[384,768]{1,0:T(8,128)}, f32[384,768]{1,0:T(8,128)}, /*index=5*/f32[64,384]{1,0:T(8,128)}) custom-call(s32[4]{0:T(128)} %pad_add_fusion.s_ref, bf16[1024,384]{1,0:T(8,128)(2,1)} %bitcast.172, bf16[960,384]{1,0:T(8,128)(2,1)} %bitcast.174, ...), custom_call_target="tpu_custom_call" | custom-call | tf_op jit(solution)/shard_map/grad_final/pallas_call | solution.py:674
  (229 shorter events, 63.4 us)
Async XLA Ops:
  7.2 215.0 %reduce-scatter.2.cloned.1.call-start = ((), (), s32[]{:S(2)}) async-start(), calls=%async_computation.1 | async-start | bytes 5013504 | tf_op jit(solution)/shard_map/reduce_scatter | solution.py:965
  8.8 26.0 %collective-permute-start.3 = (f32[16,384]{1,0:T(8,128)}, f32[16,384]{1,0:T(8,128)}, u32[]{:S(2)}, u32[]{:S(2)}) collective-permute-start(f32[16,384]{1,0:T(8,128)} %pack_rows.1), channel_id=1, source_target_pairs={{0,1},{1,0},{2,3},{3,2},{4,5},{5,4},{6,7},{7,6},{8,9},{9,8},{10,11... | collective-permute-start | bytes 73736 | tf_op jit(solution)/shard_map/ppermute | solution.py:740
  15.4 8.5 %collective-permute-start.4 = (bf16[128,896]{1,0:T(8,128)(2,1)}, bf16[128,896]{1,0:T(8,128)(2,1)}, u32[]{:S(2)}, u32[]{:S(2)}) collective-permute-start(bf16[128,896]{1,0:T(8,128)(2,1)} %pad_maximum_fusion.12), channel_id=1, source_target_pairs={{0,4},{2,6},{4,0},{6,2},{8,12},{10,14},{12,8},{14,10},{16,20},{18,... | collective-permute-start | bytes 688136 | tf_op jit(solution)/shard_map/ppermute | solution.py:737
  20.1 37.1 %collective-permute-start = (bf16[384,768]{1,0:T(8,128)(2,1)}, bf16[384,768]{1,0:T(8,128)(2,1)}, u32[]{:S(2)}, u32[]{:S(2)}) collective-permute-start(bf16[384,768]{1,0:T(8,128)(2,1)} %get-tuple-element.202), channel_id=1, source_target_pairs={{0,1},{1,0},{2,3},{3,2},{4,5},{5,4},{6,7},{7,6},{8,9},{9,8},{10,11... | collective-permute-start | bytes 1769480 | tf_op jit(solution)/shard_map/ppermute | solution.py:740
  27.4 13.4 %collective-permute-start.7 = (bf16[2,128,896]{2,1,0:T(8,128)(2,1)}, bf16[2,128,896]{2,1,0:T(8,128)(2,1)}, u32[]{:S(2)}, u32[]{:S(2)}) collective-permute-start(bf16[2,128,896]{2,1,0:T(8,128)(2,1)} %get-tuple-element.206), channel_id=1, source_target_pairs={{8,0},{10,2},{12,4},{14,6},{16,8},{18,10},{20,12},{22,14},{24,16},... | collective-permute-start | bytes 1376264 | tf_op jit(solution)/shard_map/ppermute | solution.py:774
  28.7 13.4 %collective-permute-start.5 = (bf16[2,128,896]{2,1,0:T(8,128)(2,1)}, bf16[2,128,896]{2,1,0:T(8,128)(2,1)}, u32[]{:S(2)}, u32[]{:S(2)}) collective-permute-start(bf16[2,128,896]{2,1,0:T(8,128)(2,1)} %get-tuple-element.206), channel_id=1, source_target_pairs={{0,8},{2,10},{4,12},{6,14},{8,16},{10,18},{12,20},{14,22},{16,24},... | collective-permute-start | bytes 1376264 | tf_op jit(solution)/shard_map/ppermute | solution.py:773
  34.7 12.0 %collective-permute-start.14 = (bf16[1,2,128,896]{3,2,1,0:T(8,128)(2,1)}, bf16[1,2,128,896]{3,2,1,0:T(8,128)(2,1)}, u32[]{:S(2)}, u32[]{:S(2)}) collective-permute-start(bf16[1,2,128,896]{3,2,1,0:T(8,128)(2,1)} %get-tuple-element.205), channel_id=1, source_target_pairs={{0,2},{2,0},{4,6},{6,4},{8,10},{10,8},{12,14},{14,12},{16,18},{18,... | collective-permute-start | bytes 1376264 | tf_op jit(solution)/shard_map/ppermute | solution.py:737
  34.8 22.4 %collective-permute-start.1 = (bf16[384,768]{1,0:T(8,128)(2,1)}, bf16[384,768]{1,0:T(8,128)(2,1)S(1)}, u32[]{:S(2)}, u32[]{:S(2)}) collective-permute-start(bf16[384,768]{1,0:T(8,128)(2,1)} %get-tuple-element.204), channel_id=1, source_target_pairs={{0,1},{1,0},{2,3},{3,2},{4,5},{5,4},{6,7},{7,6},{8,9},{9,8},{10,11... | collective-permute-start | bytes 1769480 | tf_op jit(solution)/shard_map/ppermute | solution.py:740
  40.8 12.4 %collective-permute-start.8 = (bf16[2,128,896]{2,1,0:T(8,128)(2,1)}, bf16[2,128,896]{2,1,0:T(8,128)(2,1)S(1)}, u32[]{:S(2)}, u32[]{:S(2)}) collective-permute-start(bf16[2,128,896]{2,1,0:T(8,128)(2,1)} %collective-permute-done.7), channel_id=1, source_target_pairs={{8,0},{10,2},{12,4},{14,6},{16,8},{18,10},{20,12},{22,14},{24,16},... | collective-permute-start | bytes 1376264 | tf_op jit(solution)/shard_map/ppermute | solution.py:774
  42.1 12.4 %collective-permute-start.6 = (bf16[2,128,896]{2,1,0:T(8,128)(2,1)}, bf16[2,128,896]{2,1,0:T(8,128)(2,1)S(1)}, u32[]{:S(2)}, u32[]{:S(2)}) collective-permute-start(bf16[2,128,896]{2,1,0:T(8,128)(2,1)} %collective-permute-done.5), channel_id=1, source_target_pairs={{0,8},{2,10},{4,12},{6,14},{8,16},{10,18},{12,20},{14,22},{16,24},... | collective-permute-start | bytes 1376264 | tf_op jit(solution)/shard_map/ppermute | solution.py:773
  46.7 10.5 %collective-permute-start.2 = (bf16[192,768]{1,0:T(8,128)(2,1)}, bf16[192,768]{1,0:T(8,128)(2,1)}, u32[]{:S(2)}, u32[]{:S(2)}) collective-permute-start(bf16[192,768]{1,0:T(8,128)(2,1)} %constant_dynamic-slice_fusion.10), channel_id=1, source_target_pairs={{0,1},{1,0},{2,3},{3,2},{4,5},{5,4},{6,7},{7,6},{8,9},{9,8},{10,11... | collective-permute-start | bytes 884744 | tf_op jit(solution)/shard_map/ppermute | solution.py:740
  53.2 9.1 %collective-permute-start.13 = (bf16[2,2,128,896]{3,2,1,0:T(8,128)(2,1)S(1)}, bf16[2,2,128,896]{3,2,1,0:T(8,128)(2,1)S(1)}, u32[]{:S(2)}, u32[]{:S(2)}) collective-permute-start(bf16[2,2,128,896]{3,2,1,0:T(8,128)(2,1)S(1)} %pad_maximum_fusion.6), channel_id=1, source_target_pairs={{0,2},{2,0},{4,6},{6,4},{8,10},{10,8},{12,14},{14,12},{16,18},{18,... | collective-permute-start | bytes 2752520 | tf_op jit(solution)/shard_map/ppermute | solution.py:737
  54.6 18.4 %collective-permute-start.12 = (bf16[2,2,128,896]{3,2,1,0:T(8,128)(2,1)S(1)}, bf16[2,2,128,896]{3,2,1,0:T(8,128)(2,1)S(1)}, u32[]{:S(2)}, u32[]{:S(2)}) collective-permute-start(bf16[2,2,128,896]{3,2,1,0:T(8,128)(2,1)S(1)} %pad_maximum_fusion.5), channel_id=1, source_target_pairs={{0,2},{2,0},{4,6},{6,4},{8,10},{10,8},{12,14},{14,12},{16,18},{18,... | collective-permute-start | bytes 2752520 | tf_op jit(solution)/shard_map/ppermute | solution.py:737
  58.4 16.4 %collective-permute-start.11 = (bf16[96,3072]{1,0:T(8,128)(2,1)S(1)}, bf16[96,3072]{1,0:T(8,128)(2,1)}, u32[]{:S(2)}, u32[]{:S(2)}) collective-permute-start(bf16[96,3072]{1,0:T(8,128)(2,1)S(1)} %constant_dynamic-slice_fusion.8), channel_id=1, source_target_pairs={{0,1},{1,0},{2,3},{3,2},{4,5},{5,4},{6,7},{7,6},{8,9},{9,8},{10,11... | collective-permute-start | bytes 1769480 | tf_op jit(solution)/shard_map/ppermute | solution.py:740
  61.0 25.1 %collective-permute-start.10 = (bf16[384,768]{1,0:T(8,128)(2,1)S(1)}, bf16[384,768]{1,0:T(8,128)(2,1)}, u32[]{:S(2)}, u32[]{:S(2)}) collective-permute-start(bf16[384,768]{1,0:T(8,128)(2,1)S(1)} %constant_dynamic-slice_fusion.9), channel_id=1, source_target_pairs={{0,1},{1,0},{2,3},{3,2},{4,5},{5,4},{6,7},{7,6},{8,9},{9,8},{10,11... | collective-permute-start | bytes 1769480 | tf_op jit(solution)/shard_map/ppermute | solution.py:740
  61.6 2.6 collective-permute-start.9
  62.3 2.4 collective-permute-start.15
  74.8 29.4 %collective-permute-start.16 = (bf16[96,3072]{1,0:T(8,128)(2,1)}, bf16[96,3072]{1,0:T(8,128)(2,1)S(1)}, u32[]{:S(2)}, u32[]{:S(2)}) collective-permute-start(bf16[96,3072]{1,0:T(8,128)(2,1)} %collective-permute-done.11.refs_4_), channel_id=1, source_target_pairs={{0,4},{2,6},{4,0},{6,2},{8,12},{10,14},{12,8},{14,10},{16,20},{18,... | collective-permute-start | bytes 1769480 | tf_op jit(solution)/shard_map/ppermute | solution.py:737
  86.1 18.1 %collective-permute-start.17 = (bf16[384,768]{1,0:T(8,128)(2,1)}, bf16[384,768]{1,0:T(8,128)(2,1)S(1)}, u32[]{:S(2)}, u32[]{:S(2)}) collective-permute-start(bf16[384,768]{1,0:T(8,128)(2,1)} %collective-permute-done.10.refs_9_), channel_id=1, source_target_pairs={{0,4},{2,6},{4,0},{6,2},{8,12},{10,14},{12,8},{14,10},{16,20},{18,... | collective-permute-start | bytes 1769480 | tf_op jit(solution)/shard_map/ppermute | solution.py:737
  104.2 6.5 %collective-permute-start.19 = (bf16[96,3072]{1,0:T(8,128)(2,1)}, bf16[96,3072]{1,0:T(8,128)(2,1)S(1)}, u32[]{:S(2)}, u32[]{:S(2)}) collective-permute-start(bf16[96,3072]{1,0:T(8,128)(2,1)} %collective-permute-done.11.refs_4_), channel_id=1, source_target_pairs={{0,2},{2,0},{4,6},{6,4},{8,10},{10,8},{12,14},{14,12},{16,18},{18,... | collective-permute-start | bytes 1769480 | tf_op jit(solution)/shard_map/ppermute | solution.py:737
  104.3 6.8 %collective-permute-start.20 = (bf16[96,3072]{1,0:T(8,128)(2,1)S(1)}, bf16[96,3072]{1,0:T(8,128)(2,1)S(1)}, u32[]{:S(2)}, u32[]{:S(2)}) collective-permute-start(bf16[96,3072]{1,0:T(8,128)(2,1)S(1)} %collective-permute-done.16.refs_5_), channel_id=1, source_target_pairs={{0,2},{2,0},{4,6},{6,4},{8,10},{10,8},{12,14},{14,12},{16,18},{18,... | collective-permute-start | bytes 1769480 | tf_op jit(solution)/shard_map/ppermute | solution.py:737
  104.8 6.3 %collective-permute-start.21 = (bf16[384,768]{1,0:T(8,128)(2,1)}, bf16[384,768]{1,0:T(8,128)(2,1)S(1)}, u32[]{:S(2)}, u32[]{:S(2)}) collective-permute-start(bf16[384,768]{1,0:T(8,128)(2,1)} %collective-permute-done.10.refs_9_), channel_id=1, source_target_pairs={{0,2},{2,0},{4,6},{6,4},{8,10},{10,8},{12,14},{14,12},{16,18},{18,... | collective-permute-start | bytes 1769480 | tf_op jit(solution)/shard_map/ppermute | solution.py:737
  104.9 6.3 %collective-permute-start.22 = (bf16[384,768]{1,0:T(8,128)(2,1)S(1)}, bf16[384,768]{1,0:T(8,128)(2,1)S(1)}, u32[]{:S(2)}, u32[]{:S(2)}) collective-permute-start(bf16[384,768]{1,0:T(8,128)(2,1)S(1)} %collective-permute-done.17.refs_10_), channel_id=1, source_target_pairs={{0,2},{2,0},{4,6},{6,4},{8,10},{10,8},{12,14},{14,12},{16,18},{18,... | collective-permute-start | bytes 1769480 | tf_op jit(solution)/shard_map/ppermute | solution.py:737
  105.3 3.8 %collective-permute-start.18 = (bf16[192,768]{1,0:T(8,128)(2,1)}, bf16[192,768]{1,0:T(8,128)(2,1)S(1)}, u32[]{:S(2)}, u32[]{:S(2)}) collective-permute-start(bf16[192,768]{1,0:T(8,128)(2,1)} %collective-permute-done.2.refs_1_), channel_id=1, source_target_pairs={{0,2},{2,0},{4,6},{6,4},{8,10},{10,8},{12,14},{14,12},{16,18},{18,... | collective-permute-start | bytes 884744 | tf_op jit(solution)/shard_map/ppermute | solution.py:737
  109.1 15.3 %collective-permute-start.24 = (bf16[128,768]{1,0:T(8,128)(2,1)S(1)}, bf16[128,768]{1,0:T(8,128)(2,1)S(1)}, u32[]{:S(2)}, u32[]{:S(2)}) collective-permute-start(bf16[128,768]{1,0:T(8,128)(2,1)S(1)} %convert_element_type.167), channel_id=1, source_target_pairs={{0,1},{1,0},{2,3},{3,2},{4,5},{5,4},{6,7},{7,6},{8,9},{9,8},{10,11... | collective-permute-start | bytes 589832 | tf_op jit(solution)/shard_map/ppermute | solution.py:740
  110.8 13.6 %collective-permute-start.25 = (bf16[128,768]{1,0:T(8,128)(2,1)S(1)}, bf16[128,768]{1,0:T(8,128)(2,1)}, u32[]{:S(2)}, u32[]{:S(2)}) collective-permute-start(bf16[128,768]{1,0:T(8,128)(2,1)S(1)} %bitcast.178), channel_id=1, source_target_pairs={{0,1},{1,0},{2,3},{3,2},{4,5},{5,4},{6,7},{7,6},{8,9},{9,8},{10,11... | collective-permute-start | bytes 589832 | tf_op jit(solution)/shard_map/ppermute | solution.py:740
  122.7 6.7 %collective-permute-start.23 = (bf16[128,768]{1,0:T(8,128)(2,1)}, bf16[128,768]{1,0:T(8,128)(2,1)S(1)}, u32[]{:S(2)}, u32[]{:S(2)}) collective-permute-start(bf16[128,768]{1,0:T(8,128)(2,1)} %get-tuple-element.120.do_ref), channel_id=1, source_target_pairs={{0,1},{1,0},{2,3},{3,2},{4,5},{5,4},{6,7},{7,6},{8,9},{9,8},{10,11... | collective-permute-start | bytes 589832 | tf_op jit(solution)/shard_map/ppermute | solution.py:740
  145.7 173.5 %all-gather.3.cloned.1.call-start = ((), (), s32[]{:S(2)}) async-start(), calls=%async_computation.2 | async-start | bytes 5013504 | tf_op jit(solution)/shard_map/all_gather | solution.py:987
  181.0 12.2 %collective-permute-start.26 = (bf16[1216,768]{1,0:T(8,128)(2,1)S(1)}, bf16[1216,768]{1,0:T(8,128)(2,1)}, u32[]{:S(2)}, u32[]{:S(2)}) collective-permute-start(bf16[1216,768]{1,0:T(8,128)(2,1)S(1)} %dynamic-slice_bitcast_fusion), channel_id=1, source_target_pairs={{0,2},{2,0},{4,6},{6,4},{8,10},{10,8},{12,14},{14,12},{16,18},{18,... | collective-permute-start | bytes 5603336 | tf_op jit(solution)/shard_map/ppermute | solution.py:737
  181.2 7.8 %collective-permute-start.28 = (bf16[128,768]{1,0:T(8,128)(2,1)S(1)}, bf16[128,768]{1,0:T(8,128)(2,1)S(1)}, u32[]{:S(2)}, u32[]{:S(2)}) collective-permute-start(bf16[128,768]{1,0:T(8,128)(2,1)S(1)} %copy-done.29), channel_id=1, source_target_pairs={{0,1},{1,0},{2,3},{3,2},{4,5},{5,4},{6,7},{7,6},{8,9},{9,8},{10,11... | collective-permute-start | bytes 589832 | tf_op jit(solution)/shard_map/ppermute | solution.py:740
  182.8 9.9 %collective-permute-start.29 = (bf16[128,768]{1,0:T(8,128)(2,1)S(1)}, bf16[128,768]{1,0:T(8,128)(2,1)S(1)}, u32[]{:S(2)}, u32[]{:S(2)}) collective-permute-start(bf16[128,768]{1,0:T(8,128)(2,1)S(1)} %copy-done.30), channel_id=1, source_target_pairs={{0,1},{1,0},{2,3},{3,2},{4,5},{5,4},{6,7},{7,6},{8,9},{9,8},{10,11... | collective-permute-start | bytes 589832 | tf_op jit(solution)/shard_map/ppermute | solution.py:740
  193.1 4.0 %collective-permute-start.30 = (bf16[768,384]{1,0:T(8,128)(2,1)S(1)}, bf16[768,384]{1,0:T(8,128)(2,1)S(1)}, u32[]{:S(2)}, u32[]{:S(2)}) collective-permute-start(bf16[768,384]{1,0:T(8,128)(2,1)S(1)} %get-tuple-element.229), channel_id=1, source_target_pairs={{0,2},{2,0},{4,6},{6,4},{8,10},{10,8},{12,14},{14,12},{16,18},{18,... | collective-permute-start | bytes 1769480 | tf_op jit(solution)/shard_map/ppermute | solution.py:737
  195.5 23.2 %collective-permute-start.27 = (bf16[1216,384]{1,0:T(8,128)(2,1)S(1)}, bf16[1216,384]{1,0:T(8,128)(2,1)}, u32[]{:S(2)}, u32[]{:S(2)}) collective-permute-start(bf16[1216,384]{1,0:T(8,128)(2,1)S(1)} %broadcast_select_fusion.2), channel_id=1, source_target_pairs={{0,1},{1,0},{2,3},{3,2},{4,5},{5,4},{6,7},{7,6},{8,9},{9,8},{10,11... | collective-permute-start | bytes 2801672 | tf_op jit(solution)/shard_map/ppermute | solution.py:740
  224.5 25.0 %collective-permute-start.32 = (bf16[2,2,2,768,128]{4,3,0,1,2:T(8,128)(2,1)S(1)}, bf16[2,2,2,768,128]{4,3,0,1,2:T(8,128)(2,1)S(1)}, u32[]{:S(2)}, u32[]{:S(2)}) collective-permute-start(bf16[2,2,2,768,128]{4,3,0,1,2:T(8,128)(2,1)S(1)} %bitcast.185), channel_id=1, source_target_pairs={{0,2},{2,0},{4,6},{6,4},{8,10},{10,8},{12,14},{14,12},{16,18},{18,... | collective-permute-start | bytes 4718600 | tf_op jit(solution)/shard_map/ppermute | solution.py:737
  226.6 22.6 %collective-permute-start.31 = (bf16[2,2,248,384]{3,2,0,1:T(8,128)(2,1)S(1)}, bf16[2,2,248,384]{3,2,0,1:T(8,128)(2,1)S(1)}, u32[]{:S(2)}, u32[]{:S(2)}) collective-permute-start(bf16[2,2,248,384]{3,2,0,1:T(8,128)(2,1)S(1)} %bitcast.186), channel_id=1, source_target_pairs={{0,4},{2,6},{4,0},{6,2},{8,12},{10,14},{12,8},{14,10},{16,20},{18,... | collective-permute-start | bytes 2285576 | tf_op jit(solution)/shard_map/ppermute | solution.py:737
  250.0 32.0 %collective-permute-start.34 = (bf16[2,2,768,128]{3,2,0,1:T(8,128)(2,1)S(1)}, bf16[2,2,768,128]{3,2,0,1:T(8,128)(2,1)}, u32[]{:S(2)}, u32[]{:S(2)}) collective-permute-start(bf16[2,2,768,128]{3,2,0,1:T(8,128)(2,1)S(1)} %dynamic-slice_bitcast_fusion.1), channel_id=1, source_target_pairs={{0,4},{2,6},{4,0},{6,2},{8,12},{10,14},{12,8},{14,10},{16,20},{18,... | collective-permute-start | bytes 2359304 | tf_op jit(solution)/shard_map/ppermute | solution.py:737
  250.9 19.9 %collective-permute-start.33 = (bf16[2,248,384]{2,1,0:T(8,128)(2,1)S(1)}, bf16[2,248,384]{2,1,0:T(8,128)(2,1)}, u32[]{:S(2)}, u32[]{:S(2)}) collective-permute-start(bf16[2,248,384]{2,1,0:T(8,128)(2,1)S(1)} %dynamic-slice_bitcast_fusion.3), channel_id=1, source_target_pairs={{0,8},{2,10},{4,12},{6,14},{8,0},{10,2},{12,4},{14,6},{16,24},{18,... | collective-permute-start | bytes 1142792 | tf_op jit(solution)/shard_map/ppermute | solution.py:737
  283.4 15.6 %collective-permute-start.35 = (bf16[248,384]{1,0:T(8,128)(2,1)S(1)}, bf16[248,384]{1,0:T(8,128)(2,1)S(1)}, u32[]{:S(2)}, u32[]{:S(2)}) collective-permute-start(bf16[248,384]{1,0:T(8,128)(2,1)S(1)} %dynamic-slice_bitcast_fusion.5), channel_id=1, source_target_pairs={{0,16},{2,18},{4,20},{6,22},{8,24},{10,26},{12,28},{14,30},{16,0},... | collective-permute-start | bytes 571400 | tf_op jit(solution)/shard_map/ppermute | solution.py:737
  285.1 17.4 %collective-permute-start.36 = (bf16[2,768,128]{2,1,0:T(8,128)(2,1)S(1)}, bf16[2,768,128]{2,1,0:T(8,128)(2,1)S(1)}, u32[]{:S(2)}, u32[]{:S(2)}) collective-permute-start(bf16[2,768,128]{2,1,0:T(8,128)(2,1)S(1)} %dynamic-slice_bitcast_fusion.2), channel_id=1, source_target_pairs={{0,8},{2,10},{4,12},{6,14},{8,0},{10,2},{12,4},{14,6},{16,24},{18,... | collective-permute-start | bytes 1179656 | tf_op jit(solution)/shard_map/ppermute | solution.py:737
  302.6 4.6 %collective-permute-start.38 = (bf16[120,384]{1,0:T(8,128)(2,1)S(1)}, bf16[120,384]{1,0:T(8,128)(2,1)S(1)}, u32[]{:S(2)}, u32[]{:S(2)}) collective-permute-start(bf16[120,384]{1,0:T(8,128)(2,1)S(1)} %slice.51), channel_id=1, source_target_pairs={{0,4},{2,6},{4,0},{6,2},{8,12},{10,14},{12,8},{14,10},{16,20},{18,... | collective-permute-start | bytes 276488 | tf_op jit(solution)/shard_map/ppermute | solution.py:737
  303.5 11.9 %collective-permute-start.37 = (bf16[128,384]{1,0:T(8,128)(2,1)S(1)}, bf16[128,384]{1,0:T(8,128)(2,1)S(1)}, u32[]{:S(2)}, u32[]{:S(2)}) collective-permute-start(bf16[128,384]{1,0:T(8,128)(2,1)S(1)} %slice.50), channel_id=1, source_target_pairs={{0,16},{2,18},{4,20},{6,22},{8,24},{10,26},{12,28},{14,30},{16,0},... | collective-permute-start | bytes 294920 | tf_op jit(solution)/shard_map/ppermute | solution.py:737
  305.2 13.2 %collective-permute-start.39 = (bf16[768,128]{1,0:T(8,128)(2,1)S(1)}, bf16[768,128]{1,0:T(8,128)(2,1)S(1)}, u32[]{:S(2)}, u32[]{:S(2)}) collective-permute-start(bf16[768,128]{1,0:T(8,128)(2,1)S(1)} %dynamic-slice_bitcast_fusion.4), channel_id=1, source_target_pairs={{0,16},{2,18},{4,20},{6,22},{8,24},{10,26},{12,28},{14,30},{16,0},... | collective-permute-start | bytes 589832 | tf_op jit(solution)/shard_map/ppermute | solution.py:737
  319.2 10.4 %collective-permute-start.41 = (bf16[2,120,384]{2,1,0:T(8,128)(2,1)S(1)}, bf16[2,120,384]{2,1,0:T(8,128)(2,1)S(1)}, u32[]{:S(2)}, u32[]{:S(2)}) collective-permute-start(bf16[2,120,384]{2,1,0:T(8,128)(2,1)S(1)} %pad_maximum_fusion.14), channel_id=1, source_target_pairs={{0,16},{2,18},{4,20},{6,22},{8,24},{10,26},{12,28},{14,30},{16,0},... | collective-permute-start | bytes 552968 | tf_op jit(solution)/shard_map/ppermute | solution.py:737
  319.2 10.7 %collective-permute-start.40 = (bf16[2,128,384]{2,1,0:T(8,128)(2,1)S(1)}, bf16[2,128,384]{2,1,0:T(8,128)(2,1)S(1)}, u32[]{:S(2)}, u32[]{:S(2)}) collective-permute-start(bf16[2,128,384]{2,1,0:T(8,128)(2,1)S(1)} %pad_maximum_fusion.13), channel_id=1, source_target_pairs={{0,8},{2,10},{4,12},{6,14},{8,0},{10,2},{12,4},{14,6},{16,24},{18,... | collective-permute-start | bytes 589832 | tf_op jit(solution)/shard_map/ppermute | solution.py:737
  330.0 9.2 %collective-permute-start.43 = (bf16[2,2,120,384]{3,2,1,0:T(8,128)(2,1)S(1)}, bf16[2,2,120,384]{3,2,1,0:T(8,128)(2,1)S(1)}, u32[]{:S(2)}, u32[]{:S(2)}) collective-permute-start(bf16[2,2,120,384]{3,2,1,0:T(8,128)(2,1)S(1)} %pad_maximum_fusion.11), channel_id=1, source_target_pairs={{0,8},{2,10},{4,12},{6,14},{8,0},{10,2},{12,4},{14,6},{16,24},{18,... | collective-permute-start | bytes 1105928 | tf_op jit(solution)/shard_map/ppermute | solution.py:737
  330.1 9.9 %collective-permute-start.42 = (bf16[2,2,128,384]{3,2,0,1:T(8,128)(2,1)S(1)}, bf16[2,2,128,384]{3,2,0,1:T(8,128)(2,1)S(1)}, u32[]{:S(2)}, u32[]{:S(2)}) collective-permute-start(bf16[2,2,128,384]{3,2,0,1:T(8,128)(2,1)S(1)} %pad_maximum_fusion.10), channel_id=1, source_target_pairs={{0,4},{2,6},{4,0},{6,2},{8,12},{10,14},{12,8},{14,10},{16,20},{18,... | collective-permute-start | bytes 1179656 | tf_op jit(solution)/shard_map/ppermute | solution.py:737
  340.3 3.4 collective-permute-start.44
  340.4 3.3 collective-permute-start.45
  (36 other events, 153.6 us)
Sparse Core Ops, SparseCore 0:
  145.8 76.3 reduce-scatter.1
  224.8 74.6 all-gather.2

commit v5 on v4

--- a/solution.py
+++ b/solution.py
@@ -532,49 +532,55 @@
     )
 
 
-def key_grads(dkv, d_table, x_win, sinus, vectors):
+def key_grads(dkv, x_win):
     _, D, W = dkv.shape
-    WT = d_table.shape[1]
     h = D // 2
 
-    def kernel(kv_ref, t_ref, x_ref, s_ref, *refs):
+    def kernel(kv_ref, x_ref, out_ref):
+        out_ref[0] = nn(kv_ref[0], x_ref[...]).astype(BF)
+
+    return pl.pallas_call(
+        kernel,
+        grid=(4,),
+        in_specs=[
+            pl.BlockSpec((1, h, W), lambda i: (i // 2, i % 2, 0)),
+            pl.BlockSpec((W, D), lambda i: (0, 0)),
+        ],
+        out_specs=pl.BlockSpec((1, h, D), lambda i: (i // 2, i % 2, 0)),
+        out_shape=jax.ShapeDtypeStruct((2, D, D), BF),
+        compiler_params=pltpu.CompilerParams(vmem_limit_bytes=60 * 2**20),
+        cost_estimate=pl.CostEstimate(
+            flops=4 * D * D * W, bytes_accessed=6 * D * W, transcendentals=0
+        ),
+        name="key_grads",
+    )(dkv, x_win)
+
+
+def position_grads(d_table, sinus, vectors):
+    D, WT = d_table.shape
+    h = D // 2
+
+    def kernel(t_ref, s_ref, *refs):
         v_refs, out_ref = refs[:-1], refs[-1]
-        i = pl.program_id(0)
-        core, part = i // 3, i % 3
-        at = pl.ds(pl.multiple_of(part * h, h), h)
-
-        @pl.when(part < 2)
-        def _():
-            out_ref[core, at, :] = nn(kv_ref[0], x_ref[...]).astype(BF)
-
-        @pl.when(part == 2)
-        def _():
-            out_ref[core, at, :] = nn(t_ref[...], s_ref[...]).astype(BF)
-
-        @pl.when(i == 0)
-        def _():
-            small = jnp.concatenate([r[...] for r in v_refs], axis=0)
-            pad = jnp.zeros((64 - small.shape[0], D), F32)
-            out_ref[0, 3 * h :, :] = jnp.concatenate([small, pad], axis=0).astype(BF)
-            out_ref[1, 3 * h :, :] = jnp.zeros((64, D), BF)
+        out_ref[0, :h, :] = nn(t_ref[...], s_ref[...]).astype(BF)
+        small = jnp.concatenate([r[...] for r in v_refs], axis=0)
+        small = jnp.concatenate([small, jnp.zeros((64 - small.shape[0], D), F32)], axis=0)
+        out_ref[0, h:, :] = jnp.where(pl.program_id(0) == 0, small, 0.0).astype(BF)
 
     whole = lambda *shape: pl.BlockSpec(shape, lambda i: (0,) * len(shape))
     return pl.pallas_call(
         kernel,
-        grid=(6,),
-        in_specs=[
-            pl.BlockSpec((1, h, W), lambda i: (i // 3, jnp.minimum(i % 3, 1), 0)),
-            pl.BlockSpec((h, WT), lambda i: (i // 3, 0)),
-            whole(W, D),
-            whole(WT, D),
-        ]
+        grid=(2,),
+        in_specs=[pl.BlockSpec((h, WT), lambda i: (i, 0)), whole(WT, D)]
         + [whole(8, D)] * len(vectors),
-        out_specs=whole(2, 3 * h + 64, D),
-        out_shape=jax.ShapeDtypeStruct((2, 3 * h + 64, D), BF),
+        out_specs=pl.BlockSpec((1, h + 64, D), lambda i: (i, 0, 0)),
+        out_shape=jax.ShapeDtypeStruct((2, h + 64, D), BF),
         compiler_params=pltpu.CompilerParams(vmem_limit_bytes=60 * 2**20),
-        cost_estimate=pl.CostEstimate(flops=2**20, bytes_accessed=2**20, transcendentals=0),
-        name="key_grads",
-    )(dkv, d_table, x_win, sinus, *vectors)
+        cost_estimate=pl.CostEstimate(
+            flops=2 * D * D * WT, bytes_accessed=4 * D * WT, transcendentals=0
+        ),
+        name="position_grads",
+    )(d_table, sinus, *vectors)
 
 
 def hidden_grads(place, dkv, k_own, k_other, v_own, v_other, count, reach):
@@ -611,9 +617,7 @@
         ),
         out_shape=jax.ShapeDtypeStruct((count, D, T), BF),
         compiler_params=pltpu.CompilerParams(vmem_limit_bytes=60 * 2**20),
-        cost_estimate=pl.CostEstimate(
-            flops=2 * D2 * D * T * count, bytes_accessed=8 * D2 * W, transcendentals=0
-        ),
+        cost_estimate=pl.CostEstimate(flops=2**20, bytes_accessed=2**20, transcendentals=0),
         name="hidden_grads",
     )(place, dkv, dkv, k_own, k_other, v_own, v_other)
 
@@ -779,10 +783,16 @@
         planes = [g[0] for g in groups[:0:-1]] + [groups[0][0]] + [g[1] for g in groups[1:]]
         return jnp.concatenate(planes, axis=0).reshape((-1,) + block.shape)
 
+    def sides(self, a, k, axis):
+        keep = lax.dynamic_index_in_dim(a, self.bit(k), axis, keepdims=False)
+        return keep, lax.dynamic_index_in_dim(a, 1 - self.bit(k), axis, keepdims=False)
+
+    def add(self, a, b):
+        return (a.astype(F32) + b.astype(F32)).astype(BF)
+
     def halve(self, a, k, axis):
-        keep = lax.dynamic_index_in_dim(a, self.bit(k), axis, keepdims=False)
-        send = lax.dynamic_index_in_dim(a, 1 - self.bit(k), axis, keepdims=False)
-        return (keep.astype(F32) + self.flip(send, k).astype(F32)).astype(BF)
+        keep, send = self.sides(a, k, axis)
+        return self.add(keep, self.flip(send, k))
 
     def halve_cols(self, low, high):
         keep, send = self.order(low, high, self.bit(0))
@@ -964,11 +974,26 @@
         dq_got = sh.trade(dq)
         ffn = lax.psum_scatter(ffn, "ctx", scatter_dimension=0, tiled=False)
 
-        whole = key_grads(dkv, d_table, x_win, sinus, (att_vec, vec_a, vec_b))
-        whole = sh.halve(whole, 0, 0)
-        keep, send = sh.order(whole[:, :dn], whole[:, dn:], sh.f)
-        got_x = sh.trade(send)
+        d_hid = hidden_grads(
+            place, dkv.reshape(2 * D, W), key_proj, other_k, value_proj, other_v, C, R
+        )
+        keep, send = sh.sides(sh.spread(d_hid), 0, sh.bits - 1)
+        got = sh.flip(send, 0)
         dkv, _ = lax.optimization_barrier((dkv, send))
+
+        whole = key_grads(dkv, x_win)
+        whole, got = lax.optimization_barrier((whole, got))
+        d_hid = sh.add(keep, got)
+        keep, send = sh.sides(d_hid, 1, sh.bits - 2)
+        got = sh.flip(send, 1)
+        keep_w, send_w = sh.sides(whole, 0, 0)
+        got_w = sh.flip(send_w, 0)
+        d_table, _, _ = lax.optimization_barrier((d_table, send, send_w))
+        rest = position_grads(d_table, sinus, (att_vec, vec_a, vec_b))
+        rest, got_w = lax.optimization_barrier((rest, got_w))
+        whole = jnp.concatenate([sh.add(keep_w, got_w), sh.halve(rest, 0, 0)], axis=0)
+        keep_w, send_w = sh.order(whole[:, :dn], whole[:, dn:], sh.f)
+        got_x = sh.trade(send_w)
         go, gq = (
             tn(
                 jnp.concatenate([b, b_got], axis=0),
@@ -979,20 +1004,16 @@
             )
         )
         mine = sh.halve_cols(go, gq)
-
-        d_hid = hidden_grads(
-            place, dkv.reshape(2 * D, W), key_proj, other_k, value_proj, other_v, C, R
-        )
+        d_hid = sh.halve(sh.add(keep, got), 2, sh.bits - 3)
         got_x, d_hid, mine, ffn = lax.optimization_barrier((got_x, d_hid, mine, ffn))
         ffn = lax.all_gather(ffn, "ctx", axis=0, tiled=False)
-        whole = (keep.astype(F32) + got_x.astype(F32)).astype(BF)
-        grads = jnp.concatenate([whole, mine], axis=0)
+        grads = jnp.concatenate([sh.add(keep_w, got_x), mine], axis=0)
         grads = grads.reshape((2,) * (sh.bits - 1) + (-1, dn))
-        d_hid = sh.spread(d_hid)
         for k in range(1, sh.bits):
             grads = sh.halve(grads, k, grads.ndim - 3)
-            d_hid = sh.halve(d_hid, k - 1, d_hid.ndim - 3)
-            grads, d_hid = lax.optimization_barrier((grads, d_hid))
+            if k + 2 < sh.bits:
+                d_hid = sh.halve(d_hid, k + 2, d_hid.ndim - 3)
+                grads, d_hid = lax.optimization_barrier((grads, d_hid))
         n = grads.shape[0]
         cut = (n // 2 + 15) // 16 * 16
         one, two = grads[:cut], grads[cut:]
@@ -1000,8 +1021,6 @@
         for i, (k, other) in enumerate(zip(highs + [1], [1] + highs)):
             one = sh.double(one, k, one.ndim - 2)
             two = sh.double(two, other, 0 if i == 0 else i - 1)
-            if i == 0:
-                d_hid = sh.halve(d_hid, sh.bits - 1, d_hid.ndim - 3)
             if i == 0:
                 one, two, d_hid, ffn = lax.optimization_barrier((one, two, d_hid, ffn))
             if i == 1:

time: 361 us -> 351 us (0.972)
  waiting for transfers between devices: 130 us -> 109 us
  local copies, waits for them, and re-layouts: 16.4 us -> 21.1 us
    ppermute x12, waiting for transfers between devices: 29.5 us -> 11.1 us  [trade(): return lax.ppermute(a, 'fsdp', self.swap)]
    unnamed x72 -> x84, local copies, waits for them, and re-layouts: 6.49 us -> 8.62 us
    ppermute x30 -> x31, starting transfers between devices: 18.7 us -> 20.5 us  [flip(): return lax.ppermute(a, 'ctx', [(i, i ^ 1 << k) for i in range(self.count)])]
    convert_element_type x9 -> x10, other arithmetic: 7.62 us -> 6.61 us  [add(): return (a.astype(F32) + b.astype(F32)).astype(BF)]
    ppermute x30 -> x31, waiting for transfers between devices: 89.9 us -> 90.7 us  [flip(): return lax.ppermute(a, 'ctx', [(i, i ^ 1 << k) for i in range(self.count)])]
    pallas_call x1 -> x2, Pallas kernels: 16.5 us -> 16.3 us  [the longest x1 9.76 us: key_grads(): pl.pallas_call(kernel, grid=(4,), in_specs=[pl.BlockSpec((1, h, W), lambd...]
  transfers between devices with their start and end apart: 48 -> 49, of which waited for: 25 -> 20; matrix products, arithmetic and copies ran while one was open for 15% -> 18% of each run, Pallas kernels for 22% -> 23%
where the time goes in v5:
time: 351 us; the launch traced here: 349 us
  waiting for transfers between devices  109 us (31%)
  Pallas kernels  105 us (30%)
  starting transfers between devices  49.1 us (14%)
  other arithmetic  33.3 us (9%)
  local copies, waits for them, and re-layouts  21.1 us (6%)
  matrix products  16 us (5%)
  between operations  15.1 us (4%)
    ppermute x31, waiting for transfers between devices, flip(): return lax.ppermute(a, 'ctx', [(i, i ^ 1 << k) for i in range(self.count)])  90.7 us
    ppermute x31, starting transfers between devices, flip(): return lax.ppermute(a, 'ctx', [(i, i ^ 1 << k) for i in range(self.count)])  20.5 us
    pallas_call x1, Pallas kernels, att_bwd(): pl.pallas_call(att_bwd_kernel, grid=(D // 128,), in_specs=[col(T), col(16...  17.1 us
    ppermute x12, starting transfers between devices, trade(): return lax.ppermute(a, 'fsdp', self.swap)  16 us
    pallas_call x1, Pallas kernels, att_fwd(): pl.pallas_call(att_fwd_kernel, grid=(D // 128,), in_specs=[col(T), col(16...  16 us
    pallas_call x1, Pallas kernels, ffn_bwd(): pl.pallas_call(kernel, grid_spec=pltpu.PrefetchScalarGridSpec(num_scalar_...  15.6 us
    dot_general x3, matrix products, nn(): lax.dot_general(a, b, (((1,), (0,)), ((), ())), preferred_element_type=F32)  12.9 us
    pallas_call x1, Pallas kernels, hidden_grads(): pl.pallas_call(kernel, grid_spec=pltpu.PrefetchScalarGridSpec(num_scalar_...  11.1 us
  transfers between devices with their start and end apart: 49, of which 20 were waited for; matrix products, arithmetic and copies ran while one was open for 18% of the time, Pallas kernels for 23%

profile of v5, /device:TPU:0, one launch (start us, length us, event | category | flops | bytes accessed | tf_op | source)
XLA Modules:
  0.0 349.1 jit_solution(15925555021375604880)
XLA Ops:
  8.8 2.9 collective-permute-start.3
  13.8 1.6 pad_maximum_fusion.13
  17.0 2.2 constant_dynamic-update-slice_fusion.1
  24.0 1.7 select_bitcast_fusion.11
  28.7 5.3 %collective-permute-start.5 = (bf16[2,128,896]{2,1,0:T(8,128)(2,1)}, bf16[2,128,896]{2,1,0:T(8,128)(2,1)}, u32[]{:S(2)}, u32[]{:S(2)}) collective-permute-start(bf16[2,128,896]{2,1,0:T(8,128)(2,1)} %get-tuple-element.208), channel_id=1, source_target_pairs={{0,8},{2,10},{4,12},{6,14},{8,16},{10,18},{12,20},{14,22},{16,24},... | collective-permute-start | bytes 1376264 | tf_op jit(solution)/shard_map/ppermute | solution.py:777
  34.8 1.6 collective-permute-start.1
  37.2 3.7 %collective-permute-done.7 = bf16[2,128,896]{2,1,0:T(8,128)(2,1)} collective-permute-done((bf16[2,128,896]{2,1,0:T(8,128)(2,1)}, bf16[2,128,896]{2,1,0:T(8,128)(2,1)}, u32[]{:S(2)}, u32[]{:S(2)}) %collective-permute-start.7) | collective-permute-done | bytes 458784 | tf_op jit(solution)/shard_map/ppermute | solution.py:778
  42.1 4.6 %collective-permute-start.6 = (bf16[2,128,896]{2,1,0:T(8,128)(2,1)}, bf16[2,128,896]{2,1,0:T(8,128)(2,1)S(1)}, u32[]{:S(2)}, u32[]{:S(2)}) collective-permute-start(bf16[2,128,896]{2,1,0:T(8,128)(2,1)} %collective-permute-done.5), channel_id=1, source_target_pairs={{0,8},{2,10},{4,12},{6,14},{8,16},{10,18},{12,20},{14,22},{16,24},... | collective-permute-start | bytes 1376264 | tf_op jit(solution)/shard_map/ppermute | solution.py:777
  46.7 1.6 collective-permute-start.2
  50.9 2.4 collective-permute-done.8
  54.7 2.5 collective-permute-done.2.refs_1_
  68.7 4.3 %convolution_convert_fusion.t_ref = bf16[2304,768]{1,0:T(8,128)(2,1)} fusion(bf16[2304,768]{1,0:T(8,128)(2,1)S(1)} %pad_maximum_fusion.s_ref, bf16[384,768]{1,0:T(8,128)(2,1)S(1)} %get-tuple-element.192, bf16[384,768]{1,0:T(8,128)(2,1)S(1)} %get-tuple-element.191), kind=kOutput, calls=%fused_computation.2 | convolution fusion | flops 2722037760 | bytes 8257536 | tf_op jit(solution)/shard_map/dot_general | solution.py:22
  75.2 7.5 %fusion.k_ref.v_ref = bf16[2176,1536]{1,0:T(8,128)(2,1)} fusion(bf16[2176,768]{1,0:T(8,128)(2,1)S(1)} %bitcast.174, f32[1536]{0:T(1024)S(1)} %concatenate.57, bf16[384,1536]{1,0:T(8,128)(2,1)S(1)} %get-tuple-element.186, bf16[384,1536]{1,0:T(8,128)(2,1)S(1)} %get-tuple-element.185), kind=kOutput, calls=%fused_computation.1 | convolution fusion | flops 5145231360 | bytes 12392448 | tf_op jit(solution)/shard_map/dot_general | solution.py:22
  82.7 3.5 collective-permute-done.10.refs_9_
  88.2 16.0 %att_fwd.1 = (f32[128,768]{1,0:T(8,128)}, bf16[12,128,2176]{2,1,0:T(8,128)(2,1)}) custom-call(f32[128,768]{1,0:T(8,128)} %convolution_bitcast_fusion.q_ref, f32[16,768]{1,0:T(8,128)} %pad_maximum_fusion.16.v_rows.v_ref, f32[128,128]{1,0:T(8,128)} %and_select_fusion.pen_ref, f32[128,128]{1,0:T(8,128)} %broadcast_in_dim.83.kind_ref, ...), custom_call_target="tpu_custom_call" | custom-call | flops 13690208256 | bytes 16711680 | tf_op jit(solution)/shard_map/att_fwd/pallas_call | solution.py:154
  107.1 2.1 collective-permute-done.18.refs_2_
  109.2 1.6 collective-permute-start.24
  112.5 10.3 %ffn_fwd.1 = (bf16[128,768]{1,0:T(8,128)(2,1)}, bf16[128,3072]{1,0:T(8,128)(2,1)}, f32[128,3072]{1,0:T(8,128)}, bf16[128,768]{1,0:T(8,128)(2,1)}, f32[128,768]{1...) custom-call(s32[4]{0:T(128)} %pad_add_fusion.s_ref, ...), custom_call_target="tpu_custom_call" | custom-call | flops 1207959552 | bytes 9437184 | tf_op jit(solution)/shard_map/ffn_fwd/pallas_call | solution.py:414
  122.8 1.7 collective-permute-start.23
  124.5 5.0 %collective-permute-done.23.dog_ref = bf16[128,768]{1,0:T(8,128)(2,1)S(1)} collective-permute-done((bf16[128,768]{1,0:T(8,128)(2,1)}, bf16[128,768]{1,0:T(8,128)(2,1)S(1)}, u32[]{:S(2)}, u32[]{:S(2)}) %collective-permute-start.23) | collective-permute-done | bytes 196640 | tf_op jit(solution)/shard_map/ppermute | solution.py:744
  130.2 15.6 %ffn_bwd.1 = (bf16[16,384,384]{2,1,0:T(8,128)(2,1)}, f32[128,768]{1,0:T(8,128)}, bf16[128,768]{1,0:T(8,128)(2,1)}, bf16[128,768]{1,0:T(8,128)(2,1)}, f32[8,768]{1,0:T(8,128)}) custom-call(s32[4]{0:T(128)} %pad_add_fusion.s_ref, f32[128,3072]{1,0:T(8,128)} %get-tuple-element.118.pre_ref, bf16[128,3072]{1,0:T(8,128)(2,1)} %get-tuple-element.119.act_ref, ...), custom_call_target="tpu_custom_call" | custom-call | flops 4227858432 | bytes 14155776 | tf_op jit(solution)/shard_map/ffn_bwd/pallas_call | solution.py:510
  145.8 17.1 %att_bwd.1 = (bf16[128,768]{1,0:T(8,128)(2,1)}, f32[8,768]{1,0:T(8,128)}, bf16[2,768,2176]{2,1,0:T(8,128)(2,1)}, bf16[768,2304]{1,0:T(8,128)(2,1)}) custom-call(f32[128,768]{1,0:T(8,128)} %convolution_bitcast_fusion.q_ref, f32[16,768]{1,0:T(8,128)} %pad_maximum_fusion.16.v_rows.v_ref, f32[128,128]{1,0:T(8,128)} %broadcast_in_dim.83.kind_ref, ...), custom_call_target="tpu_custom_call" | custom-call | flops 1048576 | bytes 1048576 | tf_op jit(solution)/shard_map/att_bwd/pallas_call | solution.py:180
  162.9 11.1 %hidden_grads.1 = bf16[16,768,128]{2,1,0:T(8,128)(2,1)} custom-call(s32[4]{0:T(128)} %pad_add_fusion.s_ref, bf16[1536,2176]{1,0:T(8,128)(2,1)} %bitcast.166, bf16[1536,2176]{1,0:T(8,128)(2,1)} %bitcast.167, bf16[384,768]{1,0:T(8,128)(2,1)} %k0.1, bf16[384,768]{1,0:T(8,128)(2,1)} %copy-done.2, bf16[384,768]{1,0:T(8,128)(2,1)} %v0.1, bf16[384,768]{1,0:T(8,128)(2,1)} %copy-done.3), custom_call_target="tpu_custom_call" | custom-call | flops 1048576 | bytes 1048576 | tf_op jit(solution)/shard_map/hidden_grads/pallas_call | solution.py:610
  174.0 2.1 constant_dynamic-slice_fusion.6
  176.3 9.8 %key_grads.1 = bf16[2,768,768]{2,1,0:T(8,128)(2,1)} custom-call(bf16[2,768,2176]{2,1,0:T(8,128)(2,1)} %get-tuple-element.129.kv_ref, bf16[2176,768]{1,0:T(8,128)(2,1)} %bitcast.175), custom_call_target="tpu_custom_call" | custom-call | flops 5133828096 | bytes 10027008 | tf_op jit(solution)/shard_map/key_grads/pallas_call | solution.py:542
  189.0 1.7 collective-permute-start.33
  191.1 1.8 fusion.1
  195.0 6.5 %position_grads.1 = bf16[2,448,768]{2,1,0:T(8,128)(2,1)} custom-call(bf16[768,2304]{1,0:T(8,128)(2,1)} %get-tuple-element.133.t_ref, bf16[2304,768]{1,0:T(8,128)(2,1)} %copy-done.5, f32[8,768]{1,0:T(8,128)} %get-tuple-element.134.refs_0_, f32[8,768]{1,0:T(8,128)} %get-tuple-element.135.refs_1_, f32[8,768]{1,0:T(8,128)} %get-tuple-element.136.refs_2_), custom_call_target="tpu_custom_call" | custom-call | flops 2717908992 | bytes 7077888 | tf_op jit(solution)/shard_map/position_grads/pallas_call | solution.py:571
  203.2 2.7 select_convert_fusion
  206.4 1.8 collective-permute-start.30
  208.2 1.6 fusion.5
  212.6 16.7 %collective-permute-done.30 = bf16[2,2,768,128]{3,2,0,1:T(8,128)(2,1)S(1)} collective-permute-done((bf16[2,2,768,128]{3,2,0,1:T(8,128)(2,1)}, bf16[2,2,768,128]{3,2,0,1:T(8,128)(2,1)S(1)}, u32[]{:S(2)}, u32[]{:S(2)}) %collective-permute-start.30) | collective-permute-done | bytes 786464 | tf_op jit(solution)/shard_map/ppermute | solution.py:741
  232.5 2.1 add_convert_fusion.2
  234.7 7.8 %collective-permute-done.31 = bf16[2,768,128]{2,1,0:T(8,128)(2,1)S(1)} collective-permute-done((bf16[2,768,128]{2,1,0:T(8,128)(2,1)}, bf16[2,768,128]{2,1,0:T(8,128)(2,1)S(1)}, u32[]{:S(2)}, u32[]{:S(2)}) %collective-permute-start.31) | collective-permute-done | bytes 393248 | tf_op jit(solution)/shard_map/ppermute | solution.py:741
  242.6 1.6 add_convert_fusion.1
  245.0 2.7 collective-permute-start.36
  247.7 11.7 %collective-permute-done.36 = bf16[768,128]{1,0:T(8,128)(2,1)S(1)} collective-permute-done((bf16[768,128]{1,0:T(8,128)(2,1)S(1)}, bf16[768,128]{1,0:T(8,128)(2,1)S(1)}, u32[]{:S(2)}, u32[]{:S(2)}) %collective-permute-start.36) | collective-permute-done | bytes 196640 | tf_op jit(solution)/shard_map/ppermute | solution.py:741
  260.2 5.9 %collective-permute-done.35 = bf16[2,2,248,384]{3,2,0,1:T(8,128)(2,1)S(1)} collective-permute-done((bf16[2,2,248,384]{3,2,0,1:T(8,128)(2,1)S(1)}, bf16[2,2,248,384]{3,2,0,1:T(8,128)(2,1)S(1)}, u32[]{:S(2)}, u32[]{:S(2)}) %collective-permute-start.35) | collective-permute-done | bytes 761888 | tf_op jit(solution)/shard_map/ppermute | solution.py:741
  267.6 12.2 %collective-permute-done.37 = bf16[2,248,384]{2,1,0:T(8,128)(2,1)S(1)} collective-permute-done((bf16[2,248,384]{2,1,0:T(8,128)(2,1)S(1)}, bf16[2,248,384]{2,1,0:T(8,128)(2,1)S(1)}, u32[]{:S(2)}, u32[]{:S(2)}) %collective-permute-start.37) | collective-permute-done | bytes 380960 | tf_op jit(solution)/shard_map/ppermute | solution.py:741
  279.9 3.4 collective-permute-start.38
  283.3 18.4 %collective-permute-done.38 = bf16[248,384]{1,0:T(8,128)(2,1)S(1)} collective-permute-done((bf16[248,384]{1,0:T(8,128)(2,1)S(1)}, bf16[248,384]{1,0:T(8,128)(2,1)S(1)}, u32[]{:S(2)}, u32[]{:S(2)}) %collective-permute-start.38) | collective-permute-done | bytes 190496 | tf_op jit(solution)/shard_map/ppermute | solution.py:741
  302.0 4.4 %collective-permute-done.40 = bf16[120,384]{1,0:T(8,128)(2,1)S(1)} collective-permute-done((bf16[120,384]{1,0:T(8,128)(2,1)S(1)}, bf16[120,384]{1,0:T(8,128)(2,1)S(1)}, u32[]{:S(2)}, u32[]{:S(2)}) %collective-permute-start.40) | collective-permute-done | bytes 92192 | tf_op jit(solution)/shard_map/ppermute | solution.py:741
  308.2 2.4 collective-permute-start.41
  310.6 6.6 %ffn_final.1 = (f32[384,3072]{1,0:T(8,128)}, f32[1536,768]{1,0:T(8,128)}) custom-call(bf16[16,384,384]{2,1,0:T(8,128)(2,1)} %bitcast.196), custom_call_target="tpu_custom_call" | custom-call | flops 8589934592 | bytes 18874368 | tf_op jit(solution)/shard_map/ffn_final/pallas_call | solution.py:239
  319.8 3.4 input_grads.1
  323.2 5.6 %collective-permute-done.44 = bf16[2,2,120,384]{3,2,1,0:T(8,128)(2,1)S(1)} collective-permute-done((bf16[2,2,120,384]{3,2,1,0:T(8,128)(2,1)S(1)}, bf16[2,2,120,384]{3,2,1,0:T(8,128)(2,1)S(1)}, u32[]{:S(2)}, u32[]{:S(2)}) %collective-permute-start.44) | collective-permute-done | bytes 368672 | tf_op jit(solution)/shard_map/ppermute | solution.py:741
  330.2 2.8 collective-permute-done.46.d_ref
  334.8 5.9 %grad_final.1 = (f32[384,768]{1,0:T(8,128)}, f32[384,768]{1,0:T(8,128)}, f32[384,768]{1,0:T(8,128)}, f32[384,768]{1,0:T(8,128)}, f32[384,768]{1,0:T(8,128)}, /*index=5*/f32[64,384]{1,0:T(8,128)}) custom-call(s32[4]{0:T(128)} %pad_add_fusion.s_ref, bf16[1024,384]{1,0:T(8,128)(2,1)} %bitcast.177, bf16[960,384]{1,0:T(8,128)(2,1)} %bitcast.179, ...), custom_call_target="tpu_custom_call" | custom-call | tf_op jit(solution)/shard_map/grad_final/pallas_call | solution.py:678
  (246 shorter events, 66.4 us)
Async XLA Ops:
  7.2 235.4 %reduce-scatter.2.cloned.1.call-start = ((), (), s32[]{:S(2)}) async-start(), calls=%async_computation.1 | async-start | bytes 5013504 | tf_op jit(solution)/shard_map/reduce_scatter | solution.py:975
  8.8 26.0 %collective-permute-start.3 = (f32[16,384]{1,0:T(8,128)}, f32[16,384]{1,0:T(8,128)}, u32[]{:S(2)}, u32[]{:S(2)}) collective-permute-start(f32[16,384]{1,0:T(8,128)} %pack_rows.1), channel_id=1, source_target_pairs={{0,1},{1,0},{2,3},{3,2},{4,5},{5,4},{6,7},{7,6},{8,9},{9,8},{10,11... | collective-permute-start | bytes 73736 | tf_op jit(solution)/shard_map/ppermute | solution.py:744
  15.4 8.5 %collective-permute-start.4 = (bf16[128,896]{1,0:T(8,128)(2,1)}, bf16[128,896]{1,0:T(8,128)(2,1)}, u32[]{:S(2)}, u32[]{:S(2)}) collective-permute-start(bf16[128,896]{1,0:T(8,128)(2,1)} %pad_maximum_fusion.13), channel_id=1, source_target_pairs={{0,4},{2,6},{4,0},{6,2},{8,12},{10,14},{12,8},{14,10},{16,20},{18,... | collective-permute-start | bytes 688136 | tf_op jit(solution)/shard_map/ppermute | solution.py:741
  20.2 37.1 %collective-permute-start = (bf16[384,768]{1,0:T(8,128)(2,1)}, bf16[384,768]{1,0:T(8,128)(2,1)}, u32[]{:S(2)}, u32[]{:S(2)}) collective-permute-start(bf16[384,768]{1,0:T(8,128)(2,1)} %get-tuple-element.204), channel_id=1, source_target_pairs={{0,1},{1,0},{2,3},{3,2},{4,5},{5,4},{6,7},{7,6},{8,9},{9,8},{10,11... | collective-permute-start | bytes 1769480 | tf_op jit(solution)/shard_map/ppermute | solution.py:744
  27.4 13.4 %collective-permute-start.7 = (bf16[2,128,896]{2,1,0:T(8,128)(2,1)}, bf16[2,128,896]{2,1,0:T(8,128)(2,1)}, u32[]{:S(2)}, u32[]{:S(2)}) collective-permute-start(bf16[2,128,896]{2,1,0:T(8,128)(2,1)} %get-tuple-element.208), channel_id=1, source_target_pairs={{8,0},{10,2},{12,4},{14,6},{16,8},{18,10},{20,12},{22,14},{24,16},... | collective-permute-start | bytes 1376264 | tf_op jit(solution)/shard_map/ppermute | solution.py:778
  28.7 13.4 %collective-permute-start.5 = (bf16[2,128,896]{2,1,0:T(8,128)(2,1)}, bf16[2,128,896]{2,1,0:T(8,128)(2,1)}, u32[]{:S(2)}, u32[]{:S(2)}) collective-permute-start(bf16[2,128,896]{2,1,0:T(8,128)(2,1)} %get-tuple-element.208), channel_id=1, source_target_pairs={{0,8},{2,10},{4,12},{6,14},{8,16},{10,18},{12,20},{14,22},{16,24},... | collective-permute-start | bytes 1376264 | tf_op jit(solution)/shard_map/ppermute | solution.py:777
  34.8 12.0 %collective-permute-start.14 = (bf16[1,2,128,896]{3,2,1,0:T(8,128)(2,1)}, bf16[1,2,128,896]{3,2,1,0:T(8,128)(2,1)}, u32[]{:S(2)}, u32[]{:S(2)}) collective-permute-start(bf16[1,2,128,896]{3,2,1,0:T(8,128)(2,1)} %get-tuple-element.207), channel_id=1, source_target_pairs={{0,2},{2,0},{4,6},{6,4},{8,10},{10,8},{12,14},{14,12},{16,18},{18,... | collective-permute-start | bytes 1376264 | tf_op jit(solution)/shard_map/ppermute | solution.py:741
  34.8 22.4 %collective-permute-start.1 = (bf16[384,768]{1,0:T(8,128)(2,1)}, bf16[384,768]{1,0:T(8,128)(2,1)S(1)}, u32[]{:S(2)}, u32[]{:S(2)}) collective-permute-start(bf16[384,768]{1,0:T(8,128)(2,1)} %get-tuple-element.206), channel_id=1, source_target_pairs={{0,1},{1,0},{2,3},{3,2},{4,5},{5,4},{6,7},{7,6},{8,9},{9,8},{10,11... | collective-permute-start | bytes 1769480 | tf_op jit(solution)/shard_map/ppermute | solution.py:744
  40.8 12.4 %collective-permute-start.8 = (bf16[2,128,896]{2,1,0:T(8,128)(2,1)}, bf16[2,128,896]{2,1,0:T(8,128)(2,1)S(1)}, u32[]{:S(2)}, u32[]{:S(2)}) collective-permute-start(bf16[2,128,896]{2,1,0:T(8,128)(2,1)} %collective-permute-done.7), channel_id=1, source_target_pairs={{8,0},{10,2},{12,4},{14,6},{16,8},{18,10},{20,12},{22,14},{24,16},... | collective-permute-start | bytes 1376264 | tf_op jit(solution)/shard_map/ppermute | solution.py:778
  42.1 12.4 %collective-permute-start.6 = (bf16[2,128,896]{2,1,0:T(8,128)(2,1)}, bf16[2,128,896]{2,1,0:T(8,128)(2,1)S(1)}, u32[]{:S(2)}, u32[]{:S(2)}) collective-permute-start(bf16[2,128,896]{2,1,0:T(8,128)(2,1)} %collective-permute-done.5), channel_id=1, source_target_pairs={{0,8},{2,10},{4,12},{6,14},{8,16},{10,18},{12,20},{14,22},{16,24},... | collective-permute-start | bytes 1376264 | tf_op jit(solution)/shard_map/ppermute | solution.py:777
  46.7 10.5 %collective-permute-start.2 = (bf16[192,768]{1,0:T(8,128)(2,1)}, bf16[192,768]{1,0:T(8,128)(2,1)}, u32[]{:S(2)}, u32[]{:S(2)}) collective-permute-start(bf16[192,768]{1,0:T(8,128)(2,1)} %constant_dynamic-slice_fusion.10), channel_id=1, source_target_pairs={{0,1},{1,0},{2,3},{3,2},{4,5},{5,4},{6,7},{7,6},{8,9},{9,8},{10,11... | collective-permute-start | bytes 884744 | tf_op jit(solution)/shard_map/ppermute | solution.py:744
  53.3 9.1 %collective-permute-start.13 = (bf16[2,2,128,896]{3,2,1,0:T(8,128)(2,1)S(1)}, bf16[2,2,128,896]{3,2,1,0:T(8,128)(2,1)S(1)}, u32[]{:S(2)}, u32[]{:S(2)}) collective-permute-start(bf16[2,2,128,896]{3,2,1,0:T(8,128)(2,1)S(1)} %pad_maximum_fusion.7), channel_id=1, source_target_pairs={{0,2},{2,0},{4,6},{6,4},{8,10},{10,8},{12,14},{14,12},{16,18},{18,... | collective-permute-start | bytes 2752520 | tf_op jit(solution)/shard_map/ppermute | solution.py:741
  54.6 18.4 %collective-permute-start.12 = (bf16[2,2,128,896]{3,2,1,0:T(8,128)(2,1)S(1)}, bf16[2,2,128,896]{3,2,1,0:T(8,128)(2,1)S(1)}, u32[]{:S(2)}, u32[]{:S(2)}) collective-permute-start(bf16[2,2,128,896]{3,2,1,0:T(8,128)(2,1)S(1)} %pad_maximum_fusion.6), channel_id=1, source_target_pairs={{0,2},{2,0},{4,6},{6,4},{8,10},{10,8},{12,14},{14,12},{16,18},{18,... | collective-permute-start | bytes 2752520 | tf_op jit(solution)/shard_map/ppermute | solution.py:741
  58.4 16.4 %collective-permute-start.11 = (bf16[96,3072]{1,0:T(8,128)(2,1)S(1)}, bf16[96,3072]{1,0:T(8,128)(2,1)}, u32[]{:S(2)}, u32[]{:S(2)}) collective-permute-start(bf16[96,3072]{1,0:T(8,128)(2,1)S(1)} %constant_dynamic-slice_fusion.8), channel_id=1, source_target_pairs={{0,1},{1,0},{2,3},{3,2},{4,5},{5,4},{6,7},{7,6},{8,9},{9,8},{10,11... | collective-permute-start | bytes 1769480 | tf_op jit(solution)/shard_map/ppermute | solution.py:744
  61.0 25.1 %collective-permute-start.10 = (bf16[384,768]{1,0:T(8,128)(2,1)S(1)}, bf16[384,768]{1,0:T(8,128)(2,1)}, u32[]{:S(2)}, u32[]{:S(2)}) collective-permute-start(bf16[384,768]{1,0:T(8,128)(2,1)S(1)} %constant_dynamic-slice_fusion.9), channel_id=1, source_target_pairs={{0,1},{1,0},{2,3},{3,2},{4,5},{5,4},{6,7},{7,6},{8,9},{9,8},{10,11... | collective-permute-start | bytes 1769480 | tf_op jit(solution)/shard_map/ppermute | solution.py:744
  61.6 2.6 collective-permute-start.9
  74.8 29.5 %collective-permute-start.16 = (bf16[96,3072]{1,0:T(8,128)(2,1)}, bf16[96,3072]{1,0:T(8,128)(2,1)S(1)}, u32[]{:S(2)}, u32[]{:S(2)}) collective-permute-start(bf16[96,3072]{1,0:T(8,128)(2,1)} %collective-permute-done.11.refs_4_), channel_id=1, source_target_pairs={{0,4},{2,6},{4,0},{6,2},{8,12},{10,14},{12,8},{14,10},{16,20},{18,... | collective-permute-start | bytes 1769480 | tf_op jit(solution)/shard_map/ppermute | solution.py:741
  86.2 18.2 %collective-permute-start.17 = (bf16[384,768]{1,0:T(8,128)(2,1)}, bf16[384,768]{1,0:T(8,128)(2,1)S(1)}, u32[]{:S(2)}, u32[]{:S(2)}) collective-permute-start(bf16[384,768]{1,0:T(8,128)(2,1)} %collective-permute-done.10.refs_9_), channel_id=1, source_target_pairs={{0,4},{2,6},{4,0},{6,2},{8,12},{10,14},{12,8},{14,10},{16,20},{18,... | collective-permute-start | bytes 1769480 | tf_op jit(solution)/shard_map/ppermute | solution.py:741
  104.3 6.5 %collective-permute-start.19 = (bf16[96,3072]{1,0:T(8,128)(2,1)}, bf16[96,3072]{1,0:T(8,128)(2,1)S(1)}, u32[]{:S(2)}, u32[]{:S(2)}) collective-permute-start(bf16[96,3072]{1,0:T(8,128)(2,1)} %collective-permute-done.11.refs_4_), channel_id=1, source_target_pairs={{0,2},{2,0},{4,6},{6,4},{8,10},{10,8},{12,14},{14,12},{16,18},{18,... | collective-permute-start | bytes 1769480 | tf_op jit(solution)/shard_map/ppermute | solution.py:741
  104.4 6.8 %collective-permute-start.20 = (bf16[96,3072]{1,0:T(8,128)(2,1)S(1)}, bf16[96,3072]{1,0:T(8,128)(2,1)S(1)}, u32[]{:S(2)}, u32[]{:S(2)}) collective-permute-start(bf16[96,3072]{1,0:T(8,128)(2,1)S(1)} %collective-permute-done.16.refs_5_), channel_id=1, source_target_pairs={{0,2},{2,0},{4,6},{6,4},{8,10},{10,8},{12,14},{14,12},{16,18},{18,... | collective-permute-start | bytes 1769480 | tf_op jit(solution)/shard_map/ppermute | solution.py:741
  104.9 6.3 %collective-permute-start.21 = (bf16[384,768]{1,0:T(8,128)(2,1)}, bf16[384,768]{1,0:T(8,128)(2,1)S(1)}, u32[]{:S(2)}, u32[]{:S(2)}) collective-permute-start(bf16[384,768]{1,0:T(8,128)(2,1)} %collective-permute-done.10.refs_9_), channel_id=1, source_target_pairs={{0,2},{2,0},{4,6},{6,4},{8,10},{10,8},{12,14},{14,12},{16,18},{18,... | collective-permute-start | bytes 1769480 | tf_op jit(solution)/shard_map/ppermute | solution.py:741
  105.0 6.3 %collective-permute-start.22 = (bf16[384,768]{1,0:T(8,128)(2,1)S(1)}, bf16[384,768]{1,0:T(8,128)(2,1)S(1)}, u32[]{:S(2)}, u32[]{:S(2)}) collective-permute-start(bf16[384,768]{1,0:T(8,128)(2,1)S(1)} %collective-permute-done.17.refs_10_), channel_id=1, source_target_pairs={{0,2},{2,0},{4,6},{6,4},{8,10},{10,8},{12,14},{14,12},{16,18},{18,... | collective-permute-start | bytes 1769480 | tf_op jit(solution)/shard_map/ppermute | solution.py:741
  105.4 3.8 %collective-permute-start.18 = (bf16[192,768]{1,0:T(8,128)(2,1)}, bf16[192,768]{1,0:T(8,128)(2,1)S(1)}, u32[]{:S(2)}, u32[]{:S(2)}) collective-permute-start(bf16[192,768]{1,0:T(8,128)(2,1)} %collective-permute-done.2.refs_1_), channel_id=1, source_target_pairs={{0,2},{2,0},{4,6},{6,4},{8,10},{10,8},{12,14},{14,12},{16,18},{18,... | collective-permute-start | bytes 884744 | tf_op jit(solution)/shard_map/ppermute | solution.py:741
  109.2 15.3 %collective-permute-start.24 = (bf16[128,768]{1,0:T(8,128)(2,1)S(1)}, bf16[128,768]{1,0:T(8,128)(2,1)S(1)}, u32[]{:S(2)}, u32[]{:S(2)}) collective-permute-start(bf16[128,768]{1,0:T(8,128)(2,1)S(1)} %convert_element_type.179), channel_id=1, source_target_pairs={{0,1},{1,0},{2,3},{3,2},{4,5},{5,4},{6,7},{7,6},{8,9},{9,8},{10,11... | collective-permute-start | bytes 589832 | tf_op jit(solution)/shard_map/ppermute | solution.py:744
  110.8 13.6 %collective-permute-start.25 = (bf16[128,768]{1,0:T(8,128)(2,1)S(1)}, bf16[128,768]{1,0:T(8,128)(2,1)}, u32[]{:S(2)}, u32[]{:S(2)}) collective-permute-start(bf16[128,768]{1,0:T(8,128)(2,1)S(1)} %bitcast.183), channel_id=1, source_target_pairs={{0,1},{1,0},{2,3},{3,2},{4,5},{5,4},{6,7},{7,6},{8,9},{9,8},{10,11... | collective-permute-start | bytes 589832 | tf_op jit(solution)/shard_map/ppermute | solution.py:744
  122.8 6.8 %collective-permute-start.23 = (bf16[128,768]{1,0:T(8,128)(2,1)}, bf16[128,768]{1,0:T(8,128)(2,1)S(1)}, u32[]{:S(2)}, u32[]{:S(2)}) collective-permute-start(bf16[128,768]{1,0:T(8,128)(2,1)} %get-tuple-element.121.do_ref), channel_id=1, source_target_pairs={{0,1},{1,0},{2,3},{3,2},{4,5},{5,4},{6,7},{7,6},{8,9},{9,8},{10,11... | collective-permute-start | bytes 589832 | tf_op jit(solution)/shard_map/ppermute | solution.py:744
  145.8 162.3 %all-gather.3.cloned.1.call-start = ((), (), s32[]{:S(2)}) async-start(), calls=%async_computation.2 | async-start | bytes 5013504 | tf_op jit(solution)/shard_map/all_gather | solution.py:1009
  176.2 9.9 %collective-permute-start.26 = (bf16[2,2,2,768,128]{4,3,0,1,2:T(8,128)(2,1)S(1)}, bf16[2,2,2,768,128]{4,3,0,1,2:T(8,128)(2,1)}, u32[]{:S(2)}, u32[]{:S(2)}) collective-permute-start(bf16[2,2,2,768,128]{4,3,0,1,2:T(8,128)(2,1)S(1)} %bitcast.190), channel_id=1, source_target_pairs={{0,2},{2,0},{4,6},{6,4},{8,10},{10,8},{12,14},{14,12},{16,18},{18,... | collective-permute-start | bytes 4718600 | tf_op jit(solution)/shard_map/ppermute | solution.py:741
  187.6 14.0 %collective-permute-start.27 = (bf16[768,768]{1,0:T(8,128)(2,1)S(1)}, bf16[768,768]{1,0:T(8,128)(2,1)}, u32[]{:S(2)}, u32[]{:S(2)}) collective-permute-start(bf16[768,768]{1,0:T(8,128)(2,1)S(1)} %dynamic-slice_bitcast_fusion), channel_id=1, source_target_pairs={{0,2},{2,0},{4,6},{6,4},{8,10},{10,8},{12,14},{14,12},{16,18},{18,... | collective-permute-start | bytes 3538952 | tf_op jit(solution)/shard_map/ppermute | solution.py:741
  189.0 14.2 %collective-permute-start.33 = (bf16[128,768]{1,0:T(8,128)(2,1)S(1)}, bf16[128,768]{1,0:T(8,128)(2,1)}, u32[]{:S(2)}, u32[]{:S(2)}) collective-permute-start(bf16[128,768]{1,0:T(8,128)(2,1)S(1)} %copy-done.36), channel_id=1, source_target_pairs={{0,1},{1,0},{2,3},{3,2},{4,5},{5,4},{6,7},{7,6},{8,9},{9,8},{10,11... | collective-permute-start | bytes 589832 | tf_op jit(solution)/shard_map/ppermute | solution.py:744
  190.7 12.1 %collective-permute-start.32 = (bf16[128,768]{1,0:T(8,128)(2,1)S(1)}, bf16[128,768]{1,0:T(8,128)(2,1)S(1)}, u32[]{:S(2)}, u32[]{:S(2)}) collective-permute-start(bf16[128,768]{1,0:T(8,128)(2,1)S(1)} %copy-done.35), channel_id=1, source_target_pairs={{0,1},{1,0},{2,3},{3,2},{4,5},{5,4},{6,7},{7,6},{8,9},{9,8},{10,11... | collective-permute-start | bytes 589832 | tf_op jit(solution)/shard_map/ppermute | solution.py:744
  202.7 7.1 %collective-permute-start.28 = (bf16[448,768]{1,0:T(8,128)(2,1)S(1)}, bf16[448,768]{1,0:T(8,128)(2,1)S(1)}, u32[]{:S(2)}, u32[]{:S(2)}) collective-permute-start(bf16[448,768]{1,0:T(8,128)(2,1)S(1)} %dynamic-slice_bitcast_fusion.2), channel_id=1, source_target_pairs={{0,2},{2,0},{4,6},{6,4},{8,10},{10,8},{12,14},{14,12},{16,18},{18,... | collective-permute-start | bytes 2064392 | tf_op jit(solution)/shard_map/ppermute | solution.py:741
  205.9 26.6 %collective-permute-start.34 = (bf16[768,384]{1,0:T(8,128)(2,1)}, bf16[768,384]{1,0:T(8,128)(2,1)}, u32[]{:S(2)}, u32[]{:S(2)}) collective-permute-start(bf16[768,384]{1,0:T(8,128)(2,1)} %get-tuple-element.231), channel_id=1, source_target_pairs={{0,2},{2,0},{4,6},{6,4},{8,10},{10,8},{12,14},{14,12},{16,18},{18,... | collective-permute-start | bytes 1769480 | tf_op jit(solution)/shard_map/ppermute | solution.py:741
  206.4 22.9 %collective-permute-start.30 = (bf16[2,2,768,128]{3,2,0,1:T(8,128)(2,1)}, bf16[2,2,768,128]{3,2,0,1:T(8,128)(2,1)S(1)}, u32[]{:S(2)}, u32[]{:S(2)}) collective-permute-start(bf16[2,2,768,128]{3,2,0,1:T(8,128)(2,1)} %dynamic-slice_bitcast_fusion.1), channel_id=1, source_target_pairs={{0,4},{2,6},{4,0},{6,2},{8,12},{10,14},{12,8},{14,10},{16,20},{18,... | collective-permute-start | bytes 2359304 | tf_op jit(solution)/shard_map/ppermute | solution.py:741
  211.2 31.4 %collective-permute-start.29 = (bf16[1216,384]{1,0:T(8,128)(2,1)}, bf16[1216,384]{1,0:T(8,128)(2,1)}, u32[]{:S(2)}, u32[]{:S(2)}) collective-permute-start(bf16[1216,384]{1,0:T(8,128)(2,1)} %broadcast_select_fusion.2), channel_id=1, source_target_pairs={{0,1},{1,0},{2,3},{3,2},{4,5},{5,4},{6,7},{7,6},{8,9},{9,8},{10,11... | collective-permute-start | bytes 2801672 | tf_op jit(solution)/shard_map/ppermute | solution.py:744
  231.2 11.3 %collective-permute-start.31 = (bf16[2,768,128]{2,1,0:T(8,128)(2,1)}, bf16[2,768,128]{2,1,0:T(8,128)(2,1)S(1)}, u32[]{:S(2)}, u32[]{:S(2)}) collective-permute-start(bf16[2,768,128]{2,1,0:T(8,128)(2,1)} %dynamic-slice_bitcast_fusion.3), channel_id=1, source_target_pairs={{0,8},{2,10},{4,12},{6,14},{8,0},{10,2},{12,4},{14,6},{16,24},{18,... | collective-permute-start | bytes 1179656 | tf_op jit(solution)/shard_map/ppermute | solution.py:741
  244.7 21.3 %collective-permute-start.35 = (bf16[2,2,248,384]{3,2,0,1:T(8,128)(2,1)S(1)}, bf16[2,2,248,384]{3,2,0,1:T(8,128)(2,1)S(1)}, u32[]{:S(2)}, u32[]{:S(2)}) collective-permute-start(bf16[2,2,248,384]{3,2,0,1:T(8,128)(2,1)S(1)} %bitcast.191), channel_id=1, source_target_pairs={{0,4},{2,6},{4,0},{6,2},{8,12},{10,14},{12,8},{14,10},{16,20},{18,... | collective-permute-start | bytes 2285576 | tf_op jit(solution)/shard_map/ppermute | solution.py:741
  245.0 14.5 %collective-permute-start.36 = (bf16[768,128]{1,0:T(8,128)(2,1)S(1)}, bf16[768,128]{1,0:T(8,128)(2,1)S(1)}, u32[]{:S(2)}, u32[]{:S(2)}) collective-permute-start(bf16[768,128]{1,0:T(8,128)(2,1)S(1)} %dynamic-slice_bitcast_fusion.5), channel_id=1, source_target_pairs={{0,16},{2,18},{4,20},{6,22},{8,24},{10,26},{12,28},{14,30},{16,0},... | collective-permute-start | bytes 589832 | tf_op jit(solution)/shard_map/ppermute | solution.py:741
  266.3 13.5 %collective-permute-start.37 = (bf16[2,248,384]{2,1,0:T(8,128)(2,1)S(1)}, bf16[2,248,384]{2,1,0:T(8,128)(2,1)S(1)}, u32[]{:S(2)}, u32[]{:S(2)}) collective-permute-start(bf16[2,248,384]{2,1,0:T(8,128)(2,1)S(1)} %dynamic-slice_bitcast_fusion.4), channel_id=1, source_target_pairs={{0,8},{2,10},{4,12},{6,14},{8,0},{10,2},{12,4},{14,6},{16,24},{18,... | collective-permute-start | bytes 1142792 | tf_op jit(solution)/shard_map/ppermute | solution.py:741
  279.9 21.8 %collective-permute-start.38 = (bf16[248,384]{1,0:T(8,128)(2,1)S(1)}, bf16[248,384]{1,0:T(8,128)(2,1)S(1)}, u32[]{:S(2)}, u32[]{:S(2)}) collective-permute-start(bf16[248,384]{1,0:T(8,128)(2,1)S(1)} %dynamic-slice_bitcast_fusion.6), channel_id=1, source_target_pairs={{0,16},{2,18},{4,20},{6,22},{8,24},{10,26},{12,28},{14,30},{16,0},... | collective-permute-start | bytes 571400 | tf_op jit(solution)/shard_map/ppermute | solution.py:741
  301.8 4.6 %collective-permute-start.40 = (bf16[120,384]{1,0:T(8,128)(2,1)S(1)}, bf16[120,384]{1,0:T(8,128)(2,1)S(1)}, u32[]{:S(2)}, u32[]{:S(2)}) collective-permute-start(bf16[120,384]{1,0:T(8,128)(2,1)S(1)} %slice.61), channel_id=1, source_target_pairs={{0,4},{2,6},{4,0},{6,2},{8,12},{10,14},{12,8},{14,10},{16,20},{18,... | collective-permute-start | bytes 276488 | tf_op jit(solution)/shard_map/ppermute | solution.py:741
  301.9 6.1 %collective-permute-start.39 = (bf16[128,384]{1,0:T(8,128)(2,1)S(1)}, bf16[128,384]{1,0:T(8,128)(2,1)S(1)}, u32[]{:S(2)}, u32[]{:S(2)}) collective-permute-start(bf16[128,384]{1,0:T(8,128)(2,1)S(1)} %slice.60), channel_id=1, source_target_pairs={{0,16},{2,18},{4,20},{6,22},{8,24},{10,26},{12,28},{14,30},{16,0},... | collective-permute-start | bytes 294920 | tf_op jit(solution)/shard_map/ppermute | solution.py:741
  308.1 10.0 %collective-permute-start.42 = (bf16[2,120,384]{2,1,0:T(8,128)(2,1)S(1)}, bf16[2,120,384]{2,1,0:T(8,128)(2,1)S(1)}, u32[]{:S(2)}, u32[]{:S(2)}) collective-permute-start(bf16[2,120,384]{2,1,0:T(8,128)(2,1)S(1)} %pad_maximum_fusion.15), channel_id=1, source_target_pairs={{0,16},{2,18},{4,20},{6,22},{8,24},{10,26},{12,28},{14,30},{16,0},... | collective-permute-start | bytes 552968 | tf_op jit(solution)/shard_map/ppermute | solution.py:741
  308.2 10.0 %collective-permute-start.41 = (bf16[2,128,384]{2,1,0:T(8,128)(2,1)S(1)}, bf16[2,128,384]{2,1,0:T(8,128)(2,1)S(1)}, u32[]{:S(2)}, u32[]{:S(2)}) collective-permute-start(bf16[2,128,384]{2,1,0:T(8,128)(2,1)S(1)} %pad_maximum_fusion.14), channel_id=1, source_target_pairs={{0,8},{2,10},{4,12},{6,14},{8,0},{10,2},{12,4},{14,6},{16,24},{18,... | collective-permute-start | bytes 589832 | tf_op jit(solution)/shard_map/ppermute | solution.py:741
  318.3 10.5 %collective-permute-start.44 = (bf16[2,2,120,384]{3,2,1,0:T(8,128)(2,1)S(1)}, bf16[2,2,120,384]{3,2,1,0:T(8,128)(2,1)S(1)}, u32[]{:S(2)}, u32[]{:S(2)}) collective-permute-start(bf16[2,2,120,384]{3,2,1,0:T(8,128)(2,1)S(1)} %pad_maximum_fusion.12), channel_id=1, source_target_pairs={{0,8},{2,10},{4,12},{6,14},{8,0},{10,2},{12,4},{14,6},{16,24},{18,... | collective-permute-start | bytes 1105928 | tf_op jit(solution)/shard_map/ppermute | solution.py:741
  318.4 11.0 %collective-permute-start.43 = (bf16[2,2,128,384]{3,2,0,1:T(8,128)(2,1)S(1)}, bf16[2,2,128,384]{3,2,0,1:T(8,128)(2,1)S(1)}, u32[]{:S(2)}, u32[]{:S(2)}) collective-permute-start(bf16[2,2,128,384]{3,2,0,1:T(8,128)(2,1)S(1)} %pad_maximum_fusion.11), channel_id=1, source_target_pairs={{0,4},{2,6},{4,0},{6,2},{8,12},{10,14},{12,8},{14,10},{16,20},{18,... | collective-permute-start | bytes 1179656 | tf_op jit(solution)/shard_map/ppermute | solution.py:741
  329.7 3.4 collective-permute-start.45
  329.8 3.3 collective-permute-start.46
  (43 other events, 194.1 us)
Sparse Core Ops, SparseCore 0:
  145.9 79.1 reduce-scatter.1
  242.7 64.0 all-gather.2

commit v6 on v5

--- a/solution.py
+++ b/solution.py
@@ -26,7 +26,9 @@
     return lax.dot_general(a, b, (((0,), (0,)), ((), ())), preferred_element_type=F32)
 
 
-def att_fwd_kernel(q_ref, v_rows, pen_ref, kind_ref, k_ref, v_ref, t_ref, ka_ref, o_ref, p_ref):
+def att_fwd_kernel(
+    q_ref, v_rows, pen_ref, kind_ref, k_ref, v_ref, t_ref, ka_ref, o_ref, low_ref, p_ref
+):
     T = q_ref.shape[0]
     W = k_ref.shape[0]
     blocks = W // T
@@ -78,7 +80,9 @@
         p_ref[h] = p
         probs.append(p)
     out = nn(jnp.concatenate(probs, axis=0), v_ref[...])
-    o_ref[...] = jnp.where(lane < DH, out[:T], out[T:])
+    out = jnp.where(lane < DH, out[:T], out[T:])
+    o_ref[...] = out
+    low_ref[...] = out.astype(BF)
 
 
 def att_bwd_kernel(
@@ -155,9 +159,10 @@
         att_fwd_kernel,
         grid=(D // 128,),
         in_specs=[col(T), col(16), fixed(T), fixed(T), keys, values, col(W + T), fixed(W)],
-        out_specs=[col(T), pl.BlockSpec((2, T, W), lambda i: (i, 0, 0))],
+        out_specs=[col(T), col(T), pl.BlockSpec((2, T, W), lambda i: (i, 0, 0))],
         out_shape=[
             jax.ShapeDtypeStruct((T, D), F32),
+            jax.ShapeDtypeStruct((T, D), BF),
             jax.ShapeDtypeStruct((heads, T, W), BF),
         ],
         compiler_params=pltpu.CompilerParams(vmem_limit_bytes=60 * 2**20),
@@ -532,55 +537,87 @@
     )
 
 
-def key_grads(dkv, x_win):
+def key_grads(place, dkv, x_win):
     _, D, W = dkv.shape
     h = D // 2
 
-    def kernel(kv_ref, x_ref, out_ref):
-        out_ref[0] = nn(kv_ref[0], x_ref[...]).astype(BF)
+    def kernel(s_ref, kv_ref, x_ref, send_ref, keep_ref):
+        g = nn(kv_ref[0], x_ref[...]).astype(BF)
+
+        @pl.when(pl.program_id(0) < 2)
+        def _():
+            send_ref[...] = g
+
+        @pl.when(pl.program_id(0) >= 2)
+        def _():
+            keep_ref[...] = g
 
     return pl.pallas_call(
         kernel,
-        grid=(4,),
-        in_specs=[
-            pl.BlockSpec((1, h, W), lambda i: (i // 2, i % 2, 0)),
-            pl.BlockSpec((W, D), lambda i: (0, 0)),
-        ],
-        out_specs=pl.BlockSpec((1, h, D), lambda i: (i // 2, i % 2, 0)),
-        out_shape=jax.ShapeDtypeStruct((2, D, D), BF),
+        grid_spec=pltpu.PrefetchScalarGridSpec(
+            num_scalar_prefetch=1,
+            grid=(4,),
+            in_specs=[
+                pl.BlockSpec((1, h, W), lambda i, s: (jnp.where(i < 2, 1 - s[1], s[1]), i % 2, 0)),
+                pl.BlockSpec((W, D), lambda i, s: (0, 0)),
+            ],
+            out_specs=[
+                pl.BlockSpec((h, D), lambda i, s: (jnp.minimum(i, 1), 0)),
+                pl.BlockSpec((h, D), lambda i, s: (jnp.maximum(i - 2, 0), 0)),
+            ],
+        ),
+        out_shape=[jax.ShapeDtypeStruct((D, D), BF)] * 2,
         compiler_params=pltpu.CompilerParams(vmem_limit_bytes=60 * 2**20),
         cost_estimate=pl.CostEstimate(
             flops=4 * D * D * W, bytes_accessed=6 * D * W, transcendentals=0
         ),
         name="key_grads",
-    )(dkv, x_win)
-
-
-def position_grads(d_table, sinus, vectors):
+    )(place, dkv, x_win)
+
+
+def position_grads(place, d_table, sinus, vectors):
     D, WT = d_table.shape
     h = D // 2
 
-    def kernel(t_ref, s_ref, *refs):
-        v_refs, out_ref = refs[:-1], refs[-1]
-        out_ref[0, :h, :] = nn(t_ref[...], s_ref[...]).astype(BF)
+    def kernel(s_ref, t_ref, x_ref, *refs):
+        v_refs, (send_ref, keep_ref) = refs[:-2], refs[-2:]
+        i = pl.program_id(0)
+        g = nn(t_ref[...], x_ref[...]).astype(BF)
         small = jnp.concatenate([r[...] for r in v_refs], axis=0)
         small = jnp.concatenate([small, jnp.zeros((64 - small.shape[0], D), F32)], axis=0)
-        out_ref[0, h:, :] = jnp.where(pl.program_id(0) == 0, small, 0.0).astype(BF)
-
-    whole = lambda *shape: pl.BlockSpec(shape, lambda i: (0,) * len(shape))
+        even = jnp.where(i == 0, 1 - s_ref[1], s_ref[1]) == 0
+        small = jnp.where(even, small, 0.0).astype(BF)
+
+        @pl.when(i == 0)
+        def _():
+            send_ref[:h] = g
+            send_ref[h:] = small
+
+        @pl.when(i == 1)
+        def _():
+            keep_ref[:h] = g
+            keep_ref[h:] = small
+
+    whole = lambda *shape: pl.BlockSpec(shape, lambda i, s: (0,) * len(shape))
     return pl.pallas_call(
         kernel,
-        grid=(2,),
-        in_specs=[pl.BlockSpec((h, WT), lambda i: (i, 0)), whole(WT, D)]
-        + [whole(8, D)] * len(vectors),
-        out_specs=pl.BlockSpec((1, h + 64, D), lambda i: (i, 0, 0)),
-        out_shape=jax.ShapeDtypeStruct((2, h + 64, D), BF),
+        grid_spec=pltpu.PrefetchScalarGridSpec(
+            num_scalar_prefetch=1,
+            grid=(2,),
+            in_specs=[
+                pl.BlockSpec((h, WT), lambda i, s: (jnp.where(i == 0, 1 - s[1], s[1]), 0)),
+                whole(WT, D),
+            ]
+            + [whole(8, D)] * len(vectors),
+            out_specs=[whole(h + 64, D)] * 2,
+        ),
+        out_shape=[jax.ShapeDtypeStruct((h + 64, D), BF)] * 2,
         compiler_params=pltpu.CompilerParams(vmem_limit_bytes=60 * 2**20),
         cost_estimate=pl.CostEstimate(
             flops=2 * D * D * WT, bytes_accessed=4 * D * WT, transcendentals=0
         ),
         name="position_grads",
-    )(d_table, sinus, *vectors)
+    )(place, d_table, sinus, *vectors)
 
 
 def hidden_grads(place, dkv, k_own, k_other, v_own, v_other, count, reach):
@@ -590,18 +627,20 @@
     T = 128
     blocks = W // T
 
-    def kernel(s_ref, a_ref, b_ref, k0, k1, v0, v1, out_ref):
+    def kernel(s_ref, a_ref, b_ref, k0, k1, v0, v1, send_ref, keep_ref):
         s = pl.program_id(0)
+        odd = s_ref[1] == 1
         x = jnp.concatenate([a_ref[...], b_ref[...]], axis=1)
         for at, k, v in ((s_ref[0], k0, v0), (1 - s_ref[0], k1, v1)):
             g = nn(jnp.concatenate([k[...], v[...]], axis=1), x).astype(BF)
+            parts = []
             for n in range(2):
                 rel = 2 * s + n - s_ref[3] + reach
-                ok = (rel >= 0) & (rel < blocks)
                 part = g[:, T * n : T * (n + 1)]
-                out_ref[n, pl.ds(pl.multiple_of(at * h, h), h), :] = jnp.where(
-                    ok, part, jnp.zeros_like(part)
-                )
+                parts.append(jnp.where((rel >= 0) & (rel < blocks), part, jnp.zeros_like(part)))
+            rows = pl.ds(pl.multiple_of(at * h, h), h)
+            send_ref[0, rows, :] = jnp.where(odd, parts[0], parts[1])
+            keep_ref[0, rows, :] = jnp.where(odd, parts[1], parts[0])
 
     whole = pl.BlockSpec((h, D), lambda s, p: (0, 0))
     block = lambda n: pl.BlockSpec(
@@ -613,9 +652,9 @@
             num_scalar_prefetch=1,
             grid=(count // 2,),
             in_specs=[block(0), block(1), whole, whole, whole, whole],
-            out_specs=pl.BlockSpec((2, D, T), lambda s, p: (s, 0, 0)),
-        ),
-        out_shape=jax.ShapeDtypeStruct((count, D, T), BF),
+            out_specs=[pl.BlockSpec((1, D, T), lambda s, p: (s, 0, 0))] * 2,
+        ),
+        out_shape=[jax.ShapeDtypeStruct((count // 2, D, T), BF)] * 2,
         compiler_params=pltpu.CompilerParams(vmem_limit_bytes=60 * 2**20),
         cost_estimate=pl.CostEstimate(flops=2**20, bytes_accessed=2**20, transcendentals=0),
         name="hidden_grads",
@@ -909,13 +948,13 @@
         i_y = sh.flip(i_got, 1)
         u_got, key_values = lax.optimization_barrier((u_got, key_values))
         u_y = sh.flip(u_got, 1)
-    mixed_f, probs = att_fwd(q_lin, vecs, pen, kind_q, key_values, table, kaug)
-    mixed_low = mixed_f.astype(BF)
+    mixed_f, mixed_low, probs = att_fwd(q_lin, vecs, pen, kind_q, key_values, table, kaug)
     if sh.pair:
         place = jnp.stack([sh.f, sh.bit(0), sh.bit(1), ctx])
-        mixed_f, hid, fetched = lax.optimization_barrier((mixed_f, hidden, (i_got, i_y, u_got, u_y)))
+        mixed_f, mixed_low, hid, fetched = lax.optimization_barrier(
+            (mixed_f, mixed_low, hidden, (i_got, i_y, u_got, u_y))
+        )
         hidden_got = sh.trade(hid)
-        mixed_low = mixed_f.astype(BF)
         parts = (
             (output_proj, got_o, flip_o),
             (inner_proj,) + sh.pieces(*fetched[:2]),
@@ -974,24 +1013,24 @@
         dq_got = sh.trade(dq)
         ffn = lax.psum_scatter(ffn, "ctx", scatter_dimension=0, tiled=False)
 
-        d_hid = hidden_grads(
+        send, keep = hidden_grads(
             place, dkv.reshape(2 * D, W), key_proj, other_k, value_proj, other_v, C, R
         )
-        keep, send = sh.sides(sh.spread(d_hid), 0, sh.bits - 1)
         got = sh.flip(send, 0)
         dkv, _ = lax.optimization_barrier((dkv, send))
 
-        whole = key_grads(dkv, x_win)
-        whole, got = lax.optimization_barrier((whole, got))
-        d_hid = sh.add(keep, got)
+        send_w, keep_w = key_grads(place, dkv, x_win)
+        send_w, keep_w, got = lax.optimization_barrier((send_w, keep_w, got))
+        d_hid = sh.add(keep, got).reshape((2,) * (sh.bits - 1) + (D, T))
         keep, send = sh.sides(d_hid, 1, sh.bits - 2)
         got = sh.flip(send, 1)
-        keep_w, send_w = sh.sides(whole, 0, 0)
         got_w = sh.flip(send_w, 0)
-        d_table, _, _ = lax.optimization_barrier((d_table, send, send_w))
-        rest = position_grads(d_table, sinus, (att_vec, vec_a, vec_b))
-        rest, got_w = lax.optimization_barrier((rest, got_w))
-        whole = jnp.concatenate([sh.add(keep_w, got_w), sh.halve(rest, 0, 0)], axis=0)
+        d_table, _ = lax.optimization_barrier((d_table, send))
+        send_p, keep_p = position_grads(place, d_table, sinus, (att_vec, vec_a, vec_b))
+        send_p, keep_p, got_w = lax.optimization_barrier((send_p, keep_p, got_w))
+        whole = jnp.concatenate(
+            [sh.add(keep_w, got_w), sh.add(keep_p, sh.flip(send_p, 0))], axis=0
+        )
         keep_w, send_w = sh.order(whole[:, :dn], whole[:, dn:], sh.f)
         got_x = sh.trade(send_w)
         go, gq = (
@@ -1004,7 +1043,7 @@
             )
         )
         mine = sh.halve_cols(go, gq)
-        d_hid = sh.halve(sh.add(keep, got), 2, sh.bits - 3)
+        d_hid = sh.add(keep, got)
         got_x, d_hid, mine, ffn = lax.optimization_barrier((got_x, d_hid, mine, ffn))
         ffn = lax.all_gather(ffn, "ctx", axis=0, tiled=False)
         grads = jnp.concatenate([sh.add(keep_w, got_x), mine], axis=0)
@@ -1012,7 +1051,7 @@
         for k in range(1, sh.bits):
             grads = sh.halve(grads, k, grads.ndim - 3)
             if k + 2 < sh.bits:
-                d_hid = sh.halve(d_hid, k + 2, d_hid.ndim - 3)
+                d_hid = sh.halve(d_hid, k + 1, d_hid.ndim - 3)
                 grads, d_hid = lax.optimization_barrier((grads, d_hid))
         n = grads.shape[0]
         cut = (n // 2 + 15) // 16 * 16
@@ -1024,6 +1063,7 @@
             if i == 0:
                 one, two, d_hid, ffn = lax.optimization_barrier((one, two, d_hid, ffn))
             if i == 1:
+                d_hid = sh.halve(d_hid, sh.bits - 1, d_hid.ndim - 3)
                 gi, gu = ffn_final(ffn, inner_bias.shape[0] * 2, D)
                 one, two, gi, gu, d_hid = lax.optimization_barrier((one, two, gi, gu, d_hid))
                 input_grad = input_grads(place, d_res1, dq, query_proj, other_q, d_hid)

time: 351 us -> 344 us (0.980)
  waiting for transfers between devices: 109 us -> 118 us
  other arithmetic: 33.3 us -> 25 us
  local copies, waits for them, and re-layouts: 21.1 us -> 12.9 us
    squeeze x7 -> x4, local copies, waits for them, and re-layouts: 4.38 us -> 0.13 us  [sides(): lax.dynamic_index_in_dim(a, 1 - self.bit(k), axis, keepdims=False)]
    ppermute x2, waiting for transfers between devices: 6.08 us -> 9.6 us  [window(): lax.ppermute(down, 'ctx', [(i + 4, i) for i in range(self.count - 4)])]
    unnamed x84 -> x74, local copies, waits for them, and re-layouts: 8.62 us -> 5.8 us
  transfers between devices with their start and end apart: 49 -> 49, of which waited for: 20 -> 22; matrix products, arithmetic and copies ran while one was open for 18% -> 14% of each run, Pallas kernels for 23% -> 24%
where the time goes in v6:
time: 344 us; the launch traced here: 342 us
  waiting for transfers between devices  118 us (34%)
  Pallas kernels  108 us (31%)
  starting transfers between devices  47.9 us (14%)
  other arithmetic  25 us (7%)
  matrix products  15.9 us (5%)
  between operations  15.1 us (4%)
  local copies, waits for them, and re-layouts  12.9 us (4%)
    ppermute x31, waiting for transfers between devices, flip(): return lax.ppermute(a, 'ctx', [(i, i ^ 1 << k) for i in range(self.count)])  92.2 us
    ppermute x31, starting transfers between devices, flip(): return lax.ppermute(a, 'ctx', [(i, i ^ 1 << k) for i in range(self.count)])  20 us
    pallas_call x1, Pallas kernels, att_bwd(): pl.pallas_call(att_bwd_kernel, grid=(D // 128,), in_specs=[col(T), col(16...  17 us
    pallas_call x1, Pallas kernels, att_fwd(): pl.pallas_call(att_fwd_kernel, grid=(D // 128,), in_specs=[col(T), col(16...  16.3 us
    ppermute x12, starting transfers between devices, trade(): return lax.ppermute(a, 'fsdp', self.swap)  16.1 us
    pallas_call x1, Pallas kernels, ffn_bwd(): pl.pallas_call(kernel, grid_spec=pltpu.PrefetchScalarGridSpec(num_scalar_...  15.6 us
    ppermute x12, waiting for transfers between devices, trade(): return lax.ppermute(a, 'fsdp', self.swap)  14.5 us
    dot_general x3, matrix products, nn(): lax.dot_general(a, b, (((1,), (0,)), ((), ())), preferred_element_type=F32)  13 us
  transfers between devices with their start and end apart: 49, of which 22 were waited for; matrix products, arithmetic and copies ran while one was open for 14% of the time, Pallas kernels for 24%

profile of v6, /device:TPU:0, one launch (start us, length us, event | category | flops | bytes accessed | tf_op | source)
XLA Modules:
  0.0 342.3 jit_solution(2871714410789369099)
XLA Ops:
  7.3 1.5 pack_rows.1
  8.8 2.9 collective-permute-start.3
  14.1 1.6 collective-permute-start.4
  20.6 2.1 pad_maximum_fusion.x_ref
  26.7 4.6 %collective-permute-start.5 = (bf16[2,128,896]{2,1,0:T(8,128)(2,1)}, bf16[2,128,896]{2,1,0:T(8,128)(2,1)S(1)}, u32[]{:S(2)}, u32[]{:S(2)}) collective-permute-start(bf16[2,128,896]{2,1,0:T(8,128)(2,1)} %get-tuple-element.228), channel_id=1, source_target_pairs={{0,8},{2,10},{4,12},{6,14},{8,16},{10,18},{12,20},{14,22},{16,24},... | collective-permute-start | bytes 1376264 | tf_op jit(solution)/shard_map/ppermute | solution.py:816
  32.1 1.6 collective-permute-start.1
  33.7 5.1 %collective-permute-done.7 = bf16[2,128,896]{2,1,0:T(8,128)(2,1)S(1)} collective-permute-done((bf16[2,128,896]{2,1,0:T(8,128)(2,1)}, bf16[2,128,896]{2,1,0:T(8,128)(2,1)S(1)}, u32[]{:S(2)}, u32[]{:S(2)}) %collective-permute-start.7) | collective-permute-done | bytes 458784 | tf_op jit(solution)/shard_map/ppermute | solution.py:817
  40.1 4.6 %collective-permute-start.6 = (bf16[2,128,896]{2,1,0:T(8,128)(2,1)S(1)}, bf16[2,128,896]{2,1,0:T(8,128)(2,1)S(1)}, u32[]{:S(2)}, u32[]{:S(2)}) collective-permute-start(bf16[2,128,896]{2,1,0:T(8,128)(2,1)S(1)} %collective-permute-done.5), channel_id=1, source_target_pairs={{0,8},{2,10},{4,12},{6,14},{8,16},{10,18},{12,20},{14,22},{16,24},... | collective-permute-start | bytes 1376264 | tf_op jit(solution)/shard_map/ppermute | solution.py:816
  44.7 1.6 collective-permute-start.2
  46.4 4.5 %collective-permute-done.8 = bf16[2,128,896]{2,1,0:T(8,128)(2,1)S(1)} collective-permute-done((bf16[2,128,896]{2,1,0:T(8,128)(2,1)S(1)}, bf16[2,128,896]{2,1,0:T(8,128)(2,1)S(1)}, u32[]{:S(2)}, u32[]{:S(2)}) %collective-permute-start.8) | collective-permute-done | bytes 458784 | tf_op jit(solution)/shard_map/ppermute | solution.py:817
  52.3 1.9 collective-permute-done.2.refs_1_
  55.5 1.6 collective-permute-start.11
  66.0 4.4 %convolution_convert_fusion.t_ref = bf16[2304,768]{1,0:T(8,128)(2,1)} fusion(bf16[2304,768]{1,0:T(8,128)(2,1)S(1)} %copy-done.3, bf16[384,768]{1,0:T(8,128)(2,1)S(1)} %get-tuple-element.210, bf16[384,768]{1,0:T(8,128)(2,1)S(1)} %get-tuple-element.209), kind=kOutput, calls=%fused_computation.2 | convolution fusion | flops 2722037760 | bytes 8257536 | tf_op jit(solution)/shard_map/dot_general | solution.py:22
  72.4 7.5 %fusion.k_ref.v_ref = bf16[2176,1536]{1,0:T(8,128)(2,1)} fusion(bf16[2176,768]{1,0:T(8,128)(2,1)S(1)} %bitcast.159, f32[1536]{0:T(1024)S(1)} %concatenate.57, bf16[384,1536]{1,0:T(8,128)(2,1)S(1)} %get-tuple-element.204, bf16[384,1536]{1,0:T(8,128)(2,1)S(1)} %get-tuple-element.203), kind=kOutput, calls=%fused_computation.1 | convolution fusion | flops 5145231360 | bytes 12392448 | tf_op jit(solution)/shard_map/dot_general | solution.py:22
  79.9 3.0 collective-permute-done.10.refs_9_
  84.9 16.3 %att_fwd.1 = (f32[128,768]{1,0:T(8,128)}, bf16[128,768]{1,0:T(8,128)(2,1)}, bf16[12,128,2176]{2,1,0:T(8,128)(2,1)}) custom-call(f32[128,768]{1,0:T(8,128)} %convolution_bitcast_fusion.q_ref, f32[16,768]{1,0:T(8,128)} %pad_maximum_fusion.16.v_rows.v_ref, f32[128,128]{1,0:T(8,128)} %and_select_fusion.pen_ref, f32[128,128]{1,0:T(8,128)} %broadcast_in_dim.83.kind_ref, ...), custom_call_target="tpu_custom_call" | custom-call | flops 13690208256 | bytes 16711680 | tf_op jit(solution)/shard_map/att_fwd/pallas_call | solution.py:158
  102.9 3.3 collective-permute-done.18.refs_2_
  106.2 1.7 collective-permute-start.25
  110.1 10.3 %ffn_fwd.1 = (bf16[128,768]{1,0:T(8,128)(2,1)}, bf16[128,3072]{1,0:T(8,128)(2,1)}, f32[128,3072]{1,0:T(8,128)}, bf16[128,768]{1,0:T(8,128)(2,1)}, f32[128,768]{1...) custom-call(s32[4]{0:T(128)} %pad_add_fusion.s_ref, ...), custom_call_target="tpu_custom_call" | custom-call | flops 1207959552 | bytes 9437184 | tf_op jit(solution)/shard_map/ffn_fwd/pallas_call | solution.py:419
  120.4 1.8 collective-permute-start.23
  122.2 5.0 %collective-permute-done.23.dog_ref = bf16[128,768]{1,0:T(8,128)(2,1)S(1)} collective-permute-done((bf16[128,768]{1,0:T(8,128)(2,1)}, bf16[128,768]{1,0:T(8,128)(2,1)S(1)}, u32[]{:S(2)}, u32[]{:S(2)}) %collective-permute-start.23) | collective-permute-done | bytes 196640 | tf_op jit(solution)/shard_map/ppermute | solution.py:783
  127.9 15.6 %ffn_bwd.1 = (bf16[16,384,384]{2,1,0:T(8,128)(2,1)}, f32[128,768]{1,0:T(8,128)}, bf16[128,768]{1,0:T(8,128)(2,1)}, bf16[128,768]{1,0:T(8,128)(2,1)}, f32[8,768]{1,0:T(8,128)}) custom-call(s32[4]{0:T(128)} %pad_add_fusion.s_ref, f32[128,3072]{1,0:T(8,128)} %get-tuple-element.129.pre_ref, bf16[128,3072]{1,0:T(8,128)(2,1)} %get-tuple-element.130.act_ref, ...), custom_call_target="tpu_custom_call" | custom-call | flops 4227858432 | bytes 14155776 | tf_op jit(solution)/shard_map/ffn_bwd/pallas_call | solution.py:515
  143.6 17.0 %att_bwd.1 = (bf16[128,768]{1,0:T(8,128)(2,1)}, f32[8,768]{1,0:T(8,128)}, bf16[2,768,2176]{2,1,0:T(8,128)(2,1)}, bf16[768,2304]{1,0:T(8,128)(2,1)}) custom-call(f32[128,768]{1,0:T(8,128)} %convolution_bitcast_fusion.q_ref, f32[16,768]{1,0:T(8,128)} %pad_maximum_fusion.16.v_rows.v_ref, f32[128,128]{1,0:T(8,128)} %broadcast_in_dim.83.kind_ref, ...), custom_call_target="tpu_custom_call" | custom-call | flops 1048576 | bytes 1048576 | tf_op jit(solution)/shard_map/att_bwd/pallas_call | solution.py:185
  160.5 11.1 %hidden_grads.1 = (bf16[8,768,128]{2,1,0:T(8,128)(2,1)}, bf16[8,768,128]{2,1,0:T(8,128)(2,1)}) custom-call(s32[4]{0:T(128)} %pad_add_fusion.s_ref, bf16[1536,2176]{1,0:T(8,128)(2,1)} %bitcast.151, bf16[1536,2176]{1,0:T(8,128)(2,1)} %bitcast.152, bf16[384,768]{1,0:T(8,128)(2,1)} %k0.1, bf16[384,768]{1,0:T(8,128)(2,1)} %copy-done, bf16[384,768]{1,0:T(8,128)(2,1)} %v0.1, ...), custom_call_target="tpu_custom_call" | custom-call | flops 1048576 | bytes 1048576 | tf_op jit(solution)/shard_map/hidden_grads/pallas_call | solution.py:649
  171.7 11.1 %key_grads.1 = (bf16[768,768]{1,0:T(8,128)(2,1)}, bf16[768,768]{1,0:T(8,128)(2,1)}) custom-call(s32[4]{0:T(128)} %pad_add_fusion.s_ref, bf16[2,768,2176]{2,1,0:T(8,128)(2,1)} %get-tuple-element.142.kv_ref, bf16[2176,768]{1,0:T(8,128)(2,1)} %bitcast.160), custom_call_target="tpu_custom_call" | custom-call | flops 5133828096 | bytes 10027008 | tf_op jit(solution)/shard_map/key_grads/pallas_call | solution.py:555
  188.0 7.6 %position_grads.1 = (bf16[448,768]{1,0:T(8,128)(2,1)}, bf16[448,768]{1,0:T(8,128)(2,1)}) custom-call(s32[4]{0:T(128)} %pad_add_fusion.s_ref, bf16[768,2304]{1,0:T(8,128)(2,1)} %get-tuple-element.149.t_ref, bf16[2304,768]{1,0:T(8,128)(2,1)} %pad_maximum_fusion.x_ref, f32[8,768]{1,0:T(8,128)} %get-tuple-element.150.refs_0_, ...), custom_call_target="tpu_custom_call" | custom-call | flops 2717908992 | bytes 7077888 | tf_op jit(solution)/shard_map/position_grads/pallas_call | solution.py:602
  199.8 1.8 collective-permute-start.30
  201.6 1.6 add_convert_fusion.2
  206.1 16.8 %collective-permute-done.30 = bf16[2,2,768,128]{3,2,0,1:T(8,128)(2,1)S(1)} collective-permute-done((bf16[2,2,768,128]{3,2,0,1:T(8,128)(2,1)S(1)}, bf16[2,2,768,128]{3,2,0,1:T(8,128)(2,1)S(1)}, u32[]{:S(2)}, u32[]{:S(2)}) %collective-permute-start.30) | collective-permute-done | bytes 786464 | tf_op jit(solution)/shard_map/ppermute | solution.py:780
  223.1 3.4 %collective-permute-done.29 = bf16[1216,384]{1,0:T(8,128)(2,1)} collective-permute-done((bf16[1216,384]{1,0:T(8,128)(2,1)S(1)}, bf16[1216,384]{1,0:T(8,128)(2,1)}, u32[]{:S(2)}, u32[]{:S(2)}) %collective-permute-start.29) | collective-permute-done | bytes 933920 | tf_op jit(solution)/shard_map/ppermute | solution.py:783
  226.6 1.6 add_convert_fusion.3
  229.0 2.8 collective-permute-start.35
  231.8 12.3 %collective-permute-done.35 = bf16[2,768,128]{2,1,0:T(8,128)(2,1)} collective-permute-done((bf16[2,768,128]{2,1,0:T(8,128)(2,1)S(1)}, bf16[2,768,128]{2,1,0:T(8,128)(2,1)}, u32[]{:S(2)}, u32[]{:S(2)}) %collective-permute-start.35) | collective-permute-done | bytes 393248 | tf_op jit(solution)/shard_map/ppermute | solution.py:780
  245.2 5.0 %collective-permute-done.34 = bf16[2,2,248,384]{3,2,0,1:T(8,128)(2,1)S(1)} collective-permute-done((bf16[2,2,248,384]{3,2,0,1:T(8,128)(2,1)S(1)}, bf16[2,2,248,384]{3,2,0,1:T(8,128)(2,1)S(1)}, u32[]{:S(2)}, u32[]{:S(2)}) %collective-permute-start.34) | collective-permute-done | bytes 761888 | tf_op jit(solution)/shard_map/ppermute | solution.py:780
  250.4 2.3 collective-permute-start.36
  252.7 12.2 %collective-permute-done.36 = bf16[2,248,384]{2,1,0:T(8,128)(2,1)S(1)} collective-permute-done((bf16[2,248,384]{2,1,0:T(8,128)(2,1)S(1)}, bf16[2,248,384]{2,1,0:T(8,128)(2,1)S(1)}, u32[]{:S(2)}, u32[]{:S(2)}) %collective-permute-start.36) | collective-permute-done | bytes 380960 | tf_op jit(solution)/shard_map/ppermute | solution.py:780
  265.1 4.4 %collective-permute-start.37 = (bf16[248,384]{1,0:T(8,128)(2,1)S(1)}, bf16[248,384]{1,0:T(8,128)(2,1)S(1)}, u32[]{:S(2)}, u32[]{:S(2)}) collective-permute-start(bf16[248,384]{1,0:T(8,128)(2,1)S(1)} %dynamic-slice_bitcast_fusion.3), channel_id=1, source_target_pairs={{0,16},{2,18},{4,20},{6,22},{8,24},{10,26},{12,28},{14,30},{16,0},... | collective-permute-start | bytes 571400 | tf_op jit(solution)/shard_map/ppermute | solution.py:780
  269.5 18.0 %collective-permute-done.37 = bf16[248,384]{1,0:T(8,128)(2,1)S(1)} collective-permute-done((bf16[248,384]{1,0:T(8,128)(2,1)S(1)}, bf16[248,384]{1,0:T(8,128)(2,1)S(1)}, u32[]{:S(2)}, u32[]{:S(2)}) %collective-permute-start.37) | collective-permute-done | bytes 190496 | tf_op jit(solution)/shard_map/ppermute | solution.py:780
  287.8 4.4 %collective-permute-done.39 = bf16[120,384]{1,0:T(8,128)(2,1)S(1)} collective-permute-done((bf16[120,384]{1,0:T(8,128)(2,1)S(1)}, bf16[120,384]{1,0:T(8,128)(2,1)S(1)}, u32[]{:S(2)}, u32[]{:S(2)}) %collective-permute-start.39) | collective-permute-done | bytes 92192 | tf_op jit(solution)/shard_map/ppermute | solution.py:780
  292.3 6.7 %collective-permute-done.38 = bf16[128,384]{1,0:T(8,128)(2,1)S(1)} collective-permute-done((bf16[128,384]{1,0:T(8,128)(2,1)S(1)}, bf16[128,384]{1,0:T(8,128)(2,1)S(1)}, u32[]{:S(2)}, u32[]{:S(2)}) %collective-permute-start.38) | collective-permute-done | bytes 98336 | tf_op jit(solution)/shard_map/ppermute | solution.py:780
  299.1 3.0 collective-permute-start.42
  302.1 6.6 %ffn_final.1 = (f32[384,3072]{1,0:T(8,128)}, f32[1536,768]{1,0:T(8,128)}) custom-call(bf16[16,384,384]{2,1,0:T(8,128)(2,1)} %bitcast.185), custom_call_target="tpu_custom_call" | custom-call | flops 8589934592 | bytes 18874368 | tf_op jit(solution)/shard_map/ffn_final/pallas_call | solution.py:244
  308.8 4.7 %collective-permute-done.40 = bf16[2,128,384]{2,1,0:T(8,128)(2,1)S(1)} collective-permute-done((bf16[2,128,384]{2,1,0:T(8,128)(2,1)S(1)}, bf16[2,128,384]{2,1,0:T(8,128)(2,1)S(1)}, u32[]{:S(2)}, u32[]{:S(2)}) %collective-permute-start.40) | collective-permute-done | bytes 196640 | tf_op jit(solution)/shard_map/ppermute | solution.py:780
  314.3 3.4 input_grads.1
  317.7 4.1 %collective-permute-done.44 = bf16[2,2,120,384]{3,2,1,0:T(8,128)(2,1)S(1)} collective-permute-done((bf16[2,2,120,384]{3,2,1,0:T(8,128)(2,1)S(1)}, bf16[2,2,120,384]{3,2,1,0:T(8,128)(2,1)S(1)}, u32[]{:S(2)}, u32[]{:S(2)}) %collective-permute-start.44) | collective-permute-done | bytes 368672 | tf_op jit(solution)/shard_map/ppermute | solution.py:780
  323.4 2.8 collective-permute-done.46.d_ref
  328.0 5.9 %grad_final.1 = (f32[384,768]{1,0:T(8,128)}, f32[384,768]{1,0:T(8,128)}, f32[384,768]{1,0:T(8,128)}, f32[384,768]{1,0:T(8,128)}, f32[384,768]{1,0:T(8,128)}, /*index=5*/f32[64,384]{1,0:T(8,128)}) custom-call(s32[4]{0:T(128)} %pad_add_fusion.s_ref, bf16[1024,384]{1,0:T(8,128)(2,1)} %bitcast.162, bf16[960,384]{1,0:T(8,128)(2,1)} %bitcast.164, ...), custom_call_target="tpu_custom_call" | custom-call | tf_op jit(solution)/shard_map/grad_final/pallas_call | solution.py:717
  333.9 1.5 unpack_rows.1
  (232 shorter events, 52.9 us)
Async XLA Ops:
  7.2 219.3 %reduce-scatter.2.cloned.1.call-start = ((), (), s32[]{:S(2)}) async-start(), calls=%async_computation.1 | async-start | bytes 5013504 | tf_op jit(solution)/shard_map/reduce_scatter | solution.py:1014
  8.8 23.3 %collective-permute-start.3 = (f32[16,384]{1,0:T(8,128)}, f32[16,384]{1,0:T(8,128)S(1)}, u32[]{:S(2)}, u32[]{:S(2)}) collective-permute-start(f32[16,384]{1,0:T(8,128)} %pack_rows.1), channel_id=1, source_target_pairs={{0,1},{1,0},{2,3},{3,2},{4,5},{5,4},{6,7},{7,6},{8,9},{9,8},{10,11... | collective-permute-start | bytes 73736 | tf_op jit(solution)/shard_map/ppermute | solution.py:783
  14.1 9.3 %collective-permute-start.4 = (bf16[128,896]{1,0:T(8,128)(2,1)S(1)}, bf16[128,896]{1,0:T(8,128)(2,1)}, u32[]{:S(2)}, u32[]{:S(2)}) collective-permute-start(bf16[128,896]{1,0:T(8,128)(2,1)S(1)} %pad_maximum_fusion.13), channel_id=1, source_target_pairs={{0,4},{2,6},{4,0},{6,2},{8,12},{10,14},{12,8},{14,10},{16,20},{18,... | collective-permute-start | bytes 688136 | tf_op jit(solution)/shard_map/ppermute | solution.py:780
  18.1 36.1 %collective-permute-start = (bf16[384,768]{1,0:T(8,128)(2,1)}, bf16[384,768]{1,0:T(8,128)(2,1)}, u32[]{:S(2)}, u32[]{:S(2)}) collective-permute-start(bf16[384,768]{1,0:T(8,128)(2,1)} %get-tuple-element.224), channel_id=1, source_target_pairs={{0,1},{1,0},{2,3},{3,2},{4,5},{5,4},{6,7},{7,6},{8,9},{9,8},{10,11... | collective-permute-start | bytes 1769480 | tf_op jit(solution)/shard_map/ppermute | solution.py:783
  25.4 13.3 %collective-permute-start.7 = (bf16[2,128,896]{2,1,0:T(8,128)(2,1)}, bf16[2,128,896]{2,1,0:T(8,128)(2,1)S(1)}, u32[]{:S(2)}, u32[]{:S(2)}) collective-permute-start(bf16[2,128,896]{2,1,0:T(8,128)(2,1)} %get-tuple-element.228), channel_id=1, source_target_pairs={{8,0},{10,2},{12,4},{14,6},{16,8},{18,10},{20,12},{22,14},{24,16},... | collective-permute-start | bytes 1376264 | tf_op jit(solution)/shard_map/ppermute | solution.py:817
  26.7 13.3 %collective-permute-start.5 = (bf16[2,128,896]{2,1,0:T(8,128)(2,1)}, bf16[2,128,896]{2,1,0:T(8,128)(2,1)S(1)}, u32[]{:S(2)}, u32[]{:S(2)}) collective-permute-start(bf16[2,128,896]{2,1,0:T(8,128)(2,1)} %get-tuple-element.228), channel_id=1, source_target_pairs={{0,8},{2,10},{4,12},{6,14},{8,16},{10,18},{12,20},{14,22},{16,24},... | collective-permute-start | bytes 1376264 | tf_op jit(solution)/shard_map/ppermute | solution.py:816
  32.1 12.6 %collective-permute-start.14 = (bf16[1,2,128,896]{3,2,1,0:T(8,128)(2,1)}, bf16[1,2,128,896]{3,2,1,0:T(8,128)(2,1)S(1)}, u32[]{:S(2)}, u32[]{:S(2)}) collective-permute-start(bf16[1,2,128,896]{3,2,1,0:T(8,128)(2,1)} %get-tuple-element.227), channel_id=1, source_target_pairs={{0,2},{2,0},{4,6},{6,4},{8,10},{10,8},{12,14},{14,12},{16,18},{18,... | collective-permute-start | bytes 1376264 | tf_op jit(solution)/shard_map/ppermute | solution.py:780
  32.1 22.1 %collective-permute-start.1 = (bf16[384,768]{1,0:T(8,128)(2,1)S(1)}, bf16[384,768]{1,0:T(8,128)(2,1)S(1)}, u32[]{:S(2)}, u32[]{:S(2)}) collective-permute-start(bf16[384,768]{1,0:T(8,128)(2,1)S(1)} %get-tuple-element.226), channel_id=1, source_target_pairs={{0,1},{1,0},{2,3},{3,2},{4,5},{5,4},{6,7},{7,6},{8,9},{9,8},{10,11... | collective-permute-start | bytes 1769480 | tf_op jit(solution)/shard_map/ppermute | solution.py:783
  38.8 12.2 %collective-permute-start.8 = (bf16[2,128,896]{2,1,0:T(8,128)(2,1)S(1)}, bf16[2,128,896]{2,1,0:T(8,128)(2,1)S(1)}, u32[]{:S(2)}, u32[]{:S(2)}) collective-permute-start(bf16[2,128,896]{2,1,0:T(8,128)(2,1)S(1)} %collective-permute-done.7), channel_id=1, source_target_pairs={{8,0},{10,2},{12,4},{14,6},{16,8},{18,10},{20,12},{22,14},{24,16},... | collective-permute-start | bytes 1376264 | tf_op jit(solution)/shard_map/ppermute | solution.py:817
  40.1 12.1 %collective-permute-start.6 = (bf16[2,128,896]{2,1,0:T(8,128)(2,1)S(1)}, bf16[2,128,896]{2,1,0:T(8,128)(2,1)S(1)}, u32[]{:S(2)}, u32[]{:S(2)}) collective-permute-start(bf16[2,128,896]{2,1,0:T(8,128)(2,1)S(1)} %collective-permute-done.5), channel_id=1, source_target_pairs={{0,8},{2,10},{4,12},{6,14},{8,16},{10,18},{12,20},{14,22},{16,24},... | collective-permute-start | bytes 1376264 | tf_op jit(solution)/shard_map/ppermute | solution.py:816
  44.7 9.6 %collective-permute-start.2 = (bf16[192,768]{1,0:T(8,128)(2,1)}, bf16[192,768]{1,0:T(8,128)(2,1)S(1)}, u32[]{:S(2)}, u32[]{:S(2)}) collective-permute-start(bf16[192,768]{1,0:T(8,128)(2,1)} %constant_dynamic-slice_fusion.10), channel_id=1, source_target_pairs={{0,1},{1,0},{2,3},{3,2},{4,5},{5,4},{6,7},{7,6},{8,9},{9,8},{10,11... | collective-permute-start | bytes 884744 | tf_op jit(solution)/shard_map/ppermute | solution.py:783
  51.0 8.4 %collective-permute-start.13 = (bf16[2,2,128,896]{3,2,1,0:T(8,128)(2,1)S(1)}, bf16[2,2,128,896]{3,2,1,0:T(8,128)(2,1)S(1)}, u32[]{:S(2)}, u32[]{:S(2)}) collective-permute-start(bf16[2,2,128,896]{3,2,1,0:T(8,128)(2,1)S(1)} %pad_maximum_fusion.7), channel_id=1, source_target_pairs={{0,2},{2,0},{4,6},{6,4},{8,10},{10,8},{12,14},{14,12},{16,18},{18,... | collective-permute-start | bytes 2752520 | tf_op jit(solution)/shard_map/ppermute | solution.py:780
  52.3 18.1 %collective-permute-start.12 = (bf16[2,2,128,896]{3,2,1,0:T(8,128)(2,1)S(1)}, bf16[2,2,128,896]{3,2,1,0:T(8,128)(2,1)S(1)}, u32[]{:S(2)}, u32[]{:S(2)}) collective-permute-start(bf16[2,2,128,896]{3,2,1,0:T(8,128)(2,1)S(1)} %pad_maximum_fusion.6), channel_id=1, source_target_pairs={{0,2},{2,0},{4,6},{6,4},{8,10},{10,8},{12,14},{14,12},{16,18},{18,... | collective-permute-start | bytes 2752520 | tf_op jit(solution)/shard_map/ppermute | solution.py:780
  55.5 16.5 %collective-permute-start.11 = (bf16[96,3072]{1,0:T(8,128)(2,1)S(1)}, bf16[96,3072]{1,0:T(8,128)(2,1)S(1)}, u32[]{:S(2)}, u32[]{:S(2)}) collective-permute-start(bf16[96,3072]{1,0:T(8,128)(2,1)S(1)} %constant_dynamic-slice_fusion.8), channel_id=1, source_target_pairs={{0,1},{1,0},{2,3},{3,2},{4,5},{5,4},{6,7},{7,6},{8,9},{9,8},{10,11... | collective-permute-start | bytes 1769480 | tf_op jit(solution)/shard_map/ppermute | solution.py:783
  58.1 24.7 %collective-permute-start.10 = (bf16[384,768]{1,0:T(8,128)(2,1)S(1)}, bf16[384,768]{1,0:T(8,128)(2,1)S(1)}, u32[]{:S(2)}, u32[]{:S(2)}) collective-permute-start(bf16[384,768]{1,0:T(8,128)(2,1)S(1)} %constant_dynamic-slice_fusion.9), channel_id=1, source_target_pairs={{0,1},{1,0},{2,3},{3,2},{4,5},{5,4},{6,7},{7,6},{8,9},{9,8},{10,11... | collective-permute-start | bytes 1769480 | tf_op jit(solution)/shard_map/ppermute | solution.py:783
  59.4 2.4 collective-permute-start.15
  72.0 29.1 %collective-permute-start.16 = (bf16[96,3072]{1,0:T(8,128)(2,1)S(1)}, bf16[96,3072]{1,0:T(8,128)(2,1)S(1)}, u32[]{:S(2)}, u32[]{:S(2)}) collective-permute-start(bf16[96,3072]{1,0:T(8,128)(2,1)S(1)} %collective-permute-done.11.refs_4_), channel_id=1, source_target_pairs={{0,4},{2,6},{4,0},{6,2},{8,12},{10,14},{12,8},{14,10},{16,20},{18,... | collective-permute-start | bytes 1769480 | tf_op jit(solution)/shard_map/ppermute | solution.py:780
  82.9 18.3 %collective-permute-start.17 = (bf16[384,768]{1,0:T(8,128)(2,1)S(1)}, bf16[384,768]{1,0:T(8,128)(2,1)S(1)}, u32[]{:S(2)}, u32[]{:S(2)}) collective-permute-start(bf16[384,768]{1,0:T(8,128)(2,1)S(1)} %collective-permute-done.10.refs_9_), channel_id=1, source_target_pairs={{0,4},{2,6},{4,0},{6,2},{8,12},{10,14},{12,8},{14,10},{16,20},{18,... | collective-permute-start | bytes 1769480 | tf_op jit(solution)/shard_map/ppermute | solution.py:780
  101.2 6.7 %collective-permute-start.19 = (bf16[96,3072]{1,0:T(8,128)(2,1)S(1)}, bf16[96,3072]{1,0:T(8,128)(2,1)S(1)}, u32[]{:S(2)}, u32[]{:S(2)}) collective-permute-start(bf16[96,3072]{1,0:T(8,128)(2,1)S(1)} %collective-permute-done.11.refs_4_), channel_id=1, source_target_pairs={{0,2},{2,0},{4,6},{6,4},{8,10},{10,8},{12,14},{14,12},{16,18},{18,... | collective-permute-start | bytes 1769480 | tf_op jit(solution)/shard_map/ppermute | solution.py:780
  101.3 7.0 %collective-permute-start.20 = (bf16[96,3072]{1,0:T(8,128)(2,1)S(1)}, bf16[96,3072]{1,0:T(8,128)(2,1)S(1)}, u32[]{:S(2)}, u32[]{:S(2)}) collective-permute-start(bf16[96,3072]{1,0:T(8,128)(2,1)S(1)} %collective-permute-done.16.refs_5_), channel_id=1, source_target_pairs={{0,2},{2,0},{4,6},{6,4},{8,10},{10,8},{12,14},{14,12},{16,18},{18,... | collective-permute-start | bytes 1769480 | tf_op jit(solution)/shard_map/ppermute | solution.py:780
  101.8 6.5 %collective-permute-start.21 = (bf16[384,768]{1,0:T(8,128)(2,1)S(1)}, bf16[384,768]{1,0:T(8,128)(2,1)S(1)}, u32[]{:S(2)}, u32[]{:S(2)}) collective-permute-start(bf16[384,768]{1,0:T(8,128)(2,1)S(1)} %collective-permute-done.10.refs_9_), channel_id=1, source_target_pairs={{0,2},{2,0},{4,6},{6,4},{8,10},{10,8},{12,14},{14,12},{16,18},{18,... | collective-permute-start | bytes 1769480 | tf_op jit(solution)/shard_map/ppermute | solution.py:780
  101.8 6.4 %collective-permute-start.22 = (bf16[384,768]{1,0:T(8,128)(2,1)S(1)}, bf16[384,768]{1,0:T(8,128)(2,1)S(1)}, u32[]{:S(2)}, u32[]{:S(2)}) collective-permute-start(bf16[384,768]{1,0:T(8,128)(2,1)S(1)} %collective-permute-done.17.refs_10_), channel_id=1, source_target_pairs={{0,2},{2,0},{4,6},{6,4},{8,10},{10,8},{12,14},{14,12},{16,18},{18,... | collective-permute-start | bytes 1769480 | tf_op jit(solution)/shard_map/ppermute | solution.py:780
  102.3 3.9 %collective-permute-start.18 = (bf16[192,768]{1,0:T(8,128)(2,1)S(1)}, bf16[192,768]{1,0:T(8,128)(2,1)S(1)}, u32[]{:S(2)}, u32[]{:S(2)}) collective-permute-start(bf16[192,768]{1,0:T(8,128)(2,1)S(1)} %collective-permute-done.2.refs_1_), channel_id=1, source_target_pairs={{0,2},{2,0},{4,6},{6,4},{8,10},{10,8},{12,14},{14,12},{16,18},{18,... | collective-permute-start | bytes 884744 | tf_op jit(solution)/shard_map/ppermute | solution.py:780
  106.2 16.0 %collective-permute-start.25 = (bf16[128,768]{1,0:T(8,128)(2,1)S(1)}, bf16[128,768]{1,0:T(8,128)(2,1)}, u32[]{:S(2)}, u32[]{:S(2)}) collective-permute-start(bf16[128,768]{1,0:T(8,128)(2,1)S(1)} %bitcast.168), channel_id=1, source_target_pairs={{0,1},{1,0},{2,3},{3,2},{4,5},{5,4},{6,7},{7,6},{8,9},{9,8},{10,11... | collective-permute-start | bytes 589832 | tf_op jit(solution)/shard_map/ppermute | solution.py:783
  107.9 14.3 %collective-permute-start.24 = (bf16[128,768]{1,0:T(8,128)(2,1)}, bf16[128,768]{1,0:T(8,128)(2,1)S(1)}, u32[]{:S(2)}, u32[]{:S(2)}) collective-permute-start(bf16[128,768]{1,0:T(8,128)(2,1)} %get-tuple-element.136), channel_id=1, source_target_pairs={{0,1},{1,0},{2,3},{3,2},{4,5},{5,4},{6,7},{7,6},{8,9},{9,8},{10,11... | collective-permute-start | bytes 589832 | tf_op jit(solution)/shard_map/ppermute | solution.py:783
  120.4 6.8 %collective-permute-start.23 = (bf16[128,768]{1,0:T(8,128)(2,1)}, bf16[128,768]{1,0:T(8,128)(2,1)S(1)}, u32[]{:S(2)}, u32[]{:S(2)}) collective-permute-start(bf16[128,768]{1,0:T(8,128)(2,1)} %get-tuple-element.132.do_ref), channel_id=1, source_target_pairs={{0,1},{1,0},{2,3},{3,2},{4,5},{5,4},{6,7},{7,6},{8,9},{9,8},{10,11... | collective-permute-start | bytes 589832 | tf_op jit(solution)/shard_map/ppermute | solution.py:783
  143.5 155.5 %all-gather.3.cloned.1.call-start = ((), (), s32[]{:S(2)}) async-start(), calls=%async_computation.2 | async-start | bytes 5013504 | tf_op jit(solution)/shard_map/all_gather | solution.py:1048
  171.7 11.1 %collective-permute-start.26 = (bf16[8,768,128]{2,1,0:T(8,128)(2,1)}, bf16[8,768,128]{2,1,0:T(8,128)(2,1)S(1)}, u32[]{:S(2)}, u32[]{:S(2)}) collective-permute-start(bf16[8,768,128]{2,1,0:T(8,128)(2,1)} %get-tuple-element.141), channel_id=1, source_target_pairs={{0,2},{2,0},{4,6},{6,4},{8,10},{10,8},{12,14},{14,12},{16,18},{18,... | collective-permute-start | bytes 4718600 | tf_op jit(solution)/shard_map/ppermute | solution.py:780
  182.8 12.7 %collective-permute-start.27 = (bf16[768,768]{1,0:T(8,128)(2,1)}, bf16[768,768]{1,0:T(8,128)(2,1)}, u32[]{:S(2)}, u32[]{:S(2)}) collective-permute-start(bf16[768,768]{1,0:T(8,128)(2,1)} %get-tuple-element.155), channel_id=1, source_target_pairs={{0,2},{2,0},{4,6},{6,4},{8,10},{10,8},{12,14},{14,12},{16,18},{18,... | collective-permute-start | bytes 3538952 | tf_op jit(solution)/shard_map/ppermute | solution.py:780
  185.3 12.9 %collective-permute-start.32 = (bf16[128,768]{1,0:T(8,128)(2,1)}, bf16[128,768]{1,0:T(8,128)(2,1)}, u32[]{:S(2)}, u32[]{:S(2)}) collective-permute-start(bf16[128,768]{1,0:T(8,128)(2,1)} %get-tuple-element.160.dq_ref), channel_id=1, source_target_pairs={{0,1},{1,0},{2,3},{3,2},{4,5},{5,4},{6,7},{7,6},{8,9},{9,8},{10,11... | collective-permute-start | bytes 589832 | tf_op jit(solution)/shard_map/ppermute | solution.py:783
  186.8 9.9 %collective-permute-start.31 = (bf16[128,768]{1,0:T(8,128)(2,1)}, bf16[128,768]{1,0:T(8,128)(2,1)}, u32[]{:S(2)}, u32[]{:S(2)}) collective-permute-start(bf16[128,768]{1,0:T(8,128)(2,1)} %get-tuple-element.159), channel_id=1, source_target_pairs={{0,1},{1,0},{2,3},{3,2},{4,5},{5,4},{6,7},{7,6},{8,9},{9,8},{10,11... | collective-permute-start | bytes 589832 | tf_op jit(solution)/shard_map/ppermute | solution.py:783
  195.5 7.7 %collective-permute-start.28 = (bf16[448,768]{1,0:T(8,128)(2,1)}, bf16[448,768]{1,0:T(8,128)(2,1)S(1)}, u32[]{:S(2)}, u32[]{:S(2)}) collective-permute-start(bf16[448,768]{1,0:T(8,128)(2,1)} %get-tuple-element.158), channel_id=1, source_target_pairs={{0,2},{2,0},{4,6},{6,4},{8,10},{10,8},{12,14},{14,12},{16,18},{18,... | collective-permute-start | bytes 2064392 | tf_op jit(solution)/shard_map/ppermute | solution.py:780
  199.7 5.4 %collective-permute-start.33 = (bf16[768,384]{1,0:T(8,128)(2,1)S(1)}, bf16[768,384]{1,0:T(8,128)(2,1)S(1)}, u32[]{:S(2)}, u32[]{:S(2)}) collective-permute-start(bf16[768,384]{1,0:T(8,128)(2,1)S(1)} %get-tuple-element.251), channel_id=1, source_target_pairs={{0,2},{2,0},{4,6},{6,4},{8,10},{10,8},{12,14},{14,12},{16,18},{18,... | collective-permute-start | bytes 1769480 | tf_op jit(solution)/shard_map/ppermute | solution.py:780
  199.8 23.1 %collective-permute-start.30 = (bf16[2,2,768,128]{3,2,0,1:T(8,128)(2,1)S(1)}, bf16[2,2,768,128]{3,2,0,1:T(8,128)(2,1)S(1)}, u32[]{:S(2)}, u32[]{:S(2)}) collective-permute-start(bf16[2,2,768,128]{3,2,0,1:T(8,128)(2,1)S(1)} %bitcast.179), channel_id=1, source_target_pairs={{0,4},{2,6},{4,0},{6,2},{8,12},{10,14},{12,8},{14,10},{16,20},{18,... | collective-permute-start | bytes 2359304 | tf_op jit(solution)/shard_map/ppermute | solution.py:780
  203.6 22.9 %collective-permute-start.29 = (bf16[1216,384]{1,0:T(8,128)(2,1)S(1)}, bf16[1216,384]{1,0:T(8,128)(2,1)}, u32[]{:S(2)}, u32[]{:S(2)}) collective-permute-start(bf16[1216,384]{1,0:T(8,128)(2,1)S(1)} %broadcast_select_fusion.2), channel_id=1, source_target_pairs={{0,1},{1,0},{2,3},{3,2},{4,5},{5,4},{6,7},{7,6},{8,9},{9,8},{10,11... | collective-permute-start | bytes 2801672 | tf_op jit(solution)/shard_map/ppermute | solution.py:783
  228.7 21.5 %collective-permute-start.34 = (bf16[2,2,248,384]{3,2,0,1:T(8,128)(2,1)S(1)}, bf16[2,2,248,384]{3,2,0,1:T(8,128)(2,1)S(1)}, u32[]{:S(2)}, u32[]{:S(2)}) collective-permute-start(bf16[2,2,248,384]{3,2,0,1:T(8,128)(2,1)S(1)} %bitcast.180), channel_id=1, source_target_pairs={{0,4},{2,6},{4,0},{6,2},{8,12},{10,14},{12,8},{14,10},{16,20},{18,... | collective-permute-start | bytes 2285576 | tf_op jit(solution)/shard_map/ppermute | solution.py:780
  229.0 15.1 %collective-permute-start.35 = (bf16[2,768,128]{2,1,0:T(8,128)(2,1)S(1)}, bf16[2,768,128]{2,1,0:T(8,128)(2,1)}, u32[]{:S(2)}, u32[]{:S(2)}) collective-permute-start(bf16[2,768,128]{2,1,0:T(8,128)(2,1)S(1)} %dynamic-slice_bitcast_fusion), channel_id=1, source_target_pairs={{0,8},{2,10},{4,12},{6,14},{8,0},{10,2},{12,4},{14,6},{16,24},{18,... | collective-permute-start | bytes 1179656 | tf_op jit(solution)/shard_map/ppermute | solution.py:780
  250.4 14.5 %collective-permute-start.36 = (bf16[2,248,384]{2,1,0:T(8,128)(2,1)S(1)}, bf16[2,248,384]{2,1,0:T(8,128)(2,1)S(1)}, u32[]{:S(2)}, u32[]{:S(2)}) collective-permute-start(bf16[2,248,384]{2,1,0:T(8,128)(2,1)S(1)} %dynamic-slice_bitcast_fusion.1), channel_id=1, source_target_pairs={{0,8},{2,10},{4,12},{6,14},{8,0},{10,2},{12,4},{14,6},{16,24},{18,... | collective-permute-start | bytes 1142792 | tf_op jit(solution)/shard_map/ppermute | solution.py:780
  265.1 22.4 %collective-permute-start.37 = (bf16[248,384]{1,0:T(8,128)(2,1)S(1)}, bf16[248,384]{1,0:T(8,128)(2,1)S(1)}, u32[]{:S(2)}, u32[]{:S(2)}) collective-permute-start(bf16[248,384]{1,0:T(8,128)(2,1)S(1)} %dynamic-slice_bitcast_fusion.3), channel_id=1, source_target_pairs={{0,16},{2,18},{4,20},{6,22},{8,24},{10,26},{12,28},{14,30},{16,0},... | collective-permute-start | bytes 571400 | tf_op jit(solution)/shard_map/ppermute | solution.py:780
  287.6 4.6 %collective-permute-start.39 = (bf16[120,384]{1,0:T(8,128)(2,1)S(1)}, bf16[120,384]{1,0:T(8,128)(2,1)S(1)}, u32[]{:S(2)}, u32[]{:S(2)}) collective-permute-start(bf16[120,384]{1,0:T(8,128)(2,1)S(1)} %slice.61), channel_id=1, source_target_pairs={{0,4},{2,6},{4,0},{6,2},{8,12},{10,14},{12,8},{14,10},{16,20},{18,... | collective-permute-start | bytes 276488 | tf_op jit(solution)/shard_map/ppermute | solution.py:780
  287.7 11.2 %collective-permute-start.38 = (bf16[128,384]{1,0:T(8,128)(2,1)S(1)}, bf16[128,384]{1,0:T(8,128)(2,1)S(1)}, u32[]{:S(2)}, u32[]{:S(2)}) collective-permute-start(bf16[128,384]{1,0:T(8,128)(2,1)S(1)} %slice.60), channel_id=1, source_target_pairs={{0,16},{2,18},{4,20},{6,22},{8,24},{10,26},{12,28},{14,30},{16,0},... | collective-permute-start | bytes 294920 | tf_op jit(solution)/shard_map/ppermute | solution.py:780
  299.0 9.7 %collective-permute-start.41 = (bf16[2,120,384]{2,1,0:T(8,128)(2,1)S(1)}, bf16[2,120,384]{2,1,0:T(8,128)(2,1)S(1)}, u32[]{:S(2)}, u32[]{:S(2)}) collective-permute-start(bf16[2,120,384]{2,1,0:T(8,128)(2,1)S(1)} %pad_maximum_fusion.15), channel_id=1, source_target_pairs={{0,16},{2,18},{4,20},{6,22},{8,24},{10,26},{12,28},{14,30},{16,0},... | collective-permute-start | bytes 552968 | tf_op jit(solution)/shard_map/ppermute | solution.py:780
  299.1 14.4 %collective-permute-start.42 = (bf16[768,128]{1,0:T(8,128)(2,1)S(1)}, bf16[768,128]{1,0:T(8,128)(2,1)S(1)}, u32[]{:S(2)}, u32[]{:S(2)}) collective-permute-start(bf16[768,128]{1,0:T(8,128)(2,1)S(1)} %dynamic-slice_bitcast_fusion.2), channel_id=1, source_target_pairs={{0,16},{2,18},{4,20},{6,22},{8,24},{10,26},{12,28},{14,30},{16,0},... | collective-permute-start | bytes 589832 | tf_op jit(solution)/shard_map/ppermute | solution.py:780
  302.1 11.4 %collective-permute-start.40 = (bf16[2,128,384]{2,1,0:T(8,128)(2,1)S(1)}, bf16[2,128,384]{2,1,0:T(8,128)(2,1)S(1)}, u32[]{:S(2)}, u32[]{:S(2)}) collective-permute-start(bf16[2,128,384]{2,1,0:T(8,128)(2,1)S(1)} %pad_maximum_fusion.14), channel_id=1, source_target_pairs={{0,8},{2,10},{4,12},{6,14},{8,0},{10,2},{12,4},{14,6},{16,24},{18,... | collective-permute-start | bytes 589832 | tf_op jit(solution)/shard_map/ppermute | solution.py:780
  314.3 7.5 %collective-permute-start.44 = (bf16[2,2,120,384]{3,2,1,0:T(8,128)(2,1)S(1)}, bf16[2,2,120,384]{3,2,1,0:T(8,128)(2,1)S(1)}, u32[]{:S(2)}, u32[]{:S(2)}) collective-permute-start(bf16[2,2,120,384]{3,2,1,0:T(8,128)(2,1)S(1)} %pad_maximum_fusion.12), channel_id=1, source_target_pairs={{0,8},{2,10},{4,12},{6,14},{8,0},{10,2},{12,4},{14,6},{16,24},{18,... | collective-permute-start | bytes 1105928 | tf_op jit(solution)/shard_map/ppermute | solution.py:780
  314.3 8.2 %collective-permute-start.43 = (bf16[2,2,128,384]{3,2,0,1:T(8,128)(2,1)S(1)}, bf16[2,2,128,384]{3,2,0,1:T(8,128)(2,1)S(1)}, u32[]{:S(2)}, u32[]{:S(2)}) collective-permute-start(bf16[2,2,128,384]{3,2,0,1:T(8,128)(2,1)S(1)} %pad_maximum_fusion.11), channel_id=1, source_target_pairs={{0,4},{2,6},{4,0},{6,2},{8,12},{10,14},{12,8},{14,10},{16,20},{18,... | collective-permute-start | bytes 1179656 | tf_op jit(solution)/shard_map/ppermute | solution.py:780
  322.8 3.4 collective-permute-start.45
  322.9 3.3 collective-permute-start.46
  (38 other events, 252.3 us)
Sparse Core Ops, SparseCore 0:
  143.6 80.0 reduce-scatter.1
  226.7 65.0 all-gather.2

commit v7 on v6

--- a/solution.py
+++ b/solution.py
@@ -723,6 +723,7 @@
             out_specs=[out] * 5 + [lanes(64)],
         ),
         out_shape=[jax.ShapeDtypeStruct((dn, D), F32)] * 5 + [jax.ShapeDtypeStruct((64, dn), F32)],
+        compiler_params=pltpu.CompilerParams(vmem_limit_bytes=60 * 2**20),
         name="grad_final",
     )(place, one, two, one_got, two_got)
 

time: 344 us -> 344 us (level)
  no operation moved by 1% of the time
where the time goes in v7:
time: 344 us; the launch traced here: 342 us
  waiting for transfers between devices  118 us (34%)
  Pallas kernels  108 us (31%)
  starting transfers between devices  47.9 us (14%)
  other arithmetic  25 us (7%)
  matrix products  15.9 us (5%)
  between operations  15.1 us (4%)
  local copies, waits for them, and re-layouts  12.9 us (4%)
    ppermute x31, waiting for transfers between devices, flip(): return lax.ppermute(a, 'ctx', [(i, i ^ 1 << k) for i in range(self.count)])  92.2 us
    ppermute x31, starting transfers between devices, flip(): return lax.ppermute(a, 'ctx', [(i, i ^ 1 << k) for i in range(self.count)])  20 us
    pallas_call x1, Pallas kernels, att_bwd(): pl.pallas_call(att_bwd_kernel, grid=(D // 128,), in_specs=[col(T), col(16...  17 us
    pallas_call x1, Pallas kernels, att_fwd(): pl.pallas_call(att_fwd_kernel, grid=(D // 128,), in_specs=[col(T), col(16...  16.3 us
    ppermute x12, starting transfers between devices, trade(): return lax.ppermute(a, 'fsdp', self.swap)  16.1 us
    pallas_call x1, Pallas kernels, ffn_bwd(): pl.pallas_call(kernel, grid_spec=pltpu.PrefetchScalarGridSpec(num_scalar_...  15.6 us
    ppermute x12, waiting for transfers between devices, trade(): return lax.ppermute(a, 'fsdp', self.swap)  14.5 us
    dot_general x3, matrix products, nn(): lax.dot_general(a, b, (((1,), (0,)), ((), ())), preferred_element_type=F32)  13 us
  transfers between devices with their start and end apart: 49, of which 22 were waited for; matrix products, arithmetic and copies ran while one was open for 14% of the time, Pallas kernels for 24%

profile of v7, /device:TPU:0, one launch (start us, length us, event | category | flops | bytes accessed | tf_op | source)
XLA Modules:
  0.0 342.3 jit_solution(12752282270924085836)
XLA Ops:
  7.3 1.5 pack_rows.1
  8.8 2.9 collective-permute-start.3
  14.1 1.6 collective-permute-start.4
  20.6 2.1 pad_maximum_fusion.x_ref
  26.7 4.6 %collective-permute-start.5 = (bf16[2,128,896]{2,1,0:T(8,128)(2,1)}, bf16[2,128,896]{2,1,0:T(8,128)(2,1)S(1)}, u32[]{:S(2)}, u32[]{:S(2)}) collective-permute-start(bf16[2,128,896]{2,1,0:T(8,128)(2,1)} %get-tuple-element.228), channel_id=1, source_target_pairs={{0,8},{2,10},{4,12},{6,14},{8,16},{10,18},{12,20},{14,22},{16,24},... | collective-permute-start | bytes 1376264 | tf_op jit(solution)/shard_map/ppermute | solution.py:817
  32.1 1.6 collective-permute-start.1
  33.7 5.1 %collective-permute-done.7 = bf16[2,128,896]{2,1,0:T(8,128)(2,1)S(1)} collective-permute-done((bf16[2,128,896]{2,1,0:T(8,128)(2,1)}, bf16[2,128,896]{2,1,0:T(8,128)(2,1)S(1)}, u32[]{:S(2)}, u32[]{:S(2)}) %collective-permute-start.7) | collective-permute-done | bytes 458784 | tf_op jit(solution)/shard_map/ppermute | solution.py:818
  40.1 4.6 %collective-permute-start.6 = (bf16[2,128,896]{2,1,0:T(8,128)(2,1)S(1)}, bf16[2,128,896]{2,1,0:T(8,128)(2,1)S(1)}, u32[]{:S(2)}, u32[]{:S(2)}) collective-permute-start(bf16[2,128,896]{2,1,0:T(8,128)(2,1)S(1)} %collective-permute-done.5), channel_id=1, source_target_pairs={{0,8},{2,10},{4,12},{6,14},{8,16},{10,18},{12,20},{14,22},{16,24},... | collective-permute-start | bytes 1376264 | tf_op jit(solution)/shard_map/ppermute | solution.py:817
  44.7 1.6 collective-permute-start.2
  46.4 4.5 %collective-permute-done.8 = bf16[2,128,896]{2,1,0:T(8,128)(2,1)S(1)} collective-permute-done((bf16[2,128,896]{2,1,0:T(8,128)(2,1)S(1)}, bf16[2,128,896]{2,1,0:T(8,128)(2,1)S(1)}, u32[]{:S(2)}, u32[]{:S(2)}) %collective-permute-start.8) | collective-permute-done | bytes 458784 | tf_op jit(solution)/shard_map/ppermute | solution.py:818
  52.3 1.9 collective-permute-done.2.refs_1_
  55.5 1.6 collective-permute-start.11
  66.0 4.4 %convolution_convert_fusion.t_ref = bf16[2304,768]{1,0:T(8,128)(2,1)} fusion(bf16[2304,768]{1,0:T(8,128)(2,1)S(1)} %copy-done.3, bf16[384,768]{1,0:T(8,128)(2,1)S(1)} %get-tuple-element.210, bf16[384,768]{1,0:T(8,128)(2,1)S(1)} %get-tuple-element.209), kind=kOutput, calls=%fused_computation.2 | convolution fusion | flops 2722037760 | bytes 8257536 | tf_op jit(solution)/shard_map/dot_general | solution.py:22
  72.4 7.5 %fusion.k_ref.v_ref = bf16[2176,1536]{1,0:T(8,128)(2,1)} fusion(bf16[2176,768]{1,0:T(8,128)(2,1)S(1)} %bitcast.159, f32[1536]{0:T(1024)S(1)} %concatenate.57, bf16[384,1536]{1,0:T(8,128)(2,1)S(1)} %get-tuple-element.204, bf16[384,1536]{1,0:T(8,128)(2,1)S(1)} %get-tuple-element.203), kind=kOutput, calls=%fused_computation.1 | convolution fusion | flops 5145231360 | bytes 12392448 | tf_op jit(solution)/shard_map/dot_general | solution.py:22
  79.9 3.0 collective-permute-done.10.refs_9_
  84.9 16.3 %att_fwd.1 = (f32[128,768]{1,0:T(8,128)}, bf16[128,768]{1,0:T(8,128)(2,1)}, bf16[12,128,2176]{2,1,0:T(8,128)(2,1)}) custom-call(f32[128,768]{1,0:T(8,128)} %convolution_bitcast_fusion.q_ref, f32[16,768]{1,0:T(8,128)} %pad_maximum_fusion.16.v_rows.v_ref, f32[128,128]{1,0:T(8,128)} %and_select_fusion.pen_ref, f32[128,128]{1,0:T(8,128)} %broadcast_in_dim.83.kind_ref, ...), custom_call_target="tpu_custom_call" | custom-call | flops 13690208256 | bytes 16711680 | tf_op jit(solution)/shard_map/att_fwd/pallas_call | solution.py:158
  102.9 3.3 collective-permute-done.18.refs_2_
  106.2 1.7 collective-permute-start.25
  110.1 10.3 %ffn_fwd.1 = (bf16[128,768]{1,0:T(8,128)(2,1)}, bf16[128,3072]{1,0:T(8,128)(2,1)}, f32[128,3072]{1,0:T(8,128)}, bf16[128,768]{1,0:T(8,128)(2,1)}, f32[128,768]{1...) custom-call(s32[4]{0:T(128)} %pad_add_fusion.s_ref, ...), custom_call_target="tpu_custom_call" | custom-call | flops 1207959552 | bytes 9437184 | tf_op jit(solution)/shard_map/ffn_fwd/pallas_call | solution.py:419
  120.4 1.8 collective-permute-start.23
  122.2 5.0 %collective-permute-done.23.dog_ref = bf16[128,768]{1,0:T(8,128)(2,1)S(1)} collective-permute-done((bf16[128,768]{1,0:T(8,128)(2,1)}, bf16[128,768]{1,0:T(8,128)(2,1)S(1)}, u32[]{:S(2)}, u32[]{:S(2)}) %collective-permute-start.23) | collective-permute-done | bytes 196640 | tf_op jit(solution)/shard_map/ppermute | solution.py:784
  127.9 15.6 %ffn_bwd.1 = (bf16[16,384,384]{2,1,0:T(8,128)(2,1)}, f32[128,768]{1,0:T(8,128)}, bf16[128,768]{1,0:T(8,128)(2,1)}, bf16[128,768]{1,0:T(8,128)(2,1)}, f32[8,768]{1,0:T(8,128)}) custom-call(s32[4]{0:T(128)} %pad_add_fusion.s_ref, f32[128,3072]{1,0:T(8,128)} %get-tuple-element.129.pre_ref, bf16[128,3072]{1,0:T(8,128)(2,1)} %get-tuple-element.130.act_ref, ...), custom_call_target="tpu_custom_call" | custom-call | flops 4227858432 | bytes 14155776 | tf_op jit(solution)/shard_map/ffn_bwd/pallas_call | solution.py:515
  143.6 17.0 %att_bwd.1 = (bf16[128,768]{1,0:T(8,128)(2,1)}, f32[8,768]{1,0:T(8,128)}, bf16[2,768,2176]{2,1,0:T(8,128)(2,1)}, bf16[768,2304]{1,0:T(8,128)(2,1)}) custom-call(f32[128,768]{1,0:T(8,128)} %convolution_bitcast_fusion.q_ref, f32[16,768]{1,0:T(8,128)} %pad_maximum_fusion.16.v_rows.v_ref, f32[128,128]{1,0:T(8,128)} %broadcast_in_dim.83.kind_ref, ...), custom_call_target="tpu_custom_call" | custom-call | flops 1048576 | bytes 1048576 | tf_op jit(solution)/shard_map/att_bwd/pallas_call | solution.py:185
  160.5 11.1 %hidden_grads.1 = (bf16[8,768,128]{2,1,0:T(8,128)(2,1)}, bf16[8,768,128]{2,1,0:T(8,128)(2,1)}) custom-call(s32[4]{0:T(128)} %pad_add_fusion.s_ref, bf16[1536,2176]{1,0:T(8,128)(2,1)} %bitcast.151, bf16[1536,2176]{1,0:T(8,128)(2,1)} %bitcast.152, bf16[384,768]{1,0:T(8,128)(2,1)} %k0.1, bf16[384,768]{1,0:T(8,128)(2,1)} %copy-done, bf16[384,768]{1,0:T(8,128)(2,1)} %v0.1, ...), custom_call_target="tpu_custom_call" | custom-call | flops 1048576 | bytes 1048576 | tf_op jit(solution)/shard_map/hidden_grads/pallas_call | solution.py:649
  171.7 11.1 %key_grads.1 = (bf16[768,768]{1,0:T(8,128)(2,1)}, bf16[768,768]{1,0:T(8,128)(2,1)}) custom-call(s32[4]{0:T(128)} %pad_add_fusion.s_ref, bf16[2,768,2176]{2,1,0:T(8,128)(2,1)} %get-tuple-element.142.kv_ref, bf16[2176,768]{1,0:T(8,128)(2,1)} %bitcast.160), custom_call_target="tpu_custom_call" | custom-call | flops 5133828096 | bytes 10027008 | tf_op jit(solution)/shard_map/key_grads/pallas_call | solution.py:555
  188.0 7.6 %position_grads.1 = (bf16[448,768]{1,0:T(8,128)(2,1)}, bf16[448,768]{1,0:T(8,128)(2,1)}) custom-call(s32[4]{0:T(128)} %pad_add_fusion.s_ref, bf16[768,2304]{1,0:T(8,128)(2,1)} %get-tuple-element.149.t_ref, bf16[2304,768]{1,0:T(8,128)(2,1)} %pad_maximum_fusion.x_ref, f32[8,768]{1,0:T(8,128)} %get-tuple-element.150.refs_0_, ...), custom_call_target="tpu_custom_call" | custom-call | flops 2717908992 | bytes 7077888 | tf_op jit(solution)/shard_map/position_grads/pallas_call | solution.py:602
  199.8 1.8 collective-permute-start.30
  201.6 1.6 add_convert_fusion.2
  206.1 16.8 %collective-permute-done.30 = bf16[2,2,768,128]{3,2,0,1:T(8,128)(2,1)S(1)} collective-permute-done((bf16[2,2,768,128]{3,2,0,1:T(8,128)(2,1)S(1)}, bf16[2,2,768,128]{3,2,0,1:T(8,128)(2,1)S(1)}, u32[]{:S(2)}, u32[]{:S(2)}) %collective-permute-start.30) | collective-permute-done | bytes 786464 | tf_op jit(solution)/shard_map/ppermute | solution.py:781
  223.1 3.4 %collective-permute-done.29 = bf16[1216,384]{1,0:T(8,128)(2,1)} collective-permute-done((bf16[1216,384]{1,0:T(8,128)(2,1)S(1)}, bf16[1216,384]{1,0:T(8,128)(2,1)}, u32[]{:S(2)}, u32[]{:S(2)}) %collective-permute-start.29) | collective-permute-done | bytes 933920 | tf_op jit(solution)/shard_map/ppermute | solution.py:784
  226.6 1.6 add_convert_fusion.3
  229.0 2.8 collective-permute-start.35
  231.8 12.3 %collective-permute-done.35 = bf16[2,768,128]{2,1,0:T(8,128)(2,1)} collective-permute-done((bf16[2,768,128]{2,1,0:T(8,128)(2,1)S(1)}, bf16[2,768,128]{2,1,0:T(8,128)(2,1)}, u32[]{:S(2)}, u32[]{:S(2)}) %collective-permute-start.35) | collective-permute-done | bytes 393248 | tf_op jit(solution)/shard_map/ppermute | solution.py:781
  245.2 5.0 %collective-permute-done.34 = bf16[2,2,248,384]{3,2,0,1:T(8,128)(2,1)S(1)} collective-permute-done((bf16[2,2,248,384]{3,2,0,1:T(8,128)(2,1)S(1)}, bf16[2,2,248,384]{3,2,0,1:T(8,128)(2,1)S(1)}, u32[]{:S(2)}, u32[]{:S(2)}) %collective-permute-start.34) | collective-permute-done | bytes 761888 | tf_op jit(solution)/shard_map/ppermute | solution.py:781
  250.4 2.3 collective-permute-start.36
  252.7 12.2 %collective-permute-done.36 = bf16[2,248,384]{2,1,0:T(8,128)(2,1)S(1)} collective-permute-done((bf16[2,248,384]{2,1,0:T(8,128)(2,1)S(1)}, bf16[2,248,384]{2,1,0:T(8,128)(2,1)S(1)}, u32[]{:S(2)}, u32[]{:S(2)}) %collective-permute-start.36) | collective-permute-done | bytes 380960 | tf_op jit(solution)/shard_map/ppermute | solution.py:781
  265.1 4.4 %collective-permute-start.37 = (bf16[248,384]{1,0:T(8,128)(2,1)S(1)}, bf16[248,384]{1,0:T(8,128)(2,1)S(1)}, u32[]{:S(2)}, u32[]{:S(2)}) collective-permute-start(bf16[248,384]{1,0:T(8,128)(2,1)S(1)} %dynamic-slice_bitcast_fusion.3), channel_id=1, source_target_pairs={{0,16},{2,18},{4,20},{6,22},{8,24},{10,26},{12,28},{14,30},{16,0},... | collective-permute-start | bytes 571400 | tf_op jit(solution)/shard_map/ppermute | solution.py:781
  269.5 18.0 %collective-permute-done.37 = bf16[248,384]{1,0:T(8,128)(2,1)S(1)} collective-permute-done((bf16[248,384]{1,0:T(8,128)(2,1)S(1)}, bf16[248,384]{1,0:T(8,128)(2,1)S(1)}, u32[]{:S(2)}, u32[]{:S(2)}) %collective-permute-start.37) | collective-permute-done | bytes 190496 | tf_op jit(solution)/shard_map/ppermute | solution.py:781
  287.8 4.4 %collective-permute-done.39 = bf16[120,384]{1,0:T(8,128)(2,1)S(1)} collective-permute-done((bf16[120,384]{1,0:T(8,128)(2,1)S(1)}, bf16[120,384]{1,0:T(8,128)(2,1)S(1)}, u32[]{:S(2)}, u32[]{:S(2)}) %collective-permute-start.39) | collective-permute-done | bytes 92192 | tf_op jit(solution)/shard_map/ppermute | solution.py:781
  292.3 6.7 %collective-permute-done.38 = bf16[128,384]{1,0:T(8,128)(2,1)S(1)} collective-permute-done((bf16[128,384]{1,0:T(8,128)(2,1)S(1)}, bf16[128,384]{1,0:T(8,128)(2,1)S(1)}, u32[]{:S(2)}, u32[]{:S(2)}) %collective-permute-start.38) | collective-permute-done | bytes 98336 | tf_op jit(solution)/shard_map/ppermute | solution.py:781
  299.1 3.0 collective-permute-start.42
  302.1 6.6 %ffn_final.1 = (f32[384,3072]{1,0:T(8,128)}, f32[1536,768]{1,0:T(8,128)}) custom-call(bf16[16,384,384]{2,1,0:T(8,128)(2,1)} %bitcast.185), custom_call_target="tpu_custom_call" | custom-call | flops 8589934592 | bytes 18874368 | tf_op jit(solution)/shard_map/ffn_final/pallas_call | solution.py:244
  308.8 4.7 %collective-permute-done.40 = bf16[2,128,384]{2,1,0:T(8,128)(2,1)S(1)} collective-permute-done((bf16[2,128,384]{2,1,0:T(8,128)(2,1)S(1)}, bf16[2,128,384]{2,1,0:T(8,128)(2,1)S(1)}, u32[]{:S(2)}, u32[]{:S(2)}) %collective-permute-start.40) | collective-permute-done | bytes 196640 | tf_op jit(solution)/shard_map/ppermute | solution.py:781
  314.3 3.4 input_grads.1
  317.7 4.1 %collective-permute-done.44 = bf16[2,2,120,384]{3,2,1,0:T(8,128)(2,1)S(1)} collective-permute-done((bf16[2,2,120,384]{3,2,1,0:T(8,128)(2,1)S(1)}, bf16[2,2,120,384]{3,2,1,0:T(8,128)(2,1)S(1)}, u32[]{:S(2)}, u32[]{:S(2)}) %collective-permute-start.44) | collective-permute-done | bytes 368672 | tf_op jit(solution)/shard_map/ppermute | solution.py:781
  323.4 2.8 collective-permute-done.46.d_ref
  328.0 5.9 %grad_final.1 = (f32[384,768]{1,0:T(8,128)}, f32[384,768]{1,0:T(8,128)}, f32[384,768]{1,0:T(8,128)}, f32[384,768]{1,0:T(8,128)}, f32[384,768]{1,0:T(8,128)}, /*index=5*/f32[64,384]{1,0:T(8,128)}) custom-call(s32[4]{0:T(128)} %pad_add_fusion.s_ref, bf16[1024,384]{1,0:T(8,128)(2,1)} %bitcast.162, bf16[960,384]{1,0:T(8,128)(2,1)} %bitcast.164, ...), custom_call_target="tpu_custom_call" | custom-call | tf_op jit(solution)/shard_map/grad_final/pallas_call | solution.py:717
  333.9 1.5 unpack_rows.1
  (232 shorter events, 52.9 us)
Async XLA Ops:
  7.2 219.3 %reduce-scatter.2.cloned.1.call-start = ((), (), s32[]{:S(2)}) async-start(), calls=%async_computation.1 | async-start | bytes 5013504 | tf_op jit(solution)/shard_map/reduce_scatter | solution.py:1015
  8.8 23.3 %collective-permute-start.3 = (f32[16,384]{1,0:T(8,128)}, f32[16,384]{1,0:T(8,128)S(1)}, u32[]{:S(2)}, u32[]{:S(2)}) collective-permute-start(f32[16,384]{1,0:T(8,128)} %pack_rows.1), channel_id=1, source_target_pairs={{0,1},{1,0},{2,3},{3,2},{4,5},{5,4},{6,7},{7,6},{8,9},{9,8},{10,11... | collective-permute-start | bytes 73736 | tf_op jit(solution)/shard_map/ppermute | solution.py:784
  14.1 9.3 %collective-permute-start.4 = (bf16[128,896]{1,0:T(8,128)(2,1)S(1)}, bf16[128,896]{1,0:T(8,128)(2,1)}, u32[]{:S(2)}, u32[]{:S(2)}) collective-permute-start(bf16[128,896]{1,0:T(8,128)(2,1)S(1)} %pad_maximum_fusion.13), channel_id=1, source_target_pairs={{0,4},{2,6},{4,0},{6,2},{8,12},{10,14},{12,8},{14,10},{16,20},{18,... | collective-permute-start | bytes 688136 | tf_op jit(solution)/shard_map/ppermute | solution.py:781
  18.1 36.1 %collective-permute-start = (bf16[384,768]{1,0:T(8,128)(2,1)}, bf16[384,768]{1,0:T(8,128)(2,1)}, u32[]{:S(2)}, u32[]{:S(2)}) collective-permute-start(bf16[384,768]{1,0:T(8,128)(2,1)} %get-tuple-element.224), channel_id=1, source_target_pairs={{0,1},{1,0},{2,3},{3,2},{4,5},{5,4},{6,7},{7,6},{8,9},{9,8},{10,11... | collective-permute-start | bytes 1769480 | tf_op jit(solution)/shard_map/ppermute | solution.py:784
  25.4 13.3 %collective-permute-start.7 = (bf16[2,128,896]{2,1,0:T(8,128)(2,1)}, bf16[2,128,896]{2,1,0:T(8,128)(2,1)S(1)}, u32[]{:S(2)}, u32[]{:S(2)}) collective-permute-start(bf16[2,128,896]{2,1,0:T(8,128)(2,1)} %get-tuple-element.228), channel_id=1, source_target_pairs={{8,0},{10,2},{12,4},{14,6},{16,8},{18,10},{20,12},{22,14},{24,16},... | collective-permute-start | bytes 1376264 | tf_op jit(solution)/shard_map/ppermute | solution.py:818
  26.7 13.3 %collective-permute-start.5 = (bf16[2,128,896]{2,1,0:T(8,128)(2,1)}, bf16[2,128,896]{2,1,0:T(8,128)(2,1)S(1)}, u32[]{:S(2)}, u32[]{:S(2)}) collective-permute-start(bf16[2,128,896]{2,1,0:T(8,128)(2,1)} %get-tuple-element.228), channel_id=1, source_target_pairs={{0,8},{2,10},{4,12},{6,14},{8,16},{10,18},{12,20},{14,22},{16,24},... | collective-permute-start | bytes 1376264 | tf_op jit(solution)/shard_map/ppermute | solution.py:817
  32.1 12.6 %collective-permute-start.14 = (bf16[1,2,128,896]{3,2,1,0:T(8,128)(2,1)}, bf16[1,2,128,896]{3,2,1,0:T(8,128)(2,1)S(1)}, u32[]{:S(2)}, u32[]{:S(2)}) collective-permute-start(bf16[1,2,128,896]{3,2,1,0:T(8,128)(2,1)} %get-tuple-element.227), channel_id=1, source_target_pairs={{0,2},{2,0},{4,6},{6,4},{8,10},{10,8},{12,14},{14,12},{16,18},{18,... | collective-permute-start | bytes 1376264 | tf_op jit(solution)/shard_map/ppermute | solution.py:781
  32.1 22.1 %collective-permute-start.1 = (bf16[384,768]{1,0:T(8,128)(2,1)S(1)}, bf16[384,768]{1,0:T(8,128)(2,1)S(1)}, u32[]{:S(2)}, u32[]{:S(2)}) collective-permute-start(bf16[384,768]{1,0:T(8,128)(2,1)S(1)} %get-tuple-element.226), channel_id=1, source_target_pairs={{0,1},{1,0},{2,3},{3,2},{4,5},{5,4},{6,7},{7,6},{8,9},{9,8},{10,11... | collective-permute-start | bytes 1769480 | tf_op jit(solution)/shard_map/ppermute | solution.py:784
  38.8 12.2 %collective-permute-start.8 = (bf16[2,128,896]{2,1,0:T(8,128)(2,1)S(1)}, bf16[2,128,896]{2,1,0:T(8,128)(2,1)S(1)}, u32[]{:S(2)}, u32[]{:S(2)}) collective-permute-start(bf16[2,128,896]{2,1,0:T(8,128)(2,1)S(1)} %collective-permute-done.7), channel_id=1, source_target_pairs={{8,0},{10,2},{12,4},{14,6},{16,8},{18,10},{20,12},{22,14},{24,16},... | collective-permute-start | bytes 1376264 | tf_op jit(solution)/shard_map/ppermute | solution.py:818
  40.1 12.1 %collective-permute-start.6 = (bf16[2,128,896]{2,1,0:T(8,128)(2,1)S(1)}, bf16[2,128,896]{2,1,0:T(8,128)(2,1)S(1)}, u32[]{:S(2)}, u32[]{:S(2)}) collective-permute-start(bf16[2,128,896]{2,1,0:T(8,128)(2,1)S(1)} %collective-permute-done.5), channel_id=1, source_target_pairs={{0,8},{2,10},{4,12},{6,14},{8,16},{10,18},{12,20},{14,22},{16,24},... | collective-permute-start | bytes 1376264 | tf_op jit(solution)/shard_map/ppermute | solution.py:817
  44.7 9.6 %collective-permute-start.2 = (bf16[192,768]{1,0:T(8,128)(2,1)}, bf16[192,768]{1,0:T(8,128)(2,1)S(1)}, u32[]{:S(2)}, u32[]{:S(2)}) collective-permute-start(bf16[192,768]{1,0:T(8,128)(2,1)} %constant_dynamic-slice_fusion.10), channel_id=1, source_target_pairs={{0,1},{1,0},{2,3},{3,2},{4,5},{5,4},{6,7},{7,6},{8,9},{9,8},{10,11... | collective-permute-start | bytes 884744 | tf_op jit(solution)/shard_map/ppermute | solution.py:784
  51.0 8.4 %collective-permute-start.13 = (bf16[2,2,128,896]{3,2,1,0:T(8,128)(2,1)S(1)}, bf16[2,2,128,896]{3,2,1,0:T(8,128)(2,1)S(1)}, u32[]{:S(2)}, u32[]{:S(2)}) collective-permute-start(bf16[2,2,128,896]{3,2,1,0:T(8,128)(2,1)S(1)} %pad_maximum_fusion.7), channel_id=1, source_target_pairs={{0,2},{2,0},{4,6},{6,4},{8,10},{10,8},{12,14},{14,12},{16,18},{18,... | collective-permute-start | bytes 2752520 | tf_op jit(solution)/shard_map/ppermute | solution.py:781
  52.3 18.1 %collective-permute-start.12 = (bf16[2,2,128,896]{3,2,1,0:T(8,128)(2,1)S(1)}, bf16[2,2,128,896]{3,2,1,0:T(8,128)(2,1)S(1)}, u32[]{:S(2)}, u32[]{:S(2)}) collective-permute-start(bf16[2,2,128,896]{3,2,1,0:T(8,128)(2,1)S(1)} %pad_maximum_fusion.6), channel_id=1, source_target_pairs={{0,2},{2,0},{4,6},{6,4},{8,10},{10,8},{12,14},{14,12},{16,18},{18,... | collective-permute-start | bytes 2752520 | tf_op jit(solution)/shard_map/ppermute | solution.py:781
  55.5 16.5 %collective-permute-start.11 = (bf16[96,3072]{1,0:T(8,128)(2,1)S(1)}, bf16[96,3072]{1,0:T(8,128)(2,1)S(1)}, u32[]{:S(2)}, u32[]{:S(2)}) collective-permute-start(bf16[96,3072]{1,0:T(8,128)(2,1)S(1)} %constant_dynamic-slice_fusion.8), channel_id=1, source_target_pairs={{0,1},{1,0},{2,3},{3,2},{4,5},{5,4},{6,7},{7,6},{8,9},{9,8},{10,11... | collective-permute-start | bytes 1769480 | tf_op jit(solution)/shard_map/ppermute | solution.py:784
  58.1 24.7 %collective-permute-start.10 = (bf16[384,768]{1,0:T(8,128)(2,1)S(1)}, bf16[384,768]{1,0:T(8,128)(2,1)S(1)}, u32[]{:S(2)}, u32[]{:S(2)}) collective-permute-start(bf16[384,768]{1,0:T(8,128)(2,1)S(1)} %constant_dynamic-slice_fusion.9), channel_id=1, source_target_pairs={{0,1},{1,0},{2,3},{3,2},{4,5},{5,4},{6,7},{7,6},{8,9},{9,8},{10,11... | collective-permute-start | bytes 1769480 | tf_op jit(solution)/shard_map/ppermute | solution.py:784
  59.4 2.4 collective-permute-start.15
  72.0 29.1 %collective-permute-start.16 = (bf16[96,3072]{1,0:T(8,128)(2,1)S(1)}, bf16[96,3072]{1,0:T(8,128)(2,1)S(1)}, u32[]{:S(2)}, u32[]{:S(2)}) collective-permute-start(bf16[96,3072]{1,0:T(8,128)(2,1)S(1)} %collective-permute-done.11.refs_4_), channel_id=1, source_target_pairs={{0,4},{2,6},{4,0},{6,2},{8,12},{10,14},{12,8},{14,10},{16,20},{18,... | collective-permute-start | bytes 1769480 | tf_op jit(solution)/shard_map/ppermute | solution.py:781
  82.9 18.3 %collective-permute-start.17 = (bf16[384,768]{1,0:T(8,128)(2,1)S(1)}, bf16[384,768]{1,0:T(8,128)(2,1)S(1)}, u32[]{:S(2)}, u32[]{:S(2)}) collective-permute-start(bf16[384,768]{1,0:T(8,128)(2,1)S(1)} %collective-permute-done.10.refs_9_), channel_id=1, source_target_pairs={{0,4},{2,6},{4,0},{6,2},{8,12},{10,14},{12,8},{14,10},{16,20},{18,... | collective-permute-start | bytes 1769480 | tf_op jit(solution)/shard_map/ppermute | solution.py:781
  101.2 6.7 %collective-permute-start.19 = (bf16[96,3072]{1,0:T(8,128)(2,1)S(1)}, bf16[96,3072]{1,0:T(8,128)(2,1)S(1)}, u32[]{:S(2)}, u32[]{:S(2)}) collective-permute-start(bf16[96,3072]{1,0:T(8,128)(2,1)S(1)} %collective-permute-done.11.refs_4_), channel_id=1, source_target_pairs={{0,2},{2,0},{4,6},{6,4},{8,10},{10,8},{12,14},{14,12},{16,18},{18,... | collective-permute-start | bytes 1769480 | tf_op jit(solution)/shard_map/ppermute | solution.py:781
  101.3 7.0 %collective-permute-start.20 = (bf16[96,3072]{1,0:T(8,128)(2,1)S(1)}, bf16[96,3072]{1,0:T(8,128)(2,1)S(1)}, u32[]{:S(2)}, u32[]{:S(2)}) collective-permute-start(bf16[96,3072]{1,0:T(8,128)(2,1)S(1)} %collective-permute-done.16.refs_5_), channel_id=1, source_target_pairs={{0,2},{2,0},{4,6},{6,4},{8,10},{10,8},{12,14},{14,12},{16,18},{18,... | collective-permute-start | bytes 1769480 | tf_op jit(solution)/shard_map/ppermute | solution.py:781
  101.8 6.5 %collective-permute-start.21 = (bf16[384,768]{1,0:T(8,128)(2,1)S(1)}, bf16[384,768]{1,0:T(8,128)(2,1)S(1)}, u32[]{:S(2)}, u32[]{:S(2)}) collective-permute-start(bf16[384,768]{1,0:T(8,128)(2,1)S(1)} %collective-permute-done.10.refs_9_), channel_id=1, source_target_pairs={{0,2},{2,0},{4,6},{6,4},{8,10},{10,8},{12,14},{14,12},{16,18},{18,... | collective-permute-start | bytes 1769480 | tf_op jit(solution)/shard_map/ppermute | solution.py:781
  101.8 6.4 %collective-permute-start.22 = (bf16[384,768]{1,0:T(8,128)(2,1)S(1)}, bf16[384,768]{1,0:T(8,128)(2,1)S(1)}, u32[]{:S(2)}, u32[]{:S(2)}) collective-permute-start(bf16[384,768]{1,0:T(8,128)(2,1)S(1)} %collective-permute-done.17.refs_10_), channel_id=1, source_target_pairs={{0,2},{2,0},{4,6},{6,4},{8,10},{10,8},{12,14},{14,12},{16,18},{18,... | collective-permute-start | bytes 1769480 | tf_op jit(solution)/shard_map/ppermute | solution.py:781
  102.3 3.9 %collective-permute-start.18 = (bf16[192,768]{1,0:T(8,128)(2,1)S(1)}, bf16[192,768]{1,0:T(8,128)(2,1)S(1)}, u32[]{:S(2)}, u32[]{:S(2)}) collective-permute-start(bf16[192,768]{1,0:T(8,128)(2,1)S(1)} %collective-permute-done.2.refs_1_), channel_id=1, source_target_pairs={{0,2},{2,0},{4,6},{6,4},{8,10},{10,8},{12,14},{14,12},{16,18},{18,... | collective-permute-start | bytes 884744 | tf_op jit(solution)/shard_map/ppermute | solution.py:781
  106.2 16.0 %collective-permute-start.25 = (bf16[128,768]{1,0:T(8,128)(2,1)S(1)}, bf16[128,768]{1,0:T(8,128)(2,1)}, u32[]{:S(2)}, u32[]{:S(2)}) collective-permute-start(bf16[128,768]{1,0:T(8,128)(2,1)S(1)} %bitcast.168), channel_id=1, source_target_pairs={{0,1},{1,0},{2,3},{3,2},{4,5},{5,4},{6,7},{7,6},{8,9},{9,8},{10,11... | collective-permute-start | bytes 589832 | tf_op jit(solution)/shard_map/ppermute | solution.py:784
  107.9 14.3 %collective-permute-start.24 = (bf16[128,768]{1,0:T(8,128)(2,1)}, bf16[128,768]{1,0:T(8,128)(2,1)S(1)}, u32[]{:S(2)}, u32[]{:S(2)}) collective-permute-start(bf16[128,768]{1,0:T(8,128)(2,1)} %get-tuple-element.136), channel_id=1, source_target_pairs={{0,1},{1,0},{2,3},{3,2},{4,5},{5,4},{6,7},{7,6},{8,9},{9,8},{10,11... | collective-permute-start | bytes 589832 | tf_op jit(solution)/shard_map/ppermute | solution.py:784
  120.4 6.8 %collective-permute-start.23 = (bf16[128,768]{1,0:T(8,128)(2,1)}, bf16[128,768]{1,0:T(8,128)(2,1)S(1)}, u32[]{:S(2)}, u32[]{:S(2)}) collective-permute-start(bf16[128,768]{1,0:T(8,128)(2,1)} %get-tuple-element.132.do_ref), channel_id=1, source_target_pairs={{0,1},{1,0},{2,3},{3,2},{4,5},{5,4},{6,7},{7,6},{8,9},{9,8},{10,11... | collective-permute-start | bytes 589832 | tf_op jit(solution)/shard_map/ppermute | solution.py:784
  143.5 155.5 %all-gather.3.cloned.1.call-start = ((), (), s32[]{:S(2)}) async-start(), calls=%async_computation.2 | async-start | bytes 5013504 | tf_op jit(solution)/shard_map/all_gather | solution.py:1049
  171.7 11.1 %collective-permute-start.26 = (bf16[8,768,128]{2,1,0:T(8,128)(2,1)}, bf16[8,768,128]{2,1,0:T(8,128)(2,1)S(1)}, u32[]{:S(2)}, u32[]{:S(2)}) collective-permute-start(bf16[8,768,128]{2,1,0:T(8,128)(2,1)} %get-tuple-element.141), channel_id=1, source_target_pairs={{0,2},{2,0},{4,6},{6,4},{8,10},{10,8},{12,14},{14,12},{16,18},{18,... | collective-permute-start | bytes 4718600 | tf_op jit(solution)/shard_map/ppermute | solution.py:781
  182.8 12.7 %collective-permute-start.27 = (bf16[768,768]{1,0:T(8,128)(2,1)}, bf16[768,768]{1,0:T(8,128)(2,1)}, u32[]{:S(2)}, u32[]{:S(2)}) collective-permute-start(bf16[768,768]{1,0:T(8,128)(2,1)} %get-tuple-element.155), channel_id=1, source_target_pairs={{0,2},{2,0},{4,6},{6,4},{8,10},{10,8},{12,14},{14,12},{16,18},{18,... | collective-permute-start | bytes 3538952 | tf_op jit(solution)/shard_map/ppermute | solution.py:781
  185.3 12.9 %collective-permute-start.32 = (bf16[128,768]{1,0:T(8,128)(2,1)}, bf16[128,768]{1,0:T(8,128)(2,1)}, u32[]{:S(2)}, u32[]{:S(2)}) collective-permute-start(bf16[128,768]{1,0:T(8,128)(2,1)} %get-tuple-element.160.dq_ref), channel_id=1, source_target_pairs={{0,1},{1,0},{2,3},{3,2},{4,5},{5,4},{6,7},{7,6},{8,9},{9,8},{10,11... | collective-permute-start | bytes 589832 | tf_op jit(solution)/shard_map/ppermute | solution.py:784
  186.8 9.9 %collective-permute-start.31 = (bf16[128,768]{1,0:T(8,128)(2,1)}, bf16[128,768]{1,0:T(8,128)(2,1)}, u32[]{:S(2)}, u32[]{:S(2)}) collective-permute-start(bf16[128,768]{1,0:T(8,128)(2,1)} %get-tuple-element.159), channel_id=1, source_target_pairs={{0,1},{1,0},{2,3},{3,2},{4,5},{5,4},{6,7},{7,6},{8,9},{9,8},{10,11... | collective-permute-start | bytes 589832 | tf_op jit(solution)/shard_map/ppermute | solution.py:784
  195.5 7.7 %collective-permute-start.28 = (bf16[448,768]{1,0:T(8,128)(2,1)}, bf16[448,768]{1,0:T(8,128)(2,1)S(1)}, u32[]{:S(2)}, u32[]{:S(2)}) collective-permute-start(bf16[448,768]{1,0:T(8,128)(2,1)} %get-tuple-element.158), channel_id=1, source_target_pairs={{0,2},{2,0},{4,6},{6,4},{8,10},{10,8},{12,14},{14,12},{16,18},{18,... | collective-permute-start | bytes 2064392 | tf_op jit(solution)/shard_map/ppermute | solution.py:781
  199.7 5.4 %collective-permute-start.33 = (bf16[768,384]{1,0:T(8,128)(2,1)S(1)}, bf16[768,384]{1,0:T(8,128)(2,1)S(1)}, u32[]{:S(2)}, u32[]{:S(2)}) collective-permute-start(bf16[768,384]{1,0:T(8,128)(2,1)S(1)} %get-tuple-element.251), channel_id=1, source_target_pairs={{0,2},{2,0},{4,6},{6,4},{8,10},{10,8},{12,14},{14,12},{16,18},{18,... | collective-permute-start | bytes 1769480 | tf_op jit(solution)/shard_map/ppermute | solution.py:781
  199.8 23.1 %collective-permute-start.30 = (bf16[2,2,768,128]{3,2,0,1:T(8,128)(2,1)S(1)}, bf16[2,2,768,128]{3,2,0,1:T(8,128)(2,1)S(1)}, u32[]{:S(2)}, u32[]{:S(2)}) collective-permute-start(bf16[2,2,768,128]{3,2,0,1:T(8,128)(2,1)S(1)} %bitcast.179), channel_id=1, source_target_pairs={{0,4},{2,6},{4,0},{6,2},{8,12},{10,14},{12,8},{14,10},{16,20},{18,... | collective-permute-start | bytes 2359304 | tf_op jit(solution)/shard_map/ppermute | solution.py:781
  203.6 22.9 %collective-permute-start.29 = (bf16[1216,384]{1,0:T(8,128)(2,1)S(1)}, bf16[1216,384]{1,0:T(8,128)(2,1)}, u32[]{:S(2)}, u32[]{:S(2)}) collective-permute-start(bf16[1216,384]{1,0:T(8,128)(2,1)S(1)} %broadcast_select_fusion.2), channel_id=1, source_target_pairs={{0,1},{1,0},{2,3},{3,2},{4,5},{5,4},{6,7},{7,6},{8,9},{9,8},{10,11... | collective-permute-start | bytes 2801672 | tf_op jit(solution)/shard_map/ppermute | solution.py:784
  228.7 21.5 %collective-permute-start.34 = (bf16[2,2,248,384]{3,2,0,1:T(8,128)(2,1)S(1)}, bf16[2,2,248,384]{3,2,0,1:T(8,128)(2,1)S(1)}, u32[]{:S(2)}, u32[]{:S(2)}) collective-permute-start(bf16[2,2,248,384]{3,2,0,1:T(8,128)(2,1)S(1)} %bitcast.180), channel_id=1, source_target_pairs={{0,4},{2,6},{4,0},{6,2},{8,12},{10,14},{12,8},{14,10},{16,20},{18,... | collective-permute-start | bytes 2285576 | tf_op jit(solution)/shard_map/ppermute | solution.py:781
  229.0 15.1 %collective-permute-start.35 = (bf16[2,768,128]{2,1,0:T(8,128)(2,1)S(1)}, bf16[2,768,128]{2,1,0:T(8,128)(2,1)}, u32[]{:S(2)}, u32[]{:S(2)}) collective-permute-start(bf16[2,768,128]{2,1,0:T(8,128)(2,1)S(1)} %dynamic-slice_bitcast_fusion), channel_id=1, source_target_pairs={{0,8},{2,10},{4,12},{6,14},{8,0},{10,2},{12,4},{14,6},{16,24},{18,... | collective-permute-start | bytes 1179656 | tf_op jit(solution)/shard_map/ppermute | solution.py:781
  250.4 14.5 %collective-permute-start.36 = (bf16[2,248,384]{2,1,0:T(8,128)(2,1)S(1)}, bf16[2,248,384]{2,1,0:T(8,128)(2,1)S(1)}, u32[]{:S(2)}, u32[]{:S(2)}) collective-permute-start(bf16[2,248,384]{2,1,0:T(8,128)(2,1)S(1)} %dynamic-slice_bitcast_fusion.1), channel_id=1, source_target_pairs={{0,8},{2,10},{4,12},{6,14},{8,0},{10,2},{12,4},{14,6},{16,24},{18,... | collective-permute-start | bytes 1142792 | tf_op jit(solution)/shard_map/ppermute | solution.py:781
  265.1 22.4 %collective-permute-start.37 = (bf16[248,384]{1,0:T(8,128)(2,1)S(1)}, bf16[248,384]{1,0:T(8,128)(2,1)S(1)}, u32[]{:S(2)}, u32[]{:S(2)}) collective-permute-start(bf16[248,384]{1,0:T(8,128)(2,1)S(1)} %dynamic-slice_bitcast_fusion.3), channel_id=1, source_target_pairs={{0,16},{2,18},{4,20},{6,22},{8,24},{10,26},{12,28},{14,30},{16,0},... | collective-permute-start | bytes 571400 | tf_op jit(solution)/shard_map/ppermute | solution.py:781
  287.6 4.6 %collective-permute-start.39 = (bf16[120,384]{1,0:T(8,128)(2,1)S(1)}, bf16[120,384]{1,0:T(8,128)(2,1)S(1)}, u32[]{:S(2)}, u32[]{:S(2)}) collective-permute-start(bf16[120,384]{1,0:T(8,128)(2,1)S(1)} %slice.61), channel_id=1, source_target_pairs={{0,4},{2,6},{4,0},{6,2},{8,12},{10,14},{12,8},{14,10},{16,20},{18,... | collective-permute-start | bytes 276488 | tf_op jit(solution)/shard_map/ppermute | solution.py:781
  287.7 11.2 %collective-permute-start.38 = (bf16[128,384]{1,0:T(8,128)(2,1)S(1)}, bf16[128,384]{1,0:T(8,128)(2,1)S(1)}, u32[]{:S(2)}, u32[]{:S(2)}) collective-permute-start(bf16[128,384]{1,0:T(8,128)(2,1)S(1)} %slice.60), channel_id=1, source_target_pairs={{0,16},{2,18},{4,20},{6,22},{8,24},{10,26},{12,28},{14,30},{16,0},... | collective-permute-start | bytes 294920 | tf_op jit(solution)/shard_map/ppermute | solution.py:781
  299.0 9.7 %collective-permute-start.41 = (bf16[2,120,384]{2,1,0:T(8,128)(2,1)S(1)}, bf16[2,120,384]{2,1,0:T(8,128)(2,1)S(1)}, u32[]{:S(2)}, u32[]{:S(2)}) collective-permute-start(bf16[2,120,384]{2,1,0:T(8,128)(2,1)S(1)} %pad_maximum_fusion.15), channel_id=1, source_target_pairs={{0,16},{2,18},{4,20},{6,22},{8,24},{10,26},{12,28},{14,30},{16,0},... | collective-permute-start | bytes 552968 | tf_op jit(solution)/shard_map/ppermute | solution.py:781
  299.1 14.4 %collective-permute-start.42 = (bf16[768,128]{1,0:T(8,128)(2,1)S(1)}, bf16[768,128]{1,0:T(8,128)(2,1)S(1)}, u32[]{:S(2)}, u32[]{:S(2)}) collective-permute-start(bf16[768,128]{1,0:T(8,128)(2,1)S(1)} %dynamic-slice_bitcast_fusion.2), channel_id=1, source_target_pairs={{0,16},{2,18},{4,20},{6,22},{8,24},{10,26},{12,28},{14,30},{16,0},... | collective-permute-start | bytes 589832 | tf_op jit(solution)/shard_map/ppermute | solution.py:781
  302.1 11.4 %collective-permute-start.40 = (bf16[2,128,384]{2,1,0:T(8,128)(2,1)S(1)}, bf16[2,128,384]{2,1,0:T(8,128)(2,1)S(1)}, u32[]{:S(2)}, u32[]{:S(2)}) collective-permute-start(bf16[2,128,384]{2,1,0:T(8,128)(2,1)S(1)} %pad_maximum_fusion.14), channel_id=1, source_target_pairs={{0,8},{2,10},{4,12},{6,14},{8,0},{10,2},{12,4},{14,6},{16,24},{18,... | collective-permute-start | bytes 589832 | tf_op jit(solution)/shard_map/ppermute | solution.py:781
  314.3 7.5 %collective-permute-start.44 = (bf16[2,2,120,384]{3,2,1,0:T(8,128)(2,1)S(1)}, bf16[2,2,120,384]{3,2,1,0:T(8,128)(2,1)S(1)}, u32[]{:S(2)}, u32[]{:S(2)}) collective-permute-start(bf16[2,2,120,384]{3,2,1,0:T(8,128)(2,1)S(1)} %pad_maximum_fusion.12), channel_id=1, source_target_pairs={{0,8},{2,10},{4,12},{6,14},{8,0},{10,2},{12,4},{14,6},{16,24},{18,... | collective-permute-start | bytes 1105928 | tf_op jit(solution)/shard_map/ppermute | solution.py:781
  314.3 8.2 %collective-permute-start.43 = (bf16[2,2,128,384]{3,2,0,1:T(8,128)(2,1)S(1)}, bf16[2,2,128,384]{3,2,0,1:T(8,128)(2,1)S(1)}, u32[]{:S(2)}, u32[]{:S(2)}) collective-permute-start(bf16[2,2,128,384]{3,2,0,1:T(8,128)(2,1)S(1)} %pad_maximum_fusion.11), channel_id=1, source_target_pairs={{0,4},{2,6},{4,0},{6,2},{8,12},{10,14},{12,8},{14,10},{16,20},{18,... | collective-permute-start | bytes 1179656 | tf_op jit(solution)/shard_map/ppermute | solution.py:781
  322.8 3.4 collective-permute-start.45
  322.9 3.3 collective-permute-start.46
  (38 other events, 252.3 us)
Sparse Core Ops, SparseCore 0:
  143.6 80.0 reduce-scatter.1
  226.7 65.0 all-gather.2
